TPU v7x, 32 devices: a whole 2x2x4 slice. The times are simulated.
32 devices in a mesh: section: 4 (over y, x), dp: 8 (over z, core).
Axes of the slice: x: 2, y: 2, z: 4, core: 2. Of those that a mesh axis runs over, the one named last changes fastest.
Arguments:
- latents: float32 [32, 256, 16], P('dp'), may hold values from -6 to 6
- noise: float32 [32, 256, 16], P('dp'), may hold values from -6 to 6
- timesteps: int32 [32], P('dp'), may hold values from 0 to 999
- labels: int32 [32], P('dp'), may hold values from 0 to 999
- patch_mask: int32 [32, 256], P('dp'), may hold values from 0 to 1, as said below
- w_in: float32 [4, 1152, 16128], P('section', 'dp'), may hold values from -0.1875 to 0.1875
- w_down: float32 [4, 4608, 1152], P('section', 'dp'), may hold values from -0.09375 to 0.09375
- b_blk: float32 [4, 16128], P('section', 'dp'), may hold values from -1.25 to 1.25
- small_mats: float32 [1152, 4744], P('dp', 'section')
- small_bias: float32 [5776], P('section'), may hold values from -1.25 to 1.25
- m_in: float32 [4, 1152, 16128], P('section', 'dp'), may hold values from -5.9604645e-07 to 5.9604645e-07
- m_down: float32 [4, 4608, 1152], P('section', 'dp'), may hold values from -5.722046e-06 to 5.722046e-06
- m_bias: float32 [4, 16128], P('section', 'dp'), may hold values from -1.9073486e-06 to 1.9073486e-06
- m_small: float32 [1152, 4744], P('dp', 'section'), may hold values from -5.722046e-06 to 5.722046e-06
- m_sbias: float32 [5776], P('section'), may hold values from -2.2888184e-05 to 2.2888184e-05
- v_in: float32 [4, 1152, 16128], P('section', 'dp'), may hold values from 4.946241e-18 to 7.9139857e-17
- v_down: float32 [4, 4608, 1152], P('section', 'dp'), may hold values from 4.946241e-18 to 7.9139857e-17
- v_bias: float32 [4, 16128], P('section', 'dp'), may hold values from 7.9139857e-17 to 1.2662377e-15
- v_small: float32 [1152, 4744], P('dp', 'section'), may hold values from 4.946241e-18 to 8.6805556e-15
- v_sbias: float32 [5776], P('section'), may hold values from 7.9139857e-17 to 1.2662377e-15
Outputs:
- loss: float32 [], replicated
- grad_norm: float32 [], replicated
- w_in_new: float32 [4, 1152, 16128], P('section', 'dp')
- m_in_new: float32 [4, 1152, 16128], P('section', 'dp')
- v_in_new: float32 [4, 1152, 16128], P('section', 'dp')
- w_down_new: float32 [4, 4608, 1152], P('section', 'dp')
- m_down_new: float32 [4, 4608, 1152], P('section', 'dp')
- v_down_new: float32 [4, 4608, 1152], P('section', 'dp')
- b_blk_new: float32 [4, 16128], P('section', 'dp')
- m_bias_new: float32 [4, 16128], P('section', 'dp')
- v_bias_new: float32 [4, 16128], P('section', 'dp')
- small_mats_new: float32 [1152, 4744], P('dp', 'section')
- m_small_new: float32 [1152, 4744], P('dp', 'section')
- v_small_new: float32 [1152, 4744], P('dp', 'section')
- small_bias_new: float32 [5776], P('section')
- m_sbias_new: float32 [5776], P('section')
- v_sbias_new: float32 [5776], P('section')
Inputs may be any that keep to these rules, and one draw needn't show every extreme that they name: `patch_mask`: the first patch of every image counts.
All inputs are finite; a program needn't handle non-finite values.
Results may differ from a plain program's by a relative error of at most 0.0022.
Values may be sent and summed in bfloat16 or wider, within the bound.
A program may use at most 640 MiB of HBM per device.

v0:
```python
import math

import jax
import jax.numpy as jnp
from jax import lax
from jax.sharding import PartitionSpec as P

D = 1152
HEADS = 16
HEAD_DIM = 72
FF = 4608
CLASSES = 1000
FREQ = 256
PATCH_IN = 16
GRID = 16
MICRO = 2


EPS_NORM = 1e-06
CLIP = 0.001
RATE = 0.005
BETA_ONE = 0.9
BETA_TWO = 0.999
ADAM_EPS = 1e-08
DECAY = 0.01
STEP_POWER = 10.0


def passed_along(value, axis, steps):
    count = lax.axis_size(axis)
    first, last = (max(0, -steps), min(count, count - steps))
    return lax.ppermute(value, axis, [(source, source + steps) for source in range(first, last)])


def matmul(left_side, right_side):
    return jnp.dot(left_side, right_side, preferred_element_type=jnp.float32)


def matmul_tn(left_side, right_side):
    return lax.dot_general(
        left_side, right_side, (((0,), (0,)), ((), ())), preferred_element_type=jnp.float32
    )


def matmul_nt(left_side, right_side):
    return lax.dot_general(
        left_side, right_side, (((1,), (1,)), ((), ())), preferred_element_type=jnp.float32
    )


def column_sum(values):
    return jnp.sum(values.astype(jnp.float32), axis=0)


def normalize(values):
    center = values - jnp.mean(values, axis=-1, keepdims=True)
    invstd = lax.rsqrt(jnp.mean(center * center, axis=-1, keepdims=True) + EPS_NORM)
    return (center * invstd, invstd)


def norm_back(grad_normed, normed, invstd):
    return invstd * (
        grad_normed
        - jnp.mean(grad_normed, axis=-1, keepdims=True)
        - normed * jnp.mean(grad_normed * normed, axis=-1, keepdims=True)
    )


def gelu_tanh(values):
    return (
        0.5
        * values
        * (1.0 + jnp.tanh(0.7978845608028654 * (values + 0.044715 * values * values * values)))
    )


def gelu_grad(values):
    inner = jnp.tanh(0.7978845608028654 * (values + 0.044715 * values * values * values))
    return 0.5 * (1.0 + inner) + 0.5 * values * (1.0 - inner * inner) * 0.7978845608028654 * (
        1.0 + 0.134145 * values * values
    )


def silu_grad(values):
    sigma = jax.nn.sigmoid(values)
    return sigma * (1.0 + values * (1.0 - sigma))


def positions(patches):
    quarter = D // 4
    omega = jnp.exp(-math.log(10000.0) * jnp.arange(quarter, dtype=jnp.float32) / quarter)
    spot = jnp.arange(patches, dtype=jnp.int32)
    row_angle = (spot // GRID).astype(jnp.float32)[:, None] * omega[None, :]
    col_angle = (spot % GRID).astype(jnp.float32)[:, None] * omega[None, :]
    return jnp.concatenate(
        [jnp.sin(row_angle), jnp.cos(row_angle), jnp.sin(col_angle), jnp.cos(col_angle)], axis=1
    )


def time_features(time_steps):
    half = FREQ // 2
    freqs = jnp.exp(-math.log(10000.0) * jnp.arange(half, dtype=jnp.float32) / half)
    angles = time_steps.astype(jnp.float32)[:, None] * freqs[None, :]
    return jnp.concatenate([jnp.cos(angles), jnp.sin(angles)], axis=1)


def alpha_bar(time_steps):
    return jnp.cos((time_steps.astype(jnp.float32) / 1000.0 + 0.008) / 1.008 * (math.pi / 2)) ** 2


def label_table(label_part):
    return (label_part[:, None] == jnp.arange(CLASSES, dtype=jnp.int32)[None, :]).astype(
        jnp.bfloat16
    )


def time_side(time_part, small_full, small_used):
    time_low = time_features(time_part).astype(jnp.bfloat16)
    time_hidden = (
        matmul_nt(time_low, small_full[:, PATCH_IN : PATCH_IN + FREQ]) + small_used[D : 2 * D]
    )
    time_act = jax.nn.silu(time_hidden).astype(jnp.bfloat16)
    return (time_low, time_hidden, time_act)


def attend(qkv_low, images, patches):
    by_head = qkv_low.reshape(images, patches, 3, HEADS, HEAD_DIM)
    scores = jnp.einsum(
        "bqhe,bkhe->bhqk", by_head[:, :, 0], by_head[:, :, 1], preferred_element_type=jnp.float32
    ) * HEAD_DIM ** (-0.5)
    log_total = jax.nn.logsumexp(scores, axis=-1)
    attention_low = jnp.exp(scores - log_total[..., None]).astype(jnp.bfloat16)
    attended = jnp.einsum(
        "bhqk,bkhe->bqhe", attention_low, by_head[:, :, 2], preferred_element_type=jnp.float32
    )
    return (attended.reshape(images * patches, D), log_total)


def attend_back(qkv_low, log_total, d_att, images, patches):
    by_head = qkv_low.reshape(images, patches, 3, HEADS, HEAD_DIM)
    queries, key_heads, value_heads = (by_head[:, :, 0], by_head[:, :, 1], by_head[:, :, 2])
    scaling = HEAD_DIM ** (-0.5)
    scores = (
        jnp.einsum("bqhe,bkhe->bhqk", queries, key_heads, preferred_element_type=jnp.float32)
        * scaling
    )
    attention = jnp.exp(scores - log_total[..., None])
    grad_heads = d_att.reshape(images, patches, HEADS, HEAD_DIM)
    d_probs = jnp.einsum(
        "bqhe,bkhe->bhqk", grad_heads, value_heads, preferred_element_type=jnp.float32
    )
    d_scores = (
        attention * (d_probs - jnp.sum(attention * d_probs, axis=-1, keepdims=True))
    ).astype(jnp.bfloat16)
    d_query = (
        jnp.einsum("bhqk,bkhe->bqhe", d_scores, key_heads, preferred_element_type=jnp.float32)
        * scaling
    )
    d_key = (
        jnp.einsum("bhqk,bqhe->bkhe", d_scores, queries, preferred_element_type=jnp.float32)
        * scaling
    )
    d_value = jnp.einsum(
        "bhqk,bqhe->bkhe",
        attention.astype(jnp.bfloat16),
        grad_heads,
        preferred_element_type=jnp.float32,
    )
    return (
        jnp.stack([d_query, d_key, d_value], axis=2)
        .astype(jnp.bfloat16)
        .reshape(images * patches, 3 * D)
    )


def block_forward(residual, condition, weights):
    w_full, w_second, b_full = weights
    bias_full = b_full.astype(jnp.float32)
    images, patches = (residual.shape[0], residual.shape[1])
    row_count = images * patches
    ada_at = 4 * D + FF
    act_cond = jax.nn.silu(condition).astype(jnp.bfloat16)
    ada = matmul(act_cond, w_full[:, ada_at:]) + bias_full[ada_at:]
    modulation = jnp.split(ada, 6, axis=1)
    normed_one, invstd_one = normalize(residual)
    mixed_one = (
        (normed_one * (1.0 + modulation[1][:, None]) + modulation[0][:, None])
        .astype(jnp.bfloat16)
        .reshape(row_count, D)
    )
    qkv_bias = jnp.concatenate([bias_full[:D], jnp.zeros((D,), jnp.float32), bias_full[D : 2 * D]])
    qkv_low = (matmul(mixed_one, w_full[:, : 3 * D]) + qkv_bias).astype(jnp.bfloat16)
    attended, log_total = attend(qkv_low, images, patches)
    att_low = attended.astype(jnp.bfloat16)
    branch = (matmul(att_low, w_full[:, 3 * D : 4 * D]) + bias_full[2 * D : 3 * D]).reshape(
        images, patches, D
    )
    middle = residual + modulation[2][:, None] * branch
    normed_two, invstd_two = normalize(middle)
    mixed_two = (
        (normed_two * (1.0 + modulation[4][:, None]) + modulation[3][:, None])
        .astype(jnp.bfloat16)
        .reshape(row_count, D)
    )
    pre_act = matmul(mixed_two, w_full[:, 4 * D : ada_at]) + bias_full[3 * D : 3 * D + FF]
    act_low = gelu_tanh(pre_act).astype(jnp.bfloat16)
    second = (matmul(act_low, w_second) + bias_full[3 * D + FF : ada_at]).reshape(
        images, patches, D
    )
    output = middle + modulation[5][:, None] * second
    kept_items = (
        condition,
        act_cond,
        ada,
        normed_one,
        invstd_one,
        mixed_one,
        qkv_low,
        log_total,
        att_low,
        branch,
        normed_two,
        invstd_two,
        mixed_two,
        pre_act,
        second,
    )
    return (output, kept_items)


def kept_zeros(micro, per_batch, patches):
    row_count = per_batch * patches
    stored_shape = (row_count, FF)
    wide_float = jnp.float32
    narrow = jnp.bfloat16
    shapes = [
        ((per_batch, D), wide_float),
        ((per_batch, D), narrow),
        ((per_batch, 6 * D), wide_float),
        ((per_batch, patches, D), wide_float),
        ((per_batch, patches, 1), wide_float),
        ((row_count, D), narrow),
        ((row_count, 3 * D), narrow),
        ((per_batch, HEADS, patches), wide_float),
        ((row_count, D), narrow),
        ((per_batch, patches, D), wide_float),
        ((per_batch, patches, D), wide_float),
        ((per_batch, patches, 1), wide_float),
        ((row_count, D), narrow),
        (stored_shape, wide_float),
        ((per_batch, patches, D), wide_float),
    ]
    return tuple((jnp.zeros((micro,) + shape, kind) for shape, kind in shapes))


def block_backward(grad_out, grad_cond, kept_items, weights):
    w_full, w_second, b_full = weights
    (
        condition,
        act_cond,
        ada,
        normed_one,
        invstd_one,
        mixed_one,
        qkv_low,
        log_total,
        att_low,
        branch,
        normed_two,
        invstd_two,
        mixed_two,
        stored,
        second,
    ) = kept_items
    images, patches = (grad_out.shape[0], grad_out.shape[1])
    row_count = images * patches
    ada_at = 4 * D + FF
    modulation = jnp.split(ada, 6, axis=1)
    act_low = gelu_tanh(stored).astype(jnp.bfloat16)
    d_second = (grad_out * modulation[5][:, None]).astype(jnp.bfloat16).reshape(row_count, D)
    d_gate_two = jnp.sum(grad_out * second, axis=1)
    g_down = matmul_tn(act_low, d_second)
    d_pre = (matmul_nt(d_second, w_second) * gelu_grad(stored)).astype(jnp.bfloat16)
    g_hidden = matmul_tn(mixed_two, d_pre)
    d_mixed_two = matmul_nt(d_pre, w_full[:, 4 * D : ada_at]).reshape(images, patches, D)
    d_shift_two = jnp.sum(d_mixed_two, axis=1)
    d_scale_two = jnp.sum(d_mixed_two * normed_two, axis=1)
    d_middle = grad_out + norm_back(
        d_mixed_two * (1.0 + modulation[4][:, None]), normed_two, invstd_two
    )
    d_gate_one = jnp.sum(d_middle * branch, axis=1)
    d_branch = (d_middle * modulation[2][:, None]).astype(jnp.bfloat16).reshape(row_count, D)
    g_proj = matmul_tn(att_low, d_branch)
    d_att = matmul_nt(d_branch, w_full[:, 3 * D : 4 * D]).astype(jnp.bfloat16)
    d_qkv = attend_back(qkv_low, log_total, d_att, images, patches)
    g_qkv = matmul_tn(mixed_one, d_qkv)
    d_mixed_one = matmul_nt(d_qkv, w_full[:, : 3 * D]).reshape(images, patches, D)
    d_shift_one = jnp.sum(d_mixed_one, axis=1)
    d_scale_one = jnp.sum(d_mixed_one * normed_one, axis=1)
    d_residual = d_middle + norm_back(
        d_mixed_one * (1.0 + modulation[1][:, None]), normed_one, invstd_one
    )
    d_ada = jnp.concatenate(
        [d_shift_one, d_scale_one, d_gate_one, d_shift_two, d_scale_two, d_gate_two], axis=1
    ).astype(jnp.bfloat16)
    d_cond = grad_cond + matmul_nt(d_ada, w_full[:, ada_at:]) * silu_grad(condition)
    qkv_sums = column_sum(d_qkv)
    g_bias = jnp.concatenate(
        [
            qkv_sums[:D],
            qkv_sums[2 * D :],
            column_sum(d_branch),
            column_sum(d_pre),
            column_sum(d_second),
            column_sum(d_ada),
        ]
    )
    g_dense = jnp.concatenate([g_qkv, g_proj, g_hidden], axis=1)
    return (d_residual, d_cond, g_dense, g_down, g_bias, d_ada)


def embed_forward(latent_part, noise_part, time_part, label_part, small_full, small_used):
    o_label = PATCH_IN + FREQ
    o_second = o_label + CLASSES
    fade = alpha_bar(time_part)[:, None, None]
    noisy_low = (jnp.sqrt(fade) * latent_part + jnp.sqrt(1.0 - fade) * noise_part).astype(
        jnp.bfloat16
    )
    tokens = jnp.einsum(
        "bpi,di->bpd", noisy_low, small_full[:, :PATCH_IN], preferred_element_type=jnp.float32
    )
    tokens = tokens + small_used[:D] + positions(latent_part.shape[1])[None]
    time_low, time_hidden, time_act = time_side(time_part, small_full, small_used)
    one_hot = label_table(label_part)
    label_rows = matmul_nt(one_hot, small_full[:, o_label:o_second])
    condition = (
        matmul(time_act, small_full[:, o_second : o_second + D])
        + small_used[2 * D : 3 * D]
        + label_rows
    )
    return (tokens, condition, (noisy_low, time_low, time_hidden, time_act, one_hot))


def embed_backward(d_resid_low, d_cond_low, saved, small_full):
    noisy_low, time_low, time_hidden, time_act, one_hot = saved
    o_second = PATCH_IN + FREQ + CLASSES
    g_patch = jnp.einsum("bpd,bpi->di", d_resid_low, noisy_low, preferred_element_type=jnp.float32)
    d_time = (
        matmul_nt(d_cond_low, small_full[:, o_second : o_second + D]) * silu_grad(time_hidden)
    ).astype(jnp.bfloat16)
    bias_pieces = jnp.concatenate(
        [
            jnp.sum(d_resid_low.astype(jnp.float32), axis=(0, 1)),
            column_sum(d_time),
            column_sum(d_cond_low),
        ]
    )
    return (g_patch, d_time, bias_pieces)


def head_step(residual, condition, noise_part, mask_part, inv_count, small_full, small_used):
    o_film = PATCH_IN + FREQ + CLASSES + D
    o_out = o_film + 2 * D
    act_low = jax.nn.silu(condition).astype(jnp.bfloat16)
    film_out = matmul(act_low, small_full[:, o_film:o_out]) + small_used[3 * D : 5 * D]
    shifting, scaling = (film_out[:, :D], film_out[:, D:])
    normed, invstd = normalize(residual)
    mixed = (normed * (1.0 + scaling[:, None]) + shifting[:, None]).astype(jnp.bfloat16)
    output = (
        jnp.einsum("bpd,dj->bpj", mixed, small_full[:, o_out:], preferred_element_type=jnp.float32)
        + small_used[5 * D :]
    )
    mismatch = output - noise_part
    mask_float = mask_part.astype(jnp.float32)[:, :, None]
    squared = jnp.sum(mask_float * mismatch * mismatch)
    d_output = (2.0 * inv_count * mask_float * mismatch).astype(jnp.bfloat16)
    g_output = jnp.einsum("bpd,bpj->dj", mixed, d_output, preferred_element_type=jnp.float32)
    d_mixed = jnp.einsum(
        "bpj,dj->bpd", d_output, small_full[:, o_out:], preferred_element_type=jnp.float32
    )
    d_film = jnp.concatenate(
        [jnp.sum(d_mixed, axis=1), jnp.sum(d_mixed * normed, axis=1)], axis=1
    ).astype(jnp.bfloat16)
    d_residual = norm_back(d_mixed * (1.0 + scaling[:, None]), normed, invstd)
    d_cond = matmul_nt(d_film, small_full[:, o_film:o_out]) * silu_grad(condition)
    g_bias = jnp.concatenate(
        [column_sum(d_film), jnp.sum(d_output.astype(jnp.float32), axis=(0, 1))]
    )
    return (squared, d_residual, d_cond, act_low, d_film, g_output, g_bias)


def adam_update(weight, gradient, first_moment, second_moment, scaling):
    gradient = gradient * scaling
    first_new = BETA_ONE * first_moment + (1.0 - BETA_ONE) * gradient
    second_new = BETA_TWO * second_moment + (1.0 - BETA_TWO) * gradient * gradient
    ratio = (
        first_new
        / (1.0 - BETA_ONE**STEP_POWER)
        / (jnp.sqrt(second_new / (1.0 - BETA_TWO**STEP_POWER)) + ADAM_EPS)
    )
    return (weight - RATE * (ratio + DECAY * weight), first_new, second_new)


def body(
    latents,
    noise,
    timesteps,
    labels,
    patch_mask,
    w_in,
    w_down,
    b_blk,
    small_mats,
    small_bias,
    m_in,
    m_down,
    m_bias,
    m_small,
    m_sbias,
    v_in,
    v_down,
    v_bias,
    v_small,
    v_sbias,
):
    section_index = lax.axis_index("section")
    sections = lax.axis_size("section")
    is_first = section_index == 0
    is_last = section_index == sections - 1
    on_first = is_first.astype(jnp.float32)
    on_last = is_last.astype(jnp.float32)
    weights = (
        lax.all_gather(w_in[0].astype(jnp.bfloat16), "dp", axis=0, tiled=True),
        lax.all_gather(w_down[0].astype(jnp.bfloat16), "dp", axis=0, tiled=True),
        lax.all_gather(b_blk[0].astype(jnp.bfloat16), "dp", axis=0, tiled=True),
    )
    small_cols, bias_whole = (
        lax.all_gather(small_mats.astype(jnp.bfloat16), "section", axis=1, tiled=True),
        lax.all_gather(small_bias.astype(jnp.bfloat16), "section", axis=0, tiled=True),
    )
    small_full = lax.all_gather(small_cols, "dp", axis=0, tiled=True)
    small_used = bias_whole.astype(jnp.float32)
    valid_total = lax.psum(jnp.sum(patch_mask).astype(jnp.float32), "dp")
    inv_count = 1.0 / (valid_total * PATCH_IN)
    images, patches = patch_mask.shape
    micro = MICRO
    per_batch = images // micro
    ada_at = 4 * D + FF
    o_label = PATCH_IN + FREQ
    o_second = o_label + CLASSES
    o_film = o_second + D
    o_out = o_film + 2 * D
    ticks = micro + sections - 1

    def take_part(source, slot_index):
        return lax.dynamic_slice_in_dim(source, slot_index * per_batch, per_batch, 0)

    film_rows = jnp.zeros((1, 1), jnp.bfloat16)
    embed_rows = (jnp.zeros((1, 1), jnp.bfloat16), jnp.zeros((1, 1), jnp.bfloat16))

    def forward_tick(tick_index, state):
        slot_raw = tick_index - section_index
        is_valid = (slot_raw >= 0) & (slot_raw < micro)
        slot_index = jnp.clip(slot_raw, 0, micro - 1)

        def forward_run(carried):
            (
                incoming_h,
                incoming_c,
                kept_all,
                resid_all,
                cond_all,
                grad_small,
                grad_sbias,
                loss_sum,
                film_all,
            ) = carried
            tokens, start_cond, unused = embed_forward(
                take_part(latents, slot_index),
                take_part(noise, slot_index),
                take_part(timesteps, slot_index),
                take_part(labels, slot_index),
                small_full,
                small_used,
            )
            residual = jnp.where(is_first, tokens, incoming_h.astype(jnp.float32))
            condition = jnp.where(is_first, start_cond, incoming_c.astype(jnp.float32))
            output, kept_items = block_forward(residual, condition, weights)
            kept_all = jax.tree.map(
                lambda whole, piece: lax.dynamic_update_index_in_dim(whole, piece, slot_index, 0),
                kept_all,
                kept_items,
            )
            squared, d_resid, d_cond, act_low, d_film, g_output, g_hbias = head_step(
                output,
                condition,
                take_part(noise, slot_index),
                take_part(patch_mask, slot_index),
                inv_count,
                small_full,
                small_used,
            )
            resid_all = lax.dynamic_update_index_in_dim(resid_all, d_resid, slot_index, 0)
            cond_all = lax.dynamic_update_index_in_dim(cond_all, d_cond, slot_index, 0)
            grad_small = grad_small.at[:, o_out:].add(on_last * g_output)
            grad_small = grad_small.at[:, o_film:o_out].add(on_last * matmul_tn(act_low, d_film))
            grad_sbias = grad_sbias.at[3 * D :].add(on_last * g_hbias)
            loss_sum = loss_sum + on_last * squared * inv_count
            return (
                output.astype(jnp.bfloat16),
                condition.astype(jnp.bfloat16),
                kept_all,
                resid_all,
                cond_all,
                grad_small,
                grad_sbias,
                loss_sum,
                film_all,
            )

        def forward_skip(carried):
            return (jnp.zeros_like(carried[0]), jnp.zeros_like(carried[1])) + tuple(carried[2:])

        sent = lax.cond(is_valid, forward_run, forward_skip, state)
        arrived = passed_along((sent[0], sent[1]), "section", 1)
        return (arrived[0], arrived[1]) + tuple(sent[2:])

    start_state = (
        jnp.zeros((per_batch, patches, D), jnp.bfloat16),
        jnp.zeros((per_batch, D), jnp.bfloat16),
        kept_zeros(micro, per_batch, patches),
        jnp.zeros((micro, per_batch, patches, D), jnp.float32),
        jnp.zeros((micro, per_batch, D), jnp.float32),
        jnp.zeros((D, small_full.shape[1]), jnp.float32),
        jnp.zeros(bias_whole.shape, jnp.float32),
        jnp.zeros((), jnp.float32),
        film_rows,
    )
    final_state = lax.fori_loop(0, ticks, forward_tick, start_state)
    (
        unused_h,
        unused_c,
        kept_buffer,
        head_resid,
        head_cond,
        small_grad,
        sbias_grad,
        loss_part,
        film_rows,
    ) = final_state
    grad_ada = jnp.zeros((D, 6 * D), jnp.float32)

    def backward_tick(tick_index, state):
        slot_raw = tick_index - (sections - 1 - section_index)
        is_valid = (slot_raw >= 0) & (slot_raw < micro)
        slot_index = jnp.clip(slot_raw, 0, micro - 1)

        def backward_run(carried):
            (
                incoming_h,
                incoming_c,
                g_dense,
                g_down,
                g_bias,
                g_ada,
                grad_small,
                grad_sbias,
                emb_all,
            ) = carried
            kept_items = jax.tree.map(
                lambda whole: lax.dynamic_index_in_dim(whole, slot_index, 0, keepdims=False),
                kept_buffer,
            )
            grad_out = jnp.where(
                is_last,
                lax.dynamic_index_in_dim(head_resid, slot_index, 0, keepdims=False),
                incoming_h.astype(jnp.float32),
            )
            grad_cond = jnp.where(
                is_last,
                lax.dynamic_index_in_dim(head_cond, slot_index, 0, keepdims=False),
                incoming_c.astype(jnp.float32),
            )
            d_resid, d_cond, piece_dense, piece_down, piece_bias, d_ada = block_backward(
                grad_out, grad_cond, kept_items, weights
            )
            g_dense = g_dense + piece_dense
            g_down = g_down + piece_down
            g_bias = g_bias + piece_bias
            g_ada = g_ada + matmul_tn(kept_items[1], d_ada)
            d_resid_low = d_resid.astype(jnp.bfloat16)
            d_cond_low = d_cond.astype(jnp.bfloat16)
            unused_tokens, unused_cond, saved = embed_forward(
                take_part(latents, slot_index),
                take_part(noise, slot_index),
                take_part(timesteps, slot_index),
                take_part(labels, slot_index),
                small_full,
                small_used,
            )
            g_patch, d_time, bias_pieces = embed_backward(
                d_resid_low, d_cond_low, saved, small_full
            )
            grad_small = grad_small.at[:, :PATCH_IN].add(on_first * g_patch)
            g_time = matmul_tn(d_time, saved[1])
            g_label = matmul_tn(d_cond_low, saved[4])
            g_second = matmul_tn(saved[3], d_cond_low)
            rest = jnp.concatenate([g_time, g_label, g_second], axis=1)
            grad_small = grad_small.at[:, PATCH_IN:o_film].add(on_first * rest)
            grad_sbias = grad_sbias.at[: 3 * D].add(on_first * bias_pieces)
            return (
                d_resid_low,
                d_cond_low,
                g_dense,
                g_down,
                g_bias,
                g_ada,
                grad_small,
                grad_sbias,
                emb_all,
            )

        def backward_skip(carried):
            return (jnp.zeros_like(carried[0]), jnp.zeros_like(carried[1])) + tuple(carried[2:])

        sent = lax.cond(is_valid, backward_run, backward_skip, state)
        arrived = passed_along((sent[0], sent[1]), "section", -1)
        return (arrived[0], arrived[1]) + tuple(sent[2:])

    back_state = (
        jnp.zeros((per_batch, patches, D), jnp.bfloat16),
        jnp.zeros((per_batch, D), jnp.bfloat16),
        jnp.zeros((D, ada_at), jnp.float32),
        jnp.zeros((FF, D), jnp.float32),
        jnp.zeros((weights[2].shape[0],), jnp.float32),
        grad_ada,
        small_grad,
        sbias_grad,
        embed_rows,
    )
    back_state = lax.fori_loop(0, ticks, backward_tick, back_state)
    (
        unused_h,
        unused_c,
        grad_dense,
        grad_down,
        grad_bias,
        grad_ada,
        small_grad,
        sbias_grad,
        embed_rows,
    ) = back_state
    shard_dense, shard_ada, shard_down, shard_bias = (
        lax.psum_scatter(grad_dense, "dp", scatter_dimension=0, tiled=True),
        lax.psum_scatter(grad_ada, "dp", scatter_dimension=0, tiled=True),
        lax.psum_scatter(grad_down, "dp", scatter_dimension=0, tiled=True),
        lax.psum_scatter(grad_bias, "dp", scatter_dimension=0, tiled=True),
    )
    small_rows = lax.psum_scatter(small_grad, "dp", scatter_dimension=0, tiled=True)
    shard_in = jnp.concatenate([shard_dense, shard_ada], axis=1)
    sbias_rows = lax.psum(sbias_grad, "dp")
    small_shard, sbias_shard = (
        lax.psum_scatter(small_rows, "section", scatter_dimension=1, tiled=True),
        lax.psum_scatter(sbias_rows, "section", scatter_dimension=0, tiled=True),
    )
    dp_zero = (lax.axis_index("dp") == 0).astype(jnp.float32)
    squares = (
        jnp.sum(shard_in * shard_in)
        + jnp.sum(shard_down * shard_down)
        + jnp.sum(shard_bias * shard_bias)
        + jnp.sum(small_shard * small_shard)
        + dp_zero * jnp.sum(sbias_shard * sbias_shard)
    )
    norm_square, loss = lax.psum((squares, loss_part), ("section", "dp"))
    grad_norm = jnp.sqrt(norm_square)
    scaling = jnp.minimum(1.0, CLIP / grad_norm)
    new_in, first_in, second_in = adam_update(w_in, shard_in[None], m_in, v_in, scaling)
    new_down, first_down, second_down = adam_update(
        w_down, shard_down[None], m_down, v_down, scaling
    )
    new_bias, first_bias, second_bias = adam_update(
        b_blk, shard_bias[None], m_bias, v_bias, scaling
    )
    new_small, first_small, second_small = adam_update(
        small_mats, small_shard, m_small, v_small, scaling
    )
    new_sbias, first_sbias, second_sbias = adam_update(
        small_bias, sbias_shard, m_sbias, v_sbias, scaling
    )
    return (
        loss,
        grad_norm,
        new_in,
        first_in,
        second_in,
        new_down,
        first_down,
        second_down,
        new_bias,
        first_bias,
        second_bias,
        new_small,
        first_small,
        second_small,
        new_sbias,
        first_sbias,
        second_sbias,
    )


def solution(mesh):
    in_specs = (
        P("dp", None, None),
        P("dp", None, None),
        P("dp"),
        P("dp"),
        P("dp", None),
        P("section", "dp", None),
        P("section", "dp", None),
        P("section", "dp"),
        P("dp", "section"),
        P("section"),
        P("section", "dp", None),
        P("section", "dp", None),
        P("section", "dp"),
        P("dp", "section"),
        P("section"),
        P("section", "dp", None),
        P("section", "dp", None),
        P("section", "dp"),
        P("dp", "section"),
        P("section"),
    )
    out_specs = (
        P(),
        P(),
        P("section", "dp", None),
        P("section", "dp", None),
        P("section", "dp", None),
        P("section", "dp", None),
        P("section", "dp", None),
        P("section", "dp", None),
        P("section", "dp"),
        P("section", "dp"),
        P("section", "dp"),
        P("dp", "section"),
        P("dp", "section"),
        P("dp", "section"),
        P("section"),
        P("section"),
        P("section"),
    )
    return jax.shard_map(body, mesh=mesh, in_specs=in_specs, out_specs=out_specs, check_vma=False)
```

profile of v0, /device:TPU:0, one launch (start us, length us, event | category | flops | bytes accessed | tf_op | source)
XLA Modules:
  0.0 4894.4 jit_solution(312884592654842937)
XLA Ops:
  9.2 34.1 all-gather.15.cloned.1.call-done
  60.1 17.5 psum.28
  79.3 15.0 all-reduce
  96.6 31.7 all-reduce.1
  128.2 28.6 all-gather.9.cloned.1.call-done
  156.8 15.7 copy.164
  172.5 85.5 %all-gather.13.cloned.1.call-done = bf16[1,4608,1152]{2,1,0:T(8,128)(2,1)} async-done(((bf16[1,576,1152]{2,1,0:T(8,128)(2,1)}), bf16[1,4608,1152]{2,1,0:T(8,128)(2,1)}) %all-gather.13.cloned.1.call-update) | async-done | bytes 10616848 | tf_op jit(solution)/shard_map/all_gather | solution.py:434
  258.0 320.2 %all-gather.11.cloned.1.call-done = bf16[1,1152,16128]{2,1,0:T(8,128)(2,1)} async-done(((bf16[1,144,16128]{2,1,0:T(8,128)(2,1)}), bf16[1,1152,16128]{2,1,0:T(8,128)(2,1)}) %all-gather.11.cloned.1.call-update) | async-done | bytes 37158928 | tf_op jit(solution)/shard_map/all_gather | solution.py:433
  622.7 1240.6 %while.90 = (s32[]{:T(128)}, bf16[2,256,1152]{2,1,0:T(8,128)(2,1)}, bf16[2,1152]{1,0:T(2,128)(2,1)}, f32[2,2,1152]{2,1,0:T(2,128)}, bf16[2,2,1152]{2,1,0:T(2,128...) while((s32[]{:T(128)}, bf16[2,256,1152]{2,1,0:T(8,128)(2,1)}, ...), condition=%wide.region_21.22_spmd, body=%wide.region_2.21_spmd.sunk | while | flops 17154225152 | bytes 548551744 | solution.py:539
  623.0 272.7 %conditional.4 = (bf16[2,256,1152]{2,1,0:T(8,128)(2,1)}, bf16[2,1152]{1,0:T(2,128)(2,1)}, f32[2,2,1152]{2,1,0:T(2,128)}, bf16[2,2,1152]{2,1,0:T(2,128)(2,1)}, f3...) conditional(s32[]{:T(128)} %convert_element_type.353, ...), branch_computations={%region_3.3_spmd, %region_4.20_spmd} | conditional | flops 17154225152 | bytes 539076864 | solution.py:524
  664.3 13.6 reshape.553
  714.4 14.7 bitcast_dynamic-update-slice_fusion
  778.5 21.8 copy.146
  808.1 12.2 add_select_fusion
  820.3 50.1 %scatter-add.6 = f32[1152,4744]{1,0:T(8,128)} dynamic-update-slice(f32[1152,4744]{1,0:T(8,128)} %scatter-add.1, f32[1152,2304]{1,0:T(8,128)} %add_select_fusion, s32[]{:T(128)} %constant.500.clone, s32[]{:T(128)} %constant.525.clone) | dynamic-update-slice | bytes 21233668 | tf_op jit(solution)/shard_map/while/body/eval_jaxpr/cond/branch_1_fun/scatter-add | solution.py:506
  870.4 22.8 copy.148
  898.3 24.9 collective-permute-done.1
  924.8 272.6 %conditional.4 = (bf16[2,256,1152]{2,1,0:T(8,128)(2,1)}, bf16[2,1152]{1,0:T(2,128)(2,1)}, f32[2,2,1152]{2,1,0:T(2,128)}, bf16[2,2,1152]{2,1,0:T(2,128)(2,1)}, f3...) conditional(s32[]{:T(128)} %convert_element_type.353, ...), branch_computations={%region_3.3_spmd, %region_4.20_spmd} | conditional | flops 17154225152 | bytes 539076864 | solution.py:524
  965.8 13.6 reshape.553
  1015.9 14.7 bitcast_dynamic-update-slice_fusion
  1080.0 21.8 copy.146
  1109.6 12.2 add_select_fusion
  1121.9 50.1 %scatter-add.6 = f32[1152,4744]{1,0:T(8,128)} dynamic-update-slice(f32[1152,4744]{1,0:T(8,128)} %scatter-add.1, f32[1152,2304]{1,0:T(8,128)} %add_select_fusion, s32[]{:T(128)} %constant.500.clone, s32[]{:T(128)} %constant.525.clone) | dynamic-update-slice | bytes 21233668 | tf_op jit(solution)/shard_map/while/body/eval_jaxpr/cond/branch_1_fun/scatter-add | solution.py:506
  1171.9 22.8 copy.148
  1200.1 24.4 collective-permute-done.1
  1233.4 269.4 %collective-permute-start = (bf16[2,256,1152]{2,1,0:T(8,128)(2,1)}, bf16[2,256,1152]{2,1,0:T(8,128)(2,1)S(1)}, u32[]{:S(2)}, u32[]{:S(2)}) collective-permute-start(bf16[2,256,1152]{2,1,0:T(8,128)(2,1)} %get-tuple-element.3074), channel_id=1, source_target_pairs={{0,8},{8,16},{16,24},{1,9},{9,17},{17,25},{2,10},{10,18},{18,26},{... | collective-permute-start | bytes 3538952 | tf_op jit(solution)/shard_map/while/body/eval_jaxpr/ppermute | solution.py:32
  1504.7 22.9 collective-permute-done.1
  1530.4 11.0 collective-permute-start
  1541.4 267.7 %collective-permute-start.1 = (bf16[2,1152]{1,0:T(2,128)(2,1)}, bf16[2,1152]{1,0:T(2,128)(2,1)S(1)}, u32[]{:S(2)}, u32[]{:S(2)}) collective-permute-start(bf16[2,1152]{1,0:T(2,128)(2,1)} %get-tuple-element.3075), channel_id=1, source_target_pairs={{0,8},{8,16},{16,24},{1,9},{9,17},{17,25},{2,10},{10,18},{18,26},{... | collective-permute-start | bytes 13832 | tf_op jit(solution)/shard_map/while/body/eval_jaxpr/ppermute | solution.py:32
  1813.4 22.9 collective-permute-start
  1836.3 11.5 collective-permute-start.1
  1847.9 11.6 collective-permute-done.1
  1878.5 13.9 broadcast_in_dim.121
  1901.4 10.6 broadcast_in_dim.124
  1912.0 1576.3 %while.91 = (s32[]{:T(128)}, bf16[2,256,1152]{2,1,0:T(8,128)(2,1)S(1)}, bf16[2,1152]{1,0:T(2,128)(2,1)}, f32[1152,9216]{1,0:T(8,128)}, f32[4608,1152]{1,0:T(8,12...) while((s32[]{:T(128)}, ...), condition=%wide.region_47.48_spmd, body=%wide.region_23.47_spmd.sunk | while | flops 34417291264 | bytes 706159040 | solution.py:641
  1922.1 276.6 %collective-permute-done.3 = bf16[2,1152]{1,0:T(2,128)(2,1)S(1)} collective-permute-done((bf16[2,1152]{1,0:T(2,128)(2,1)}, bf16[2,1152]{1,0:T(2,128)(2,1)S(1)}, u32[]{:S(2)}, u32[]{:S(2)}) %collective-permute-start.3) | collective-permute-done | bytes 4640 | tf_op jit(solution)/shard_map/while/body/eval_jaxpr/ppermute | solution.py:32
  2203.6 42.4 collective-permute-done.3
  2250.9 711.9 %collective-permute-done.3 = bf16[2,1152]{1,0:T(2,128)(2,1)S(1)} collective-permute-done((bf16[2,1152]{1,0:T(2,128)(2,1)}, bf16[2,1152]{1,0:T(2,128)(2,1)S(1)}, u32[]{:S(2)}, u32[]{:S(2)}) %collective-permute-start.3) | collective-permute-done | bytes 4640 | tf_op jit(solution)/shard_map/while/body/eval_jaxpr/ppermute | solution.py:32
  2963.3 233.0 %conditional.5 = (bf16[2,256,1152]{2,1,0:T(8,128)(2,1)}, bf16[2,1152]{1,0:T(2,128)(2,1)}, f32[1152,9216]{1,0:T(8,128)}, f32[4608,1152]{1,0:T(8,128)}, f32[16128]...) conditional(s32[]{:T(128)} %convert_element_type.354, (f32[1152,9216]{1,0:T(8,128)}, ...), branch_computations={%region_24.24_spmd, %region_25.46_spmd} | conditional | flops 34417291264 | bytes 701402880 | solution.py:626
  2967.6 15.5 convert_reduce_fusion.2
  2983.1 10.9 fusion.164
  3055.9 12.5 fusion.188
  3086.0 41.7 maximum_add_fusion
  3127.8 17.7 convolution_add_fusion.5
  3145.9 23.6 convolution_add_fusion.4
  3198.9 23.4 collective-permute-done.3
  3223.1 233.1 %conditional.5 = (bf16[2,256,1152]{2,1,0:T(8,128)(2,1)}, bf16[2,1152]{1,0:T(2,128)(2,1)}, f32[1152,9216]{1,0:T(8,128)}, f32[4608,1152]{1,0:T(8,128)}, f32[16128]...) conditional(s32[]{:T(128)} %convert_element_type.354, (f32[1152,9216]{1,0:T(8,128)}, ...), branch_computations={%region_24.24_spmd, %region_25.46_spmd} | conditional | flops 34417291264 | bytes 701402880 | solution.py:626
  3227.3 15.5 convert_reduce_fusion.2
  3242.8 10.9 fusion.164
  3316.1 12.4 fusion.188
  3346.1 41.7 maximum_add_fusion
  3387.9 17.7 convolution_add_fusion.5
  3406.0 23.6 convolution_add_fusion.4
  3458.8 21.5 collective-permute-done.3
  3488.4 21.8 copy.167
  3510.8 14.5 all-reduce.4
  3526.8 202.1 %reduce-scatter.12.cloned.1.call-done = f32[144,4744]{1,0:T(8,128)} async-done(((f32[1152,4744]{1,0:T(8,128)}), f32[144,4744]{1,0:T(8,128)}) %reduce-scatter.12.cloned.1.call-update) | async-done | bytes 2732560 | tf_op jit(solution)/shard_map/reduce_scatter | solution.py:659
  3731.5 48.9 all-reduce.12.cloned.1.call-done
  3783.7 211.6 %reduce-scatter.10.cloned.1.call-done = f32[576,1152]{1,0:T(8,128)} async-done(((f32[4608,1152]{1,0:T(8,128)}), f32[576,1152]{1,0:T(8,128)}) %reduce-scatter.10.cloned.1.call-update) | async-done | bytes 2654224 | tf_op jit(solution)/shard_map/reduce_scatter | solution.py:656
  3998.4 80.0 %all-reduce.10.cloned.1.call-done = f32[144,4744]{1,0:T(8,128)} async-done(((f32[144,4744]{1,0:T(8,128)}), f32[144,4744]{1,0:T(8,128)}) %all-reduce.10.cloned.1.call-update) | async-done | bytes 2732560
  4080.3 311.2 %reduce-scatter.8.cloned.1.call-done = f32[144,6912]{1,0:T(8,128)} async-done(((f32[1152,6912]{1,0:T(8,128)}), f32[144,6912]{1,0:T(8,128)}) %reduce-scatter.8.cloned.1.call-update) | async-done | bytes 3981328 | tf_op jit(solution)/shard_map/reduce_scatter | solution.py:655
  4391.5 410.0 %reduce-scatter.6.cloned.1.call-done = f32[144,9216]{1,0:T(8,128)} async-done(((f32[1152,9216]{1,0:T(8,128)}), f32[144,9216]{1,0:T(8,128)}) %reduce-scatter.6.cloned.1.call-update) | async-done | bytes 5308432 | tf_op jit(solution)/shard_map/reduce_scatter | solution.py:654
  4810.8 38.5 all-reduce.5
  4851.6 23.9 multiply_subtract_fusion
  (790 shorter events, 671.6 us)
Async XLA Ops:
  7.2 36.1 all-gather.15.cloned.1.call-start
  9.2 41.4 copy-start.22
  9.2 147.6 %all-gather.9.cloned.1.call-start = ((), (), s32[]{:S(2)}) async-start(), calls=%async_computation.4 | async-start | bytes 12607488 | tf_op jit(solution)/shard_map/all_gather | solution.py:441
  50.5 207.5 %all-gather.13.cloned.1.call-start = ((), (), s32[]{:S(2)}) async-start(), calls=%async_computation.10 | async-start | bytes 11943936 | tf_op jit(solution)/shard_map/all_gather | solution.py:434
  51.8 526.4 %all-gather.11.cloned.1.call-start = ((), (), s32[]{:S(2)}) async-start(), calls=%async_computation.9 | async-start | bytes 41803776 | tf_op jit(solution)/shard_map/all_gather | solution.py:433
  58.2 19.5 copy-start.89
  58.2 19.5 copy-start.90
  58.2 38.1 copy-start.81
  58.2 3670.7 %reduce-scatter.12.cloned.1.call-start = ((), (), s32[]{:S(2)}) async-start(), calls=%async_computation.8 | async-start | bytes 25214976 | tf_op jit(solution)/shard_map/reduce_scatter | solution.py:659
  712.4 26.7 copy-start.1
  778.5 21.8 copy-start.34
  778.5 21.8 copy-start.45
  870.4 22.9 copy-start.83
  895.6 27.6 collective-permute-start
  897.0 26.2 collective-permute-start.1
  1013.9 26.8 copy-start.1
  1080.0 21.8 copy-start.34
  1080.0 21.8 copy-start.45
  1171.9 22.9 copy-start.83
  1197.4 27.0 collective-permute-start
  1198.8 25.7 collective-permute-start.1
  1233.4 294.2 %collective-permute-start = (bf16[2,256,1152]{2,1,0:T(8,128)(2,1)}, bf16[2,256,1152]{2,1,0:T(8,128)(2,1)S(1)}, u32[]{:S(2)}, u32[]{:S(2)}) collective-permute-start(bf16[2,256,1152]{2,1,0:T(8,128)(2,1)} %get-tuple-element.3074), channel_id=1, source_target_pairs={{0,8},{8,16},{16,24},{1,9},{9,17},{17,25},{2,10},{10,18},{18,26},{... | collective-permute-start | bytes 3538952 | tf_op jit(solution)/shard_map/while/body/eval_jaxpr/ppermute | solution.py:32
  1502.9 24.8 collective-permute-start.1
  1530.4 280.2 %collective-permute-start = (bf16[2,256,1152]{2,1,0:T(8,128)(2,1)}, bf16[2,256,1152]{2,1,0:T(8,128)(2,1)S(1)}, u32[]{:S(2)}, u32[]{:S(2)}) collective-permute-start(bf16[2,256,1152]{2,1,0:T(8,128)(2,1)} %get-tuple-element.3074), channel_id=1, source_target_pairs={{0,8},{8,16},{16,24},{1,9},{9,17},{17,25},{2,10},{10,18},{18,26},{... | collective-permute-start | bytes 3538952 | tf_op jit(solution)/shard_map/while/body/eval_jaxpr/ppermute | solution.py:32
  1541.4 269.2 %collective-permute-start.1 = (bf16[2,1152]{1,0:T(2,128)(2,1)}, bf16[2,1152]{1,0:T(2,128)(2,1)S(1)}, u32[]{:S(2)}, u32[]{:S(2)}) collective-permute-start(bf16[2,1152]{1,0:T(2,128)(2,1)} %get-tuple-element.3075), channel_id=1, source_target_pairs={{0,8},{8,16},{16,24},{1,9},{9,17},{17,25},{2,10},{10,18},{18,26},{... | collective-permute-start | bytes 13832 | tf_op jit(solution)/shard_map/while/body/eval_jaxpr/ppermute | solution.py:32
  1813.4 46.1 collective-permute-start
  1836.3 23.2 collective-permute-start.1
  1919.5 279.2 %collective-permute-start.2 = (bf16[2,256,1152]{2,1,0:T(8,128)(2,1)}, bf16[2,256,1152]{2,1,0:T(8,128)(2,1)S(1)}, u32[]{:S(2)}, u32[]{:S(2)}) collective-permute-start(bf16[2,256,1152]{2,1,0:T(8,128)(2,1)} %get-tuple-element.3133), channel_id=1, source_target_pairs={{8,0},{16,8},{24,16},{9,1},{17,9},{25,17},{10,2},{18,10},{26,18},{... | collective-permute-start | bytes 3538952 | tf_op jit(solution)/shard_map/while/body/eval_jaxpr/ppermute | solution.py:32
  1920.8 277.9 %collective-permute-start.3 = (bf16[2,1152]{1,0:T(2,128)(2,1)}, bf16[2,1152]{1,0:T(2,128)(2,1)S(1)}, u32[]{:S(2)}, u32[]{:S(2)}) collective-permute-start(bf16[2,1152]{1,0:T(2,128)(2,1)} %get-tuple-element.3134), channel_id=1, source_target_pairs={{8,0},{16,8},{24,16},{9,1},{17,9},{25,17},{10,2},{18,10},{26,18},{... | collective-permute-start | bytes 13832 | tf_op jit(solution)/shard_map/while/body/eval_jaxpr/ppermute | solution.py:32
  2201.0 45.0 collective-permute-start.2
  2202.3 43.7 collective-permute-start.3
  2248.3 714.4 %collective-permute-start.2 = (bf16[2,256,1152]{2,1,0:T(8,128)(2,1)}, bf16[2,256,1152]{2,1,0:T(8,128)(2,1)S(1)}, u32[]{:S(2)}, u32[]{:S(2)}) collective-permute-start(bf16[2,256,1152]{2,1,0:T(8,128)(2,1)} %get-tuple-element.3133), channel_id=1, source_target_pairs={{8,0},{16,8},{24,16},{9,1},{17,9},{25,17},{10,2},{18,10},{26,18},{... | collective-permute-start | bytes 3538952 | tf_op jit(solution)/shard_map/while/body/eval_jaxpr/ppermute | solution.py:32
  2249.6 713.2 %collective-permute-start.3 = (bf16[2,1152]{1,0:T(2,128)(2,1)}, bf16[2,1152]{1,0:T(2,128)(2,1)S(1)}, u32[]{:S(2)}, u32[]{:S(2)}) collective-permute-start(bf16[2,1152]{1,0:T(2,128)(2,1)} %get-tuple-element.3134), channel_id=1, source_target_pairs={{8,0},{16,8},{24,16},{9,1},{17,9},{25,17},{10,2},{18,10},{26,18},{... | collective-permute-start | bytes 13832 | tf_op jit(solution)/shard_map/while/body/eval_jaxpr/ppermute | solution.py:32
  2964.8 29.3 slice-start
  2967.6 26.5 slice-start.1
  3086.0 41.7 copy-start.16
  3145.9 23.6 copy-start.29
  3145.9 25.1 copy-start.35
  3145.9 25.1 copy-start.36
  3196.3 26.0 collective-permute-start.2
  3197.6 24.7 collective-permute-start.3
  3224.5 29.3 slice-start
  3227.3 26.5 slice-start.1
  3346.1 41.7 copy-start.16
  3405.9 23.6 copy-start.29
  3405.9 25.1 copy-start.35
  3406.0 25.1 copy-start.36
  3456.2 24.1 collective-permute-start.2
  3457.5 22.8 collective-permute-start.3
  3510.2 270.2 %all-reduce.12.cloned.1.call-start = ((), (), s32[]{:S(2)}) async-start(), calls=%async_computation.13 | async-start | bytes 147456
  3526.0 469.4 %reduce-scatter.10.cloned.1.call-start = ((), (), s32[]{:S(2)}) async-start(), calls=%async_computation.7 | async-start | bytes 23887872 | tf_op jit(solution)/shard_map/reduce_scatter | solution.py:656
  3526.7 551.6 %all-reduce.10.cloned.1.call-start = ((), (), s32[]{:S(2)}) async-start(), calls=%async_computation.12 | async-start | bytes 5603328
  3728.9 662.6 %reduce-scatter.8.cloned.1.call-start = ((), (), s32[]{:S(2)}) async-start(), calls=%async_computation.6 | async-start | bytes 35831808 | tf_op jit(solution)/shard_map/reduce_scatter | solution.py:655
  3729.7 1071.9 %reduce-scatter.6.cloned.1.call-start = ((), (), s32[]{:S(2)}) async-start(), calls=%async_computation.5 | async-start | bytes 47775744 | tf_op jit(solution)/shard_map/reduce_scatter | solution.py:654
  4080.3 770.5 %copy-start.79 = (f32[1444]{0:T(1024)S(1)}, f32[1444]{0:T(1024)}, u32[]{:S(2)}) copy-start(f32[1444]{0:T(1024)} %param.49) | copy-start | bytes 17332
  4080.3 770.5 %copy-start.80 = (f32[1444]{0:T(1024)S(1)}, f32[1444]{0:T(1024)}, u32[]{:S(2)}) copy-start(f32[1444]{0:T(1024)} %get-tuple-element.2514) | copy-start | bytes 17332
  4080.3 770.5 %copy-start.84 = (f32[1444]{0:T(1024)S(1)}, f32[1444]{0:T(1024)}, u32[]{:S(2)}) copy-start(f32[1444]{0:T(1024)} %param.54) | copy-start | bytes 17332
  4080.3 770.6 %copy-start.85 = (f32[1444]{0:T(1024)S(1)}, f32[1444]{0:T(1024)}, u32[]{:S(2)}) copy-start(f32[1444]{0:T(1024)} %param.59) | copy-start | bytes 17332
  4851.5 23.9 copy-start.82
  4851.5 23.9 copy-start.86
  4851.5 23.9 copy-start.87
  4851.5 24.6 copy-start.23
  4851.5 24.6 copy-start.24
  4851.6 24.6 copy-start.31
  (158 other events, 1036.8 us)
Sparse Core Ops, SparseCore 0:
  10.4 32.8 all-gather.14
  50.7 106.0 all-gather.8
  159.0 98.9 all-gather.12
  260.1 318.0 all-gather.10
  3510.3 218.5 reduce-scatter.11
  3732.3 47.9 all-reduce.11
  3782.8 212.4 reduce-scatter.9
  3998.5 79.7 all-reduce.9
  4080.7 310.7 reduce-scatter.7
  4393.9 407.6 reduce-scatter.5
where the time goes:
time: 4910 us; the launch traced here: 4890 us
  waiting for transfers between devices  2900 us (59%)
  starting transfers between devices  603 us (12%)
  local copies, waits for them, and re-layouts  527 us (11%)
  matrix products  452 us (9%)
  other arithmetic  247 us (5%)
  blocking collectives  117 us (2%)
    ppermute x20, waiting for transfers between devices, passed_along(): lax.ppermute(value, axis, [(source, source + steps) for source in range(f...  1160 us
    ppermute x20, starting transfers between devices, passed_along(): lax.ppermute(value, axis, [(source, source + steps) for source in range(f...  603 us
    reduce_scatter x1, waiting for transfers between devices, body(): lax.psum_scatter(grad_dense, 'dp', scatter_dimension=0, tiled=True)  410 us
    all_gather x1, waiting for transfers between devices, body(): lax.all_gather(w_in[0].astype(jnp.bfloat16), 'dp', axis=0, tiled=True)  320 us
    reduce_scatter x1, waiting for transfers between devices, body(): lax.psum_scatter(grad_ada, 'dp', scatter_dimension=0, tiled=True)  311 us
    reduce_scatter x1, waiting for transfers between devices, body(): lax.psum_scatter(grad_down, 'dp', scatter_dimension=0, tiled=True)  212 us
    reduce_scatter x1, waiting for transfers between devices, body(): lax.psum_scatter(small_grad, 'dp', scatter_dimension=0, tiled=True)  202 us
    dot_general x18, matrix products, matmul_tn(): lax.dot_general(left_side, right_side, (((0,), (0,)), ((), ())), preferre...  166 us
  transfers between devices with their start and end apart: 30, of which 20 were waited for; matrix products, arithmetic and copies ran while one was open for 1% of the time, Pallas kernels for 0%

commit v1 on v0

v1 whole, which is shorter than its diff:
```python
import functools
import math

import jax
import jax.numpy as jnp
from jax import lax
from jax.experimental import pallas as pl
from jax.experimental.pallas import tpu as pltpu
from jax.sharding import PartitionSpec as P

D = 1152
HEADS = 16
HEAD_DIM = 72
FF = 4608
CLASSES = 1000
FREQ = 256
PATCH_IN = 16
GRID = 16


EPS_NORM = 1e-06
CLIP = 0.001
RATE = 0.005
BETA_ONE = 0.9
BETA_TWO = 0.999
ADAM_EPS = 1e-08
DECAY = 0.01
STEP_POWER = 10.0


def passed_along(value, axis, steps):
    count = lax.axis_size(axis)
    first, last = (max(0, -steps), min(count, count - steps))
    return lax.ppermute(value, axis, [(source, source + steps) for source in range(first, last)])


def matmul(left_side, right_side):
    return jnp.dot(left_side, right_side, preferred_element_type=jnp.float32)


def matmul_tn(left_side, right_side):
    return lax.dot_general(
        left_side, right_side, (((0,), (0,)), ((), ())), preferred_element_type=jnp.float32
    )


def matmul_nt(left_side, right_side):
    return lax.dot_general(
        left_side, right_side, (((1,), (1,)), ((), ())), preferred_element_type=jnp.float32
    )


def column_sum(values):
    return jnp.sum(values.astype(jnp.float32), axis=0)


def normalize(values):
    center = values - jnp.mean(values, axis=-1, keepdims=True)
    invstd = lax.rsqrt(jnp.mean(center * center, axis=-1, keepdims=True) + EPS_NORM)
    return (center * invstd, invstd)


def norm_back(grad_normed, normed, invstd):
    return invstd * (
        grad_normed
        - jnp.mean(grad_normed, axis=-1, keepdims=True)
        - normed * jnp.mean(grad_normed * normed, axis=-1, keepdims=True)
    )


def gelu_tanh(values):
    return (
        0.5
        * values
        * (1.0 + jnp.tanh(0.7978845608028654 * (values + 0.044715 * values * values * values)))
    )


def gelu_grad(values):
    inner = jnp.tanh(0.7978845608028654 * (values + 0.044715 * values * values * values))
    return 0.5 * (1.0 + inner) + 0.5 * values * (1.0 - inner * inner) * 0.7978845608028654 * (
        1.0 + 0.134145 * values * values
    )


def silu_grad(values):
    sigma = jax.nn.sigmoid(values)
    return sigma * (1.0 + values * (1.0 - sigma))


def positions(patches):
    quarter = D // 4
    omega = jnp.exp(-math.log(10000.0) * jnp.arange(quarter, dtype=jnp.float32) / quarter)
    spot = jnp.arange(patches, dtype=jnp.int32)
    row_angle = (spot // GRID).astype(jnp.float32)[:, None] * omega[None, :]
    col_angle = (spot % GRID).astype(jnp.float32)[:, None] * omega[None, :]
    return jnp.concatenate(
        [jnp.sin(row_angle), jnp.cos(row_angle), jnp.sin(col_angle), jnp.cos(col_angle)], axis=1
    )


def time_features(time_steps):
    half = FREQ // 2
    freqs = jnp.exp(-math.log(10000.0) * jnp.arange(half, dtype=jnp.float32) / half)
    angles = time_steps.astype(jnp.float32)[:, None] * freqs[None, :]
    return jnp.concatenate([jnp.cos(angles), jnp.sin(angles)], axis=1)


def alpha_bar(time_steps):
    return jnp.cos((time_steps.astype(jnp.float32) / 1000.0 + 0.008) / 1.008 * (math.pi / 2)) ** 2


def label_table(label_part):
    return (label_part[:, None] == jnp.arange(CLASSES, dtype=jnp.int32)[None, :]).astype(
        jnp.bfloat16
    )


MESH = pl.DeviceIdType.MESH
DIRECT = 8


def rounded(values):
    return lax.reduce_precision(values, 8, 7)


def meet(axis, count, here):
    barrier = pltpu.get_barrier_semaphore()
    for step in range(1, count):
        pl.semaphore_signal(
            barrier, inc=1, device_id={axis: lax.rem(here + step, count)}, device_id_type=MESH
        )
    pl.semaphore_wait(barrier, count - 1)


def share_kernel(axis, count, personal, in_ref, out_ref, send_sem, recv_sem):
    here = lax.axis_index(axis)
    meet(axis, count, here)
    copies = []
    for step in range(1, count):
        target = lax.rem(here + step, count)
        copy = pltpu.make_async_remote_copy(
            src_ref=in_ref.at[target] if personal else in_ref,
            dst_ref=out_ref.at[here],
            send_sem=send_sem.at[step - 1],
            recv_sem=recv_sem.at[step - 1],
            device_id={axis: target},
            device_id_type=MESH,
        )
        copy.start()
        copies.append(copy)
    out_ref[here] = in_ref[here] if personal else in_ref[...]
    for copy in copies:
        copy.wait()


def share(value, axis, personal, ident):
    count = lax.axis_size(axis)
    shape = value.shape if personal else (count,) + value.shape
    return pl.pallas_call(
        functools.partial(share_kernel, axis, count, personal),
        out_shape=jax.ShapeDtypeStruct(shape, value.dtype),
        in_specs=[pl.BlockSpec(memory_space=pltpu.VMEM)],
        out_specs=pl.BlockSpec(memory_space=pltpu.VMEM),
        scratch_shapes=[
            pltpu.SemaphoreType.DMA((count - 1,)),
            pltpu.SemaphoreType.DMA((count - 1,)),
        ],
        compiler_params=pltpu.CompilerParams(collective_id=ident, has_side_effects=True),
        name="share",
    )(value)


def spread(value, axis, ident):
    if lax.axis_size(axis) > DIRECT:
        return lax.all_gather(value, axis)
    return share(value, axis, False, ident)


def exchange(value, axis, ident):
    if lax.axis_size(axis) > DIRECT:
        return lax.all_to_all(value, axis, 0, 0)
    return share(value, axis, True, ident)


def row_sums(left_side, right_side):
    product = matmul_tn(left_side, right_side)
    count = lax.axis_size("dp")
    if count != DIRECT:
        return lax.psum_scatter(product, "dp", scatter_dimension=0, tiled=True)
    here = lax.axis_index("dp")
    core, chip, chips = (here % 2, here // 2, count // 2)
    parted = product.reshape(chips, 2, product.shape[0] // count, product.shape[1])
    other = lax.dynamic_index_in_dim(parted, 1 - core, 1, keepdims=False)
    same = lax.dynamic_index_in_dim(parted, core, 1, keepdims=False)
    both = same + lax.ppermute(other, "dp", [(i, i ^ 1) for i in range(count)])
    total = lax.dynamic_index_in_dim(both, chip, 0, keepdims=False)
    for step in range(1, chips):
        block = lax.dynamic_index_in_dim(both, (chip + step) % chips, 0, keepdims=False)
        arrived = lax.ppermute(
            block.astype(jnp.bfloat16),
            "dp",
            [(i, (i + 2 * step) % count) for i in range(count)],
        )
        total = total + arrived.astype(jnp.float32)
    return total


def attend_kernel(qkv_ref, out_ref):
    for head in range(HEADS):
        at = head * HEAD_DIM
        query = qkv_ref[:, at : at + HEAD_DIM]
        key = qkv_ref[:, D + at : D + at + HEAD_DIM]
        value = qkv_ref[:, 2 * D + at : 2 * D + at + HEAD_DIM]
        scores = matmul_nt(query, key) * HEAD_DIM ** (-0.5)
        attention = jnp.exp(scores - jnp.max(scores, axis=-1, keepdims=True))
        attention = attention * (1.0 / jnp.sum(attention, axis=-1, keepdims=True))
        out_ref[:, at : at + HEAD_DIM] = matmul(attention.astype(jnp.bfloat16), value).astype(
            jnp.bfloat16
        )


def attend(qkv_low):
    patches = qkv_low.shape[0]
    return pl.pallas_call(
        attend_kernel,
        out_shape=jax.ShapeDtypeStruct((patches, D), jnp.bfloat16),
        cost_estimate=pl.CostEstimate(
            flops=4 * patches * patches * D,
            bytes_accessed=8 * patches * D,
            transcendentals=HEADS * patches * patches,
        ),
        name="attend",
    )(qkv_low)


def attend_back_kernel(qkv_ref, grad_ref, out_ref):
    scaling = HEAD_DIM ** (-0.5)
    for head in range(HEADS):
        at = head * HEAD_DIM
        query = qkv_ref[:, at : at + HEAD_DIM]
        key = qkv_ref[:, D + at : D + at + HEAD_DIM]
        value = qkv_ref[:, 2 * D + at : 2 * D + at + HEAD_DIM]
        grad = grad_ref[:, at : at + HEAD_DIM]
        scores = matmul_nt(query, key) * scaling
        attention = jnp.exp(scores - jnp.max(scores, axis=-1, keepdims=True))
        attention = attention * (1.0 / jnp.sum(attention, axis=-1, keepdims=True))
        d_probs = matmul_nt(grad, value)
        d_scores = (
            attention * (d_probs - jnp.sum(attention * d_probs, axis=-1, keepdims=True))
        ).astype(jnp.bfloat16)
        attention_low = attention.astype(jnp.bfloat16)
        out_ref[:, at : at + HEAD_DIM] = (matmul(d_scores, key) * scaling).astype(jnp.bfloat16)
        out_ref[:, D + at : D + at + HEAD_DIM] = (matmul_tn(d_scores, query) * scaling).astype(
            jnp.bfloat16
        )
        out_ref[:, 2 * D + at : 2 * D + at + HEAD_DIM] = matmul_tn(attention_low, grad).astype(
            jnp.bfloat16
        )


def attend_back(qkv_low, grad):
    patches = qkv_low.shape[0]
    return pl.pallas_call(
        attend_back_kernel,
        out_shape=jax.ShapeDtypeStruct((patches, 3 * D), jnp.bfloat16),
        cost_estimate=pl.CostEstimate(
            flops=10 * patches * patches * D,
            bytes_accessed=14 * patches * D,
            transcendentals=HEADS * patches * patches,
        ),
        name="attend_back",
    )(qkv_low, grad)


def image_forward(residual, modulation, weights):
    w_qkv, w_proj, w_hidden, w_second, bias = weights
    normed_one, unused = normalize(residual)
    mixed_one = (normed_one * (1.0 + modulation[1]) + modulation[0]).astype(jnp.bfloat16)
    qkv_bias = jnp.concatenate([bias[:D], jnp.zeros((D,), jnp.float32), bias[D : 2 * D]])
    qkv_low = (matmul(mixed_one, w_qkv) + qkv_bias).astype(jnp.bfloat16)
    att_low = attend(qkv_low)
    branch = matmul(att_low, w_proj) + bias[2 * D : 3 * D]
    middle = residual + modulation[2] * branch
    normed_two, unused = normalize(middle)
    mixed_two = (normed_two * (1.0 + modulation[4]) + modulation[3]).astype(jnp.bfloat16)
    pre_act = matmul(mixed_two, w_hidden) + bias[3 * D : 3 * D + FF]
    act_low = gelu_tanh(pre_act).astype(jnp.bfloat16)
    second = matmul(act_low, w_second) + bias[3 * D + FF : 4 * D + FF]
    output = middle + modulation[5] * second
    return (
        output,
        (
            residual,
            mixed_one,
            qkv_low,
            att_low,
            branch,
            middle,
            mixed_two,
            pre_act,
            act_low,
            second,
        ),
    )


def image_backward(grad_out, kept, modulation, weights):
    w_qkv, w_proj, w_hidden, w_second, unused = weights
    residual, qkv_low, branch, middle, pre_act, second = kept
    d_second = (grad_out * modulation[5]).astype(jnp.bfloat16)
    d_gate_two = jnp.sum(grad_out * second, axis=0)
    d_pre = (matmul_nt(d_second, w_second) * gelu_grad(pre_act)).astype(jnp.bfloat16)
    d_mixed_two = matmul_nt(d_pre, w_hidden)
    normed_two, invstd_two = normalize(middle)
    d_shift_two = jnp.sum(d_mixed_two, axis=0)
    d_scale_two = jnp.sum(d_mixed_two * normed_two, axis=0)
    d_middle = grad_out + norm_back(d_mixed_two * (1.0 + modulation[4]), normed_two, invstd_two)
    d_gate_one = jnp.sum(d_middle * branch, axis=0)
    d_branch = (d_middle * modulation[2]).astype(jnp.bfloat16)
    d_att = matmul_nt(d_branch, w_proj).astype(jnp.bfloat16)
    d_qkv = attend_back(qkv_low, d_att)
    d_mixed_one = matmul_nt(d_qkv, w_qkv)
    normed_one, invstd_one = normalize(residual)
    d_shift_one = jnp.sum(d_mixed_one, axis=0)
    d_scale_one = jnp.sum(d_mixed_one * normed_one, axis=0)
    d_residual = d_middle + norm_back(
        d_mixed_one * (1.0 + modulation[1]), normed_one, invstd_one
    )
    d_ada = jnp.concatenate(
        [d_shift_one, d_scale_one, d_gate_one, d_shift_two, d_scale_two, d_gate_two]
    ).astype(jnp.bfloat16)
    return (d_residual, (d_second, d_pre, d_branch, d_qkv, d_ada))


def head_step(residual, film, noise_part, mask_part, inv_count, w_out, b_out):
    shifting, scaling = (film[:, :D], film[:, D:])
    normed, invstd = normalize(residual)
    mixed = (normed * (1.0 + scaling[:, None]) + shifting[:, None]).astype(jnp.bfloat16)
    output = (
        jnp.einsum("bpd,dj->bpj", mixed, w_out, preferred_element_type=jnp.float32) + b_out
    )
    mismatch = output - noise_part
    mask_float = mask_part.astype(jnp.float32)[:, :, None]
    squared = jnp.sum(mask_float * mismatch * mismatch)
    d_output = (2.0 * inv_count * mask_float * mismatch).astype(jnp.bfloat16)
    g_output = jnp.einsum("bpd,bpj->dj", mixed, d_output, preferred_element_type=jnp.float32)
    d_mixed = jnp.einsum("bpj,dj->bpd", d_output, w_out, preferred_element_type=jnp.float32)
    d_film = jnp.concatenate(
        [jnp.sum(d_mixed, axis=1), jnp.sum(d_mixed * normed, axis=1)], axis=1
    ).astype(jnp.bfloat16)
    d_residual = norm_back(d_mixed * (1.0 + scaling[:, None]), normed, invstd)
    g_bias = jnp.sum(d_output.astype(jnp.float32), axis=(0, 1))
    return (squared, d_residual, d_film, g_output, g_bias)


def adam_update(weight, gradient, first_moment, second_moment, scaling):
    gradient = gradient * scaling
    first_new = BETA_ONE * first_moment + (1.0 - BETA_ONE) * gradient
    second_new = BETA_TWO * second_moment + (1.0 - BETA_TWO) * gradient * gradient
    ratio = (
        first_new
        / (1.0 - BETA_ONE**STEP_POWER)
        / (jnp.sqrt(second_new / (1.0 - BETA_TWO**STEP_POWER)) + ADAM_EPS)
    )
    return (weight - RATE * (ratio + DECAY * weight), first_new, second_new)


def body(
    latents,
    noise,
    timesteps,
    labels,
    patch_mask,
    w_in,
    w_down,
    b_blk,
    small_mats,
    small_bias,
    m_in,
    m_down,
    m_bias,
    m_small,
    m_sbias,
    v_in,
    v_down,
    v_bias,
    v_small,
    v_sbias,
):
    section_index = lax.axis_index("section")
    dp_index = lax.axis_index("dp")
    sections = lax.axis_size("section")
    is_first = section_index == 0
    is_last = section_index == sections - 1
    low = jnp.bfloat16
    images, patches = patch_mask.shape
    rows = w_in.shape[1]
    row_at = dp_index * rows
    ada_at = 4 * D + FF
    o_label = PATCH_IN + FREQ
    o_second = o_label + CLASSES
    o_film = o_second + D
    o_out = o_film + 2 * D

    def gathered(value, axis="dp", dim=0):
        return lax.all_gather(value, axis, axis=dim, tiled=True)

    in_low = w_in[0].astype(low)
    w_ada = in_low[:, ada_at:]
    w_qkv = gathered(in_low[:, : 3 * D])
    w_proj = gathered(in_low[:, 3 * D : 4 * D])
    w_hidden = gathered(in_low[:, 4 * D : ada_at])
    w_second = gathered(w_down[0].astype(low))

    small_low = small_mats.astype(low)
    edge_own = jnp.where(is_first, small_mats[:, :PATCH_IN], small_mats[:, -PATCH_IN:])
    bias_width = b_blk.shape[1]
    pieces = [
        b_blk[0],
        edge_own.reshape(-1),
        timesteps.astype(jnp.float32),
        labels.astype(jnp.float32),
        jnp.sum(patch_mask).astype(jnp.float32)[None],
    ]
    block = jnp.concatenate(pieces)[None]
    blocks = spread(block, "dp", 1)[:, 0]
    ends = [0]
    for piece in pieces:
        ends.append(ends[-1] + piece.shape[0])
    bias_full = rounded(blocks[:, : ends[1]].reshape(-1))
    w_edge = blocks[:, ends[1] : ends[2]].reshape(D, PATCH_IN).astype(low)
    times_all = blocks[:, ends[2] : ends[3]].reshape(-1).astype(jnp.int32)
    labels_all = blocks[:, ends[3] : ends[4]].reshape(-1).astype(jnp.int32)
    valid_total = jnp.sum(blocks[:, ends[4]])
    inv_count = 1.0 / (valid_total * PATCH_IN)
    weights = (w_qkv, w_proj, w_hidden, w_second, bias_full)

    small_width = small_mats.shape[1]
    sbias_width = small_bias.shape[0]
    extra = -(-sbias_width // small_width)
    sbias_rows = jnp.pad(small_bias, (0, extra * small_width - sbias_width)).astype(low)
    small_block = jnp.concatenate([small_low, sbias_rows.reshape(extra, small_width)], axis=0)
    small_blocks = spread(small_block, "section", 2)
    small_rows = jnp.concatenate([small_blocks[i, :rows] for i in range(sections)], axis=1)
    small_used = (
        small_blocks[:, rows:].reshape(sections, -1)[:, :sbias_width].reshape(-1)
    ).astype(jnp.float32)

    shards = lax.axis_size("dp")
    time_low = time_features(times_all).astype(low)
    one_hot = label_table(labels_all)
    time_hidden = matmul_nt(time_low, small_rows[:, PATCH_IN:o_label]) + lax.dynamic_slice_in_dim(
        small_used, D + row_at, rows, 0
    )
    time_act = jax.nn.silu(time_hidden).astype(low)
    cond_part = matmul(time_act, small_rows[:, o_second:o_film])
    label_part = matmul_nt(one_hot, small_rows[:, o_label:o_second])
    cond_part = jnp.concatenate([cond_part, label_part], axis=1).reshape(shards, images, D + rows)
    cond_got = exchange(cond_part, "dp", 3)
    cond_own = (
        jnp.sum(cond_got[:, :, :D], axis=0)
        + small_used[2 * D : 3 * D]
        + jnp.swapaxes(cond_got[:, :, D:], 0, 1).reshape(images, D)
    )
    cond_cols = exchange(jnp.swapaxes(cond_own.reshape(images, shards, rows), 0, 1), "dp", 4)
    cond_first = cond_cols.reshape(shards * images, rows)
    cond_later = rounded(cond_first)
    cond_here = jnp.where(is_first, cond_first, cond_later)
    act_here = jax.nn.silu(cond_here).astype(low)
    act_later = jax.nn.silu(cond_later).astype(low)
    ada_part = jnp.concatenate(
        [matmul(act_here, w_ada), matmul(act_later, small_rows[:, o_film:o_out])], axis=1
    )
    ada_got = exchange(ada_part.reshape(shards, images * 8 * D // 128, 128), "dp", 5)
    ada_own = jnp.sum(ada_got, axis=0).reshape(images, 8 * D)
    film = ada_own[:, 6 * D :] + small_used[3 * D : 5 * D]
    ada = (ada_own[:, : 6 * D] + bias_full[ada_at:]).reshape(images, 6, D)

    fade = alpha_bar(timesteps)[:, None, None]
    noisy_low = (jnp.sqrt(fade) * latents + jnp.sqrt(1.0 - fade) * noise).astype(low)
    tokens = jnp.einsum(
        "bpi,di->bpd", noisy_low, w_edge, preferred_element_type=jnp.float32
    )
    tokens = tokens + small_used[:D] + positions(patches)[None]

    def slot_of(raw):
        return (jnp.where((raw >= 0) & (raw < images), raw, images), jnp.clip(raw, 0, images - 1))

    def put(whole, piece, slot):
        return lax.dynamic_update_index_in_dim(whole, piece, slot, 0)

    def buffers(widths):
        return [jnp.zeros((images + 1, patches) + (width,), kind) for width, kind in widths]

    ticks = images + sections - 1
    wide = jnp.float32
    kept_all = buffers(
        [
            (D, wide),
            (D, low),
            (3 * D, low),
            (D, low),
            (D, wide),
            (D, wide),
            (D, low),
            (FF, wide),
            (FF, low),
            (D, wide),
            (D, wide),
        ]
    )
    arrived = jnp.zeros((patches, D), low)
    for tick in range(ticks):
        store_at, read_at = slot_of(tick - section_index)
        residual = jnp.where(is_first, tokens[min(tick, images - 1)], arrived.astype(wide))
        modulation = lax.dynamic_index_in_dim(ada, read_at, 0, keepdims=False)
        output, kept = image_forward(residual, modulation, weights)
        if tick < ticks - 1:
            arrived = passed_along(output.astype(low), "section", 1)
        kept_all = [put(whole, piece, store_at) for whole, piece in zip(kept_all, kept + (output,))]

    (
        residual_all,
        mixed_one_all,
        qkv_all,
        att_all,
        branch_all,
        middle_all,
        mixed_two_all,
        pre_all,
        act_all,
        second_all,
        output_all,
    ) = kept_all

    squared, head_grad, d_film, g_output, g_out_bias = head_step(
        output_all[:images],
        film,
        noise,
        patch_mask,
        inv_count,
        w_edge,
        small_used[5 * D :],
    )
    loss_part = jnp.where(is_last, squared * inv_count, 0.0)
    film_all = spread(d_film, "dp", 6).reshape(shards * images, 2 * D)
    film_all = spread(film_all, "section", 7)[sections - 1]

    grads_all = buffers([(D, low), (FF, low), (D, low), (3 * D, low)])
    ada_grads = jnp.zeros((images + 1, 6 * D), low)
    token_grads = jnp.zeros((images + 1, patches, D), low)
    arrived = jnp.zeros((patches, D), low)
    for tick in range(ticks):
        store_at, read_at = slot_of(tick - (sections - 1 - section_index))
        grad_out = jnp.where(
            is_last, head_grad[min(tick, images - 1)], arrived.astype(jnp.float32)
        )
        kept = [
            lax.dynamic_index_in_dim(whole, read_at, 0, keepdims=False)
            for whole in (residual_all, qkv_all, branch_all, middle_all, pre_all, second_all)
        ]
        modulation = lax.dynamic_index_in_dim(ada, read_at, 0, keepdims=False)
        d_residual, pieces = image_backward(grad_out, kept, modulation, weights)
        d_low = d_residual.astype(low)
        if tick < ticks - 1:
            arrived = passed_along(d_low, "section", -1)
        grads_all = [put(whole, piece, store_at) for whole, piece in zip(grads_all, pieces[:4])]
        ada_grads = put(ada_grads, pieces[4], store_at)
        token_grads = put(token_grads, d_low, store_at)

    def flat(whole):
        return whole[:images].reshape(images * patches, whole.shape[2])

    d_second, d_pre, d_branch, d_qkv = [flat(whole) for whole in grads_all]
    d_tokens = flat(token_grads)
    d_ada = ada_grads[:images]

    shard_proj = row_sums(flat(att_all), d_branch)
    shard_down = row_sums(flat(act_all), d_second)
    shard_hidden = row_sums(flat(mixed_two_all), d_pre)
    shard_qkv = row_sums(flat(mixed_one_all), d_qkv)
    d_ada_all = spread(d_ada, "dp", 8).reshape(shards * images, 6 * D)
    shard_ada = matmul_tn(act_here, d_ada_all)
    shard_in = jnp.concatenate([shard_qkv, shard_proj, shard_hidden, shard_ada], axis=1)

    cond_piece = matmul_nt(d_ada_all, w_ada) * silu_grad(cond_here)
    cond_pieces = spread(cond_piece, "section", 9)
    d_cond = matmul_nt(film_all, small_rows[:, o_film:o_out]) * silu_grad(cond_later)
    for layer in reversed(range(sections)):
        d_cond = rounded(d_cond + cond_pieces[layer])
    d_cond_rows = d_cond.astype(low)
    d_cond_all = jnp.swapaxes(spread(d_cond_rows, "dp", 10), 0, 1).reshape(shards * images, D)
    d_time = (
        matmul_nt(d_cond_all, small_rows[:, o_second:o_film]) * silu_grad(time_hidden)
    ).astype(low)
    g_edge = jnp.where(
        is_first,
        matmul_tn(d_tokens, noisy_low.reshape(images * patches, PATCH_IN)),
        g_output,
    )
    qkv_sums = column_sum(d_qkv)
    bias_sums = jnp.concatenate(
        [
            qkv_sums[:D],
            qkv_sums[2 * D :],
            column_sum(d_branch),
            column_sum(d_pre),
            column_sum(d_second),
            column_sum(d_ada),
        ]
    )
    sums = jnp.concatenate(
        [
            bias_sums.reshape(shards, -1),
            g_edge.reshape(shards, -1),
            jnp.broadcast_to(column_sum(d_tokens), (shards, D)),
            jnp.broadcast_to(g_out_bias, (shards, PATCH_IN)),
            jnp.broadcast_to(column_sum(d_time), (shards, rows)),
        ],
        axis=1,
    )
    sums = exchange(sums[:, None], "dp", 11)[:, 0]
    edge_end = bias_width + rows * PATCH_IN
    shard_bias = jnp.sum(sums[:, :bias_width], axis=0)
    edge_rows = jnp.sum(sums[:, bias_width:edge_end], axis=0).reshape(rows, PATCH_IN)
    token_sums = jnp.sum(sums[:, edge_end : edge_end + D], axis=0)
    out_sums = jnp.sum(sums[:, edge_end + D : edge_end + D + PATCH_IN], axis=0)
    time_sums = sums[:, edge_end + D + PATCH_IN :].reshape(-1)
    small_grad = jnp.concatenate(
        [
            edge_rows,
            matmul_tn(d_time, time_low),
            matmul_tn(d_cond_rows, one_hot),
            matmul_tn(time_act, d_cond_all),
            matmul_tn(act_later, film_all),
            edge_rows,
        ],
        axis=1,
    )
    small_shard = lax.dynamic_slice_in_dim(small_grad, section_index * small_width, small_width, 1)
    sbias_grad = jnp.concatenate(
        [token_sums, time_sums, column_sum(d_cond_all), column_sum(film_all), out_sums]
    )
    sbias_shard = lax.dynamic_slice_in_dim(
        sbias_grad, section_index * sbias_width, sbias_width, 0
    )

    dp_zero = (dp_index == 0).astype(jnp.float32)
    squares = (
        jnp.sum(shard_in * shard_in)
        + jnp.sum(shard_down * shard_down)
        + jnp.sum(shard_bias * shard_bias)
        + jnp.sum(small_shard * small_shard)
        + dp_zero * jnp.sum(sbias_shard * sbias_shard)
    )
    norm_square, loss = lax.psum((squares, loss_part), ("section", "dp"))
    grad_norm = jnp.sqrt(norm_square)
    scaling = jnp.minimum(1.0, CLIP / grad_norm)
    new_in, first_in, second_in = adam_update(w_in, shard_in[None], m_in, v_in, scaling)
    new_down, first_down, second_down = adam_update(
        w_down, shard_down[None], m_down, v_down, scaling
    )
    new_bias, first_bias, second_bias = adam_update(
        b_blk, shard_bias[None], m_bias, v_bias, scaling
    )
    new_small, first_small, second_small = adam_update(
        small_mats, small_shard, m_small, v_small, scaling
    )
    new_sbias, first_sbias, second_sbias = adam_update(
        small_bias, sbias_shard, m_sbias, v_sbias, scaling
    )
    return (
        loss,
        grad_norm,
        new_in,
        first_in,
        second_in,
        new_down,
        first_down,
        second_down,
        new_bias,
        first_bias,
        second_bias,
        new_small,
        first_small,
        second_small,
        new_sbias,
        first_sbias,
        second_sbias,
    )


def solution(mesh):
    in_specs = (
        P("dp", None, None),
        P("dp", None, None),
        P("dp"),
        P("dp"),
        P("dp", None),
        P("section", "dp", None),
        P("section", "dp", None),
        P("section", "dp"),
        P("dp", "section"),
        P("section"),
        P("section", "dp", None),
        P("section", "dp", None),
        P("section", "dp"),
        P("dp", "section"),
        P("section"),
        P("section", "dp", None),
        P("section", "dp", None),
        P("section", "dp"),
        P("dp", "section"),
        P("section"),
    )
    out_specs = (
        P(),
        P(),
        P("section", "dp", None),
        P("section", "dp", None),
        P("section", "dp", None),
        P("section", "dp", None),
        P("section", "dp", None),
        P("section", "dp", None),
        P("section", "dp"),
        P("section", "dp"),
        P("section", "dp"),
        P("dp", "section"),
        P("dp", "section"),
        P("dp", "section"),
        P("section"),
        P("section"),
        P("section"),
    )
    return jax.shard_map(body, mesh=mesh, in_specs=in_specs, out_specs=out_specs, check_vma=False)
```

time: 4910 us -> 2060 us (0.42)
  waiting for transfers between devices: 2900 us -> 518 us
  starting transfers between devices: 603 us -> 81.1 us
  Pallas kernels: 0 us -> 338 us
  local copies, waits for them, and re-layouts: 527 us -> 228 us
  blocking collectives: 117 us -> 36.9 us
  matrix products: 452 us -> 519 us
    reduce_scatter x4 -> x0, waiting for transfers between devices: 1130 us -> none  [the longest x1 410 us: body(): lax.psum_scatter(grad_dense, 'dp', scatter_dimension=0, tiled=True)]
    ppermute x20 -> x12, waiting for transfers between devices: 1160 us -> 117 us  [passed_along(): lax.ppermute(value, axis, [(source, source + steps) for source in range(f...]
    ppermute x20 -> x12, starting transfers between devices: 603 us -> 37.4 us  [passed_along(): lax.ppermute(value, axis, [(source, source + steps) for source in range(f...]
    all_gather x4, waiting for transfers between devices: 468 us -> 125 us  [gathered(): return lax.all_gather(value, axis, axis=dim, tiled=True)]
    pallas_call x0 -> x25, Pallas kernels: none -> 338 us  [the longest x11 159 us: share(): pl.pallas_call(functools.partial(share_kernel, axis, count, personal), ou...]
    ppermute x0 -> x16, waiting for transfers between devices: none -> 276 us  [the longest x12 276 us: row_sums(): lax.ppermute(block.astype(jnp.bfloat16), 'dp', [(i, (i + 2 * step) % coun...]
    unnamed x12 -> x4, waiting for transfers between devices: 131 us -> 0.07 us
    dot_general x18 -> x33, matrix products: 117 us -> 230 us  [matmul_nt(): lax.dot_general(left_side, right_side, (((1,), (1,)), ((), ())), preferre...]
  transfers between devices with their start and end apart: 30 -> 32, of which waited for: 20 -> 23; matrix products, arithmetic and copies ran while one was open for 1% -> 13% of each run, Pallas kernels for 0% -> 6%
where the time goes in v1:
time: 2060 us; the launch traced here: 2040 us
  matrix products  519 us (25%)
  waiting for transfers between devices  518 us (25%)
  Pallas kernels  338 us (16%)
  other arithmetic  296 us (14%)
  local copies, waits for them, and re-layouts  228 us (11%)
  starting transfers between devices  81.1 us (4%)
  blocking collectives  36.9 us (2%)
  between operations  25.7 us (1%)
    ppermute x12, waiting for transfers between devices, row_sums(): lax.ppermute(block.astype(jnp.bfloat16), 'dp', [(i, (i + 2 * step) % coun...  276 us
    dot_general x33, matrix products, matmul_nt(): lax.dot_general(left_side, right_side, (((1,), (1,)), ((), ())), preferre...  230 us
    dot_general x31, matrix products, matmul(): return jnp.dot(left_side, right_side, preferred_element_type=jnp.float32)  219 us
    pallas_call x11, Pallas kernels, share(): pl.pallas_call(functools.partial(share_kernel, axis, count, personal), ou...  159 us
    all_gather x4, waiting for transfers between devices, gathered(): return lax.all_gather(value, axis, axis=dim, tiled=True)  125 us
    ppermute x12, waiting for transfers between devices, passed_along(): lax.ppermute(value, axis, [(source, source + steps) for source in range(f...  117 us
    dynamic_update_slice x50, other arithmetic, put(): return lax.dynamic_update_index_in_dim(whole, piece, slot, 0)  107 us
    pallas_call x7, Pallas kernels, attend_back(): pl.pallas_call(attend_back_kernel, out_shape=jax.ShapeDtypeStruct((patche...  98.5 us
  transfers between devices with their start and end apart: 32, of which 23 were waited for; matrix products, arithmetic and copies ran while one was open for 13% of the time, Pallas kernels for 6%

profile of v1, /device:TPU:0, one launch (start us, length us, event | category | flops | bytes accessed | tf_op | source)
XLA Modules:
  0.0 2042.1 jit_solution(12686539250188766526)
XLA Ops:
  23.4 12.0 share.11
  38.1 23.4 %share.12 = bf16[4,146,1186]{2,1,0:T(8,128)(2,1)} custom-call(bf16[146,1186]{1,0:T(8,128)(2,1)} %pad_maximum_fusion.4.in_ref), custom_call_target="tpu_custom_call" | custom-call | tf_op jit(solution)/shard_map/share/pallas_call | solution.py:160
  68.8 12.4 share.13
  83.7 9.9 share.14
  99.5 40.9 %share.15 = f32[8,288,128]{2,1,0:T(8,128)} custom-call(f32[8,288,128]{2,1,0:T(8,128)} %reshape.1787.in_ref), custom_call_target="tpu_custom_call" | custom-call | tf_op jit(solution)/shard_map/share/pallas_call | solution.py:160
  174.7 11.5 attend.7
  205.1 54.0 %all-gather.10.cloned.1.call-done = bf16[1152,4608]{1,0:T(8,128)(2,1)} async-done(((bf16[144,4608]{1,0:T(8,128)(2,1)}), bf16[1152,4608]{1,0:T(8,128)(2,1)}) %all-gather.10.cloned.1.call-update) | async-done | bytes 10616848 | tf_op jit(solution)/shard_map/all_gather | solution.py:407
  259.1 12.5 broadcast_in_dim.563
  289.0 71.0 %all-gather.12.cloned.1.call-done = bf16[1,4608,1152]{2,1,0:T(8,128)(2,1)} async-done(((bf16[1,576,1152]{2,1,0:T(8,128)(2,1)}), bf16[1,4608,1152]{2,1,0:T(8,128)(2,1)}) %all-gather.12.cloned.1.call-update) | async-done | bytes 10616848 | tf_op jit(solution)/shard_map/all_gather | solution.py:407
  402.8 11.5 attend.8
  421.6 10.3 bitcast_dynamic-update-slice_fusion.5
  434.4 9.2 bitcast_dynamic-update-slice_fusion.40
  450.2 10.2 collective-permute-done.1
  476.5 11.5 attend.9
  495.2 10.1 bitcast_dynamic-update-slice_fusion.4
  507.9 9.2 bitcast_dynamic-update-slice_fusion.39
  523.6 9.3 collective-permute-done.2
  548.9 11.5 attend.10
  567.7 10.3 bitcast_dynamic-update-slice_fusion.3
  580.5 9.2 bitcast_dynamic-update-slice_fusion.38
  621.6 11.5 attend.11
  640.3 10.0 bitcast_dynamic-update-slice_fusion.2
  652.9 9.1 bitcast_dynamic-update-slice_fusion.37
  693.0 11.5 attend.12
  711.8 10.3 bitcast_dynamic-update-slice_fusion.1
  724.5 9.1 bitcast_dynamic-update-slice_fusion.36
  777.0 11.5 attend.13
  821.2 9.6 dynamic-slice_bitcast_fusion.4
  830.8 9.9 bitcast_dynamic-update-slice_fusion
  853.2 12.6 copy.65
  865.8 10.5 bitcast_dynamic-update-slice_fusion.35
  901.7 15.3 share.18
  927.1 17.3 bitcast_dynamic-update-slice_fusion.20
  944.4 12.7 multiply_reduce_fusion.19
  964.7 13.9 attend_back.7
  984.1 10.7 multiply_reduce_fusion.43
  1019.7 13.6 bitcast_dynamic-update-slice_fusion.19
  1043.8 14.2 attend_back.8
  1070.4 13.2 collective-permute-done.7
  1084.7 13.4 bitcast_dynamic-update-slice_fusion.18
  1111.1 14.2 attend_back.9
  1137.7 12.3 collective-permute-done.8
  1151.1 13.4 bitcast_dynamic-update-slice_fusion.17
  1177.4 14.0 attend_back.10
  1203.8 12.0 collective-permute-done.9
  1216.9 13.6 bitcast_dynamic-update-slice_fusion.16
  1244.5 14.0 attend_back.11
  1270.9 11.3 collective-permute-done.10
  1283.2 13.3 bitcast_dynamic-update-slice_fusion.15
  1310.5 14.2 attend_back.12
  1337.1 10.3 collective-permute-done.11
  1348.5 13.5 bitcast_dynamic-update-slice_fusion.14
  1382.9 13.9 attend_back.13
  1445.9 12.1 share.16
  1510.6 18.0 fusion.459
  1537.5 15.9 fusion.460
  1616.6 33.2 %collective-permute-done.18 = bf16[144,1152]{1,0:T(8,128)(2,1)} collective-permute-done((bf16[144,1152]{1,0:T(8,128)(2,1)}, bf16[144,1152]{1,0:T(8,128)(2,1)}, u32[]{:S(2)}, u32[]{:S(2)}) %collective-permute-start.18) | collective-permute-done | bytes 331808 | tf_op jit(solution)/shard_map/ppermute | solution.py:200
  1665.6 47.9 %collective-permute-done.14 = bf16[144,3456]{1,0:T(8,128)(2,1)S(1)} collective-permute-done((bf16[144,3456]{1,0:T(8,128)(2,1)S(1)}, bf16[144,3456]{1,0:T(8,128)(2,1)S(1)}, u32[]{:S(2)}, u32[]{:S(2)}) %collective-permute-start.14) | collective-permute-done | bytes 995360 | tf_op jit(solution)/shard_map/ppermute | solution.py:200
  1741.0 16.4 collective-permute-done.21
  1757.4 27.3 %collective-permute-start.26 = (bf16[576,1152]{1,0:T(8,128)(2,1)}, bf16[576,1152]{1,0:T(8,128)(2,1)}, u32[]{:S(2)}, u32[]{:S(2)}) collective-permute-start(bf16[576,1152]{1,0:T(8,128)(2,1)} %get-tuple-element.273), channel_id=1, source_target_pairs={{0,4},{1,5},{2,6},{3,7},{4,0},{5,1},{6,2},{7,3},{8,12},{9,13},{10,... | collective-permute-start | bytes 3981320 | tf_op jit(solution)/shard_map/ppermute | solution.py:200
  1787.8 81.2 %collective-permute-done.22 = bf16[144,4608]{1,0:T(8,128)(2,1)} collective-permute-done((bf16[144,4608]{1,0:T(8,128)(2,1)S(1)}, bf16[144,4608]{1,0:T(8,128)(2,1)}, u32[]{:S(2)}, u32[]{:S(2)}) %collective-permute-start.22) | collective-permute-done | bytes 1327136 | tf_op jit(solution)/shard_map/ppermute | solution.py:200
  1874.7 78.5 %collective-permute-done.26 = bf16[576,1152]{1,0:T(8,128)(2,1)} collective-permute-done((bf16[576,1152]{1,0:T(8,128)(2,1)}, bf16[576,1152]{1,0:T(8,128)(2,1)}, u32[]{:S(2)}, u32[]{:S(2)}) %collective-permute-start.26) | collective-permute-done | bytes 1327136 | tf_op jit(solution)/shard_map/ppermute | solution.py:200
  1959.9 36.9 %all-reduce.1 = (f32[]{:T(128)}, f32[]{:T(128)}) all-reduce(f32[]{:T(128)S(6)} %select_n.521, f32[]{:T(128)S(6)} %add.1954), channel_id=1, replica_groups=mesh['section'=4,'dp'=8] {'section','dp'}, use_global_device_ids=true, to_apply=%region_35.36 | all-reduce | flops 2 | bytes 16 | tf_op jit(solution)/shard_map/psum | solution.py:657
  2011.8 22.2 %multiply_subtract_fusion = (f32[1,144,16128]{2,1,0:T(8,128)}, f32[1,144,16128]{2,1,0:T(8,128)}, f32[1,144,16128]{2,1,0:T(8,128)}) fusion(f32[1,144,16128]{2,1,0:T(8,128)} %param.25, f32[]{:T(128)S(6)} %min.60, f32[1,144,6912]{2,1,0:T(8,128)} %bitcast.1044, f32[1,144,4608]{2,1,0:T(8,128)S(1)} %bitcast.1042, f32[1,144,1152]{2,1,0:T(8,128)S(1)} %bitcast.1056, ...), kind=kLoop, calls=%fused_computation.39 | loop fusion | flops 44126208 | bytes 65028100 | tf_op jit(solution)/shard_map/sub | solution.py:366
  (1082 shorter events, 856.9 us)
Async XLA Ops:
  7.2 154.9 %all-gather.6.cloned.1.call-start = ((), (), s32[]{:S(2)}) async-start(), calls=%async_computation | async-start | bytes 8957952 | tf_op jit(solution)/shard_map/all_gather | solution.py:407
  14.5 171.8 %all-gather.8.cloned.1.call-start = ((), (), s32[]{:S(2)}) async-start(), calls=%async_computation.1 | async-start | bytes 2985984 | tf_op jit(solution)/shard_map/all_gather | solution.py:407
  16.4 242.7 %all-gather.10.cloned.1.call-start = ((), (), s32[]{:S(2)}) async-start(), calls=%async_computation.2 | async-start | bytes 11943936 | tf_op jit(solution)/shard_map/all_gather | solution.py:407
  19.0 341.1 %all-gather.12.cloned.1.call-start = ((), (), s32[]{:S(2)}) async-start(), calls=%async_computation.3 | async-start | bytes 11943936 | tf_op jit(solution)/shard_map/all_gather | solution.py:407
  36.5 30.1 %copy-start.95 = (f32[16128]{0:T(1024)}, f32[16128]{0:T(1024)S(1)}, u32[]{:S(2)}) copy-start(f32[16128]{0:T(1024)S(1)} %reduce_precision.27) | copy-start | bytes 193540
  64.2 87.5 %copy-start.88 = (bf16[1152,16]{1,0:T(8,128)(2,1)}, bf16[1152,16]{1,0:T(8,128)(2,1)S(1)}, u32[]{:S(2)}) copy-start(bf16[1152,16]{1,0:T(8,128)(2,1)S(1)} %convert_element_type.580) | copy-start | bytes 110596
  66.6 29.6 %copy-start.81 = (bf16[144,1186]{1,0:T(8,128)(2,1)}, bf16[144,1186]{1,0:T(8,128)(2,1)S(1)}, u32[]{:S(2)}) copy-start(bf16[144,1186]{1,0:T(8,128)(2,1)S(1)} %get-tuple-element.295) | copy-start | bytes 1024708
  66.6 29.6 %copy-start.94 = (bf16[144,1186]{1,0:T(8,128)(2,1)}, bf16[144,1186]{1,0:T(8,128)(2,1)S(1)}, u32[]{:S(2)}) copy-start(bf16[144,1186]{1,0:T(8,128)(2,1)S(1)} %get-tuple-element.294) | copy-start | bytes 1024708
  99.5 42.4 %slice-start.19 = ((f32[16128]{0:T(1024)}), f32[6912]{0:T(1024)S(1)}, s32[]{:S(2)}) async-start(f32[16128]{0:T(1024)} %copy-done.95), calls=%async_computation.23 | async-start | bytes 57344 | tf_op jit(solution)/shard_map/slice | solution.py:478
  205.1 66.6 %copy-start.195 = (f32[4608]{0:T(1024)S(1)}, f32[4608]{0:T(1024)}, u32[]{:S(2)}) copy-start(f32[4608]{0:T(1024)} %slice.682) | copy-start | bytes 55300
  370.3 16.4 collective-permute-start
  443.7 16.7 collective-permute-start.1
  517.2 15.7 collective-permute-start.2
  589.8 15.7 collective-permute-start.3
  662.1 14.8 collective-permute-start.4
  733.8 14.1 collective-permute-start.5
  767.6 216.5 %copy-start.239 = (f32[256]{0:T(256)}, f32[256]{0:T(256)S(1)}, u32[]{:S(2)}) copy-start(f32[256]{0:T(256)S(1)} %broadcast_multiply_fusion.7) | copy-start | bytes 3076
  819.6 124.8 %copy-start.220 = (f32[256]{0:T(256)}, f32[256]{0:T(256)S(1)}, u32[]{:S(2)}) copy-start(f32[256]{0:T(256)S(1)} %broadcast_multiply_fusion.10) | copy-start | bytes 3076
  879.0 37.9 %copy-start.132 = (f32[4,256]{1,0:T(4,128)}, f32[4,256]{1,0:T(4,128)S(1)}, u32[]{:S(2)}) copy-start(f32[4,256]{1,0:T(4,128)S(1)} %broadcast_multiply_fusion.4) | copy-start | bytes 12292
  882.1 34.8 %copy-start.208 = (f32[4,256]{1,0:T(4,128)}, f32[4,256]{1,0:T(4,128)S(1)}, u32[]{:S(2)}) copy-start(f32[4,256]{1,0:T(4,128)S(1)} %add_rsqrt_fusion) | copy-start | bytes 12292
  921.4 36.6 %copy-start = (f32[4,256,1152]{2,1,0:T(8,128)}, f32[4,256,1152]{2,1,0:T(8,128)S(1)}, u32[]{:S(2)}) copy-start(f32[4,256,1152]{2,1,0:T(8,128)S(1)} %subtract_multiply_fusion) | copy-start | bytes 14155780
  1000.1 17.1 collective-permute-start.6
  1005.4 27.9 %slice-start.20 = ((s8[10616832]{0:T(1024)(128)(4,1)}), s8[4194304]{0:T(1024)(128)(4,1)S(1)}, s32[]{:S(2)}) async-start(s8[10616832]{0:T(1024)(128)(4,1)} %bitcast.1074), calls=%async_computation.24 | async-start | bytes 8388608
  1043.8 39.9 %slice-start = ((s8[4718592]{0:T(1024)(128)(4,1)}), s8[524288]{0:T(1024)(128)(4,1)S(1)}, s32[]{:S(2)}) async-start(s8[4718592]{0:T(1024)(128)(4,1)} %bitcast.1027), calls=%async_computation.4 | async-start | bytes 1048576
  1058.0 25.7 %slice-start.1 = ((s8[4718592]{0:T(1024)(128)(4,1)}), s8[4194304]{0:T(1024)(128)(4,1)S(1)}, s32[]{:S(2)}) async-start(s8[4718592]{0:T(1024)(128)(4,1)} %bitcast.1027), calls=%async_computation.5 | async-start | bytes 8388608
  1067.6 16.0 collective-permute-start.7
  1111.1 39.0 %slice-start.2 = ((s8[4718592]{0:T(1024)(128)(4,1)}), s8[524288]{0:T(1024)(128)(4,1)S(1)}, s32[]{:S(2)}) async-start(s8[4718592]{0:T(1024)(128)(4,1)} %bitcast.1029), calls=%async_computation.6 | async-start | bytes 1048576
  1125.3 24.8 %slice-start.3 = ((s8[4718592]{0:T(1024)(128)(4,1)}), s8[4194304]{0:T(1024)(128)(4,1)S(1)}, s32[]{:S(2)}) async-start(s8[4718592]{0:T(1024)(128)(4,1)} %bitcast.1029), calls=%async_computation.7 | async-start | bytes 8388608
  1134.9 15.1 collective-permute-start.8
  1177.4 38.4 %slice-start.4 = ((s8[4718592]{0:T(1024)(128)(4,1)}), s8[524288]{0:T(1024)(128)(4,1)S(1)}, s32[]{:S(2)}) async-start(s8[4718592]{0:T(1024)(128)(4,1)} %bitcast.1031), calls=%async_computation.8 | async-start | bytes 1048576
  1191.4 24.4 %slice-start.5 = ((s8[4718592]{0:T(1024)(128)(4,1)}), s8[4194304]{0:T(1024)(128)(4,1)S(1)}, s32[]{:S(2)}) async-start(s8[4718592]{0:T(1024)(128)(4,1)} %bitcast.1031), calls=%async_computation.9 | async-start | bytes 8388608
  1201.1 14.8 collective-permute-start.9
  1242.7 39.6 %slice-start.6 = ((s8[4718592]{0:T(1024)(128)(4,1)}), s8[524288]{0:T(1024)(128)(4,1)S(1)}, s32[]{:S(2)}) async-start(s8[4718592]{0:T(1024)(128)(4,1)} %bitcast.1033), calls=%async_computation.10 | async-start | bytes 1048576
  1258.5 23.7 %slice-start.7 = ((s8[4718592]{0:T(1024)(128)(4,1)}), s8[4194304]{0:T(1024)(128)(4,1)S(1)}, s32[]{:S(2)}) async-start(s8[4718592]{0:T(1024)(128)(4,1)} %bitcast.1033), calls=%async_computation.11 | async-start | bytes 8388608
  1268.1 14.1 collective-permute-start.10
  1308.7 38.8 %slice-start.8 = ((s8[4718592]{0:T(1024)(128)(4,1)}), s8[524288]{0:T(1024)(128)(4,1)S(1)}, s32[]{:S(2)}) async-start(s8[4718592]{0:T(1024)(128)(4,1)} %bitcast.1035), calls=%async_computation.12 | async-start | bytes 1048576
  1334.3 13.1 collective-permute-start.11
  1337.1 24.9 %copy-start.130 = (bf16[1,6912]{1,0:T(2,128)(2,1)}, bf16[1,6912]{1,0:T(2,128)(2,1)S(1)}, u32[]{:S(2)}) copy-start(bf16[1,6912]{1,0:T(2,128)(2,1)S(1)} %constant_dynamic-update-slice_fusion.34) | copy-start | bytes 41476
  1347.4 23.1 %copy-start.65 = (bf16[256,1152]{1,0:T(8,128)(2,1)}, bf16[256,1152]{1,0:T(8,128)(2,1)S(1)}, u32[]{:S(2)}) copy-start(bf16[256,1152]{1,0:T(8,128)(2,1)S(1)} %collective-permute-done.11) | copy-start | bytes 1769476
  1445.0 25.4 %copy-start.82 = (bf16[144,1186]{1,0:T(8,128)(2,1)S(1)}, bf16[144,1186]{1,0:T(8,128)(2,1)}, u32[]{:S(2)}) copy-start(bf16[144,1186]{1,0:T(8,128)(2,1)} %copy-done.81) | copy-start | bytes 1024708
  1492.4 98.5 %collective-permute-start.16 = (f32[4,144,1152]{2,1,0:T(8,128)}, f32[4,144,1152]{2,1,0:T(8,128)}, u32[]{:S(2)}, u32[]{:S(2)}) collective-permute-start(f32[4,144,1152]{2,1,0:T(8,128)} %dynamic-slice_bitcast_fusion.3), channel_id=1, source_target_pairs={{0,1},{1,0},{2,3},{3,2},{4,5},{5,4},{6,7},{7,6},{8,9},{9,8},{10,11... | collective-permute-start | bytes 7962632 | tf_op jit(solution)/shard_map/ppermute | solution.py:196
  1501.3 36.2 %slice-start.14 = ((s8[9437184]{0:T(1024)(128)(4,1)}), s8[1048576]{0:T(1024)(128)(4,1)S(1)}, s32[]{:S(2)}) async-start(s8[9437184]{0:T(1024)(128)(4,1)} %bitcast.1046), calls=%async_computation.18 | async-start | bytes 2097152
  1510.2 88.5 %collective-permute-start.12 = (f32[4,144,3456]{2,1,0:T(8,128)}, f32[4,144,3456]{2,1,0:T(8,128)}, u32[]{:S(2)}, u32[]{:S(2)}) collective-permute-start(f32[4,144,3456]{2,1,0:T(8,128)} %dynamic-slice_bitcast_fusion.2), channel_id=1, source_target_pairs={{0,1},{1,0},{2,3},{3,2},{4,5},{5,4},{6,7},{7,6},{8,9},{9,8},{10,11... | collective-permute-start | bytes 23887880 | tf_op jit(solution)/shard_map/ppermute | solution.py:196
  1510.6 26.9 %slice-start.15 = ((s8[9437184]{0:T(1024)(128)(4,1)}), s8[4194304]{0:T(1024)(128)(4,1)S(1)}, s32[]{:S(2)}) async-start(s8[9437184]{0:T(1024)(128)(4,1)} %bitcast.1046), calls=%async_computation.19 | async-start | bytes 8388608
  1510.6 26.9 %slice-start.16 = ((s8[9437184]{0:T(1024)(128)(4,1)}), s8[4194304]{0:T(1024)(128)(4,1)S(1)}, s32[]{:S(2)}) async-start(s8[9437184]{0:T(1024)(128)(4,1)} %bitcast.1046), calls=%async_computation.20 | async-start | bytes 8388608
  1537.4 178.0 %collective-permute-start.20 = (f32[4,144,4608]{2,1,0:T(8,128)}, f32[4,144,4608]{2,1,0:T(8,128)}, u32[]{:S(2)}, u32[]{:S(2)}) collective-permute-start(f32[4,144,4608]{2,1,0:T(8,128)} %dynamic-slice_bitcast_fusion.1), channel_id=1, source_target_pairs={{0,1},{1,0},{2,3},{3,2},{4,5},{5,4},{6,7},{7,6},{8,9},{9,8},{10,11... | collective-permute-start | bytes 31850504 | tf_op jit(solution)/shard_map/ppermute | solution.py:196
  1562.3 165.1 %collective-permute-start.24 = (f32[4,576,1152]{2,1,0:T(8,128)}, f32[4,576,1152]{2,1,0:T(8,128)}, u32[]{:S(2)}, u32[]{:S(2)}) collective-permute-start(f32[4,576,1152]{2,1,0:T(8,128)} %dynamic-slice_bitcast_fusion), channel_id=1, source_target_pairs={{0,1},{1,0},{2,3},{3,2},{4,5},{5,4},{6,7},{7,6},{8,9},{9,8},{10,11... | collective-permute-start | bytes 31850504 | tf_op jit(solution)/shard_map/ppermute | solution.py:196
  1594.8 12.7 collective-permute-start.17
  1596.4 17.1 collective-permute-start.19
  1598.7 51.1 %collective-permute-start.18 = (bf16[144,1152]{1,0:T(8,128)(2,1)}, bf16[144,1152]{1,0:T(8,128)(2,1)}, u32[]{:S(2)}, u32[]{:S(2)}) collective-permute-start(bf16[144,1152]{1,0:T(8,128)(2,1)} %get-tuple-element.292), channel_id=1, source_target_pairs={{0,4},{1,5},{2,6},{3,7},{4,0},{5,1},{6,2},{7,3},{8,12},{9,13},{10,... | collective-permute-start | bytes 995336 | tf_op jit(solution)/shard_map/ppermute | solution.py:200
  1605.3 46.5 %copy-start.86 = (bf16[8,4,6912]{2,1,0:T(4,128)(2,1)S(1)}, bf16[8,4,6912]{2,1,0:T(4,128)(2,1)}, u32[]{:S(2)}) copy-start(bf16[8,4,6912]{2,1,0:T(4,128)(2,1)} %share.16) | copy-start | bytes 1327108
  1605.3 46.5 %copy-start.99 = (f32[8,4,144]{2,1,0:T(4,128)S(1)}, f32[8,4,144]{2,1,0:T(4,128)}, u32[]{:S(2)}) copy-start(f32[8,4,144]{2,1,0:T(4,128)} %share.14) | copy-start | bytes 55300
  1607.5 49.2 %collective-permute-start.13 = (bf16[144,3456]{1,0:T(8,128)(2,1)S(1)}, bf16[144,3456]{1,0:T(8,128)(2,1)S(1)}, u32[]{:S(2)}, u32[]{:S(2)}) collective-permute-start(bf16[144,3456]{1,0:T(8,128)(2,1)S(1)} %get-tuple-element.285), channel_id=1, source_target_pairs={{0,2},{1,3},{2,4},{3,5},{4,6},{5,7},{6,0},{7,1},{8,10},{9,11},{10,... | collective-permute-start | bytes 2985992 | tf_op jit(solution)/shard_map/ppermute | solution.py:200
  1613.5 52.2 %collective-permute-start.15 = (bf16[144,3456]{1,0:T(8,128)(2,1)S(1)}, bf16[144,3456]{1,0:T(8,128)(2,1)S(1)}, u32[]{:S(2)}, u32[]{:S(2)}) collective-permute-start(bf16[144,3456]{1,0:T(8,128)(2,1)S(1)} %get-tuple-element.286), channel_id=1, source_target_pairs={{0,6},{1,7},{2,0},{3,1},{4,2},{5,3},{6,4},{7,5},{8,14},{9,15},{10,... | collective-permute-start | bytes 2985992 | tf_op jit(solution)/shard_map/ppermute | solution.py:200
  1649.7 63.8 %collective-permute-start.14 = (bf16[144,3456]{1,0:T(8,128)(2,1)S(1)}, bf16[144,3456]{1,0:T(8,128)(2,1)S(1)}, u32[]{:S(2)}, u32[]{:S(2)}) collective-permute-start(bf16[144,3456]{1,0:T(8,128)(2,1)S(1)} %get-tuple-element.287), channel_id=1, source_target_pairs={{0,4},{1,5},{2,6},{3,7},{4,0},{5,1},{6,2},{7,3},{8,12},{9,13},{10,... | collective-permute-start | bytes 2985992 | tf_op jit(solution)/shard_map/ppermute | solution.py:200
  1723.5 33.9 %collective-permute-start.21 = (bf16[144,4608]{1,0:T(8,128)(2,1)S(1)}, bf16[144,4608]{1,0:T(8,128)(2,1)S(1)}, u32[]{:S(2)}, u32[]{:S(2)}) collective-permute-start(bf16[144,4608]{1,0:T(8,128)(2,1)S(1)} %get-tuple-element.274), channel_id=1, source_target_pairs={{0,2},{1,3},{2,4},{3,5},{4,6},{5,7},{6,0},{7,1},{8,10},{9,11},{10,... | collective-permute-start | bytes 3981320 | tf_op jit(solution)/shard_map/ppermute | solution.py:200
  1723.6 63.2 %collective-permute-start.23 = (bf16[144,4608]{1,0:T(8,128)(2,1)S(1)}, bf16[144,4608]{1,0:T(8,128)(2,1)S(1)}, u32[]{:S(2)}, u32[]{:S(2)}) collective-permute-start(bf16[144,4608]{1,0:T(8,128)(2,1)S(1)} %get-tuple-element.275), channel_id=1, source_target_pairs={{0,6},{1,7},{2,0},{3,1},{4,2},{5,3},{6,4},{7,5},{8,14},{9,15},{10,... | collective-permute-start | bytes 3981320 | tf_op jit(solution)/shard_map/ppermute | solution.py:200
  1727.4 141.7 %collective-permute-start.22 = (bf16[144,4608]{1,0:T(8,128)(2,1)S(1)}, bf16[144,4608]{1,0:T(8,128)(2,1)}, u32[]{:S(2)}, u32[]{:S(2)}) collective-permute-start(bf16[144,4608]{1,0:T(8,128)(2,1)S(1)} %get-tuple-element.276), channel_id=1, source_target_pairs={{0,4},{1,5},{2,6},{3,7},{4,0},{5,1},{6,2},{7,3},{8,12},{9,13},{10,... | collective-permute-start | bytes 3981320 | tf_op jit(solution)/shard_map/ppermute | solution.py:200
  1737.2 137.5 %collective-permute-start.25 = (bf16[576,1152]{1,0:T(8,128)(2,1)}, bf16[576,1152]{1,0:T(8,128)(2,1)S(1)}, u32[]{:S(2)}, u32[]{:S(2)}) collective-permute-start(bf16[576,1152]{1,0:T(8,128)(2,1)} %get-tuple-element.271), channel_id=1, source_target_pairs={{0,2},{1,3},{2,4},{3,5},{4,6},{5,7},{6,0},{7,1},{8,10},{9,11},{10,... | collective-permute-start | bytes 3981320 | tf_op jit(solution)/shard_map/ppermute | solution.py:200
  1737.8 136.9 %collective-permute-start.27 = (bf16[576,1152]{1,0:T(8,128)(2,1)}, bf16[576,1152]{1,0:T(8,128)(2,1)S(1)}, u32[]{:S(2)}, u32[]{:S(2)}) collective-permute-start(bf16[576,1152]{1,0:T(8,128)(2,1)} %get-tuple-element.272), channel_id=1, source_target_pairs={{0,6},{1,7},{2,0},{3,1},{4,2},{5,3},{6,4},{7,5},{8,14},{9,15},{10,... | collective-permute-start | bytes 3981320 | tf_op jit(solution)/shard_map/ppermute | solution.py:200
  1757.4 114.0 %copy-start.21 = (f32[144,3456]{1,0:T(8,128)S(1)}, f32[144,3456]{1,0:T(8,128)}, u32[]{:S(2)}) copy-start(f32[144,3456]{1,0:T(8,128)} %fusion.195) | copy-start | bytes 5971972
  1757.4 114.0 %copy-start.24 = (f32[144,6912,1]{1,0,2:T(8,128)S(1)}, f32[144,6912,1]{1,0,2:T(8,128)}, u32[]{:S(2)}) copy-start(f32[144,6912,1]{1,0,2:T(8,128)} %fusion.308) | copy-start | bytes 11943940
  1757.4 114.0 %copy-start.54 = (f32[144,1152]{1,0:T(8,128)S(1)}, f32[144,1152]{1,0:T(8,128)}, u32[]{:S(2)}) copy-start(f32[144,1152]{1,0:T(8,128)} %fusion.258) | copy-start | bytes 1990660
  1757.4 195.7 %collective-permute-start.26 = (bf16[576,1152]{1,0:T(8,128)(2,1)}, bf16[576,1152]{1,0:T(8,128)(2,1)}, u32[]{:S(2)}, u32[]{:S(2)}) collective-permute-start(bf16[576,1152]{1,0:T(8,128)(2,1)} %get-tuple-element.273), channel_id=1, source_target_pairs={{0,4},{1,5},{2,6},{3,7},{4,0},{5,1},{6,2},{7,3},{8,12},{9,13},{10,... | collective-permute-start | bytes 3981320 | tf_op jit(solution)/shard_map/ppermute | solution.py:200
  (244 other events, 1656.1 us)
Sparse Core Ops, SparseCore 0:
  14.6 88.6 all-gather.5
  105.5 47.0 all-gather.7
  154.8 104.2 all-gather.9
  261.2 98.8 all-gather.11

commit v2 on v1

--- a/solution.py
+++ b/solution.py
@@ -183,27 +183,41 @@
     return share(value, axis, True, ident)
 
 
-def row_sums(left_side, right_side):
-    product = matmul_tn(left_side, right_side)
+def row_sums(pairs):
     count = lax.axis_size("dp")
     if count != DIRECT:
-        return lax.psum_scatter(product, "dp", scatter_dimension=0, tiled=True)
+        products = [matmul_tn(left_side, right_side) for left_side, right_side in pairs]
+        return (
+            [lax.psum_scatter(one, "dp", scatter_dimension=0, tiled=True) for one in products],
+            products[-1],
+        )
     here = lax.axis_index("dp")
     core, chip, chips = (here % 2, here // 2, count // 2)
-    parted = product.reshape(chips, 2, product.shape[0] // count, product.shape[1])
-    other = lax.dynamic_index_in_dim(parted, 1 - core, 1, keepdims=False)
-    same = lax.dynamic_index_in_dim(parted, core, 1, keepdims=False)
-    both = same + lax.ppermute(other, "dp", [(i, i ^ 1) for i in range(count)])
-    total = lax.dynamic_index_in_dim(both, chip, 0, keepdims=False)
-    for step in range(1, chips):
-        block = lax.dynamic_index_in_dim(both, (chip + step) % chips, 0, keepdims=False)
-        arrived = lax.ppermute(
-            block.astype(jnp.bfloat16),
-            "dp",
-            [(i, (i + 2 * step) % count) for i in range(count)],
-        )
-        total = total + arrived.astype(jnp.float32)
-    return total
+    totals, blocks = ([], [])
+    for index, pair in enumerate(pairs):
+        if index >= 2:
+            pair = lax.optimization_barrier((pair, blocks[index - 2]))[0]
+        product = matmul_tn(*pair)
+        parted = product.reshape(chips, 2, product.shape[0] // count, product.shape[1])
+        other = lax.dynamic_index_in_dim(parted, 1 - core, 1, keepdims=False)
+        same = lax.dynamic_index_in_dim(parted, core, 1, keepdims=False)
+        both = same + lax.ppermute(other, "dp", [(i, i ^ 1) for i in range(count)])
+        total = lax.dynamic_index_in_dim(both, chip, 0, keepdims=False)
+        blocks.append(
+            [
+                lax.dynamic_index_in_dim(both, (chip + step) % chips, 0, keepdims=False).astype(
+                    jnp.bfloat16
+                )
+                for step in range(1, chips)
+            ]
+        )
+        for step in range(1, chips):
+            arrived = lax.ppermute(
+                blocks[-1][step - 1], "dp", [(i, (i + 2 * step) % count) for i in range(count)]
+            )
+            total = total + arrived.astype(jnp.float32)
+        totals.append(total)
+    return (totals, blocks[-1])
 
 
 def attend_kernel(qkv_ref, out_ref):
@@ -218,20 +232,6 @@
         out_ref[:, at : at + HEAD_DIM] = matmul(attention.astype(jnp.bfloat16), value).astype(
             jnp.bfloat16
         )
-
-
-def attend(qkv_low):
-    patches = qkv_low.shape[0]
-    return pl.pallas_call(
-        attend_kernel,
-        out_shape=jax.ShapeDtypeStruct((patches, D), jnp.bfloat16),
-        cost_estimate=pl.CostEstimate(
-            flops=4 * patches * patches * D,
-            bytes_accessed=8 * patches * D,
-            transcendentals=HEADS * patches * patches,
-        ),
-        name="attend",
-    )(qkv_low)
 
 
 def attend_back_kernel(qkv_ref, grad_ref, out_ref):
@@ -259,78 +259,355 @@
         )
 
 
-def attend_back(qkv_low, grad):
-    patches = qkv_low.shape[0]
-    return pl.pallas_call(
-        attend_back_kernel,
-        out_shape=jax.ShapeDtypeStruct((patches, 3 * D), jnp.bfloat16),
-        cost_estimate=pl.CostEstimate(
-            flops=10 * patches * patches * D,
-            bytes_accessed=14 * patches * D,
-            transcendentals=HEADS * patches * patches,
-        ),
-        name="attend_back",
-    )(qkv_low, grad)
-
-
-def image_forward(residual, modulation, weights):
-    w_qkv, w_proj, w_hidden, w_second, bias = weights
-    normed_one, unused = normalize(residual)
-    mixed_one = (normed_one * (1.0 + modulation[1]) + modulation[0]).astype(jnp.bfloat16)
-    qkv_bias = jnp.concatenate([bias[:D], jnp.zeros((D,), jnp.float32), bias[D : 2 * D]])
-    qkv_low = (matmul(mixed_one, w_qkv) + qkv_bias).astype(jnp.bfloat16)
-    att_low = attend(qkv_low)
-    branch = matmul(att_low, w_proj) + bias[2 * D : 3 * D]
-    middle = residual + modulation[2] * branch
-    normed_two, unused = normalize(middle)
-    mixed_two = (normed_two * (1.0 + modulation[4]) + modulation[3]).astype(jnp.bfloat16)
-    pre_act = matmul(mixed_two, w_hidden) + bias[3 * D : 3 * D + FF]
-    act_low = gelu_tanh(pre_act).astype(jnp.bfloat16)
-    second = matmul(act_low, w_second) + bias[3 * D + FF : 4 * D + FF]
-    output = middle + modulation[5] * second
-    return (
-        output,
-        (
-            residual,
-            mixed_one,
-            qkv_low,
-            att_low,
-            branch,
-            middle,
-            mixed_two,
-            pre_act,
-            act_low,
-            second,
-        ),
-    )
-
-
-def image_backward(grad_out, kept, modulation, weights):
-    w_qkv, w_proj, w_hidden, w_second, unused = weights
-    residual, qkv_low, branch, middle, pre_act, second = kept
-    d_second = (grad_out * modulation[5]).astype(jnp.bfloat16)
-    d_gate_two = jnp.sum(grad_out * second, axis=0)
-    d_pre = (matmul_nt(d_second, w_second) * gelu_grad(pre_act)).astype(jnp.bfloat16)
-    d_mixed_two = matmul_nt(d_pre, w_hidden)
-    normed_two, invstd_two = normalize(middle)
-    d_shift_two = jnp.sum(d_mixed_two, axis=0)
-    d_scale_two = jnp.sum(d_mixed_two * normed_two, axis=0)
-    d_middle = grad_out + norm_back(d_mixed_two * (1.0 + modulation[4]), normed_two, invstd_two)
-    d_gate_one = jnp.sum(d_middle * branch, axis=0)
-    d_branch = (d_middle * modulation[2]).astype(jnp.bfloat16)
-    d_att = matmul_nt(d_branch, w_proj).astype(jnp.bfloat16)
-    d_qkv = attend_back(qkv_low, d_att)
-    d_mixed_one = matmul_nt(d_qkv, w_qkv)
-    normed_one, invstd_one = normalize(residual)
-    d_shift_one = jnp.sum(d_mixed_one, axis=0)
-    d_scale_one = jnp.sum(d_mixed_one * normed_one, axis=0)
-    d_residual = d_middle + norm_back(
-        d_mixed_one * (1.0 + modulation[1]), normed_one, invstd_one
-    )
-    d_ada = jnp.concatenate(
-        [d_shift_one, d_scale_one, d_gate_one, d_shift_two, d_scale_two, d_gate_two]
-    ).astype(jnp.bfloat16)
-    return (d_residual, (d_second, d_pre, d_branch, d_qkv, d_ada))
+ROW_BLOCK = 64
+KEPT = (
+    ("residual", D, jnp.float32),
+    ("mixed_one", D, jnp.bfloat16),
+    ("qkv", 3 * D, jnp.bfloat16),
+    ("att", D, jnp.bfloat16),
+    ("branch", D, jnp.float32),
+    ("middle", D, jnp.float32),
+    ("mixed_two", D, jnp.bfloat16),
+    ("pre", FF, jnp.float32),
+    ("act", FF, jnp.bfloat16),
+    ("second", D, jnp.float32),
+    ("output", D, jnp.float32),
+)
+READ = ("residual", "qkv", "branch", "middle", "pre", "second")
+MADE = (
+    ("d_second", D, jnp.bfloat16),
+    ("d_pre", FF, jnp.bfloat16),
+    ("d_branch", D, jnp.bfloat16),
+    ("d_qkv", 3 * D, jnp.bfloat16),
+    ("d_residual", D, jnp.bfloat16),
+)
+WEIGHTS = ((D, 3 * D), (D, D), (D, FF), (FF, D))
+
+
+def by_rows(patches, step):
+    @pl.loop(0, patches // ROW_BLOCK)
+    def run(index):
+        step(pl.ds(pl.multiple_of(index * ROW_BLOCK, ROW_BLOCK), ROW_BLOCK))
+
+
+def started(source, target, sem):
+    copy = pltpu.make_async_copy(source, target, sem)
+    copy.start()
+    return copy
+
+
+def forward_kernel(patches, given, meta, arrived, bias, ada, tokens, wq, wp, wh, ws, *refs):
+    count = len(KEPT)
+    send, outs = (refs[given], refs[given + 1 : given + 1 + count])
+    scratch = refs[given + 1 + count :]
+    kept = {name: scratch[i] for i, (name, unused, kind) in enumerate(KEPT)}
+    wq_v, wp_v, wh_v, ws_v, w_sem, x_sem, out_sem = scratch[count:]
+    loads = [started(wq.at[:, pl.ds(i * D, D)], wq_v.at[:, pl.ds(i * D, D)], w_sem.at[i]) for i in range(3)]
+    loads.append(started(wp, wp_v, w_sem.at[3]))
+    loads += [
+        started(wh.at[:, pl.ds(i * D, D)], wh_v.at[:, pl.ds(i * D, D)], w_sem.at[4 + i])
+        for i in range(FF // D)
+    ]
+    third = D // 3
+    loads += [
+        started(ws.at[:, pl.ds(i * third, third)], ws_v.at[:, pl.ds(i * third, third)], w_sem.at[8 + i])
+        for i in range(3)
+    ]
+    saves = []
+
+    def start_if_valid(copy):
+        @pl.when(meta[3] == 1)
+        def start():
+            copy.start()
+
+    def save(name):
+        index = [item[0] for item in KEPT].index(name)
+        saves.append(pltpu.make_async_copy(kept[name], outs[index].at[meta[0]], out_sem.at[index]))
+        start_if_valid(saves[-1])
+
+    residual = kept["residual"]
+
+    @pl.when(meta[2] == 1)
+    def take_tokens():
+        started(tokens.at[meta[1]], residual, x_sem).wait()
+
+    @pl.when(meta[2] == 0)
+    def take_arrived():
+        residual[...] = arrived[...].astype(jnp.float32)
+
+    save("residual")
+    modulation = ada[meta[0]]
+
+    def mix_one(at):
+        normed, unused = normalize(residual[at])
+        kept["mixed_one"][at] = (normed * (1.0 + modulation[1:2]) + modulation[0:1]).astype(
+            jnp.bfloat16
+        )
+
+    by_rows(patches, mix_one)
+    save("mixed_one")
+    for part in range(3):
+        loads[part].wait()
+        cols = slice(part * D, part * D + D)
+        kept["qkv"][:, cols] = (
+            matmul(kept["mixed_one"][...], wq_v[:, cols]) + bias[:, cols]
+        ).astype(jnp.bfloat16)
+    save("qkv")
+    attend_kernel(kept["qkv"], kept["att"])
+    save("att")
+    loads[3].wait()
+    kept["branch"][...] = matmul(kept["att"][...], wp_v[...]) + bias[:, 3 * D : 4 * D]
+    save("branch")
+
+    def mix_two(at):
+        middle = residual[at] + modulation[2:3] * kept["branch"][at]
+        kept["middle"][at] = middle
+        normed, unused = normalize(middle)
+        kept["mixed_two"][at] = (normed * (1.0 + modulation[4:5]) + modulation[3:4]).astype(
+            jnp.bfloat16
+        )
+
+    by_rows(patches, mix_two)
+    save("middle")
+    save("mixed_two")
+    for part in range(FF // D):
+        loads[4 + part].wait()
+        cols = slice(part * D, part * D + D)
+        pre = (
+            matmul(kept["mixed_two"][...], wh_v[:, cols])
+            + bias[:, 4 * D + part * D : 5 * D + part * D]
+        )
+        kept["pre"][:, cols] = pre
+        kept["act"][:, cols] = gelu_tanh(pre).astype(jnp.bfloat16)
+    save("pre")
+    save("act")
+    for part in range(3):
+        loads[8 + part].wait()
+        cols = slice(part * third, part * third + third)
+        second = (
+            matmul(kept["act"][...], ws_v[:, cols])
+            + bias[:, 4 * D + FF + part * third : 4 * D + FF + part * third + third]
+        )
+        kept["second"][:, cols] = second
+        output = kept["middle"][:, cols] + modulation[5:6, cols] * second
+        kept["output"][:, cols] = output
+        send[:, cols] = output.astype(jnp.bfloat16)
+    save("second")
+    save("output")
+
+    @pl.when(meta[3] == 1)
+    def finish():
+        for copy in saves:
+            copy.wait()
+
+
+def backward_kernel(patches, given, meta, arrived, ada, head_grad, wq, wp, wh, ws, *refs):
+    reads, made = (len(READ), len(MADE))
+    sources, refs = (refs[:reads], refs[reads + given :])
+    send, outs, ada_out = (refs[0], refs[1 : made + 1], refs[made + 1])
+    scratch = refs[made + 2 :]
+    kept = {name: scratch[i] for i, name in enumerate(READ)}
+    grads = {name: scratch[reads + i] for i, (name, unused, kind) in enumerate(MADE)}
+    (
+        flow,
+        mixed,
+        att_grad,
+        sums,
+        wq_v,
+        wp_v,
+        wh_v,
+        ws_v,
+        w_sem,
+        in_sem,
+        x_sem,
+        out_sem,
+    ) = scratch[reads + made :]
+
+    def fetch(name):
+        index = READ.index(name)
+        return started(sources[index].at[meta[0]], kept[name], in_sem.at[index])
+
+    fetched = {"second": fetch("second")}
+    loads = [started(ws.at[pl.ds(i * D, D)], ws_v.at[pl.ds(i * D, D)], w_sem.at[i]) for i in range(FF // D)]
+    for name in ("pre", "middle", "branch", "qkv", "residual"):
+        fetched[name] = fetch(name)
+    third = D // 3
+    loads += [
+        started(wh.at[pl.ds(i * third, third)], wh_v.at[pl.ds(i * third, third)], w_sem.at[4 + i])
+        for i in range(3)
+    ]
+    loads.append(started(wp, wp_v, w_sem.at[7]))
+    loads += [
+        started(wq.at[pl.ds(i * third, third)], wq_v.at[pl.ds(i * third, third)], w_sem.at[8 + i])
+        for i in range(3)
+    ]
+    saves = []
+
+    def start_if_valid(copy):
+        @pl.when(meta[3] == 1)
+        def start():
+            copy.start()
+
+    def save(name):
+        index = [item[0] for item in MADE].index(name)
+        saves.append(pltpu.make_async_copy(grads[name], outs[index].at[meta[0]], out_sem.at[index]))
+        start_if_valid(saves[-1])
+
+    @pl.when(meta[2] == 1)
+    def take_head():
+        started(head_grad.at[meta[1]], flow, x_sem).wait()
+
+    @pl.when(meta[2] == 0)
+    def take_arrived():
+        flow[...] = arrived[...].astype(jnp.float32)
+
+    modulation = ada[meta[0]]
+    sums[...] = jnp.zeros_like(sums)
+
+    def add_sum(row, values):
+        sums[row : row + 1] += jnp.sum(values, axis=0, keepdims=True)
+
+    fetched["second"].wait()
+
+    def open_second(at):
+        grad = flow[at]
+        grads["d_second"][at] = (grad * modulation[5:6]).astype(jnp.bfloat16)
+        add_sum(5, grad * kept["second"][at])
+
+    by_rows(patches, open_second)
+    save("d_second")
+    fetched["pre"].wait()
+    for part in range(FF // D):
+        loads[part].wait()
+        cols = slice(part * D, part * D + D)
+        grads["d_pre"][:, cols] = (
+            matmul_nt(grads["d_second"][...], ws_v[cols]) * gelu_grad(kept["pre"][:, cols])
+        ).astype(jnp.bfloat16)
+    save("d_pre")
+    for part in range(3):
+        loads[4 + part].wait()
+        cols = slice(part * third, part * third + third)
+        mixed[:, cols] = matmul_nt(grads["d_pre"][...], wh_v[cols])
+    fetched["middle"].wait()
+    fetched["branch"].wait()
+
+    def through_two(at):
+        normed, invstd = normalize(kept["middle"][at])
+        grad = mixed[at]
+        add_sum(3, grad)
+        add_sum(4, grad * normed)
+        total = flow[at] + norm_back(grad * (1.0 + modulation[4:5]), normed, invstd)
+        flow[at] = total
+        add_sum(2, total * kept["branch"][at])
+        grads["d_branch"][at] = (total * modulation[2:3]).astype(jnp.bfloat16)
+
+    by_rows(patches, through_two)
+    save("d_branch")
+    loads[7].wait()
+    att_grad[...] = matmul_nt(grads["d_branch"][...], wp_v[...]).astype(jnp.bfloat16)
+    fetched["qkv"].wait()
+    attend_back_kernel(kept["qkv"], att_grad, grads["d_qkv"])
+    save("d_qkv")
+    for part in range(3):
+        loads[8 + part].wait()
+        cols = slice(part * third, part * third + third)
+        mixed[:, cols] = matmul_nt(grads["d_qkv"][...], wq_v[cols])
+    fetched["residual"].wait()
+
+    def through_one(at):
+        normed, invstd = normalize(kept["residual"][at])
+        grad = mixed[at]
+        add_sum(0, grad)
+        add_sum(1, grad * normed)
+        total = flow[at] + norm_back(grad * (1.0 + modulation[1:2]), normed, invstd)
+        low = total.astype(jnp.bfloat16)
+        grads["d_residual"][at] = low
+        send[at] = low
+
+    by_rows(patches, through_one)
+    save("d_residual")
+    saves.append(pltpu.make_async_copy(sums, ada_out.at[meta[0]], x_sem))
+    start_if_valid(saves[-1])
+
+    @pl.when(meta[3] == 1)
+    def finish():
+        for copy in saves:
+            copy.wait()
+
+
+def specs(*spaces):
+    return [
+        pl.BlockSpec(memory_space={"s": pltpu.SMEM, "v": pltpu.VMEM, "h": pl.ANY}[space])
+        for space in "".join(spaces)
+    ]
+
+
+def weight_scratch():
+    return [pltpu.VMEM(shape, jnp.bfloat16) for shape in WEIGHTS] + [
+        pltpu.SemaphoreType.DMA((11,))
+    ]
+
+
+def block_cost(patches, factor):
+    area = sum(rows * columns for rows, columns in WEIGHTS)
+    return pl.CostEstimate(
+        flops=2 * patches * area + factor * patches * patches * D,
+        bytes_accessed=2 * area + 64 * patches * D,
+        transcendentals=patches * (FF + HEADS * patches),
+    )
+
+
+def image_forward(meta, arrived, bias, ada, tokens, weights, buffers):
+    patches, given, count = (arrived.shape[0], len(buffers), len(KEPT))
+    images = ada.shape[0]
+    outs = pl.pallas_call(
+        functools.partial(forward_kernel, patches, given),
+        out_shape=[jax.ShapeDtypeStruct((patches, D), jnp.bfloat16)]
+        + [jax.ShapeDtypeStruct((images, patches, width), kind) for unused, width, kind in KEPT],
+        in_specs=specs("svvv", "h" * (5 + given)),
+        out_specs=specs("v", "h" * count),
+        scratch_shapes=[pltpu.VMEM((patches, width), kind) for unused, width, kind in KEPT]
+        + weight_scratch()
+        + [pltpu.SemaphoreType.DMA, pltpu.SemaphoreType.DMA((count,))],
+        input_output_aliases={9 + i: 1 + i for i in range(given)},
+        compiler_params=pltpu.CompilerParams(vmem_limit_bytes=60 << 20),
+        cost_estimate=block_cost(patches, 4),
+        name="image_forward",
+    )(meta, arrived, bias, ada, tokens, *weights, *buffers)
+    return (outs[0], outs[1:])
+
+
+def image_backward(meta, arrived, ada, head_grad, weights, sources, buffers):
+    patches, given, images = (arrived.shape[0], len(buffers), ada.shape[0])
+    reads, made = (len(READ), len(MADE))
+    kinds = {name: (width, kind) for name, width, kind in KEPT}
+    outs = pl.pallas_call(
+        functools.partial(backward_kernel, patches, given),
+        out_shape=[jax.ShapeDtypeStruct((patches, D), jnp.bfloat16)]
+        + [jax.ShapeDtypeStruct((images, patches, width), kind) for unused, width, kind in MADE]
+        + [jax.ShapeDtypeStruct((images, 8, D), jnp.float32)],
+        in_specs=specs("svv", "h" * (5 + reads + given)),
+        out_specs=specs("v", "h" * (made + 1)),
+        scratch_shapes=[pltpu.VMEM((patches, kinds[name][0]), kinds[name][1]) for name in READ]
+        + [pltpu.VMEM((patches, width), kind) for unused, width, kind in MADE]
+        + [
+            pltpu.VMEM((patches, D), jnp.float32),
+            pltpu.VMEM((patches, D), jnp.float32),
+            pltpu.VMEM((patches, D), jnp.bfloat16),
+            pltpu.VMEM((8, D), jnp.float32),
+        ]
+        + weight_scratch()
+        + [
+            pltpu.SemaphoreType.DMA((reads,)),
+            pltpu.SemaphoreType.DMA,
+            pltpu.SemaphoreType.DMA((made,)),
+        ],
+        input_output_aliases={8 + reads + i: 1 + i for i in range(given)},
+        compiler_params=pltpu.CompilerParams(vmem_limit_bytes=60 << 20),
+        cost_estimate=block_cost(patches, 10),
+        name="image_backward",
+    )(meta, arrived, ada, head_grad, *weights, *sources, *buffers)
+    return (outs[0], outs[1:])
 
 
 def head_step(residual, film, noise_part, mask_part, inv_count, w_out, b_out):
@@ -434,7 +711,7 @@
     labels_all = blocks[:, ends[3] : ends[4]].reshape(-1).astype(jnp.int32)
     valid_total = jnp.sum(blocks[:, ends[4]])
     inv_count = 1.0 / (valid_total * PATCH_IN)
-    weights = (w_qkv, w_proj, w_hidden, w_second, bias_full)
+    weights = (w_qkv, w_proj, w_hidden, w_second)
 
     small_width = small_mats.shape[1]
     sbias_width = small_bias.shape[0]
@@ -476,6 +753,9 @@
     ada_own = jnp.sum(ada_got, axis=0).reshape(images, 8 * D)
     film = ada_own[:, 6 * D :] + small_used[3 * D : 5 * D]
     ada = (ada_own[:, : 6 * D] + bias_full[ada_at:]).reshape(images, 6, D)
+    bias_row = jnp.concatenate(
+        [bias_full[:D], jnp.zeros((D,), jnp.float32), bias_full[D:ada_at]]
+    )[None]
 
     fade = alpha_bar(timesteps)[:, None, None]
     noisy_low = (jnp.sqrt(fade) * latents + jnp.sqrt(1.0 - fade) * noise).astype(low)
@@ -484,58 +764,23 @@
     )
     tokens = tokens + small_used[:D] + positions(patches)[None]
 
-    def slot_of(raw):
-        return (jnp.where((raw >= 0) & (raw < images), raw, images), jnp.clip(raw, 0, images - 1))
-
-    def put(whole, piece, slot):
-        return lax.dynamic_update_index_in_dim(whole, piece, slot, 0)
-
-    def buffers(widths):
-        return [jnp.zeros((images + 1, patches) + (width,), kind) for width, kind in widths]
+    def meta_of(raw, edge, tick):
+        inside = (raw >= 0) & (raw < images)
+        items = [jnp.clip(raw, 0, images - 1), min(tick, images - 1), edge, inside]
+        return jnp.stack([jnp.asarray(item, jnp.int32) for item in items])
 
     ticks = images + sections - 1
-    wide = jnp.float32
-    kept_all = buffers(
-        [
-            (D, wide),
-            (D, low),
-            (3 * D, low),
-            (D, low),
-            (D, wide),
-            (D, wide),
-            (D, low),
-            (FF, wide),
-            (FF, low),
-            (D, wide),
-            (D, wide),
-        ]
-    )
+    kept_all = []
     arrived = jnp.zeros((patches, D), low)
     for tick in range(ticks):
-        store_at, read_at = slot_of(tick - section_index)
-        residual = jnp.where(is_first, tokens[min(tick, images - 1)], arrived.astype(wide))
-        modulation = lax.dynamic_index_in_dim(ada, read_at, 0, keepdims=False)
-        output, kept = image_forward(residual, modulation, weights)
+        meta = meta_of(tick - section_index, is_first, tick)
+        output, kept_all = image_forward(meta, arrived, bias_row, ada, tokens, weights, kept_all)
         if tick < ticks - 1:
-            arrived = passed_along(output.astype(low), "section", 1)
-        kept_all = [put(whole, piece, store_at) for whole, piece in zip(kept_all, kept + (output,))]
-
-    (
-        residual_all,
-        mixed_one_all,
-        qkv_all,
-        att_all,
-        branch_all,
-        middle_all,
-        mixed_two_all,
-        pre_all,
-        act_all,
-        second_all,
-        output_all,
-    ) = kept_all
+            arrived = passed_along(output, "section", 1)
+    kept_of = {item[0]: whole for item, whole in zip(KEPT, kept_all)}
 
     squared, head_grad, d_film, g_output, g_out_bias = head_step(
-        output_all[:images],
+        kept_of["output"],
         film,
         noise,
         patch_mask,
@@ -544,42 +789,33 @@
         small_used[5 * D :],
     )
     loss_part = jnp.where(is_last, squared * inv_count, 0.0)
+    made_all = []
+    arrived = jnp.zeros((patches, D), low)
+    for tick in range(ticks):
+        meta = meta_of(tick - (sections - 1 - section_index), is_last, tick)
+        d_low, made_all = image_backward(
+            meta, arrived, ada, head_grad, weights, [kept_of[name] for name in READ], made_all
+        )
+        if tick < ticks - 1:
+            arrived = passed_along(d_low, "section", -1)
+
+    def flat(whole):
+        return whole.reshape(images * patches, whole.shape[2])
+
+    d_second, d_pre, d_branch, d_qkv, d_tokens = [flat(whole) for whole in made_all[:5]]
+    d_ada = made_all[5][:, :6].astype(low).reshape(images, 6 * D)
+
+    (shard_proj, shard_down, shard_hidden, shard_qkv), late = row_sums(
+        [
+            (flat(kept_of["att"]), d_branch),
+            (flat(kept_of["act"]), d_second),
+            (flat(kept_of["mixed_two"]), d_pre),
+            (flat(kept_of["mixed_one"]), d_qkv),
+        ]
+    )
+    d_ada, d_film, unused = lax.optimization_barrier((d_ada, d_film, late))
     film_all = spread(d_film, "dp", 6).reshape(shards * images, 2 * D)
     film_all = spread(film_all, "section", 7)[sections - 1]
-
-    grads_all = buffers([(D, low), (FF, low), (D, low), (3 * D, low)])
-    ada_grads = jnp.zeros((images + 1, 6 * D), low)
-    token_grads = jnp.zeros((images + 1, patches, D), low)
-    arrived = jnp.zeros((patches, D), low)
-    for tick in range(ticks):
-        store_at, read_at = slot_of(tick - (sections - 1 - section_index))
-        grad_out = jnp.where(
-            is_last, head_grad[min(tick, images - 1)], arrived.astype(jnp.float32)
-        )
-        kept = [
-            lax.dynamic_index_in_dim(whole, read_at, 0, keepdims=False)
-            for whole in (residual_all, qkv_all, branch_all, middle_all, pre_all, second_all)
-        ]
-        modulation = lax.dynamic_index_in_dim(ada, read_at, 0, keepdims=False)
-        d_residual, pieces = image_backward(grad_out, kept, modulation, weights)
-        d_low = d_residual.astype(low)
-        if tick < ticks - 1:
-            arrived = passed_along(d_low, "section", -1)
-        grads_all = [put(whole, piece, store_at) for whole, piece in zip(grads_all, pieces[:4])]
-        ada_grads = put(ada_grads, pieces[4], store_at)
-        token_grads = put(token_grads, d_low, store_at)
-
-    def flat(whole):
-        return whole[:images].reshape(images * patches, whole.shape[2])
-
-    d_second, d_pre, d_branch, d_qkv = [flat(whole) for whole in grads_all]
-    d_tokens = flat(token_grads)
-    d_ada = ada_grads[:images]
-
-    shard_proj = row_sums(flat(att_all), d_branch)
-    shard_down = row_sums(flat(act_all), d_second)
-    shard_hidden = row_sums(flat(mixed_two_all), d_pre)
-    shard_qkv = row_sums(flat(mixed_one_all), d_qkv)
     d_ada_all = spread(d_ada, "dp", 8).reshape(shards * images, 6 * D)
     shard_ada = matmul_tn(act_here, d_ada_all)
     shard_in = jnp.concatenate([shard_qkv, shard_proj, shard_hidden, shard_ada], axis=1)

time: 2060 us -> 1770 us (0.86)
  matrix products: 519 us -> 85.4 us
  Pallas kernels: 338 us -> 698 us
  other arithmetic: 296 us -> 130 us
  local copies, waits for them, and re-layouts: 228 us -> 111 us
  starting transfers between devices: 81.1 us -> 118 us
  waiting for transfers between devices: 518 us -> 554 us
    pallas_call x14, Pallas kernels: 179 us -> 524 us  [the longest x7 271 us: image_backward(): pl.pallas_call(functools.partial(backward_kernel, patches, given), out_sh...]
    dot_general x33 -> x5, matrix products: 230 us -> 7.85 us  [matmul_nt(): lax.dot_general(left_side, right_side, (((1,), (1,)), ((), ())), preferre...]
    dot_general x31 -> x3, matrix products: 219 us -> 2.64 us  [matmul(): return jnp.dot(left_side, right_side, preferred_element_type=jnp.float32)]
    dynamic_update_slice x50 -> x0, other arithmetic: 107 us -> none  [put(): return lax.dynamic_update_index_in_dim(whole, piece, slot, 0)]
    all_gather x4, waiting for transfers between devices: 125 us -> 212 us  [gathered(): return lax.all_gather(value, axis, axis=dim, tiled=True)]
    ppermute x12, waiting for transfers between devices: 276 us -> 206 us  [row_sums(): lax.ppermute(blocks[-1][step - 1], 'dp', [(i, (i + 2 * step) % count) for...]
    ppermute x12, starting transfers between devices: 42.5 us -> 101 us  [row_sums(): lax.ppermute(blocks[-1][step - 1], 'dp', [(i, (i + 2 * step) % count) for...]
    slice x12 -> x2, local copies, waits for them, and re-layouts: 39.5 us -> 0.01 us  [the longest x1 0.01 us: body(): bias_full[D:ada_at]]
  transfers between devices with their start and end apart: 32 -> 32, of which waited for: 23 -> 21; matrix products, arithmetic and copies ran while one was open for 13% -> 10% of each run, Pallas kernels for 6% -> 6%
where the time goes in v2:
time: 1770 us; the launch traced here: 1760 us
  Pallas kernels  698 us (39%)
  waiting for transfers between devices  554 us (31%)
  other arithmetic  130 us (7%)
  starting transfers between devices  118 us (7%)
  local copies, waits for them, and re-layouts  111 us (6%)
  matrix products  85.4 us (5%)
  blocking collectives  40.5 us (2%)
  between operations  22.8 us (1%)
    pallas_call x7, Pallas kernels, image_backward(): pl.pallas_call(functools.partial(backward_kernel, patches, given), out_sh...  271 us
    pallas_call x7, Pallas kernels, image_forward(): pl.pallas_call(functools.partial(forward_kernel, patches, given), out_sha...  253 us
    all_gather x4, waiting for transfers between devices, gathered(): return lax.all_gather(value, axis, axis=dim, tiled=True)  212 us
    ppermute x12, waiting for transfers between devices, row_sums(): lax.ppermute(blocks[-1][step - 1], 'dp', [(i, (i + 2 * step) % count) for...  206 us
    pallas_call x11, Pallas kernels, share(): pl.pallas_call(functools.partial(share_kernel, axis, count, personal), ou...  174 us
    ppermute x12, waiting for transfers between devices, passed_along(): lax.ppermute(value, axis, [(source, source + steps) for source in range(f...  122 us
    ppermute x12, starting transfers between devices, row_sums(): lax.ppermute(blocks[-1][step - 1], 'dp', [(i, (i + 2 * step) % count) for...  101 us
    dot_general x10, matrix products, matmul_tn(): lax.dot_general(left_side, right_side, (((0,), (0,)), ((), ())), preferre...  63.3 us
  transfers between devices with their start and end apart: 32, of which 21 were waited for; matrix products, arithmetic and copies ran while one was open for 10% of the time, Pallas kernels for 6%

profile of v2, /device:TPU:0, one launch (start us, length us, event | category | flops | bytes accessed | tf_op | source)
XLA Modules:
  0.0 1760.7 jit_solution(1224955823234517615)
XLA Ops:
  23.4 11.9 share.11
  38.7 23.0 %share.12 = bf16[4,146,1186]{2,1,0:T(8,128)(2,1)} custom-call(bf16[146,1186]{1,0:T(8,128)(2,1)} %pad_maximum_fusion.4.in_ref), custom_call_target="tpu_custom_call" | custom-call | tf_op jit(solution)/shard_map/share/pallas_call | solution.py:160
  66.5 13.6 share.13
  82.5 11.4 share.14
  98.6 44.5 %share.15 = f32[8,288,128]{2,1,0:T(8,128)} custom-call(f32[8,288,128]{2,1,0:T(8,128)} %reshape.357.in_ref), custom_call_target="tpu_custom_call" | custom-call | tf_op jit(solution)/shard_map/share/pallas_call | solution.py:160
  153.4 10.2 all-gather.6.cloned.1.call-done.wq
  163.6 101.2 %all-gather.12.cloned.1.call-done = bf16[1,4608,1152]{2,1,0:T(8,128)(2,1)} async-done(((bf16[1,576,1152]{2,1,0:T(8,128)(2,1)}), bf16[1,4608,1152]{2,1,0:T(8,128)(2,1)}) %all-gather.12.cloned.1.call-update) | async-done | bytes 10616848 | tf_op jit(solution)/shard_map/all_gather | solution.py:684
  264.8 101.0 %all-gather.10.cloned.1.call-done.wh = bf16[1152,4608]{1,0:T(8,128)(2,1)} async-done(((bf16[144,4608]{1,0:T(8,128)(2,1)}), bf16[1152,4608]{1,0:T(8,128)(2,1)}) %all-gather.10.cloned.1.call-update) | async-done | bytes 10616848 | tf_op jit(solution)/shard_map/all_gather | solution.py:684
  366.6 36.6 %image_forward.7 = (bf16[256,1152]{1,0:T(8,128)(2,1)}, f32[4,256,1152]{2,1,0:T(8,128)}, bf16[4,256,1152]{2,1,0:T(8,128)(2,1)}, bf16[4,256,3456]{2,1,0:T(8,128)(2...) custom-call(s32[4]{0:T(128)} %fusion.94.meta, ...), custom_call_target="tpu_custom_call" | custom-call | flops 8455716864 | bytes 50724864 | tf_op jit(solution)/shard_map/image_forward/pallas_call | solution.py:563
  405.2 13.0 collective-permute-done.arrived
  419.0 37.0 %image_forward.8 = (bf16[256,1152]{1,0:T(8,128)(2,1)}, f32[4,256,1152]{2,1,0:T(8,128)}, bf16[4,256,1152]{2,1,0:T(8,128)(2,1)}, bf16[4,256,3456]{2,1,0:T(8,128)(2...) custom-call(s32[4]{0:T(128)} %fusion.98.meta, ...), custom_call_target="tpu_custom_call", output_to_operand_aliasing={{1}: (9, {}), {2}: (10, {}), {3}: (11, {}), {4}: (12, {}), ... | custom-call | flops 8455716864 | bytes 50724864 | tf_op jit(solution)/shard_map/image_forward/pallas_call | solution.py:563
  457.9 12.5 collective-permute-done.1.arrived
  471.2 36.6 %image_forward.9 = (bf16[256,1152]{1,0:T(8,128)(2,1)}, f32[4,256,1152]{2,1,0:T(8,128)}, bf16[4,256,1152]{2,1,0:T(8,128)(2,1)}, bf16[4,256,3456]{2,1,0:T(8,128)(2...) custom-call(s32[4]{0:T(128)} %fusion.102.meta, ...), custom_call_target="tpu_custom_call", output_to_operand_aliasing={{1}: (9, {}), {2}: (10, {}), {3}: (11, {}), {4}: (12, {}), ... | custom-call | flops 8455716864 | bytes 50724864 | tf_op jit(solution)/shard_map/image_forward/pallas_call | solution.py:563
  509.7 11.9 collective-permute-done.2.arrived
  522.4 36.9 %image_forward.10 = (bf16[256,1152]{1,0:T(8,128)(2,1)}, f32[4,256,1152]{2,1,0:T(8,128)}, bf16[4,256,1152]{2,1,0:T(8,128)(2,1)}, bf16[4,256,3456]{2,1,0:T(8,128)(...) custom-call(s32[4]{0:T(128)} %fusion.112.meta, ...), custom_call_target="tpu_custom_call", output_to_operand_aliasing={{1}: (9, {}), {2}: (10, {}), {3}: (11, {}), {4}: (12, {}), ... | custom-call | flops 8455716864 | bytes 50724864 | tf_op jit(solution)/shard_map/image_forward/pallas_call | solution.py:563
  563.3 9.2 collective-permute-done.3.arrived
  573.4 35.2 %image_forward.11 = (bf16[256,1152]{1,0:T(8,128)(2,1)}, f32[4,256,1152]{2,1,0:T(8,128)}, bf16[4,256,1152]{2,1,0:T(8,128)(2,1)}, bf16[4,256,3456]{2,1,0:T(8,128)(...) custom-call(s32[4]{0:T(128)} %fusion.110.meta, ...), custom_call_target="tpu_custom_call", output_to_operand_aliasing={{1}: (9, {}), {2}: (10, {}), {3}: (11, {}), {4}: (12, {}), ... | custom-call | flops 8455716864 | bytes 50724864 | tf_op jit(solution)/shard_map/image_forward/pallas_call | solution.py:563
  609.9 11.2 collective-permute-done.4.arrived
  621.9 35.5 %image_forward.12 = (bf16[256,1152]{1,0:T(8,128)(2,1)}, f32[4,256,1152]{2,1,0:T(8,128)}, bf16[4,256,1152]{2,1,0:T(8,128)(2,1)}, bf16[4,256,3456]{2,1,0:T(8,128)(...) custom-call(s32[4]{0:T(128)} %fusion.108.meta, ...), custom_call_target="tpu_custom_call", output_to_operand_aliasing={{1}: (9, {}), {2}: (10, {}), {3}: (11, {}), {4}: (12, {}), ... | custom-call | flops 8455716864 | bytes 50724864 | tf_op jit(solution)/shard_map/image_forward/pallas_call | solution.py:563
  660.0 9.4 collective-permute-done.5.arrived
  670.2 35.2 %image_forward.13 = (bf16[256,1152]{1,0:T(8,128)(2,1)}, f32[4,256,1152]{2,1,0:T(8,128)}, bf16[4,256,1152]{2,1,0:T(8,128)(2,1)}, bf16[4,256,3456]{2,1,0:T(8,128)(...) custom-call(s32[4]{0:T(128)} %fusion.106.meta, ...), custom_call_target="tpu_custom_call", output_to_operand_aliasing={{1}: (9, {}), {2}: (10, {}), {3}: (11, {}), {4}: (12, {}), ... | custom-call | flops 8455716864 | bytes 50724864 | tf_op jit(solution)/shard_map/image_forward/pallas_call | solution.py:563
  720.0 38.0 %image_backward.7 = (bf16[256,1152]{1,0:T(8,128)(2,1)}, bf16[4,256,1152]{2,1,0:T(8,128)(2,1)}, bf16[4,256,4608]{2,1,0:T(8,128)(2,1)}, bf16[4,256,1152]{2,1,0:T(8...) custom-call(s32[4]{0:T(128)} %fusion.96.meta, ...), custom_call_target="tpu_custom_call" | custom-call | flops 8908701696 | bytes 50724864 | tf_op jit(solution)/shard_map/image_backward/pallas_call | solution.py:584
  759.9 12.1 collective-permute-done.6.arrived
  772.8 38.2 %image_backward.8 = (bf16[256,1152]{1,0:T(8,128)(2,1)}, bf16[4,256,1152]{2,1,0:T(8,128)(2,1)}, bf16[4,256,4608]{2,1,0:T(8,128)(2,1)}, bf16[4,256,1152]{2,1,0:T(8...) custom-call(s32[4]{0:T(128)} %fusion.100.meta, ...), custom_call_target="tpu_custom_call", output_to_operand_aliasing={{1}: (14, {}), {2}: (15, {}), {3}: (16, {}), {4}: (17, {}),... | custom-call | flops 8908701696 | bytes 50724864 | tf_op jit(solution)/shard_map/image_backward/pallas_call | solution.py:584
  813.0 11.2 collective-permute-done.7.arrived
  824.9 38.2 %image_backward.9 = (bf16[256,1152]{1,0:T(8,128)(2,1)}, bf16[4,256,1152]{2,1,0:T(8,128)(2,1)}, bf16[4,256,4608]{2,1,0:T(8,128)(2,1)}, bf16[4,256,1152]{2,1,0:T(8...) custom-call(s32[4]{0:T(128)} %fusion.104.meta, ...), custom_call_target="tpu_custom_call", output_to_operand_aliasing={{1}: (14, {}), {2}: (15, {}), {3}: (16, {}), {4}: (17, {}),... | custom-call | flops 8908701696 | bytes 50724864 | tf_op jit(solution)/shard_map/image_backward/pallas_call | solution.py:584
  865.1 10.3 collective-permute-done.8.arrived
  876.1 39.0 %image_backward.10 = (bf16[256,1152]{1,0:T(8,128)(2,1)}, bf16[4,256,1152]{2,1,0:T(8,128)(2,1)}, bf16[4,256,4608]{2,1,0:T(8,128)(2,1)}, bf16[4,256,1152]{2,1,0:T(...) custom-call(s32[4]{0:T(128)} %fusion.120.meta, ...), custom_call_target="tpu_custom_call", output_to_operand_aliasing={{1}: (14, {}), {2}: (15, {}), {3}: (16, {}), {4}: (17, {}),... | custom-call | flops 8908701696 | bytes 50724864 | tf_op jit(solution)/shard_map/image_backward/pallas_call | solution.py:584
  917.0 10.5 collective-permute-done.9.arrived
  928.4 39.2 %image_backward.11 = (bf16[256,1152]{1,0:T(8,128)(2,1)}, bf16[4,256,1152]{2,1,0:T(8,128)(2,1)}, bf16[4,256,4608]{2,1,0:T(8,128)(2,1)}, bf16[4,256,1152]{2,1,0:T(...) custom-call(s32[4]{0:T(128)} %fusion.118.meta, ...), custom_call_target="tpu_custom_call", output_to_operand_aliasing={{1}: (14, {}), {2}: (15, {}), {3}: (16, {}), {4}: (17, {}),... | custom-call | flops 8908701696 | bytes 50724864 | tf_op jit(solution)/shard_map/image_backward/pallas_call | solution.py:584
  969.5 11.0 collective-permute-done.10.arrived
  981.3 39.2 %image_backward.12 = (bf16[256,1152]{1,0:T(8,128)(2,1)}, bf16[4,256,1152]{2,1,0:T(8,128)(2,1)}, bf16[4,256,4608]{2,1,0:T(8,128)(2,1)}, bf16[4,256,1152]{2,1,0:T(...) custom-call(s32[4]{0:T(128)} %fusion.116.meta, ...), custom_call_target="tpu_custom_call", output_to_operand_aliasing={{1}: (14, {}), {2}: (15, {}), {3}: (16, {}), {4}: (17, {}),... | custom-call | flops 8908701696 | bytes 50724864 | tf_op jit(solution)/shard_map/image_backward/pallas_call | solution.py:584
  1022.4 12.8 copy.161
  1038.5 38.9 %image_backward.13 = (bf16[256,1152]{1,0:T(8,128)(2,1)}, bf16[4,256,1152]{2,1,0:T(8,128)(2,1)}, bf16[4,256,4608]{2,1,0:T(8,128)(2,1)}, bf16[4,256,1152]{2,1,0:T(...) custom-call(s32[4]{0:T(128)} %fusion.114.meta, ...), custom_call_target="tpu_custom_call", output_to_operand_aliasing={{1}: (14, {}), {2}: (15, {}), {3}: (16, {}), {4}: (17, {}),... | custom-call | flops 8908701696 | bytes 50724864 | tf_op jit(solution)/shard_map/image_backward/pallas_call | solution.py:584
  1077.4 19.7 %fusion.141 = f32[4,2,576,1152]{3,2,1,0:T(8,128)} fusion(bf16[4,2,576,1024]{3,2,1,0:T(8,128)(2,1)} %bitcast.248, bf16[1024,1152,1,1]{1,0,3,2:T(8,128)(2,1)} %bitcast.236), kind=kOutput, calls=%fused_computation.296 | convolution fusion | flops 10871635968 | bytes 33030144 | tf_op jit(solution)/shard_map/dot_general | solution.py:42
  1097.1 8.7 dynamic-slice_bitcast_fusion.1
  1112.2 13.9 collective-permute-done.17
  1131.4 18.3 %fusion.144 = f32[1152,4608]{1,0:T(8,128)} fusion(bf16[1024,1152]{1,0:T(8,128)(2,1)S(1)} %bitcast.239, bf16[1024,4608]{1,0:T(8,128)(2,1)} %bitcast.231), kind=kOutput, calls=%fused_computation.299 | convolution fusion | flops 10871635968 | bytes 33030144 | tf_op jit(solution)/shard_map/dot_general | solution.py:42
  1149.7 8.8 dynamic-slice_bitcast_fusion
  1162.9 7.9 bitcast_add_fusion.1
  1174.1 12.0 fusion.142
  1186.2 7.2 dynamic-slice_bitcast_fusion.2
  1201.6 5.2 convert_reduce_fusion
  1211.2 7.8 bitcast_add_fusion
  1219.9 10.4 collective-permute-done.19
  1230.3 57.0 %collective-permute-start.25 = (bf16[576,1152]{1,0:T(8,128)(2,1)S(1)}, bf16[576,1152]{1,0:T(8,128)(2,1)S(1)}, u32[]{:S(2)}, u32[]{:S(2)}) collective-permute-start(bf16[576,1152]{1,0:T(8,128)(2,1)S(1)} %copy-done.24), channel_id=1, source_target_pairs={{0,2},{1,3},{2,4},{3,5},{4,6},{5,7},{6,0},{7,1},{8,10},{9,11},{10,... | collective-permute-start | bytes 3981320 | tf_op jit(solution)/shard_map/ppermute | solution.py:215
  1288.2 34.7 %collective-permute-start.22 = (bf16[144,4608]{1,0:T(8,128)(2,1)S(1)}, bf16[144,4608]{1,0:T(8,128)(2,1)S(1)}, u32[]{:S(2)}, u32[]{:S(2)}) collective-permute-start(bf16[144,4608]{1,0:T(8,128)(2,1)S(1)} %get-tuple-element.316), channel_id=1, source_target_pairs={{0,2},{1,3},{2,4},{3,5},{4,6},{5,7},{6,0},{7,1},{8,10},{9,11},{10,... | collective-permute-start | bytes 3981320 | tf_op jit(solution)/shard_map/ppermute | solution.py:215
  1323.1 56.7 %collective-permute-done.26 = bf16[576,1152]{1,0:T(8,128)(2,1)S(1)} collective-permute-done((bf16[576,1152]{1,0:T(8,128)(2,1)S(1)}, bf16[576,1152]{1,0:T(8,128)(2,1)S(1)}, u32[]{:S(2)}, u32[]{:S(2)}) %collective-permute-start.26) | collective-permute-done | bytes 1327136 | tf_op jit(solution)/shard_map/ppermute | solution.py:215
  1382.1 4.6 multiply_reduce_fusion.4
  1386.7 21.0 %collective-permute-done.24 = bf16[144,4608]{1,0:T(8,128)(2,1)S(1)} collective-permute-done((bf16[144,4608]{1,0:T(8,128)(2,1)S(1)}, bf16[144,4608]{1,0:T(8,128)(2,1)S(1)}, u32[]{:S(2)}, u32[]{:S(2)}) %collective-permute-start.24) | collective-permute-done | bytes 1327136 | tf_op jit(solution)/shard_map/ppermute | solution.py:215
  1407.8 56.9 %collective-permute-done.23 = bf16[144,4608]{1,0:T(8,128)(2,1)S(1)} collective-permute-done((bf16[144,4608]{1,0:T(8,128)(2,1)S(1)}, bf16[144,4608]{1,0:T(8,128)(2,1)S(1)}, u32[]{:S(2)}, u32[]{:S(2)}) %collective-permute-start.23) | collective-permute-done | bytes 1327136 | tf_op jit(solution)/shard_map/ppermute | solution.py:215
  1465.3 9.6 bitcast_add_fusion.2
  1474.8 4.5 fusion.38
  1479.4 12.7 share.16
  1492.8 10.3 share.17
  1504.7 22.6 %share.18 = bf16[4,32,2304]{2,1,0:T(8,128)(2,1)} custom-call(bf16[32,2304]{1,0:T(8,128)(2,1)} %reshape.373.in_ref), custom_call_target="tpu_custom_call" | custom-call | tf_op jit(solution)/shard_map/share/pallas_call | solution.py:160
  1533.9 6.6 share.19
  1542.7 8.2 share.20
  1559.4 9.0 share.21
  1595.4 4.8 concatenate.86
  1604.8 60.5 %collective-permute-done.15 = bf16[144,3456]{1,0:T(8,128)(2,1)} collective-permute-done((bf16[144,3456]{1,0:T(8,128)(2,1)}, bf16[144,3456]{1,0:T(8,128)(2,1)}, u32[]{:S(2)}, u32[]{:S(2)}) %collective-permute-start.15) | collective-permute-done | bytes 995360 | tf_op jit(solution)/shard_map/ppermute | solution.py:215
  1675.1 40.5 %all-reduce.1 = (f32[]{:T(128)}, f32[]{:T(128)}) all-reduce(f32[]{:T(128)S(6)} %select_n.157, f32[]{:T(128)S(6)} %add.459), channel_id=1, replica_groups=mesh['section'=4,'dp'=8] {'section','dp'}, use_global_device_ids=true, to_apply=%region_7.8 | all-reduce | flops 2 | bytes 16 | tf_op jit(solution)/shard_map/psum | solution.py:893
  1722.5 8.0 multiply_subtract_fusion.1
  1730.5 22.2 %multiply_subtract_fusion = (f32[1,144,16128]{2,1,0:T(8,128)}, f32[1,144,16128]{2,1,0:T(8,128)}, f32[1,144,16128]{2,1,0:T(8,128)}) fusion(f32[1,144,16128]{2,1,0:T(8,128)} %param.25, f32[]{:T(128)S(6)} %min.60, f32[1,144,6912]{2,1,0:T(8,128)} %bitcast.247, f32[1,144,4608]{2,1,0:T(8,128)S(1)} %bitcast.240, f32[1,144,1152]{2,1,0:T(8,128)S(1)} %bitcast.249, ...), kind=kLoop, calls=%fused_computation.11 | loop fusion | flops 44126208 | bytes 65028100 | tf_op jit(solution)/shard_map/sub | solution.py:643
  (383 shorter events, 191.9 us)
Async XLA Ops:
  7.2 146.2 %all-gather.8.cloned.1.call-start = ((), (), s32[]{:S(2)}) async-start(), calls=%async_computation.1 | async-start | bytes 2985984 | tf_op jit(solution)/shard_map/all_gather | solution.py:684
  14.3 149.3 %all-gather.6.cloned.1.call-start = ((), (), s32[]{:S(2)}) async-start(), calls=%async_computation | async-start | bytes 8957952 | tf_op jit(solution)/shard_map/all_gather | solution.py:684
  16.7 248.1 %all-gather.12.cloned.1.call-start = ((), (), s32[]{:S(2)}) async-start(), calls=%async_computation.3 | async-start | bytes 11943936 | tf_op jit(solution)/shard_map/all_gather | solution.py:684
  18.0 18.6 %copy-start.66 = (f32[1444]{0:T(1024)S(1)}, f32[1444]{0:T(1024)}, u32[]{:S(2)}) copy-start(f32[1444]{0:T(1024)} %param.29) | copy-start | bytes 17332
  18.0 347.7 %all-gather.10.cloned.1.call-start = ((), (), s32[]{:S(2)}) async-start(), calls=%async_computation.2 | async-start | bytes 11943936 | tf_op jit(solution)/shard_map/all_gather | solution.py:684
  36.4 29.3 %copy-start.52 = (f32[16128]{0:T(1024)}, f32[16128]{0:T(1024)S(1)}, u32[]{:S(2)}) copy-start(f32[16128]{0:T(1024)S(1)} %reduce_precision.26) | copy-start | bytes 193540
  36.9 44.1 %copy-start.78 = (s32[32]{0:T(128)}, s32[32]{0:T(128)S(1)}, u32[]{:S(2)}) copy-start(s32[32]{0:T(128)S(1)} %convert_element_type.308) | copy-start | bytes 388
  37.8 112.6 %copy-start.21 = (bf16[1152,16]{1,0:T(8,128)(2,1)}, bf16[1152,16]{1,0:T(8,128)(2,1)S(1)}, u32[]{:S(2)}) copy-start(bf16[1152,16]{1,0:T(8,128)(2,1)S(1)} %convert_element_type.314) | copy-start | bytes 110596
  63.2 32.0 %copy-start.62 = (bf16[32,128]{1,0:T(8,128)(2,1)}, bf16[32,128]{1,0:T(8,128)(2,1)S(1)}, u32[]{:S(2)}) copy-start(bf16[32,128]{1,0:T(8,128)(2,1)S(1)} %get-tuple-element.347) | copy-start | bytes 24580
  64.7 30.5 %copy-start.20 = (bf16[144,1186]{1,0:T(8,128)(2,1)}, bf16[144,1186]{1,0:T(8,128)(2,1)S(1)}, u32[]{:S(2)}) copy-start(bf16[144,1186]{1,0:T(8,128)(2,1)S(1)} %get-tuple-element.330) | copy-start | bytes 1024708
  64.7 30.5 %copy-start.43 = (bf16[144,1186]{1,0:T(8,128)(2,1)}, bf16[144,1186]{1,0:T(8,128)(2,1)S(1)}, u32[]{:S(2)}) copy-start(bf16[144,1186]{1,0:T(8,128)(2,1)S(1)} %get-tuple-element.329) | copy-start | bytes 1024708
  65.2 30.0 %copy-start.40 = (f32[32,144]{1,0:T(8,128)}, f32[32,144]{1,0:T(8,128)S(1)}, u32[]{:S(2)}) copy-start(f32[32,144]{1,0:T(8,128)S(1)} %convolution_add_fusion.2) | copy-start | bytes 55300
  97.3 47.2 %slice-start.2 = ((f32[16128]{0:T(1024)}), f32[6912]{0:T(1024)S(1)}, s32[]{:S(2)}) async-start(f32[16128]{0:T(1024)} %copy-done.52), calls=%async_computation.6 | async-start | bytes 57344 | tf_op jit(solution)/shard_map/slice | solution.py:755
  150.4 252.9 %copy-start.48 = (bf16[4,256,16]{1,2,0:T(8,128)(2,1)}, bf16[4,256,16]{1,2,0:T(8,128)(2,1)S(1)}, u32[]{:S(2)}) copy-start(bf16[4,256,16]{1,2,0:T(8,128)(2,1)S(1)} %add_convert_fusion.1) | copy-start | bytes 98308
  403.3 14.9 collective-permute-start
  456.0 14.4 collective-permute-start.1
  507.8 13.8 collective-permute-start.2
  559.4 13.2 collective-permute-start.3
  608.6 12.5 collective-permute-start.4
  657.5 11.9 collective-permute-start.5
  660.0 51.3 %copy-start.54 = (f32[4,1152]{1,0:T(4,128)}, f32[4,1152]{1,0:T(4,128)S(1)}, u32[]{:S(2)}) copy-start(f32[4,1152]{1,0:T(4,128)S(1)} %get-tuple-element.336) | copy-start | bytes 55300
  660.0 57.2 %copy-start.46 = (f32[4,1152]{1,0:T(4,128)}, f32[4,1152]{1,0:T(4,128)S(1)}, u32[]{:S(2)}) copy-start(f32[4,1152]{1,0:T(4,128)S(1)} %get-tuple-element.335) | copy-start | bytes 55300
  758.0 14.0 collective-permute-start.6
  811.0 13.1 collective-permute-start.7
  863.2 12.1 collective-permute-start.8
  915.1 12.4 collective-permute-start.9
  967.6 12.9 collective-permute-start.10
  1020.5 17.2 collective-permute-start.11
  1022.4 12.8 copy-start.2
  1105.8 57.1 %collective-permute-start.12 = (f32[4,576,1152]{2,1,0:T(8,128)}, f32[4,576,1152]{2,1,0:T(8,128)}, u32[]{:S(2)}, u32[]{:S(2)}) collective-permute-start(f32[4,576,1152]{2,1,0:T(8,128)} %dynamic-slice_bitcast_fusion.1), channel_id=1, source_target_pairs={{0,1},{1,0},{2,3},{3,2},{4,5},{5,4},{6,7},{7,6},{8,9},{9,8},{10,11... | collective-permute-start | bytes 31850504 | tf_op jit(solution)/shard_map/ppermute | solution.py:204
  1111.6 14.5 collective-permute-start.17
  1112.2 19.2 %copy-start.7 = (bf16[4,256,1152]{2,1,0:T(8,128)(2,1)S(1)}, bf16[4,256,1152]{2,1,0:T(8,128)(2,1)}, u32[]{:S(2)}) copy-start(bf16[4,256,1152]{2,1,0:T(8,128)(2,1)} %get-tuple-element.283) | copy-start | bytes 7077892
  1149.6 9.8 copy-start.47
  1149.6 9.8 copy-start.55
  1149.6 9.8 copy-start.57
  1158.5 52.7 %collective-permute-start.21 = (f32[4,144,4608]{2,1,0:T(8,128)}, f32[4,144,4608]{2,1,0:T(8,128)}, u32[]{:S(2)}, u32[]{:S(2)}) collective-permute-start(f32[4,144,4608]{2,1,0:T(8,128)} %dynamic-slice_bitcast_fusion), channel_id=1, source_target_pairs={{0,1},{1,0},{2,3},{3,2},{4,5},{5,4},{6,7},{7,6},{8,9},{9,8},{10,11... | collective-permute-start | bytes 31850504 | tf_op jit(solution)/shard_map/ppermute | solution.py:204
  1159.5 13.4 slice-start
  1162.9 10.0 slice-start.1
  1170.8 15.4 copy-start.8
  1193.4 271.8 %collective-permute-start.13 = (f32[4,144,3456]{2,1,0:T(8,128)}, f32[4,144,3456]{2,1,0:T(8,128)}, u32[]{:S(2)}, u32[]{:S(2)}) collective-permute-start(f32[4,144,3456]{2,1,0:T(8,128)} %dynamic-slice_bitcast_fusion.2), channel_id=1, source_target_pairs={{0,1},{1,0},{2,3},{3,2},{4,5},{5,4},{6,7},{7,6},{8,9},{9,8},{10,11... | collective-permute-start | bytes 23887880 | tf_op jit(solution)/shard_map/ppermute | solution.py:204
  1194.9 284.4 %copy-start.42 = (bf16[1,4,6,1152]{3,1,2,0:T(4,128)(2,1)}, bf16[1,4,6,1152]{3,1,2,0:T(4,128)(2,1)S(1)}, u32[]{:S(2)}) copy-start(bf16[1,4,6,1152]{3,1,2,0:T(4,128)(2,1)S(1)} %copy.175) | copy-start | bytes 165892
  1206.7 23.6 %copy-start.24 = (bf16[576,1152]{1,0:T(8,128)(2,1)S(1)}, bf16[576,1152]{1,0:T(8,128)(2,1)}, u32[]{:S(2)}) copy-start(bf16[576,1152]{1,0:T(8,128)(2,1)} %get-tuple-element.321) | copy-start | bytes 3981316
  1206.7 12.2 collective-permute-start.20
  1207.1 23.2 %collective-permute-start.19 = (bf16[144,1152]{1,0:T(8,128)(2,1)S(1)}, bf16[144,1152]{1,0:T(8,128)(2,1)S(1)}, u32[]{:S(2)}, u32[]{:S(2)}) collective-permute-start(bf16[144,1152]{1,0:T(8,128)(2,1)S(1)} %copy-done.44), channel_id=1, source_target_pairs={{0,4},{1,5},{2,6},{3,7},{4,0},{5,1},{6,2},{7,3},{8,12},{9,13},{10,... | collective-permute-start | bytes 995336 | tf_op jit(solution)/shard_map/ppermute | solution.py:215
  1207.6 115.4 %collective-permute-start.27 = (bf16[576,1152]{1,0:T(8,128)(2,1)S(1)}, bf16[576,1152]{1,0:T(8,128)(2,1)S(1)}, u32[]{:S(2)}, u32[]{:S(2)}) collective-permute-start(bf16[576,1152]{1,0:T(8,128)(2,1)S(1)} %copy-done.26), channel_id=1, source_target_pairs={{0,6},{1,7},{2,0},{3,1},{4,2},{5,3},{6,4},{7,5},{8,14},{9,15},{10,... | collective-permute-start | bytes 3981320 | tf_op jit(solution)/shard_map/ppermute | solution.py:215
  1211.2 168.7 %collective-permute-start.26 = (bf16[576,1152]{1,0:T(8,128)(2,1)S(1)}, bf16[576,1152]{1,0:T(8,128)(2,1)S(1)}, u32[]{:S(2)}, u32[]{:S(2)}) collective-permute-start(bf16[576,1152]{1,0:T(8,128)(2,1)S(1)} %copy-done.25), channel_id=1, source_target_pairs={{0,4},{1,5},{2,6},{3,7},{4,0},{5,1},{6,2},{7,3},{8,12},{9,13},{10,... | collective-permute-start | bytes 3981320 | tf_op jit(solution)/shard_map/ppermute | solution.py:215
  1218.9 69.2 %collective-permute-start.18 = (bf16[144,1152]{1,0:T(8,128)(2,1)S(1)}, bf16[144,1152]{1,0:T(8,128)(2,1)S(1)}, u32[]{:S(2)}, u32[]{:S(2)}) collective-permute-start(bf16[144,1152]{1,0:T(8,128)(2,1)S(1)} %get-tuple-element.327), channel_id=1, source_target_pairs={{0,2},{1,3},{2,4},{3,5},{4,6},{5,7},{6,0},{7,1},{8,10},{9,11},{10,... | collective-permute-start | bytes 995336 | tf_op jit(solution)/shard_map/ppermute | solution.py:215
  1230.3 151.8 %collective-permute-start.25 = (bf16[576,1152]{1,0:T(8,128)(2,1)S(1)}, bf16[576,1152]{1,0:T(8,128)(2,1)S(1)}, u32[]{:S(2)}, u32[]{:S(2)}) collective-permute-start(bf16[576,1152]{1,0:T(8,128)(2,1)S(1)} %copy-done.24), channel_id=1, source_target_pairs={{0,2},{1,3},{2,4},{3,5},{4,6},{5,7},{6,0},{7,1},{8,10},{9,11},{10,... | collective-permute-start | bytes 3981320 | tf_op jit(solution)/shard_map/ppermute | solution.py:215
  1288.2 98.6 %collective-permute-start.22 = (bf16[144,4608]{1,0:T(8,128)(2,1)S(1)}, bf16[144,4608]{1,0:T(8,128)(2,1)S(1)}, u32[]{:S(2)}, u32[]{:S(2)}) collective-permute-start(bf16[144,4608]{1,0:T(8,128)(2,1)S(1)} %get-tuple-element.316), channel_id=1, source_target_pairs={{0,2},{1,3},{2,4},{3,5},{4,6},{5,7},{6,0},{7,1},{8,10},{9,11},{10,... | collective-permute-start | bytes 3981320 | tf_op jit(solution)/shard_map/ppermute | solution.py:215
  1322.9 84.8 %collective-permute-start.24 = (bf16[144,4608]{1,0:T(8,128)(2,1)S(1)}, bf16[144,4608]{1,0:T(8,128)(2,1)S(1)}, u32[]{:S(2)}, u32[]{:S(2)}) collective-permute-start(bf16[144,4608]{1,0:T(8,128)(2,1)S(1)} %get-tuple-element.317), channel_id=1, source_target_pairs={{0,6},{1,7},{2,0},{3,1},{4,2},{5,3},{6,4},{7,5},{8,14},{9,15},{10,... | collective-permute-start | bytes 3981320 | tf_op jit(solution)/shard_map/ppermute | solution.py:215
  1379.8 84.8 %collective-permute-start.23 = (bf16[144,4608]{1,0:T(8,128)(2,1)S(1)}, bf16[144,4608]{1,0:T(8,128)(2,1)S(1)}, u32[]{:S(2)}, u32[]{:S(2)}) collective-permute-start(bf16[144,4608]{1,0:T(8,128)(2,1)S(1)} %get-tuple-element.318), channel_id=1, source_target_pairs={{0,4},{1,5},{2,6},{3,7},{4,0},{5,1},{6,2},{7,3},{8,12},{9,13},{10,... | collective-permute-start | bytes 3981320 | tf_op jit(solution)/shard_map/ppermute | solution.py:215
  1474.8 56.0 %copy-start.59 = (f32[32,144]{1,0:T(8,128)S(1)}, f32[32,144]{1,0:T(8,128)}, u32[]{:S(2)}) copy-start(f32[32,144]{1,0:T(8,128)} %copy-done.58) | copy-start | bytes 55300
  1479.3 74.3 %copy-start.41 = (f32[32,144]{1,0:T(8,128)S(1)}, f32[32,144]{1,0:T(8,128)}, u32[]{:S(2)}) copy-start(f32[32,144]{1,0:T(8,128)} %copy-done.40) | copy-start | bytes 55300
  1574.0 28.9 %copy-start.51 = (f32[8,4,144]{2,1,0:T(4,128)S(1)}, f32[8,4,144]{2,1,0:T(4,128)}, u32[]{:S(2)}) copy-start(f32[8,4,144]{2,1,0:T(4,128)} %share.14) | copy-start | bytes 55300
  1575.8 28.9 %collective-permute-start.16 = (bf16[144,3456]{1,0:T(8,128)(2,1)}, bf16[144,3456]{1,0:T(8,128)(2,1)}, u32[]{:S(2)}, u32[]{:S(2)}) collective-permute-start(bf16[144,3456]{1,0:T(8,128)(2,1)} %get-tuple-element.322), channel_id=1, source_target_pairs={{0,6},{1,7},{2,0},{3,1},{4,2},{5,3},{6,4},{7,5},{8,14},{9,15},{10,... | collective-permute-start | bytes 2985992 | tf_op jit(solution)/shard_map/ppermute | solution.py:215
  1579.3 86.0 %collective-permute-start.15 = (bf16[144,3456]{1,0:T(8,128)(2,1)}, bf16[144,3456]{1,0:T(8,128)(2,1)}, u32[]{:S(2)}, u32[]{:S(2)}) collective-permute-start(bf16[144,3456]{1,0:T(8,128)(2,1)} %get-tuple-element.323), channel_id=1, source_target_pairs={{0,4},{1,5},{2,6},{3,7},{4,0},{5,1},{6,2},{7,3},{8,12},{9,13},{10,... | collective-permute-start | bytes 2985992 | tf_op jit(solution)/shard_map/ppermute | solution.py:215
  1579.3 86.0 %collective-permute-start.14 = (bf16[144,3456]{1,0:T(8,128)(2,1)}, bf16[144,3456]{1,0:T(8,128)(2,1)}, u32[]{:S(2)}, u32[]{:S(2)}) collective-permute-start(bf16[144,3456]{1,0:T(8,128)(2,1)} %get-tuple-element.324), channel_id=1, source_target_pairs={{0,2},{1,3},{2,4},{3,5},{4,6},{5,7},{6,0},{7,1},{8,10},{9,11},{10,... | collective-permute-start | bytes 2985992 | tf_op jit(solution)/shard_map/ppermute | solution.py:215
  1604.7 67.7 %copy-start.12 = (f32[144,6912,1]{1,0,2:T(8,128)}, f32[144,6912,1]{1,0,2:T(8,128)S(1)}, u32[]{:S(2)}) copy-start(f32[144,6912,1]{1,0,2:T(8,128)S(1)} %fusion.74) | copy-start | bytes 11943940
  1672.4 47.9 %copy-start.67 = (f32[1444]{0:T(1024)S(1)}, f32[1444]{0:T(1024)}, u32[]{:S(2)}) copy-start(f32[1444]{0:T(1024)} %param.29) | copy-start | bytes 17332
  1672.4 47.9 %copy-start.74 = (f32[1444]{0:T(1024)S(1)}, f32[1444]{0:T(1024)}, u32[]{:S(2)}) copy-start(f32[1444]{0:T(1024)} %param.34) | copy-start | bytes 17332
  1672.4 47.9 %copy-start.75 = (f32[1444]{0:T(1024)S(1)}, f32[1444]{0:T(1024)}, u32[]{:S(2)}) copy-start(f32[1444]{0:T(1024)} %param.39) | copy-start | bytes 17332
  1672.4 49.3 %copy-start.69 = (f32[1,2016]{1,0:T(1,128)S(1)}, f32[1,2016]{1,0:T(1,128)}, u32[]{:S(2)}) copy-start(f32[1,2016]{1,0:T(1,128)} %param.27) | copy-start | bytes 24196
  1672.5 49.3 %copy-start.76 = (f32[1,2016]{1,0:T(1,128)S(1)}, f32[1,2016]{1,0:T(1,128)}, u32[]{:S(2)}) copy-start(f32[1,2016]{1,0:T(1,128)} %param.32) | copy-start | bytes 24196
  1672.5 49.3 %copy-start.77 = (f32[1,2016]{1,0:T(1,128)S(1)}, f32[1,2016]{1,0:T(1,128)}, u32[]{:S(2)}) copy-start(f32[1,2016]{1,0:T(1,128)} %param.37) | copy-start | bytes 24196
  (52 other events, 232.4 us)
Sparse Core Ops, SparseCore 0:
  14.4 39.9 all-gather.7
  56.6 106.9 all-gather.5
  165.8 98.9 all-gather.11
  266.8 98.8 all-gather.9

commit v3 on v2

--- a/solution.py
+++ b/solution.py
@@ -183,41 +183,280 @@
     return share(value, axis, True, ident)
 
 
-def row_sums(pairs):
+def products_kernel(units, rows, *refs):
+    lefts, rights = (refs[:4], refs[4:8])
+    own_out, block_outs, bias_out = (refs[8], refs[9:12], refs[12])
+    (
+        left_v,
+        right_v,
+        product,
+        got,
+        own_v,
+        low_v,
+        left_sem,
+        right_sem,
+        send_sem,
+        recv_sem,
+        own_sem,
+        low_sem,
+    ) = refs[13:]
+    here = lax.axis_index("dp")
+    core, chip = (lax.rem(here, 2), here // 2)
+    chips = 4
+    partner = {"dp": here + 1 - 2 * core}
+    barrier = pltpu.get_barrier_semaphore()
+    pl.semaphore_signal(barrier, inc=1, device_id=partner, device_id_type=MESH)
+    pl.semaphore_wait(barrier, 1)
+    tall = chips * rows
+    plan, last = ([], [None, None])
+    slots = [1, 1]
+    for left, left_at, right, right_at, gathers in units:
+        fresh = []
+        for side, key in enumerate(((left, left_at), (right, right_at))):
+            fresh.append(last[side] != key)
+            if fresh[-1]:
+                slots[side] = 1 - slots[side]
+                last[side] = key
+        plan.append((tuple(slots), tuple(fresh)))
+
+    def loads_of(index):
+        left, left_at, right, right_at, gathers = units[index]
+        (left_slot, right_slot), (left_fresh, right_fresh) = plan[index]
+        copies = []
+        if left_fresh:
+            copies.append(
+                pltpu.make_async_copy(
+                    lefts[left].at[:, pl.ds(left_at, D)], left_v.at[left_slot], left_sem.at[left_slot]
+                )
+            )
+        if right_fresh:
+            copies.append(
+                pltpu.make_async_copy(
+                    rights[right].at[:, pl.ds(right_at, D)],
+                    right_v.at[right_slot],
+                    right_sem.at[right_slot],
+                )
+            )
+        return copies
+
+    def to_partner(source, target, sems):
+        copy = pltpu.make_async_remote_copy(
+            src_ref=source,
+            dst_ref=target,
+            send_sem=send_sem.at[sems],
+            recv_sem=recv_sem.at[sems],
+            device_id=partner,
+            device_id_type=MESH,
+        )
+        copy.start()
+        return copy
+
+    pending, crossing, leaving = ({}, {}, {})
+
+    def load(index):
+        pending[index] = loads_of(index)
+        for copy in pending[index]:
+            copy.start()
+
+    def multiply(index):
+        gathers = units[index][4]
+        left_slot, right_slot = plan[index][0]
+        for copy in pending[index]:
+            copy.wait()
+        if index + 1 < len(units):
+            load(index + 1)
+        if index >= 2:
+            for copy in crossing[index - 2]:
+                copy.wait_send()
+        slot, place = (index % 2, index % 4)
+        product[slot] = lax.dot_general(
+            left_v[left_slot],
+            right_v[right_slot],
+            (((0,), (0,)), ((), ())),
+            preferred_element_type=jnp.float32,
+        )
+        if plan[index][1][1]:
+            ones = jnp.ones((8, right_v.shape[1]), jnp.bfloat16)
+            bias_out[index] = matmul(ones, right_v[right_slot])
+        if gathers is None:
+            crossing[index] = [
+                to_partner(
+                    product.at[slot, pl.ds(pl.multiple_of((2 * i + 1 - core) * rows, 8), rows)],
+                    got.at[place, pl.ds(i * rows, rows)],
+                    place * chips + i,
+                )
+                for i in range(chips)
+            ]
+        else:
+            crossing[index] = [
+                to_partner(
+                    product.at[slot, pl.ds(pl.multiple_of((1 - core) * tall, 8), tall)],
+                    got.at[place],
+                    place * chips,
+                )
+            ]
+
+    def combine(index):
+        gathers = units[index][4]
+        slot, place, side = (index % 2, index % 4, index % 2)
+        for copy in crossing[index]:
+            copy.wait_recv()
+        if index >= 2:
+            finish(index - 2)
+        at_slot = slot_of[index]
+        if gathers is None:
+            for step in range(chips):
+                other = lax.rem(chip + step, chips)
+                value = (
+                    product[slot, pl.ds(pl.multiple_of((2 * other + core) * rows, 8), rows)]
+                    + got[place, pl.ds(pl.multiple_of(other * rows, 8), rows)]
+                )
+                if step == 0:
+                    own_v[side, 0:rows] = value
+                else:
+                    low_v[side, (step - 1) * rows : step * rows] = value.astype(jnp.bfloat16)
+            copies = [
+                pltpu.make_async_copy(
+                    own_v.at[side, pl.ds(0, rows)], own_out.at[at_slot], own_sem.at[side]
+                )
+            ]
+            for step in range(1, chips):
+                copies.append(
+                    pltpu.make_async_copy(
+                        low_v.at[side, pl.ds((step - 1) * rows, rows)],
+                        block_outs[step - 1].at[at_slot],
+                        low_sem.at[side, step - 1],
+                    )
+                )
+            for copy in copies:
+                copy.start()
+            leaving[index] = [(None, copies)]
+        else:
+            step_here = lax.rem(gathers + chips - chip, chips)
+            cases = []
+            for step in range(chips):
+                held = own_v if step == 0 else low_v
+                out = own_out if step == 0 else block_outs[step - 1]
+                sem = own_sem.at[side] if step == 0 else low_sem.at[side, step - 1]
+                copies = [
+                    pltpu.make_async_copy(
+                        held.at[side, pl.ds(i * rows, rows)],
+                        out.at[at_slot + i],
+                        sem if i == 0 else more_sem(step, side, i),
+                    )
+                    for i in range(chips)
+                ]
+                cases.append((step_here == step, copies))
+
+                @pl.when(step_here == step)
+                def put(held=held, copies=copies):
+                    value = product[slot, pl.ds(pl.multiple_of(core * tall, 8), tall)] + got[place]
+                    held[side] = value.astype(held.dtype)
+                    for copy in copies:
+                        copy.start()
+
+            leaving[index] = cases
+
+    def more_sem(step, side, i):
+        return own_sem.at[2 + side * 3 + i - 1] if step == 0 else low_sem.at[side, 3 * i + step - 1]
+
+    def finish(index):
+        for condition, copies in leaving[index]:
+            if condition is None:
+                for copy in copies:
+                    copy.wait()
+            else:
+
+                @pl.when(condition)
+                def settle(copies=copies):
+                    for copy in copies:
+                        copy.wait()
+
+    slot_of, used = ({}, 0)
+    for index, unit in enumerate(units):
+        slot_of[index] = used
+        if unit[4] is None:
+            used += 1
+    load(0)
+    multiply(0)
+    for index in range(len(units)):
+        if index + 1 < len(units):
+            multiply(index + 1)
+        combine(index)
+    for index in range(max(0, len(units) - 2), len(units)):
+        finish(index)
+        for copy in crossing[index]:
+            copy.wait_send()
+
+
+def chip_products(units, lefts, rights, rows, ident):
+    tokens = lefts[0].shape[0]
+    places = sum(unit[4] is None for unit in units) + 4 * any(unit[4] is not None for unit in units)
+    outs = pl.pallas_call(
+        functools.partial(products_kernel, units, rows),
+        out_shape=[jax.ShapeDtypeStruct((places, rows, D), jnp.float32)]
+        + [jax.ShapeDtypeStruct((places, rows, D), jnp.bfloat16) for unused in range(3)]
+        + [jax.ShapeDtypeStruct((len(units), 8, D), jnp.float32)],
+        in_specs=specs("h" * 8),
+        out_specs=specs("h" * 4, "v"),
+        scratch_shapes=[
+            pltpu.VMEM((2, tokens, D), jnp.bfloat16),
+            pltpu.VMEM((2, tokens, D), jnp.bfloat16),
+            pltpu.VMEM((2, 8 * rows, D), jnp.float32),
+            pltpu.VMEM((4, 4 * rows, D), jnp.float32),
+            pltpu.VMEM((2, 4 * rows, D), jnp.float32),
+            pltpu.VMEM((2, 4 * rows, D), jnp.bfloat16),
+            pltpu.SemaphoreType.DMA((2,)),
+            pltpu.SemaphoreType.DMA((2,)),
+            pltpu.SemaphoreType.DMA((16,)),
+            pltpu.SemaphoreType.DMA((16,)),
+            pltpu.SemaphoreType.DMA((8,)),
+            pltpu.SemaphoreType.DMA((2, 12)),
+        ],
+        compiler_params=pltpu.CompilerParams(
+            collective_id=ident, has_side_effects=True, vmem_limit_bytes=60 << 20
+        ),
+        cost_estimate=pl.CostEstimate(
+            flops=2 * tokens * D * D * len(units),
+            bytes_accessed=len(units) * tokens * D * 4,
+            transcendentals=0,
+        ),
+        name="chip_products",
+    )(*lefts, *rights)
+    return (outs[0], outs[1:4], outs[4][:, 0])
+
+
+def row_sums(lefts, rights, early):
     count = lax.axis_size("dp")
     if count != DIRECT:
-        products = [matmul_tn(left_side, right_side) for left_side, right_side in pairs]
-        return (
-            [lax.psum_scatter(one, "dp", scatter_dimension=0, tiled=True) for one in products],
-            products[-1],
-        )
-    here = lax.axis_index("dp")
-    core, chip, chips = (here % 2, here // 2, count // 2)
-    totals, blocks = ([], [])
-    for index, pair in enumerate(pairs):
-        if index >= 2:
-            pair = lax.optimization_barrier((pair, blocks[index - 2]))[0]
-        product = matmul_tn(*pair)
-        parted = product.reshape(chips, 2, product.shape[0] // count, product.shape[1])
-        other = lax.dynamic_index_in_dim(parted, 1 - core, 1, keepdims=False)
-        same = lax.dynamic_index_in_dim(parted, core, 1, keepdims=False)
-        both = same + lax.ppermute(other, "dp", [(i, i ^ 1) for i in range(count)])
-        total = lax.dynamic_index_in_dim(both, chip, 0, keepdims=False)
-        blocks.append(
-            [
-                lax.dynamic_index_in_dim(both, (chip + step) % chips, 0, keepdims=False).astype(
-                    jnp.bfloat16
-                )
-                for step in range(1, chips)
-            ]
-        )
+        products = [matmul_tn(one, other) for one, other in zip(lefts, rights)]
+        sums = [lax.psum_scatter(one, "dp", scatter_dimension=0, tiled=True) for one in products]
+        wide = jnp.concatenate([sums[0], sums[1], sums[2]], axis=1)
+        return (wide, sums[3], [column_sum(one) for one in rights], products[3], early)
+    rows = D // count
+    chips = count // 2
+    parts = FF // D
+    first = [(0, 0, 0, i * D, None) for i in range(3)] + [(1, 0, 1, 0, None)]
+    rest = [(2, 0, 2, i * D, None) for i in range(parts)] + [
+        (3, i * D, 3, 0, i) for i in range(parts)
+    ]
+    totals, biases, tied = ([], [], None)
+    for ident, units in ((12, first), (13, rest)):
+        if tied is not None:
+            lefts, rights, tied, early = lax.optimization_barrier((lefts, rights, tied, early))
+        total, blocks, bias = chip_products(tuple(units), lefts, rights, rows, ident)
         for step in range(1, chips):
             arrived = lax.ppermute(
-                blocks[-1][step - 1], "dp", [(i, (i + 2 * step) % count) for i in range(count)]
+                blocks[step - 1], "dp", [(i, (i + 2 * step) % count) for i in range(count)]
             )
             total = total + arrived.astype(jnp.float32)
+        tied = blocks
         totals.append(total)
-    return (totals, blocks[-1])
+        biases.append(bias)
+    wide = [totals[0][i] for i in range(4)] + [totals[1][i] for i in range(parts)]
+    sums = [biases[0][:3].reshape(-1), biases[0][3], biases[1][:parts].reshape(-1), biases[1][parts]]
+    late = (tied, totals[0])
+    return (jnp.concatenate(wide, axis=1), totals[1][parts:].reshape(-1, D), sums, late, early)
 
 
 def attend_kernel(qkv_ref, out_ref):
@@ -805,20 +1044,21 @@
     d_second, d_pre, d_branch, d_qkv, d_tokens = [flat(whole) for whole in made_all[:5]]
     d_ada = made_all[5][:, :6].astype(low).reshape(images, 6 * D)
 
-    (shard_proj, shard_down, shard_hidden, shard_qkv), late = row_sums(
-        [
-            (flat(kept_of["att"]), d_branch),
-            (flat(kept_of["act"]), d_second),
-            (flat(kept_of["mixed_two"]), d_pre),
-            (flat(kept_of["mixed_one"]), d_qkv),
-        ]
+    token_sums = column_sum(d_tokens)
+    g_edge = jnp.where(
+        is_first,
+        matmul_tn(d_tokens, noisy_low.reshape(images * patches, PATCH_IN)),
+        g_output,
+    )
+    shard_wide, shard_down, right_sums, late, (token_sums, g_edge) = row_sums(
+        [flat(kept_of[name]) for name in ("mixed_one", "att", "mixed_two", "act")],
+        [d_qkv, d_branch, d_pre, d_second],
+        (token_sums, g_edge),
     )
     d_ada, d_film, unused = lax.optimization_barrier((d_ada, d_film, late))
     film_all = spread(d_film, "dp", 6).reshape(shards * images, 2 * D)
     film_all = spread(film_all, "section", 7)[sections - 1]
     d_ada_all = spread(d_ada, "dp", 8).reshape(shards * images, 6 * D)
-    shard_ada = matmul_tn(act_here, d_ada_all)
-    shard_in = jnp.concatenate([shard_qkv, shard_proj, shard_hidden, shard_ada], axis=1)
 
     cond_piece = matmul_nt(d_ada_all, w_ada) * silu_grad(cond_here)
     cond_pieces = spread(cond_piece, "section", 9)
@@ -830,19 +1070,13 @@
     d_time = (
         matmul_nt(d_cond_all, small_rows[:, o_second:o_film]) * silu_grad(time_hidden)
     ).astype(low)
-    g_edge = jnp.where(
-        is_first,
-        matmul_tn(d_tokens, noisy_low.reshape(images * patches, PATCH_IN)),
-        g_output,
-    )
-    qkv_sums = column_sum(d_qkv)
     bias_sums = jnp.concatenate(
         [
-            qkv_sums[:D],
-            qkv_sums[2 * D :],
-            column_sum(d_branch),
-            column_sum(d_pre),
-            column_sum(d_second),
+            right_sums[0][:D],
+            right_sums[0][2 * D :],
+            right_sums[1],
+            right_sums[2],
+            right_sums[3],
             column_sum(d_ada),
         ]
     )
@@ -850,13 +1084,27 @@
         [
             bias_sums.reshape(shards, -1),
             g_edge.reshape(shards, -1),
-            jnp.broadcast_to(column_sum(d_tokens), (shards, D)),
+            jnp.broadcast_to(token_sums, (shards, D)),
             jnp.broadcast_to(g_out_bias, (shards, PATCH_IN)),
             jnp.broadcast_to(column_sum(d_time), (shards, rows)),
         ],
         axis=1,
     )
     sums = exchange(sums[:, None], "dp", 11)[:, 0]
+    (
+        sums,
+        d_ada_all,
+        d_cond_all,
+        d_cond_rows,
+        d_time,
+        film_all,
+        shard_wide,
+        shard_down,
+    ) = lax.optimization_barrier(
+        (sums, d_ada_all, d_cond_all, d_cond_rows, d_time, film_all, shard_wide, shard_down)
+    )
+    shard_ada = matmul_tn(act_here, d_ada_all)
+    shard_in = jnp.concatenate([shard_wide, shard_ada], axis=1)
     edge_end = bias_width + rows * PATCH_IN
     shard_bias = jnp.sum(sums[:, :bias_width], axis=0)
     edge_rows = jnp.sum(sums[:, bias_width:edge_end], axis=0).reshape(rows, PATCH_IN)
@@ -890,7 +1138,10 @@
         + jnp.sum(small_shard * small_shard)
         + dp_zero * jnp.sum(sbias_shard * sbias_shard)
     )
-    norm_square, loss = lax.psum((squares, loss_part), ("section", "dp"))
+    pair = jnp.broadcast_to(jnp.stack([squares, loss_part])[:, None], (2, 128))
+    pair = jnp.sum(spread(pair, "dp", 14), axis=0)
+    pair = jnp.sum(spread(pair, "section", 15), axis=0)
+    norm_square, loss = (pair[0, 0], pair[1, 0])
     grad_norm = jnp.sqrt(norm_square)
     scaling = jnp.minimum(1.0, CLIP / grad_norm)
     new_in, first_in, second_in = adam_update(w_in, shard_in[None], m_in, v_in, scaling)

time: 1770 us -> 1630 us (0.921)
  Pallas kernels: 698 us -> 1020 us
  waiting for transfers between devices: 554 us -> 372 us
  starting transfers between devices: 118 us -> 25.2 us
  matrix products: 85.4 us -> 29.2 us
  local copies, waits for them, and re-layouts: 111 us -> 59.7 us
  blocking collectives: 40.5 us -> 0 us
  other arithmetic: 130 us -> 93.1 us
    pallas_call x11 -> x13, Pallas kernels: 174 us -> 425 us  [share(): pl.pallas_call(functools.partial(share_kernel, axis, count, personal), ou...]
    ppermute x16 -> x6, waiting for transfers between devices: 220 us -> 31.6 us  [row_sums(): lax.ppermute(blocks[step - 1], 'dp', [(i, (i + 2 * step) % count) for i i...]
    ppermute x16 -> x6, starting transfers between devices: 102 us -> 9.34 us  [row_sums(): lax.ppermute(blocks[step - 1], 'dp', [(i, (i + 2 * step) % count) for i i...]
    pallas_call x0 -> x2, Pallas kernels: none -> 72.1 us  [chip_products(): pl.pallas_call(functools.partial(products_kernel, units, rows), out_shape...]
    dot_general x10 -> x6, matrix products: 63.3 us -> 8.39 us  [matmul_tn(): lax.dot_general(left_side, right_side, (((0,), (0,)), ((), ())), preferre...]
    psum x1 -> x0, blocking collectives: 40.5 us -> none  [body(): norm_square, loss = lax.psum((squares, loss_part), ('section', 'dp'))]
    add x4 -> x0, other arithmetic: 28 us -> none  [row_sums(): both = same + lax.ppermute(other, 'dp', [(i, i ^ 1) for i in range(count)])]
    squeeze x4 -> x1, local copies, waits for them, and re-layouts: 24.9 us -> 0.92 us  [body(): film_all = spread(film_all, 'section', 7)[sections - 1]]
  transfers between devices with their start and end apart: 32 -> 22, of which waited for: 21 -> 16; matrix products, arithmetic and copies ran while one was open for 10% -> 5% of each run, Pallas kernels for 6% -> 28%
where the time goes in v3:
time: 1630 us
  Pallas kernels  1020 us (63%)
  waiting for transfers between devices  372 us (23%)
  other arithmetic  93.1 us (6%)
  local copies, waits for them, and re-layouts  59.7 us (4%)
  matrix products  29.2 us (2%)
  starting transfers between devices  25.2 us (2%)
  between operations  22.8 us (1%)
    pallas_call x13, Pallas kernels, share(): pl.pallas_call(functools.partial(share_kernel, axis, count, personal), ou...  425 us
    pallas_call x7, Pallas kernels, image_backward(): pl.pallas_call(functools.partial(backward_kernel, patches, given), out_sh...  272 us
    pallas_call x7, Pallas kernels, image_forward(): pl.pallas_call(functools.partial(forward_kernel, patches, given), out_sha...  254 us
    all_gather x4, waiting for transfers between devices, gathered(): return lax.all_gather(value, axis, axis=dim, tiled=True)  212 us
    ppermute x12, waiting for transfers between devices, passed_along(): lax.ppermute(value, axis, [(source, source + steps) for source in range(f...  128 us
    pallas_call x2, Pallas kernels, chip_products(): pl.pallas_call(functools.partial(products_kernel, units, rows), out_shape...  72.1 us
    sub x5, other arithmetic, adam_update(): return (weight - RATE * (ratio + DECAY * weight), first_new, second_new)  34.8 us
  transfers between devices with their start and end apart: 22, of which 16 were waited for; matrix products, arithmetic and copies ran while one was open for 5% of the time, Pallas kernels for 28%

profile of v3, /device:TPU:0, one launch (start us, length us, event | category | flops | bytes accessed | tf_op | source)
XLA Modules:
  0.0 1625.2 jit_solution(18093326663037526163)
XLA Ops:
  7.2 4.1 convert_bitcast_fusion
  23.3 11.9 share.13
  38.6 23.0 %share.14 = bf16[4,146,1186]{2,1,0:T(8,128)(2,1)} custom-call(bf16[146,1186]{1,0:T(8,128)(2,1)} %pad_maximum_fusion.4.in_ref), custom_call_target="tpu_custom_call" | custom-call | tf_op jit(solution)/shard_map/share/pallas_call | solution.py:160
  66.4 13.6 share.15
  82.5 11.5 share.16
  98.6 44.5 %share.17 = f32[8,288,128]{2,1,0:T(8,128)} custom-call(f32[8,288,128]{2,1,0:T(8,128)} %reshape.317.in_ref), custom_call_target="tpu_custom_call" | custom-call | tf_op jit(solution)/shard_map/share/pallas_call | solution.py:160
  145.2 2.8 multiply_cosine_fusion
  150.4 3.0 fusion.2.tokens
  153.4 10.1 all-gather.6.cloned.1.call-done.wq
  163.5 101.2 %all-gather.12.cloned.1.call-done = bf16[1,4608,1152]{2,1,0:T(8,128)(2,1)} async-done(((bf16[1,576,1152]{2,1,0:T(8,128)(2,1)}), bf16[1,4608,1152]{2,1,0:T(8,128)(2,1)}) %all-gather.12.cloned.1.call-update) | async-done | bytes 10616848 | tf_op jit(solution)/shard_map/all_gather | solution.py:923
  264.7 101.0 %all-gather.10.cloned.1.call-done.wh = bf16[1152,4608]{1,0:T(8,128)(2,1)} async-done(((bf16[144,4608]{1,0:T(8,128)(2,1)}), bf16[1152,4608]{1,0:T(8,128)(2,1)}) %all-gather.10.cloned.1.call-update) | async-done | bytes 10616848 | tf_op jit(solution)/shard_map/all_gather | solution.py:923
  366.5 37.1 %image_forward.7 = (bf16[256,1152]{1,0:T(8,128)(2,1)}, f32[4,256,1152]{2,1,0:T(8,128)}, bf16[4,256,1152]{2,1,0:T(8,128)(2,1)}, bf16[4,256,3456]{2,1,0:T(8,128)(2...) custom-call(s32[4]{0:T(128)} %fusion.65.meta, ...), custom_call_target="tpu_custom_call" | custom-call | flops 8455716864 | bytes 50724864 | tf_op jit(solution)/shard_map/image_forward/pallas_call | solution.py:802
  405.6 12.9 collective-permute-done.arrived
  419.4 36.7 %image_forward.8 = (bf16[256,1152]{1,0:T(8,128)(2,1)}, f32[4,256,1152]{2,1,0:T(8,128)}, bf16[4,256,1152]{2,1,0:T(8,128)(2,1)}, bf16[4,256,3456]{2,1,0:T(8,128)(2...) custom-call(s32[4]{0:T(128)} %fusion.69.meta, ...), custom_call_target="tpu_custom_call", output_to_operand_aliasing={{1}: (9, {}), {2}: (10, {}), {3}: (11, {}), {4}: (12, {}), ... | custom-call | flops 8455716864 | bytes 50724864 | tf_op jit(solution)/shard_map/image_forward/pallas_call | solution.py:802
  458.0 12.5 collective-permute-done.1.arrived
  471.3 37.0 %image_forward.9 = (bf16[256,1152]{1,0:T(8,128)(2,1)}, f32[4,256,1152]{2,1,0:T(8,128)}, bf16[4,256,1152]{2,1,0:T(8,128)(2,1)}, bf16[4,256,3456]{2,1,0:T(8,128)(2...) custom-call(s32[4]{0:T(128)} %fusion.73.meta, ...), custom_call_target="tpu_custom_call", output_to_operand_aliasing={{1}: (9, {}), {2}: (10, {}), {3}: (11, {}), {4}: (12, {}), ... | custom-call | flops 8455716864 | bytes 50724864 | tf_op jit(solution)/shard_map/image_forward/pallas_call | solution.py:802
  510.3 11.9 collective-permute-done.2.arrived
  523.0 36.6 %image_forward.10 = (bf16[256,1152]{1,0:T(8,128)(2,1)}, f32[4,256,1152]{2,1,0:T(8,128)}, bf16[4,256,1152]{2,1,0:T(8,128)(2,1)}, bf16[4,256,3456]{2,1,0:T(8,128)(...) custom-call(s32[4]{0:T(128)} %fusion.83.meta, ...), custom_call_target="tpu_custom_call", output_to_operand_aliasing={{1}: (9, {}), {2}: (10, {}), {3}: (11, {}), {4}: (12, {}), ... | custom-call | flops 8455716864 | bytes 50724864 | tf_op jit(solution)/shard_map/image_forward/pallas_call | solution.py:802
  563.5 9.2 collective-permute-done.3.arrived
  573.6 35.6 %image_forward.11 = (bf16[256,1152]{1,0:T(8,128)(2,1)}, f32[4,256,1152]{2,1,0:T(8,128)}, bf16[4,256,1152]{2,1,0:T(8,128)(2,1)}, bf16[4,256,3456]{2,1,0:T(8,128)(...) custom-call(s32[4]{0:T(128)} %fusion.81.meta, ...), custom_call_target="tpu_custom_call", output_to_operand_aliasing={{1}: (9, {}), {2}: (10, {}), {3}: (11, {}), {4}: (12, {}), ... | custom-call | flops 8455716864 | bytes 50724864 | tf_op jit(solution)/shard_map/image_forward/pallas_call | solution.py:802
  610.5 11.2 collective-permute-done.4.arrived
  622.5 35.2 %image_forward.12 = (bf16[256,1152]{1,0:T(8,128)(2,1)}, f32[4,256,1152]{2,1,0:T(8,128)}, bf16[4,256,1152]{2,1,0:T(8,128)(2,1)}, bf16[4,256,3456]{2,1,0:T(8,128)(...) custom-call(s32[4]{0:T(128)} %fusion.79.meta, ...), custom_call_target="tpu_custom_call", output_to_operand_aliasing={{1}: (9, {}), {2}: (10, {}), {3}: (11, {}), {4}: (12, {}), ... | custom-call | flops 8455716864 | bytes 50724864 | tf_op jit(solution)/shard_map/image_forward/pallas_call | solution.py:802
  660.3 9.4 collective-permute-done.5.arrived
  670.5 35.6 %image_forward.13 = (bf16[256,1152]{1,0:T(8,128)(2,1)}, f32[4,256,1152]{2,1,0:T(8,128)}, bf16[4,256,1152]{2,1,0:T(8,128)(2,1)}, bf16[4,256,3456]{2,1,0:T(8,128)(...) custom-call(s32[4]{0:T(128)} %fusion.77.meta, ...), custom_call_target="tpu_custom_call", output_to_operand_aliasing={{1}: (9, {}), {2}: (10, {}), {3}: (11, {}), {4}: (12, {}), ... | custom-call | flops 8455716864 | bytes 50724864 | tf_op jit(solution)/shard_map/image_forward/pallas_call | solution.py:802
  706.1 2.7 reduce_sum.258
  708.8 3.1 multiply_reduce_fusion.2
  714.3 3.5 multiply_reduce_fusion
  717.8 2.9 subtract_multiply_fusion.head_grad
  720.7 38.5 %image_backward.7 = (bf16[256,1152]{1,0:T(8,128)(2,1)}, bf16[4,256,1152]{2,1,0:T(8,128)(2,1)}, bf16[4,256,4608]{2,1,0:T(8,128)(2,1)}, bf16[4,256,1152]{2,1,0:T(8...) custom-call(s32[4]{0:T(128)} %fusion.67.meta, ...), custom_call_target="tpu_custom_call" | custom-call | flops 8908701696 | bytes 50724864 | tf_op jit(solution)/shard_map/image_backward/pallas_call | solution.py:823
  761.1 12.0 collective-permute-done.6.arrived
  774.0 38.2 %image_backward.8 = (bf16[256,1152]{1,0:T(8,128)(2,1)}, bf16[4,256,1152]{2,1,0:T(8,128)(2,1)}, bf16[4,256,4608]{2,1,0:T(8,128)(2,1)}, bf16[4,256,1152]{2,1,0:T(8...) custom-call(s32[4]{0:T(128)} %fusion.71.meta, ...), custom_call_target="tpu_custom_call", output_to_operand_aliasing={{1}: (14, {}), {2}: (15, {}), {3}: (16, {}), {4}: (17, {}),... | custom-call | flops 8908701696 | bytes 50724864 | tf_op jit(solution)/shard_map/image_backward/pallas_call | solution.py:823
  814.1 11.1 collective-permute-done.7.arrived
  826.1 38.4 %image_backward.9 = (bf16[256,1152]{1,0:T(8,128)(2,1)}, bf16[4,256,1152]{2,1,0:T(8,128)(2,1)}, bf16[4,256,4608]{2,1,0:T(8,128)(2,1)}, bf16[4,256,1152]{2,1,0:T(8...) custom-call(s32[4]{0:T(128)} %fusion.75.meta, ...), custom_call_target="tpu_custom_call", output_to_operand_aliasing={{1}: (14, {}), {2}: (15, {}), {3}: (16, {}), {4}: (17, {}),... | custom-call | flops 8908701696 | bytes 50724864 | tf_op jit(solution)/shard_map/image_backward/pallas_call | solution.py:823
  866.4 10.2 collective-permute-done.8.arrived
  877.4 39.3 %image_backward.10 = (bf16[256,1152]{1,0:T(8,128)(2,1)}, bf16[4,256,1152]{2,1,0:T(8,128)(2,1)}, bf16[4,256,4608]{2,1,0:T(8,128)(2,1)}, bf16[4,256,1152]{2,1,0:T(...) custom-call(s32[4]{0:T(128)} %fusion.91.meta, ...), custom_call_target="tpu_custom_call", output_to_operand_aliasing={{1}: (14, {}), {2}: (15, {}), {3}: (16, {}), {4}: (17, {}),... | custom-call | flops 8908701696 | bytes 50724864 | tf_op jit(solution)/shard_map/image_backward/pallas_call | solution.py:823
  918.6 10.3 collective-permute-done.9.arrived
  929.7 39.0 %image_backward.11 = (bf16[256,1152]{1,0:T(8,128)(2,1)}, bf16[4,256,1152]{2,1,0:T(8,128)(2,1)}, bf16[4,256,4608]{2,1,0:T(8,128)(2,1)}, bf16[4,256,1152]{2,1,0:T(...) custom-call(s32[4]{0:T(128)} %fusion.89.meta, ...), custom_call_target="tpu_custom_call", output_to_operand_aliasing={{1}: (14, {}), {2}: (15, {}), {3}: (16, {}), {4}: (17, {}),... | custom-call | flops 8908701696 | bytes 50724864 | tf_op jit(solution)/shard_map/image_backward/pallas_call | solution.py:823
  971.9 9.5 collective-permute-done.10.arrived
  982.2 39.0 %image_backward.12 = (bf16[256,1152]{1,0:T(8,128)(2,1)}, bf16[4,256,1152]{2,1,0:T(8,128)(2,1)}, bf16[4,256,4608]{2,1,0:T(8,128)(2,1)}, bf16[4,256,1152]{2,1,0:T(...) custom-call(s32[4]{0:T(128)} %fusion.87.meta, ...), custom_call_target="tpu_custom_call", output_to_operand_aliasing={{1}: (14, {}), {2}: (15, {}), {3}: (16, {}), {4}: (17, {}),... | custom-call | flops 8908701696 | bytes 50724864 | tf_op jit(solution)/shard_map/image_backward/pallas_call | solution.py:823
  1023.2 3.2 convolution_bitcast_fusion
  1026.5 7.9 collective-permute-done.11.arrived
  1035.2 39.2 %image_backward.13 = (bf16[256,1152]{1,0:T(8,128)(2,1)}, bf16[4,256,1152]{2,1,0:T(8,128)(2,1)}, bf16[4,256,4608]{2,1,0:T(8,128)(2,1)}, bf16[4,256,1152]{2,1,0:T(...) custom-call(s32[4]{0:T(128)} %fusion.85.meta, ...), custom_call_target="tpu_custom_call", output_to_operand_aliasing={{1}: (14, {}), {2}: (15, {}), {3}: (16, {}), {4}: (17, {}),... | custom-call | flops 8908701696 | bytes 50724864 | tf_op jit(solution)/shard_map/image_backward/pallas_call | solution.py:823
  1078.5 26.9 %chip_products.2 = (f32[4,144,1152]{2,1,0:T(8,128)}, bf16[4,144,1152]{2,1,0:T(8,128)(2,1)}, bf16[4,144,1152]{2,1,0:T(8,128)(2,1)}, bf16[4,144,1152]{2,1,0:T(8,128)(2,1)}, f32[4,8,1152]{2,1,0:T(8,128)}) custom-call(bf16[1024,1152]{1,0:T(8,128)(2,1)} %bitcast.177, bf16[1024,1152]{1,0:T(8,128)(2,1)} %bitcast.179, bf16[1024,1152]{1,0:T(8,128)(2,1)} %bitcast.181, ...), custom_call_target="tpu_custom_call" | custom-call | flops 10871635968 | bytes 18874368 | tf_op jit(solution)/shard_map/chip_products/pallas_call | solution.py:395
  1106.6 2.8 collective-permute-start.14
  1109.5 45.2 %chip_products.3 = (f32[8,144,1152]{2,1,0:T(8,128)}, bf16[8,144,1152]{2,1,0:T(8,128)(2,1)}, bf16[8,144,1152]{2,1,0:T(8,128)(2,1)}, bf16[8,144,1152]{2,1,0:T(8,128)(2,1)}, f32[8,8,1152]{2,1,0:T(8,128)}) custom-call(bf16[1024,1152]{1,0:T(8,128)(2,1)} %bitcast.178, bf16[1024,1152]{1,0:T(8,128)(2,1)} %bitcast.180, bf16[1024,1152]{1,0:T(8,128)(2,1)} %bitcast.182, ...), custom_call_target="tpu_custom_call" | custom-call | flops 21743271936 | bytes 37748736 | tf_op jit(solution)/shard_map/chip_products/pallas_call | solution.py:395
  1160.5 3.4 collective-permute-start.17
  1163.9 31.6 %collective-permute-done.13 = bf16[4,144,1152]{2,1,0:T(8,128)(2,1)S(1)} collective-permute-done((bf16[4,144,1152]{2,1,0:T(8,128)(2,1)}, bf16[4,144,1152]{2,1,0:T(8,128)(2,1)S(1)}, u32[]{:S(2)}, u32[]{:S(2)}) %collective-permute-start.13) | collective-permute-done | bytes 1327136 | tf_op jit(solution)/shard_map/ppermute | solution.py:449
  1196.6 3.4 convert_add_fusion.1
  1200.2 258.2 %share.20 = bf16[8,4,6912]{2,1,0:T(4,128)(2,1)} custom-call(bf16[4,6912]{1,0:T(4,128)(2,1)} %bitcast.199), custom_call_target="tpu_custom_call" | custom-call | tf_op jit(solution)/shard_map/share/pallas_call | solution.py:160
  1460.6 9.0 share.18
  1473.1 3.1 fusion.19.in_ref
  1476.2 13.4 share.21
  1489.6 11.6 share.19
  1503.4 7.3 share.22
  1516.2 8.8 share.23
  1530.6 5.9 convert_add_fusion
  1546.7 2.6 fusion.104
  1550.8 3.4 concatenate.86
  1555.1 6.8 fusion.1
  1565.2 6.8 share.24
  1573.3 5.8 share.25
  1582.4 3.5 multiply_subtract_fusion.2
  1587.5 8.2 multiply_subtract_fusion.1
  1596.4 20.9 %multiply_subtract_fusion = (f32[1,144,16128]{2,1,0:T(8,128)}, f32[1,144,16128]{2,1,0:T(8,128)}, f32[1,144,16128]{2,1,0:T(8,128)}) fusion(f32[1,144,16128]{2,1,0:T(8,128)S(1)} %bitcast.188, f32[]{:T(128)S(6)} %min.60, f32[1,144,6912]{2,1,0:T(8,128)} %bitcast.189, f32[1,144,9216]{2,1,0:T(8,128)} %bitcast.72, f32[1,144,16128]{2,1,0:T(8,128)} %param.30, ...), kind=kLoop, calls=%fused_computation.5 | loop fusion | flops 39481344 | bytes 65028100 | tf_op jit(solution)/shard_map/sub | solution.py:882
  (353 shorter events, 118.0 us)
Async XLA Ops:
  7.2 146.2 %all-gather.8.cloned.1.call-start = ((), (), s32[]{:S(2)}) async-start(), calls=%async_computation.1 | async-start | bytes 2985984 | tf_op jit(solution)/shard_map/all_gather | solution.py:923
  14.2 149.3 %all-gather.6.cloned.1.call-start = ((), (), s32[]{:S(2)}) async-start(), calls=%async_computation | async-start | bytes 8957952 | tf_op jit(solution)/shard_map/all_gather | solution.py:923
  16.7 248.1 %all-gather.12.cloned.1.call-start = ((), (), s32[]{:S(2)}) async-start(), calls=%async_computation.3 | async-start | bytes 11943936 | tf_op jit(solution)/shard_map/all_gather | solution.py:923
  17.9 18.5 %copy-start.58 = (f32[1444]{0:T(1024)S(1)}, f32[1444]{0:T(1024)}, u32[]{:S(2)}) copy-start(f32[1444]{0:T(1024)} %param.29) | copy-start | bytes 17332
  18.0 347.7 %all-gather.10.cloned.1.call-start = ((), (), s32[]{:S(2)}) async-start(), calls=%async_computation.2 | async-start | bytes 11943936 | tf_op jit(solution)/shard_map/all_gather | solution.py:923
  36.4 29.3 %copy-start.41 = (f32[16128]{0:T(1024)}, f32[16128]{0:T(1024)S(1)}, u32[]{:S(2)}) copy-start(f32[16128]{0:T(1024)S(1)} %reduce_precision.22) | copy-start | bytes 193540
  36.8 44.2 %copy-start.72 = (s32[32]{0:T(128)}, s32[32]{0:T(128)S(1)}, u32[]{:S(2)}) copy-start(s32[32]{0:T(128)S(1)} %convert_element_type.192) | copy-start | bytes 388
  37.8 112.6 %copy-start.11 = (bf16[1152,16]{1,0:T(8,128)(2,1)}, bf16[1152,16]{1,0:T(8,128)(2,1)S(1)}, u32[]{:S(2)}) copy-start(bf16[1152,16]{1,0:T(8,128)(2,1)S(1)} %convert_element_type.198) | copy-start | bytes 110596
  63.1 32.1 %copy-start.49 = (bf16[32,128]{1,0:T(8,128)(2,1)}, bf16[32,128]{1,0:T(8,128)(2,1)S(1)}, u32[]{:S(2)}) copy-start(bf16[32,128]{1,0:T(8,128)(2,1)S(1)} %get-tuple-element.384) | copy-start | bytes 24580
  64.6 30.5 %copy-start.9 = (bf16[144,1186]{1,0:T(8,128)(2,1)}, bf16[144,1186]{1,0:T(8,128)(2,1)S(1)}, u32[]{:S(2)}) copy-start(bf16[144,1186]{1,0:T(8,128)(2,1)S(1)} %get-tuple-element.365) | copy-start | bytes 1024708
  64.6 30.5 %copy-start.36 = (bf16[144,1186]{1,0:T(8,128)(2,1)}, bf16[144,1186]{1,0:T(8,128)(2,1)S(1)}, u32[]{:S(2)}) copy-start(bf16[144,1186]{1,0:T(8,128)(2,1)S(1)} %get-tuple-element.364) | copy-start | bytes 1024708
  65.2 30.0 %copy-start.32 = (f32[32,144]{1,0:T(8,128)}, f32[32,144]{1,0:T(8,128)S(1)}, u32[]{:S(2)}) copy-start(f32[32,144]{1,0:T(8,128)S(1)} %convolution_add_fusion.2) | copy-start | bytes 55300
  97.3 47.2 %slice-start.3 = ((f32[16128]{0:T(1024)}), f32[6912]{0:T(1024)S(1)}, s32[]{:S(2)}) async-start(f32[16128]{0:T(1024)} %copy-done.41), calls=%async_computation.7 | async-start | bytes 57344 | tf_op jit(solution)/shard_map/slice | solution.py:994
  150.4 253.3 %copy-start.39 = (bf16[4,256,16]{1,2,0:T(8,128)(2,1)}, bf16[4,256,16]{1,2,0:T(8,128)(2,1)S(1)}, u32[]{:S(2)}) copy-start(bf16[4,256,16]{1,2,0:T(8,128)(2,1)S(1)} %add_convert_fusion.1) | copy-start | bytes 98308
  403.7 14.9 collective-permute-start
  456.1 14.4 collective-permute-start.1
  508.3 13.8 collective-permute-start.2
  559.6 13.2 collective-permute-start.3
  609.2 12.5 collective-permute-start.4
  657.8 11.9 collective-permute-start.5
  660.3 51.6 %copy-start.43 = (f32[4,1152]{1,0:T(4,128)}, f32[4,1152]{1,0:T(4,128)S(1)}, u32[]{:S(2)}) copy-start(f32[4,1152]{1,0:T(4,128)S(1)} %get-tuple-element.371) | copy-start | bytes 55300
  660.3 57.5 %copy-start.37 = (f32[4,1152]{1,0:T(4,128)}, f32[4,1152]{1,0:T(4,128)S(1)}, u32[]{:S(2)}) copy-start(f32[4,1152]{1,0:T(4,128)S(1)} %get-tuple-element.370) | copy-start | bytes 55300
  708.8 9.0 copy-start.47
  759.2 14.0 collective-permute-start.6
  812.2 13.0 collective-permute-start.7
  864.5 12.1 collective-permute-start.8
  916.7 12.2 collective-permute-start.9
  968.7 12.7 collective-permute-start.10
  982.2 40.4 %copy-start.66 = (bf16[4,1152]{1,0:T(4,128)(2,1)S(1)}, bf16[4,1152]{1,0:T(4,128)(2,1)}, u32[]{:S(2)}) copy-start(bf16[4,1152]{1,0:T(4,128)(2,1)} %get-tuple-element.339) | copy-start | bytes 27652
  982.2 40.4 %copy-start.67 = (bf16[4,1152]{1,0:T(4,128)(2,1)S(1)}, bf16[4,1152]{1,0:T(4,128)(2,1)}, u32[]{:S(2)}) copy-start(bf16[4,1152]{1,0:T(4,128)(2,1)} %get-tuple-element.342) | copy-start | bytes 27652
  982.2 41.0 %copy-start.38 = (f32[4,1152]{1,0:T(4,128)S(1)}, f32[4,1152]{1,0:T(4,128)}, u32[]{:S(2)}) copy-start(f32[4,1152]{1,0:T(4,128)} %copy-done.37) | copy-start | bytes 55300
  982.2 41.0 %copy-start.44 = (f32[4,1152]{1,0:T(4,128)S(1)}, f32[4,1152]{1,0:T(4,128)}, u32[]{:S(2)}) copy-start(f32[4,1152]{1,0:T(4,128)} %copy-done.43) | copy-start | bytes 55300
  982.2 41.0 %copy-start.46 = (bf16[4,256,16]{1,2,0:T(8,128)(2,1)S(1)}, bf16[4,256,16]{1,2,0:T(8,128)(2,1)}, u32[]{:S(2)}) copy-start(bf16[4,256,16]{1,2,0:T(8,128)(2,1)} %copy-done.45) | copy-start | bytes 98308
  982.2 41.0 %copy-start.48 = (f32[4,256]{1,0:T(4,128)S(1)}, f32[4,256]{1,0:T(4,128)}, u32[]{:S(2)}) copy-start(f32[4,256]{1,0:T(4,128)} %copy-done.47) | copy-start | bytes 12292
  982.2 41.0 %copy-start.57 = (f32[4,256]{1,0:T(4,128)S(1)}, f32[4,256]{1,0:T(4,128)}, u32[]{:S(2)}) copy-start(f32[4,256]{1,0:T(4,128)} %copy-done.56) | copy-start | bytes 12292
  1021.3 13.0 collective-permute-start.11
  1035.2 41.3 %copy-start.40 = (bf16[4,256,16]{1,2,0:T(8,128)(2,1)S(1)}, bf16[4,256,16]{1,2,0:T(8,128)(2,1)}, u32[]{:S(2)}) copy-start(bf16[4,256,16]{1,2,0:T(8,128)(2,1)} %copy-done.39) | copy-start | bytes 98308
  1105.4 55.0 %collective-permute-start.12 = (bf16[4,144,1152]{2,1,0:T(8,128)(2,1)}, bf16[4,144,1152]{2,1,0:T(8,128)(2,1)S(1)}, u32[]{:S(2)}, u32[]{:S(2)}) collective-permute-start(bf16[4,144,1152]{2,1,0:T(8,128)(2,1)} %get-tuple-element.308), channel_id=1, source_target_pairs={{0,2},{1,3},{2,4},{3,5},{4,6},{5,7},{6,0},{7,1},{8,10},{9,11},{10,... | collective-permute-start | bytes 3981320 | tf_op jit(solution)/shard_map/ppermute | solution.py:449
  1105.5 90.1 %collective-permute-start.13 = (bf16[4,144,1152]{2,1,0:T(8,128)(2,1)}, bf16[4,144,1152]{2,1,0:T(8,128)(2,1)S(1)}, u32[]{:S(2)}, u32[]{:S(2)}) collective-permute-start(bf16[4,144,1152]{2,1,0:T(8,128)(2,1)} %get-tuple-element.309), channel_id=1, source_target_pairs={{0,4},{1,5},{2,6},{3,7},{4,0},{5,1},{6,2},{7,3},{8,12},{9,13},{10,... | collective-permute-start | bytes 3981320 | tf_op jit(solution)/shard_map/ppermute | solution.py:449
  1106.6 48.1 %copy-start.4 = (f32[4,8,1152]{2,1,0:T(8,128)S(1)}, f32[4,8,1152]{2,1,0:T(8,128)}, u32[]{:S(2)}) copy-start(f32[4,8,1152]{2,1,0:T(8,128)} %get-tuple-element.321) | copy-start | bytes 442372
  1106.6 89.0 %collective-permute-start.14 = (bf16[4,144,1152]{2,1,0:T(8,128)(2,1)}, bf16[4,144,1152]{2,1,0:T(8,128)(2,1)}, u32[]{:S(2)}, u32[]{:S(2)}) collective-permute-start(bf16[4,144,1152]{2,1,0:T(8,128)(2,1)} %get-tuple-element.310), channel_id=1, source_target_pairs={{0,6},{1,7},{2,0},{3,1},{4,2},{5,3},{6,4},{7,5},{8,14},{9,15},{10,... | collective-permute-start | bytes 3981320 | tf_op jit(solution)/shard_map/ppermute | solution.py:449
  1154.7 45.4 %copy-start.35 = (bf16[1,4,6,1152]{3,1,2,0:T(4,128)(2,1)}, bf16[1,4,6,1152]{3,1,2,0:T(4,128)(2,1)S(1)}, u32[]{:S(2)}) copy-start(bf16[1,4,6,1152]{3,1,2,0:T(4,128)(2,1)S(1)} %copy.157) | copy-start | bytes 165892
  1156.9 373.7 %collective-permute-start.15 = (bf16[8,144,1152]{2,1,0:T(8,128)(2,1)}, bf16[8,144,1152]{2,1,0:T(8,128)(2,1)}, u32[]{:S(2)}, u32[]{:S(2)}) collective-permute-start(bf16[8,144,1152]{2,1,0:T(8,128)(2,1)} %get-tuple-element.322), channel_id=1, source_target_pairs={{0,2},{1,3},{2,4},{3,5},{4,6},{5,7},{6,0},{7,1},{8,10},{9,11},{10,... | collective-permute-start | bytes 7962632 | tf_op jit(solution)/shard_map/ppermute | solution.py:449
  1157.3 373.2 %collective-permute-start.16 = (bf16[8,144,1152]{2,1,0:T(8,128)(2,1)}, bf16[8,144,1152]{2,1,0:T(8,128)(2,1)}, u32[]{:S(2)}, u32[]{:S(2)}) collective-permute-start(bf16[8,144,1152]{2,1,0:T(8,128)(2,1)} %get-tuple-element.323), channel_id=1, source_target_pairs={{0,4},{1,5},{2,6},{3,7},{4,0},{5,1},{6,2},{7,3},{8,12},{9,13},{10,... | collective-permute-start | bytes 7962632 | tf_op jit(solution)/shard_map/ppermute | solution.py:449
  1160.5 35.1 %copy-start.54 = (f32[16128]{0:T(1024)}, f32[16128]{0:T(1024)S(1)}, u32[]{:S(2)}) copy-start(f32[16128]{0:T(1024)S(1)} %constant_dynamic-update-slice_fusion.8) | copy-start | bytes 193540
  1160.5 35.1 %copy-start.15 = (bf16[4,144,1152]{2,1,0:T(8,128)(2,1)}, bf16[4,144,1152]{2,1,0:T(8,128)(2,1)S(1)}, u32[]{:S(2)}) copy-start(bf16[4,144,1152]{2,1,0:T(8,128)(2,1)S(1)} %collective-permute-done.12) | copy-start | bytes 3981316
  1160.5 370.1 %collective-permute-start.17 = (bf16[8,144,1152]{2,1,0:T(8,128)(2,1)}, bf16[8,144,1152]{2,1,0:T(8,128)(2,1)}, u32[]{:S(2)}, u32[]{:S(2)}) collective-permute-start(bf16[8,144,1152]{2,1,0:T(8,128)(2,1)} %get-tuple-element.324), channel_id=1, source_target_pairs={{0,6},{1,7},{2,0},{3,1},{4,2},{5,3},{6,4},{7,5},{8,14},{9,15},{10,... | collective-permute-start | bytes 7962632 | tf_op jit(solution)/shard_map/ppermute | solution.py:449
  1196.6 276.5 %copy-start.30 = (f32[32,144]{1,0:T(8,128)S(1)}, f32[32,144]{1,0:T(8,128)}, u32[]{:S(2)}) copy-start(f32[32,144]{1,0:T(8,128)} %copy-done.29) | copy-start | bytes 55300
  1200.1 301.2 %copy-start.10 = (bf16[144,1186]{1,0:T(8,128)(2,1)S(1)}, bf16[144,1186]{1,0:T(8,128)(2,1)}, u32[]{:S(2)}) copy-start(bf16[144,1186]{1,0:T(8,128)(2,1)} %copy-done.9) | copy-start | bytes 1024708
  1200.1 313.3 %copy-start.6 = (bf16[144,1186]{1,0:T(8,128)(2,1)S(1)}, bf16[144,1186]{1,0:T(8,128)(2,1)}, u32[]{:S(2)}) copy-start(bf16[144,1186]{1,0:T(8,128)(2,1)} %copy-done.5) | copy-start | bytes 1024708
  1200.1 313.3 %copy-start.33 = (f32[32,144]{1,0:T(8,128)S(1)}, f32[32,144]{1,0:T(8,128)}, u32[]{:S(2)}) copy-start(f32[32,144]{1,0:T(8,128)} %copy-done.32) | copy-start | bytes 55300
  1200.1 314.2 %copy-start.74 = (f32[16]{0:T(128)S(1)}, f32[16]{0:T(128)}, u32[]{:S(2)}) copy-start(f32[16]{0:T(128)} %get-tuple-element.361) | copy-start | bytes 196
  1537.7 8.0 copy-start.53
  1537.7 8.0 copy-start.73
  1538.6 8.1 copy-start.14
  1541.2 8.1 copy-start.64
  1555.1 27.3 %copy-start.8 = (f32[144,1186]{1,0:T(8,128)S(1)}, f32[144,1186]{1,0:T(8,128)}, u32[]{:S(2)}) copy-start(f32[144,1186]{1,0:T(8,128)} %param.28) | copy-start | bytes 2049412
  1561.8 24.1 %copy-start.59 = (f32[1444]{0:T(1024)S(1)}, f32[1444]{0:T(1024)}, u32[]{:S(2)}) copy-start(f32[1444]{0:T(1024)} %param.29) | copy-start | bytes 17332
  1585.9 10.5 slice-start
  1587.5 8.2 copy-start.61
  1587.5 8.2 copy-start.70
  1587.5 8.2 copy-start.71
  1587.5 8.9 slice-start.1
  1587.5 8.9 slice-start.2
  (39 other events, 125.8 us)
Sparse Core Ops, SparseCore 0:
  14.3 39.9 all-gather.7
  56.5 106.9 all-gather.5
  165.8 98.9 all-gather.11
  266.8 98.8 all-gather.9

commit v4 on v3

--- a/solution.py
+++ b/solution.py
@@ -183,9 +183,11 @@
     return share(value, axis, True, ident)
 
 
-def products_kernel(units, rows, *refs):
-    lefts, rights = (refs[:4], refs[4:8])
-    own_out, block_outs, bias_out = (refs[8], refs[9:12], refs[12])
+def products_kernel(units, rows, extra, *refs):
+    lefts, rights, given = (refs[:4], refs[4:8], refs[8 : 8 + extra])
+    refs = refs[8 + extra :]
+    own_out, block_outs, bias_out, spread_out = (refs[0], refs[1:4], refs[4], refs[5 : 5 + extra])
+    refs = refs[5 + extra :]
     (
         left_v,
         right_v,
@@ -199,14 +201,31 @@
         recv_sem,
         own_sem,
         low_sem,
-    ) = refs[13:]
+    ) = refs[:12]
     here = lax.axis_index("dp")
     core, chip = (lax.rem(here, 2), here // 2)
     chips = 4
     partner = {"dp": here + 1 - 2 * core}
-    barrier = pltpu.get_barrier_semaphore()
-    pl.semaphore_signal(barrier, inc=1, device_id=partner, device_id_type=MESH)
-    pl.semaphore_wait(barrier, 1)
+    spreading = []
+    if extra:
+        count = 2 * chips
+        meet("dp", count, here)
+        for step in range(1, count):
+            copy = pltpu.make_async_remote_copy(
+                src_ref=given[0],
+                dst_ref=spread_out[0].at[here],
+                send_sem=refs[12].at[step - 1],
+                recv_sem=refs[13].at[step - 1],
+                device_id={"dp": lax.rem(here + step, count)},
+                device_id_type=MESH,
+            )
+            copy.start()
+            spreading.append(copy)
+        spread_out[0][here] = given[0][...]
+    else:
+        barrier = pltpu.get_barrier_semaphore()
+        pl.semaphore_signal(barrier, inc=1, device_id=partner, device_id_type=MESH)
+        pl.semaphore_wait(barrier, 1)
     tall = chips * rows
     plan, last = ([], [None, None])
     slots = [1, 1]
@@ -387,18 +406,21 @@
         finish(index)
         for copy in crossing[index]:
             copy.wait_send()
-
-
-def chip_products(units, lefts, rights, rows, ident):
+    for copy in spreading:
+        copy.wait()
+
+
+def chip_products(units, lefts, rights, rows, ident, given=()):
     tokens = lefts[0].shape[0]
     places = sum(unit[4] is None for unit in units) + 4 * any(unit[4] is not None for unit in units)
     outs = pl.pallas_call(
-        functools.partial(products_kernel, units, rows),
+        functools.partial(products_kernel, units, rows, len(given)),
         out_shape=[jax.ShapeDtypeStruct((places, rows, D), jnp.float32)]
         + [jax.ShapeDtypeStruct((places, rows, D), jnp.bfloat16) for unused in range(3)]
-        + [jax.ShapeDtypeStruct((len(units), 8, D), jnp.float32)],
-        in_specs=specs("h" * 8),
-        out_specs=specs("h" * 4, "v"),
+        + [jax.ShapeDtypeStruct((len(units), 8, D), jnp.float32)]
+        + [jax.ShapeDtypeStruct((DIRECT,) + one.shape, one.dtype) for one in given],
+        in_specs=specs("h" * 8, "v" * len(given)),
+        out_specs=specs("h" * 4, "v", "v" * len(given)),
         scratch_shapes=[
             pltpu.VMEM((2, tokens, D), jnp.bfloat16),
             pltpu.VMEM((2, tokens, D), jnp.bfloat16),
@@ -412,7 +434,8 @@
             pltpu.SemaphoreType.DMA((16,)),
             pltpu.SemaphoreType.DMA((8,)),
             pltpu.SemaphoreType.DMA((2, 12)),
-        ],
+        ]
+        + [pltpu.SemaphoreType.DMA((DIRECT - 1,))] * (2 * len(given)),
         compiler_params=pltpu.CompilerParams(
             collective_id=ident, has_side_effects=True, vmem_limit_bytes=60 << 20
         ),
@@ -422,17 +445,19 @@
             transcendentals=0,
         ),
         name="chip_products",
-    )(*lefts, *rights)
-    return (outs[0], outs[1:4], outs[4][:, 0])
-
-
-def row_sums(lefts, rights, early):
+    )(*lefts, *rights, *given)
+    return (outs[0], outs[1:4], outs[4][:, 0], outs[5:])
+
+
+def row_sums(lefts, rights, early, given):
     count = lax.axis_size("dp")
     if count != DIRECT:
         products = [matmul_tn(one, other) for one, other in zip(lefts, rights)]
         sums = [lax.psum_scatter(one, "dp", scatter_dimension=0, tiled=True) for one in products]
         wide = jnp.concatenate([sums[0], sums[1], sums[2]], axis=1)
-        return (wide, sums[3], [column_sum(one) for one in rights], products[3], early)
+        given = lax.all_gather(given, "dp")
+        biases = [column_sum(one) for one in rights]
+        return (wide, sums[3], biases, products[3], early, given)
     rows = D // count
     chips = count // 2
     parts = FF // D
@@ -440,11 +465,14 @@
     rest = [(2, 0, 2, i * D, None) for i in range(parts)] + [
         (3, i * D, 3, 0, i) for i in range(parts)
     ]
-    totals, biases, tied = ([], [], None)
+    totals, biases, tied, given_all = ([], [], None, None)
     for ident, units in ((12, first), (13, rest)):
         if tied is not None:
             lefts, rights, tied, early = lax.optimization_barrier((lefts, rights, tied, early))
-        total, blocks, bias = chip_products(tuple(units), lefts, rights, rows, ident)
+        total, blocks, bias, shared = chip_products(
+            tuple(units), lefts, rights, rows, ident, (given,) if tied is None else ()
+        )
+        given_all = shared[0] if tied is None else given_all
         for step in range(1, chips):
             arrived = lax.ppermute(
                 blocks[step - 1], "dp", [(i, (i + 2 * step) % count) for i in range(count)]
@@ -456,45 +484,70 @@
     wide = [totals[0][i] for i in range(4)] + [totals[1][i] for i in range(parts)]
     sums = [biases[0][:3].reshape(-1), biases[0][3], biases[1][:parts].reshape(-1), biases[1][parts]]
     late = (tied, totals[0])
-    return (jnp.concatenate(wide, axis=1), totals[1][parts:].reshape(-1, D), sums, late, early)
+    down = totals[1][parts:].reshape(-1, D)
+    return (jnp.concatenate(wide, axis=1), down, sums, late, early, given_all)
+
+
+GROUP = 4
+
+
+def contract(left_side, right_side, left_axis, right_axis):
+    return lax.dot_general(
+        left_side,
+        right_side,
+        (((left_axis,), (right_axis,)), ((), ())),
+        preferred_element_type=jnp.float32,
+    )
+
+
+def heads_of(ref, at, group):
+    return [
+        ref[at + head * HEAD_DIM : at + (head + 1) * HEAD_DIM] for head in group
+    ]
+
+
+def softmax_down(scores):
+    weights = jnp.exp(scores - jnp.max(scores, axis=0, keepdims=True))
+    return weights * (1.0 / jnp.sum(weights, axis=0, keepdims=True))
+
+
+def stacked(values):
+    return jnp.concatenate([value.astype(jnp.bfloat16) for value in values], axis=0)
 
 
 def attend_kernel(qkv_ref, out_ref):
-    for head in range(HEADS):
-        at = head * HEAD_DIM
-        query = qkv_ref[:, at : at + HEAD_DIM]
-        key = qkv_ref[:, D + at : D + at + HEAD_DIM]
-        value = qkv_ref[:, 2 * D + at : 2 * D + at + HEAD_DIM]
-        scores = matmul_nt(query, key) * HEAD_DIM ** (-0.5)
-        attention = jnp.exp(scores - jnp.max(scores, axis=-1, keepdims=True))
-        attention = attention * (1.0 / jnp.sum(attention, axis=-1, keepdims=True))
-        out_ref[:, at : at + HEAD_DIM] = matmul(attention.astype(jnp.bfloat16), value).astype(
-            jnp.bfloat16
-        )
+    scaling = HEAD_DIM ** (-0.5)
+    for first in range(0, HEADS, GROUP):
+        group = range(first, first + GROUP)
+        rows = slice(first * HEAD_DIM, (first + GROUP) * HEAD_DIM)
+        queries, keys = (heads_of(qkv_ref, 0, group), heads_of(qkv_ref, D, group))
+        values = heads_of(qkv_ref, 2 * D, group)
+        scores = [contract(key, query, 0, 0) * scaling for key, query in zip(keys, queries)]
+        probs = [softmax_down(score).astype(jnp.bfloat16) for score in scores]
+        out_ref[rows] = stacked([contract(v, p, 1, 0) for v, p in zip(values, probs)])
 
 
 def attend_back_kernel(qkv_ref, grad_ref, out_ref):
     scaling = HEAD_DIM ** (-0.5)
-    for head in range(HEADS):
-        at = head * HEAD_DIM
-        query = qkv_ref[:, at : at + HEAD_DIM]
-        key = qkv_ref[:, D + at : D + at + HEAD_DIM]
-        value = qkv_ref[:, 2 * D + at : 2 * D + at + HEAD_DIM]
-        grad = grad_ref[:, at : at + HEAD_DIM]
-        scores = matmul_nt(query, key) * scaling
-        attention = jnp.exp(scores - jnp.max(scores, axis=-1, keepdims=True))
-        attention = attention * (1.0 / jnp.sum(attention, axis=-1, keepdims=True))
-        d_probs = matmul_nt(grad, value)
-        d_scores = (
-            attention * (d_probs - jnp.sum(attention * d_probs, axis=-1, keepdims=True))
-        ).astype(jnp.bfloat16)
-        attention_low = attention.astype(jnp.bfloat16)
-        out_ref[:, at : at + HEAD_DIM] = (matmul(d_scores, key) * scaling).astype(jnp.bfloat16)
-        out_ref[:, D + at : D + at + HEAD_DIM] = (matmul_tn(d_scores, query) * scaling).astype(
-            jnp.bfloat16
+    for first in range(0, HEADS, GROUP):
+        group = range(first, first + GROUP)
+        at, to = (first * HEAD_DIM, (first + GROUP) * HEAD_DIM)
+        queries, keys = (heads_of(qkv_ref, 0, group), heads_of(qkv_ref, D, group))
+        values, grads = (heads_of(qkv_ref, 2 * D, group), heads_of(grad_ref, 0, group))
+        scores = [contract(key, query, 0, 0) * scaling for key, query in zip(keys, queries)]
+        d_probs = [contract(value, grad, 0, 0) for value, grad in zip(values, grads)]
+        probs = [softmax_down(score) for score in scores]
+        d_scores = [
+            (p * (d - jnp.sum(p * d, axis=0, keepdims=True))).astype(jnp.bfloat16)
+            for p, d in zip(probs, d_probs)
+        ]
+        lows = [p.astype(jnp.bfloat16) for p in probs]
+        out_ref[at:to] = stacked([contract(k, d, 1, 0) * scaling for k, d in zip(keys, d_scores)])
+        out_ref[D + at : D + to] = stacked(
+            [contract(q, d, 1, 1) * scaling for q, d in zip(queries, d_scores)]
         )
-        out_ref[:, 2 * D + at : 2 * D + at + HEAD_DIM] = matmul_tn(attention_low, grad).astype(
-            jnp.bfloat16
+        out_ref[2 * D + at : 2 * D + to] = stacked(
+            [contract(g, p, 1, 1) for g, p in zip(grads, lows)]
         )
 
 
@@ -523,6 +576,10 @@
 WEIGHTS = ((D, 3 * D), (D, D), (D, FF), (FF, D))
 
 
+def kept_shape(name, width, kind, patches):
+    return (width, patches) if name == "qkv" else (patches, width)
+
+
 def by_rows(patches, step):
     @pl.loop(0, patches // ROW_BLOCK)
     def run(index):
@@ -535,12 +592,14 @@
     return copy
 
 
-def forward_kernel(patches, given, meta, arrived, bias, ada, tokens, wq, wp, wh, ws, *refs):
+def forward_kernel(
+    patches, given, meta, arrived, bias, qkv_bias, ada, tokens, wq, wp, wh, ws, *refs
+):
     count = len(KEPT)
     send, outs = (refs[given], refs[given + 1 : given + 1 + count])
     scratch = refs[given + 1 + count :]
     kept = {name: scratch[i] for i, (name, unused, kind) in enumerate(KEPT)}
-    wq_v, wp_v, wh_v, ws_v, w_sem, x_sem, out_sem = scratch[count:]
+    att_down, wq_v, wp_v, wh_v, ws_v, w_sem, x_sem, out_sem = scratch[count:]
     loads = [started(wq.at[:, pl.ds(i * D, D)], wq_v.at[:, pl.ds(i * D, D)], w_sem.at[i]) for i in range(3)]
     loads.append(started(wp, wp_v, w_sem.at[3]))
     loads += [
@@ -588,15 +647,18 @@
     for part in range(3):
         loads[part].wait()
         cols = slice(part * D, part * D + D)
-        kept["qkv"][:, cols] = (
-            matmul(kept["mixed_one"][...], wq_v[:, cols]) + bias[:, cols]
+        kept["qkv"][cols] = (
+            contract(wq_v[:, cols], kept["mixed_one"][...], 0, 1) + qkv_bias[cols]
         ).astype(jnp.bfloat16)
     save("qkv")
-    attend_kernel(kept["qkv"], kept["att"])
+    attend_kernel(kept["qkv"], att_down)
+    loads[3].wait()
+    kept["branch"][...] = contract(att_down[...], wp_v[...], 0, 0) + bias[:, :D]
+    kept["att"][...] = att_down[...].T
+    save("branch")
     save("att")
-    loads[3].wait()
-    kept["branch"][...] = matmul(kept["att"][...], wp_v[...]) + bias[:, 3 * D : 4 * D]
-    save("branch")
+    for load in loads[4:]:
+        load.wait()
 
     def mix_two(at):
         middle = residual[at] + modulation[2:3] * kept["branch"][at]
@@ -610,22 +672,20 @@
     save("middle")
     save("mixed_two")
     for part in range(FF // D):
-        loads[4 + part].wait()
         cols = slice(part * D, part * D + D)
         pre = (
             matmul(kept["mixed_two"][...], wh_v[:, cols])
-            + bias[:, 4 * D + part * D : 5 * D + part * D]
+            + bias[:, D + part * D : 2 * D + part * D]
         )
         kept["pre"][:, cols] = pre
         kept["act"][:, cols] = gelu_tanh(pre).astype(jnp.bfloat16)
     save("pre")
     save("act")
     for part in range(3):
-        loads[8 + part].wait()
         cols = slice(part * third, part * third + third)
         second = (
             matmul(kept["act"][...], ws_v[:, cols])
-            + bias[:, 4 * D + FF + part * third : 4 * D + FF + part * third + third]
+            + bias[:, D + FF + part * third : D + FF + part * third + third]
         )
         kept["second"][:, cols] = second
         output = kept["middle"][:, cols] + modulation[5:6, cols] * second
@@ -651,6 +711,7 @@
         flow,
         mixed,
         att_grad,
+        qkv_grad,
         sums,
         wq_v,
         wp_v,
@@ -716,15 +777,17 @@
     by_rows(patches, open_second)
     save("d_second")
     fetched["pre"].wait()
+    for load in loads[:4]:
+        load.wait()
     for part in range(FF // D):
-        loads[part].wait()
         cols = slice(part * D, part * D + D)
         grads["d_pre"][:, cols] = (
             matmul_nt(grads["d_second"][...], ws_v[cols]) * gelu_grad(kept["pre"][:, cols])
         ).astype(jnp.bfloat16)
     save("d_pre")
+    for load in loads[4:7]:
+        load.wait()
     for part in range(3):
-        loads[4 + part].wait()
         cols = slice(part * third, part * third + third)
         mixed[:, cols] = matmul_nt(grads["d_pre"][...], wh_v[cols])
     fetched["middle"].wait()
@@ -743,14 +806,16 @@
     by_rows(patches, through_two)
     save("d_branch")
     loads[7].wait()
-    att_grad[...] = matmul_nt(grads["d_branch"][...], wp_v[...]).astype(jnp.bfloat16)
+    att_grad[...] = contract(wp_v[...], grads["d_branch"][...], 1, 1).astype(jnp.bfloat16)
     fetched["qkv"].wait()
-    attend_back_kernel(kept["qkv"], att_grad, grads["d_qkv"])
+    attend_back_kernel(kept["qkv"], att_grad, qkv_grad)
+    for load in loads[8:]:
+        load.wait()
+    for part in range(3):
+        cols = slice(part * third, part * third + third)
+        mixed[:, cols] = contract(qkv_grad[...], wq_v[cols], 0, 1)
+    grads["d_qkv"][...] = qkv_grad[...].T
     save("d_qkv")
-    for part in range(3):
-        loads[8 + part].wait()
-        cols = slice(part * third, part * third + third)
-        mixed[:, cols] = matmul_nt(grads["d_qkv"][...], wq_v[cols])
     fetched["residual"].wait()
 
     def through_one(at):
@@ -796,23 +861,25 @@
     )
 
 
-def image_forward(meta, arrived, bias, ada, tokens, weights, buffers):
+def image_forward(meta, arrived, bias, qkv_bias, ada, tokens, weights, buffers):
     patches, given, count = (arrived.shape[0], len(buffers), len(KEPT))
+    sizes = [item + (patches,) for item in KEPT]
     images = ada.shape[0]
     outs = pl.pallas_call(
         functools.partial(forward_kernel, patches, given),
         out_shape=[jax.ShapeDtypeStruct((patches, D), jnp.bfloat16)]
-        + [jax.ShapeDtypeStruct((images, patches, width), kind) for unused, width, kind in KEPT],
-        in_specs=specs("svvv", "h" * (5 + given)),
+        + [jax.ShapeDtypeStruct((images,) + kept_shape(*item), item[2]) for item in sizes],
+        in_specs=specs("svvvv", "h" * (5 + given)),
         out_specs=specs("v", "h" * count),
-        scratch_shapes=[pltpu.VMEM((patches, width), kind) for unused, width, kind in KEPT]
+        scratch_shapes=[pltpu.VMEM(kept_shape(*item), item[2]) for item in sizes]
+        + [pltpu.VMEM((D, patches), jnp.bfloat16)]
         + weight_scratch()
         + [pltpu.SemaphoreType.DMA, pltpu.SemaphoreType.DMA((count,))],
-        input_output_aliases={9 + i: 1 + i for i in range(given)},
+        input_output_aliases={10 + i: 1 + i for i in range(given)},
         compiler_params=pltpu.CompilerParams(vmem_limit_bytes=60 << 20),
         cost_estimate=block_cost(patches, 4),
         name="image_forward",
-    )(meta, arrived, bias, ada, tokens, *weights, *buffers)
+    )(meta, arrived, bias, qkv_bias, ada, tokens, *weights, *buffers)
     return (outs[0], outs[1:])
 
 
@@ -827,12 +894,15 @@
         + [jax.ShapeDtypeStruct((images, 8, D), jnp.float32)],
         in_specs=specs("svv", "h" * (5 + reads + given)),
         out_specs=specs("v", "h" * (made + 1)),
-        scratch_shapes=[pltpu.VMEM((patches, kinds[name][0]), kinds[name][1]) for name in READ]
+        scratch_shapes=[
+            pltpu.VMEM(kept_shape(name, *kinds[name], patches), kinds[name][1]) for name in READ
+        ]
         + [pltpu.VMEM((patches, width), kind) for unused, width, kind in MADE]
         + [
             pltpu.VMEM((patches, D), jnp.float32),
             pltpu.VMEM((patches, D), jnp.float32),
-            pltpu.VMEM((patches, D), jnp.bfloat16),
+            pltpu.VMEM((D, patches), jnp.bfloat16),
+            pltpu.VMEM((3 * D, patches), jnp.bfloat16),
             pltpu.VMEM((8, D), jnp.float32),
         ]
         + weight_scratch()
@@ -992,9 +1062,10 @@
     ada_own = jnp.sum(ada_got, axis=0).reshape(images, 8 * D)
     film = ada_own[:, 6 * D :] + small_used[3 * D : 5 * D]
     ada = (ada_own[:, : 6 * D] + bias_full[ada_at:]).reshape(images, 6, D)
-    bias_row = jnp.concatenate(
-        [bias_full[:D], jnp.zeros((D,), jnp.float32), bias_full[D:ada_at]]
-    )[None]
+    qkv_bias = jnp.concatenate(
+        [bias_full[:D], jnp.zeros((D,), jnp.float32), bias_full[D : 2 * D]]
+    )[:, None]
+    bias_row = bias_full[None, 2 * D : ada_at]
 
     fade = alpha_bar(timesteps)[:, None, None]
     noisy_low = (jnp.sqrt(fade) * latents + jnp.sqrt(1.0 - fade) * noise).astype(low)
@@ -1013,7 +1084,9 @@
     arrived = jnp.zeros((patches, D), low)
     for tick in range(ticks):
         meta = meta_of(tick - section_index, is_first, tick)
-        output, kept_all = image_forward(meta, arrived, bias_row, ada, tokens, weights, kept_all)
+        output, kept_all = image_forward(
+            meta, arrived, bias_row, qkv_bias, ada, tokens, weights, kept_all
+        )
         if tick < ticks - 1:
             arrived = passed_along(output, "section", 1)
     kept_of = {item[0]: whole for item, whole in zip(KEPT, kept_all)}
@@ -1037,6 +1110,14 @@
         )
         if tick < ticks - 1:
             arrived = passed_along(d_low, "section", -1)
+        if tick == 1:
+            film_all = lax.optimization_barrier((d_film, d_low))[0]
+            film_all = spread(film_all, "dp", 6).reshape(shards * images, 2 * D)
+        elif tick == 2:
+            film_all = lax.optimization_barrier((film_all, d_low))[0]
+            film_all = spread(film_all, "section", 7)[sections - 1]
+        if tick in (1, 2):
+            arrived, film_all = lax.optimization_barrier((arrived, film_all))
 
     def flat(whole):
         return whole.reshape(images * patches, whole.shape[2])
@@ -1050,15 +1131,14 @@
         matmul_tn(d_tokens, noisy_low.reshape(images * patches, PATCH_IN)),
         g_output,
     )
-    shard_wide, shard_down, right_sums, late, (token_sums, g_edge) = row_sums(
+    shard_wide, shard_down, right_sums, late, (token_sums, g_edge), d_ada_all = row_sums(
         [flat(kept_of[name]) for name in ("mixed_one", "att", "mixed_two", "act")],
         [d_qkv, d_branch, d_pre, d_second],
         (token_sums, g_edge),
-    )
-    d_ada, d_film, unused = lax.optimization_barrier((d_ada, d_film, late))
-    film_all = spread(d_film, "dp", 6).reshape(shards * images, 2 * D)
-    film_all = spread(film_all, "section", 7)[sections - 1]
-    d_ada_all = spread(d_ada, "dp", 8).reshape(shards * images, 6 * D)
+        d_ada,
+    )
+    d_ada, d_ada_all, unused = lax.optimization_barrier((d_ada, d_ada_all, late))
+    d_ada_all = d_ada_all.reshape(shards * images, 6 * D)
 
     cond_piece = matmul_nt(d_ada_all, w_ada) * silu_grad(cond_here)
     cond_pieces = spread(cond_piece, "section", 9)

time: 1630 us -> 1540 us (0.945)
  Pallas kernels: 1020 us -> 817 us
  waiting for transfers between devices: 372 us -> 476 us
    pallas_call x13 -> x12, Pallas kernels: 425 us -> 298 us  [share(): pl.pallas_call(functools.partial(share_kernel, axis, count, personal), ou...]
    ppermute x6, waiting for transfers between devices: 31.6 us -> 139 us  [row_sums(): lax.ppermute(blocks[step - 1], 'dp', [(i, (i + 2 * step) % count) for i i...]
    pallas_call x7, Pallas kernels: 272 us -> 219 us  [image_backward(): pl.pallas_call(functools.partial(backward_kernel, patches, given), out_sh...]
    pallas_call x7, Pallas kernels: 254 us -> 225 us  [image_forward(): pl.pallas_call(functools.partial(forward_kernel, patches, given), out_sha...]
  transfers between devices with their start and end apart: 22 -> 22, of which waited for: 16 -> 15; matrix products, arithmetic and copies ran while one was open for 5% -> 5% of each run, Pallas kernels for 28% -> 21%
where the time goes in v4:
time: 1540 us; the launch traced here: 1530 us
  Pallas kernels  817 us (53%)
  waiting for transfers between devices  476 us (31%)
  other arithmetic  91.2 us (6%)
  local copies, waits for them, and re-layouts  69.2 us (4%)
  matrix products  29.3 us (2%)
  starting transfers between devices  24.9 us (2%)
  between operations  23.1 us (2%)
    pallas_call x12, Pallas kernels, share(): pl.pallas_call(functools.partial(share_kernel, axis, count, personal), ou...  298 us
    pallas_call x7, Pallas kernels, image_forward(): pl.pallas_call(functools.partial(forward_kernel, patches, given), out_sha...  225 us
    pallas_call x7, Pallas kernels, image_backward(): pl.pallas_call(functools.partial(backward_kernel, patches, given), out_sh...  219 us
    all_gather x4, waiting for transfers between devices, gathered(): return lax.all_gather(value, axis, axis=dim, tiled=True)  211 us
    ppermute x6, waiting for transfers between devices, row_sums(): lax.ppermute(blocks[step - 1], 'dp', [(i, (i + 2 * step) % count) for i i...  139 us
    ppermute x12, waiting for transfers between devices, passed_along(): lax.ppermute(value, axis, [(source, source + steps) for source in range(f...  126 us
    pallas_call x2, Pallas kernels, chip_products(): pl.pallas_call(functools.partial(products_kernel, units, rows, len(given)...  74.7 us
    sub x5, other arithmetic, adam_update(): return (weight - RATE * (ratio + DECAY * weight), first_new, second_new)  34.8 us
  transfers between devices with their start and end apart: 22, of which 15 were waited for; matrix products, arithmetic and copies ran while one was open for 5% of the time, Pallas kernels for 21%

profile of v4, /device:TPU:0, one launch (start us, length us, event | category | flops | bytes accessed | tf_op | source)
XLA Modules:
  0.0 1531.4 jit_solution(8621880185357613366)
XLA Ops:
  7.2 4.1 convert_bitcast_fusion
  14.3 2.3 slice.290
  18.0 2.5 slice.292
  23.5 11.9 share.12
  38.5 23.1 %share.13 = bf16[4,146,1186]{2,1,0:T(8,128)(2,1)} custom-call(bf16[146,1186]{1,0:T(8,128)(2,1)} %pad_maximum_fusion.4.in_ref), custom_call_target="tpu_custom_call" | custom-call | tf_op jit(solution)/shard_map/share/pallas_call | solution.py:160
  66.4 13.6 share.14
  82.4 11.2 share.15
  99.9 44.8 %share.16 = f32[8,288,128]{2,1,0:T(8,128)} custom-call(f32[8,288,128]{2,1,0:T(8,128)} %reshape.317.in_ref), custom_call_target="tpu_custom_call" | custom-call | tf_op jit(solution)/shard_map/share/pallas_call | solution.py:160
  146.9 2.8 multiply_cosine_fusion
  151.2 3.0 fusion.2.tokens
  154.2 9.3 all-gather.6.cloned.1.call-done.wq
  163.5 101.2 %all-gather.12.cloned.1.call-done = bf16[1,4608,1152]{2,1,0:T(8,128)(2,1)} async-done(((bf16[1,576,1152]{2,1,0:T(8,128)(2,1)}), bf16[1,4608,1152]{2,1,0:T(8,128)(2,1)}) %all-gather.12.cloned.1.call-update) | async-done | bytes 10616848 | tf_op jit(solution)/shard_map/all_gather | solution.py:993
  264.7 101.0 %all-gather.10.cloned.1.call-done.wh = bf16[1152,4608]{1,0:T(8,128)(2,1)} async-done(((bf16[144,4608]{1,0:T(8,128)(2,1)}), bf16[1152,4608]{1,0:T(8,128)(2,1)}) %all-gather.10.cloned.1.call-update) | async-done | bytes 10616848 | tf_op jit(solution)/shard_map/all_gather | solution.py:993
  366.5 32.7 %image_forward.7 = (bf16[256,1152]{1,0:T(8,128)(2,1)}, f32[4,256,1152]{2,1,0:T(8,128)}, bf16[4,256,1152]{2,1,0:T(8,128)(2,1)}, bf16[4,3456,256]{2,1,0:T(8,128)(2...) custom-call(s32[4]{0:T(128)} %fusion.65.meta, ...), custom_call_target="tpu_custom_call" | custom-call | flops 8455716864 | bytes 50724864 | tf_op jit(solution)/shard_map/image_forward/pallas_call | solution.py:868
  401.2 12.9 collective-permute-done.arrived
  414.9 32.9 %image_forward.8 = (bf16[256,1152]{1,0:T(8,128)(2,1)}, f32[4,256,1152]{2,1,0:T(8,128)}, bf16[4,256,1152]{2,1,0:T(8,128)(2,1)}, bf16[4,3456,256]{2,1,0:T(8,128)(2...) custom-call(s32[4]{0:T(128)} %fusion.69.meta, ...), custom_call_target="tpu_custom_call", output_to_operand_aliasing={{1}: (10, {}), {2}: (11, {}), {3}: (12, {}), {4}: (13, {}),... | custom-call | flops 8455716864 | bytes 50724864 | tf_op jit(solution)/shard_map/image_forward/pallas_call | solution.py:868
  449.8 12.5 collective-permute-done.1.arrived
  463.0 32.7 %image_forward.9 = (bf16[256,1152]{1,0:T(8,128)(2,1)}, f32[4,256,1152]{2,1,0:T(8,128)}, bf16[4,256,1152]{2,1,0:T(8,128)(2,1)}, bf16[4,3456,256]{2,1,0:T(8,128)(2...) custom-call(s32[4]{0:T(128)} %fusion.73.meta, ...), custom_call_target="tpu_custom_call", output_to_operand_aliasing={{1}: (10, {}), {2}: (11, {}), {3}: (12, {}), {4}: (13, {}),... | custom-call | flops 8455716864 | bytes 50724864 | tf_op jit(solution)/shard_map/image_forward/pallas_call | solution.py:868
  497.7 11.9 collective-permute-done.2.arrived
  510.4 32.8 %image_forward.10 = (bf16[256,1152]{1,0:T(8,128)(2,1)}, f32[4,256,1152]{2,1,0:T(8,128)}, bf16[4,256,1152]{2,1,0:T(8,128)(2,1)}, bf16[4,3456,256]{2,1,0:T(8,128)(...) custom-call(s32[4]{0:T(128)} %fusion.83.meta, ...), custom_call_target="tpu_custom_call", output_to_operand_aliasing={{1}: (10, {}), {2}: (11, {}), {3}: (12, {}), {4}: (13, {}),... | custom-call | flops 8455716864 | bytes 50724864 | tf_op jit(solution)/shard_map/image_forward/pallas_call | solution.py:868
  547.1 9.2 collective-permute-done.3.arrived
  557.2 31.2 %image_forward.11 = (bf16[256,1152]{1,0:T(8,128)(2,1)}, f32[4,256,1152]{2,1,0:T(8,128)}, bf16[4,256,1152]{2,1,0:T(8,128)(2,1)}, bf16[4,3456,256]{2,1,0:T(8,128)(...) custom-call(s32[4]{0:T(128)} %fusion.81.meta, ...), custom_call_target="tpu_custom_call", output_to_operand_aliasing={{1}: (10, {}), {2}: (11, {}), {3}: (12, {}), {4}: (13, {}),... | custom-call | flops 8455716864 | bytes 50724864 | tf_op jit(solution)/shard_map/image_forward/pallas_call | solution.py:868
  589.8 11.2 collective-permute-done.4.arrived
  601.8 31.4 %image_forward.12 = (bf16[256,1152]{1,0:T(8,128)(2,1)}, f32[4,256,1152]{2,1,0:T(8,128)}, bf16[4,256,1152]{2,1,0:T(8,128)(2,1)}, bf16[4,3456,256]{2,1,0:T(8,128)(...) custom-call(s32[4]{0:T(128)} %fusion.79.meta, ...), custom_call_target="tpu_custom_call", output_to_operand_aliasing={{1}: (10, {}), {2}: (11, {}), {3}: (12, {}), {4}: (13, {}),... | custom-call | flops 8455716864 | bytes 50724864 | tf_op jit(solution)/shard_map/image_forward/pallas_call | solution.py:868
  635.8 9.3 collective-permute-done.5.arrived
  645.9 31.2 %image_forward.13 = (bf16[256,1152]{1,0:T(8,128)(2,1)}, f32[4,256,1152]{2,1,0:T(8,128)}, bf16[4,256,1152]{2,1,0:T(8,128)(2,1)}, bf16[4,3456,256]{2,1,0:T(8,128)(...) custom-call(s32[4]{0:T(128)} %fusion.77.meta, ...), custom_call_target="tpu_custom_call", output_to_operand_aliasing={{1}: (10, {}), {2}: (11, {}), {3}: (12, {}), {4}: (13, {}),... | custom-call | flops 8455716864 | bytes 50724864 | tf_op jit(solution)/shard_map/image_forward/pallas_call | solution.py:868
  677.2 2.7 reduce_sum.258
  679.9 3.1 multiply_reduce_fusion.2
  685.4 2.9 multiply_reduce_fusion
  688.4 2.9 subtract_multiply_fusion.head_grad
  691.2 30.9 %image_backward.7 = (bf16[256,1152]{1,0:T(8,128)(2,1)}, bf16[4,256,1152]{2,1,0:T(8,128)(2,1)}, bf16[4,256,4608]{2,1,0:T(8,128)(2,1)}, bf16[4,256,1152]{2,1,0:T(8...) custom-call(s32[4]{0:T(128)} %get-tuple-element.409.meta, ...), custom_call_target="tpu_custom_call" | custom-call | flops 8908701696 | bytes 50724864 | tf_op jit(solution)/shard_map/image_backward/pallas_call | solution.py:890
  724.1 12.0 collective-permute-done.6.arrived
  736.9 30.9 %image_backward.8 = (bf16[256,1152]{1,0:T(8,128)(2,1)}, bf16[4,256,1152]{2,1,0:T(8,128)(2,1)}, bf16[4,256,4608]{2,1,0:T(8,128)(2,1)}, bf16[4,256,1152]{2,1,0:T(8...) custom-call(s32[4]{0:T(128)} %get-tuple-element.411.meta, ...), custom_call_target="tpu_custom_call", output_to_operand_aliasing={{1}: (14, {}), {2}: (15, {}), {3}: (16, {}), {4}: (17, {}),... | custom-call | flops 8908701696 | bytes 50724864 | tf_op jit(solution)/shard_map/image_backward/pallas_call | solution.py:890
  769.7 7.3 share.17
  778.7 2.2 collective-permute-done.7.arrived
  781.7 30.9 %image_backward.9 = (bf16[256,1152]{1,0:T(8,128)(2,1)}, bf16[4,256,1152]{2,1,0:T(8,128)(2,1)}, bf16[4,256,4608]{2,1,0:T(8,128)(2,1)}, bf16[4,256,1152]{2,1,0:T(8...) custom-call(s32[4]{0:T(128)} %get-tuple-element.412.meta, ...), custom_call_target="tpu_custom_call", output_to_operand_aliasing={{1}: (14, {}), {2}: (15, {}), {3}: (16, {}), {4}: (17, {}),... | custom-call | flops 8908701696 | bytes 50724864 | tf_op jit(solution)/shard_map/image_backward/pallas_call | solution.py:890
  813.9 23.8 %share.18 = bf16[4,32,2304]{2,1,0:T(8,128)(2,1)} custom-call(bf16[32,2304]{1,0:T(8,128)(2,1)} %reshape.324.in_ref), custom_call_target="tpu_custom_call" | custom-call | tf_op jit(solution)/shard_map/share/pallas_call | solution.py:160
  840.1 31.7 %image_backward.10 = (bf16[256,1152]{1,0:T(8,128)(2,1)}, bf16[4,256,1152]{2,1,0:T(8,128)(2,1)}, bf16[4,256,4608]{2,1,0:T(8,128)(2,1)}, bf16[4,256,1152]{2,1,0:T(...) custom-call(s32[4]{0:T(128)} %get-tuple-element.410.meta, ...), custom_call_target="tpu_custom_call", output_to_operand_aliasing={{1}: (14, {}), {2}: (15, {}), {3}: (16, {}), {4}: (17, {}),... | custom-call | flops 8908701696 | bytes 50724864 | tf_op jit(solution)/shard_map/image_backward/pallas_call | solution.py:890
  873.7 15.8 %collective-permute-done.9.arrived = bf16[256,1152]{1,0:T(8,128)(2,1)S(1)} collective-permute-done((bf16[256,1152]{1,0:T(8,128)(2,1)}, bf16[256,1152]{1,0:T(8,128)(2,1)S(1)}, u32[]{:S(2)}, u32[]{:S(2)}) %collective-permute-start.9) | collective-permute-done | bytes 589856 | tf_op jit(solution)/shard_map/ppermute | solution.py:34
  890.3 31.6 %image_backward.11 = (bf16[256,1152]{1,0:T(8,128)(2,1)}, bf16[4,256,1152]{2,1,0:T(8,128)(2,1)}, bf16[4,256,4608]{2,1,0:T(8,128)(2,1)}, bf16[4,256,1152]{2,1,0:T(...) custom-call(s32[4]{0:T(128)} %fusion.89.meta, ...), custom_call_target="tpu_custom_call", output_to_operand_aliasing={{1}: (14, {}), {2}: (15, {}), {3}: (16, {}), {4}: (17, {}),... | custom-call | flops 8908701696 | bytes 50724864 | tf_op jit(solution)/shard_map/image_backward/pallas_call | solution.py:890
  923.8 15.1 collective-permute-done.10.arrived
  939.7 31.5 %image_backward.12 = (bf16[256,1152]{1,0:T(8,128)(2,1)}, bf16[4,256,1152]{2,1,0:T(8,128)(2,1)}, bf16[4,256,4608]{2,1,0:T(8,128)(2,1)}, bf16[4,256,1152]{2,1,0:T(...) custom-call(s32[4]{0:T(128)} %fusion.87.meta, ...), custom_call_target="tpu_custom_call", output_to_operand_aliasing={{1}: (14, {}), {2}: (15, {}), {3}: (16, {}), {4}: (17, {}),... | custom-call | flops 8908701696 | bytes 50724864 | tf_op jit(solution)/shard_map/image_backward/pallas_call | solution.py:890
  973.9 3.2 convolution_bitcast_fusion
  977.2 14.1 collective-permute-done.11.arrived
  992.1 31.7 %image_backward.13 = (bf16[256,1152]{1,0:T(8,128)(2,1)}, bf16[4,256,1152]{2,1,0:T(8,128)(2,1)}, bf16[4,256,4608]{2,1,0:T(8,128)(2,1)}, bf16[4,256,1152]{2,1,0:T(...) custom-call(s32[4]{0:T(128)} %fusion.85.meta, ...), custom_call_target="tpu_custom_call", output_to_operand_aliasing={{1}: (14, {}), {2}: (15, {}), {3}: (16, {}), {4}: (17, {}),... | custom-call | flops 8908701696 | bytes 50724864 | tf_op jit(solution)/shard_map/image_backward/pallas_call | solution.py:890
  1028.7 29.6 %chip_products.2 = (f32[4,144,1152]{2,1,0:T(8,128)}, bf16[4,144,1152]{2,1,0:T(8,128)(2,1)}, bf16[4,144,1152]{2,1,0:T(8,128)(2,1)}, bf16[4,144,1152]{2,1,0:T(8,12...) custom-call(bf16[1024,1152]{1,0:T(8,128)(2,1)} %bitcast.181, bf16[1024,1152]{1,0:T(8,128)(2,1)} %bitcast.183, ...), custom_call_target="tpu_custom_call" | custom-call | flops 10871635968 | bytes 18874368 | tf_op jit(solution)/shard_map/chip_products/pallas_call | solution.py:416
  1059.1 2.4 collective-permute-start.13
  1062.9 45.1 %chip_products.3 = (f32[8,144,1152]{2,1,0:T(8,128)}, bf16[8,144,1152]{2,1,0:T(8,128)(2,1)}, bf16[8,144,1152]{2,1,0:T(8,128)(2,1)}, bf16[8,144,1152]{2,1,0:T(8,128)(2,1)}, f32[8,8,1152]{2,1,0:T(8,128)}) custom-call(bf16[1024,1152]{1,0:T(8,128)(2,1)} %bitcast.182, bf16[1024,1152]{1,0:T(8,128)(2,1)} %bitcast.184, bf16[1024,1152]{1,0:T(8,128)(2,1)} %bitcast.186, ...), custom_call_target="tpu_custom_call" | custom-call | flops 21743271936 | bytes 37748736 | tf_op jit(solution)/shard_map/chip_products/pallas_call | solution.py:416
  1120.0 2.9 collective-permute-start.17
  1122.9 138.8 %collective-permute-done.13 = bf16[4,144,1152]{2,1,0:T(8,128)(2,1)S(1)} collective-permute-done((bf16[4,144,1152]{2,1,0:T(8,128)(2,1)}, bf16[4,144,1152]{2,1,0:T(8,128)(2,1)S(1)}, u32[]{:S(2)}, u32[]{:S(2)}) %collective-permute-start.13) | collective-permute-done | bytes 1327136 | tf_op jit(solution)/shard_map/ppermute | solution.py:477
  1262.7 3.5 convert_add_fusion.1
  1270.4 3.0 fusion.19.in_ref
  1273.4 16.5 %share.19 = f32[4,32,144]{2,1,0:T(8,128)} custom-call(f32[32,144]{1,0:T(8,128)} %fusion.19.in_ref), custom_call_target="tpu_custom_call" | custom-call | tf_op jit(solution)/shard_map/share/pallas_call | solution.py:160
  1292.0 115.1 %share.20 = bf16[8,32,144]{2,1,0:T(8,128)(2,1)} custom-call(bf16[32,144]{1,0:T(8,128)(2,1)} %fusion.22.in_ref), custom_call_target="tpu_custom_call" | custom-call | tf_op jit(solution)/shard_map/share/pallas_call | solution.py:160
  1413.5 7.6 share.21
  1425.7 5.9 convert_add_fusion
  1441.9 2.6 fusion.104
  1445.9 3.5 concatenate.86
  1450.4 6.8 fusion.1
  1460.4 7.6 share.22
  1469.3 15.7 %share.23 = f32[4,2,128]{2,1,0:T(2,128)} custom-call(f32[2,128]{1,0:T(2,128)} %reduce_sum.281.in_ref), custom_call_target="tpu_custom_call" | custom-call | tf_op jit(solution)/shard_map/share/pallas_call | solution.py:160
  1488.4 3.5 multiply_subtract_fusion.2
  1493.5 8.2 multiply_subtract_fusion.1
  1502.3 20.9 %multiply_subtract_fusion = (f32[1,144,16128]{2,1,0:T(8,128)}, f32[1,144,16128]{2,1,0:T(8,128)}, f32[1,144,16128]{2,1,0:T(8,128)}) fusion(f32[1,144,16128]{2,1,0:T(8,128)S(1)} %bitcast.188, f32[]{:T(128)S(6)} %min.60, f32[1,144,6912]{2,1,0:T(8,128)} %bitcast.189, f32[1,144,9216]{2,1,0:T(8,128)} %bitcast.72, f32[1,144,16128]{2,1,0:T(8,128)} %param.30, ...), kind=kLoop, calls=%fused_computation.5 | loop fusion | flops 39481344 | bytes 65028100 | tf_op jit(solution)/shard_map/sub | solution.py:952
  (345 shorter events, 122.2 us)
Async XLA Ops:
  7.2 147.0 %all-gather.8.cloned.1.call-start = ((), (), s32[]{:S(2)}) async-start(), calls=%async_computation.1 | async-start | bytes 2985984 | tf_op jit(solution)/shard_map/all_gather | solution.py:993
  14.2 149.3 %all-gather.6.cloned.1.call-start = ((), (), s32[]{:S(2)}) async-start(), calls=%async_computation | async-start | bytes 8957952 | tf_op jit(solution)/shard_map/all_gather | solution.py:993
  16.7 5.9 copy-start.7
  16.7 6.1 copy-start.60
  16.7 248.1 %all-gather.12.cloned.1.call-start = ((), (), s32[]{:S(2)}) async-start(), calls=%async_computation.3 | async-start | bytes 11943936 | tf_op jit(solution)/shard_map/all_gather | solution.py:993
  18.0 347.7 %all-gather.10.cloned.1.call-start = ((), (), s32[]{:S(2)}) async-start(), calls=%async_computation.2 | async-start | bytes 11943936 | tf_op jit(solution)/shard_map/all_gather | solution.py:993
  36.7 28.3 %copy-start.70 = (s32[32]{0:T(128)}, s32[32]{0:T(128)S(1)}, u32[]{:S(2)}) copy-start(s32[32]{0:T(128)S(1)} %convert_element_type.192) | copy-start | bytes 388
  37.7 113.5 %copy-start.11 = (bf16[1152,16]{1,0:T(8,128)(2,1)}, bf16[1152,16]{1,0:T(8,128)(2,1)S(1)}, u32[]{:S(2)}) copy-start(bf16[1152,16]{1,0:T(8,128)(2,1)S(1)} %convert_element_type.198) | copy-start | bytes 110596
  63.1 33.6 %copy-start.49 = (bf16[32,128]{1,0:T(8,128)(2,1)}, bf16[32,128]{1,0:T(8,128)(2,1)S(1)}, u32[]{:S(2)}) copy-start(bf16[32,128]{1,0:T(8,128)(2,1)S(1)} %get-tuple-element.402) | copy-start | bytes 24580
  64.6 32.0 %copy-start.9 = (bf16[144,1186]{1,0:T(8,128)(2,1)}, bf16[144,1186]{1,0:T(8,128)(2,1)S(1)}, u32[]{:S(2)}) copy-start(bf16[144,1186]{1,0:T(8,128)(2,1)S(1)} %get-tuple-element.379) | copy-start | bytes 1024708
  64.6 32.0 %copy-start.35 = (bf16[144,1186]{1,0:T(8,128)(2,1)}, bf16[144,1186]{1,0:T(8,128)(2,1)S(1)}, u32[]{:S(2)}) copy-start(bf16[144,1186]{1,0:T(8,128)(2,1)S(1)} %get-tuple-element.378) | copy-start | bytes 1024708
  65.1 31.5 %copy-start.33 = (f32[32,144]{1,0:T(8,128)}, f32[32,144]{1,0:T(8,128)S(1)}, u32[]{:S(2)}) copy-start(f32[32,144]{1,0:T(8,128)S(1)} %convolution_add_fusion.2) | copy-start | bytes 55300
  99.9 51.2 %copy-start.40 = (f32[4,256,16]{1,2,0:T(8,128)S(1)}, f32[4,256,16]{1,2,0:T(8,128)}, u32[]{:S(2)}) copy-start(f32[4,256,16]{1,2,0:T(8,128)} %param.21) | copy-start | bytes 196612
  99.9 51.2 %copy-start.54 = (f32[4,256,16]{1,2,0:T(8,128)S(1)}, f32[4,256,16]{1,2,0:T(8,128)}, u32[]{:S(2)}) copy-start(f32[4,256,16]{1,2,0:T(8,128)} %param.20) | copy-start | bytes 196612
  151.2 248.0 %copy-start.38 = (bf16[4,256,16]{1,2,0:T(8,128)(2,1)}, bf16[4,256,16]{1,2,0:T(8,128)(2,1)S(1)}, u32[]{:S(2)}) copy-start(bf16[4,256,16]{1,2,0:T(8,128)(2,1)S(1)} %add_convert_fusion.1) | copy-start | bytes 98308
  399.2 14.9 collective-permute-start
  447.8 14.4 collective-permute-start.1
  495.8 13.8 collective-permute-start.2
  543.2 13.2 collective-permute-start.3
  588.4 12.5 collective-permute-start.4
  633.2 11.9 collective-permute-start.5
  635.8 47.2 %copy-start.43 = (f32[4,1152]{1,0:T(4,128)}, f32[4,1152]{1,0:T(4,128)S(1)}, u32[]{:S(2)}) copy-start(f32[4,1152]{1,0:T(4,128)S(1)} %get-tuple-element.389) | copy-start | bytes 55300
  635.8 52.5 %copy-start.36 = (f32[4,1152]{1,0:T(4,128)}, f32[4,1152]{1,0:T(4,128)S(1)}, u32[]{:S(2)}) copy-start(f32[4,1152]{1,0:T(4,128)S(1)} %get-tuple-element.388) | copy-start | bytes 55300
  679.9 8.5 copy-start.47
  722.1 14.0 collective-permute-start.6
  767.8 13.0 collective-permute-start.7
  812.6 26.7 %collective-permute-start.8 = (bf16[256,1152]{1,0:T(8,128)(2,1)}, bf16[256,1152]{1,0:T(8,128)(2,1)S(1)}, u32[]{:S(2)}, u32[]{:S(2)}) collective-permute-start(bf16[256,1152]{1,0:T(8,128)(2,1)} %get-tuple-element.284), channel_id=1, source_target_pairs={{8,0},{16,8},{24,16},{9,1},{17,9},{25,17},{10,2},{18,10},{26,18},{... | collective-permute-start | bytes 1769480 | tf_op jit(solution)/shard_map/ppermute | solution.py:34
  871.8 17.7 %collective-permute-start.9 = (bf16[256,1152]{1,0:T(8,128)(2,1)}, bf16[256,1152]{1,0:T(8,128)(2,1)S(1)}, u32[]{:S(2)}, u32[]{:S(2)}) collective-permute-start(bf16[256,1152]{1,0:T(8,128)(2,1)} %get-tuple-element.294), channel_id=1, source_target_pairs={{8,0},{16,8},{24,16},{9,1},{17,9},{25,17},{10,2},{18,10},{26,18},{... | collective-permute-start | bytes 1769480 | tf_op jit(solution)/shard_map/ppermute | solution.py:34
  921.9 17.0 %collective-permute-start.10 = (bf16[256,1152]{1,0:T(8,128)(2,1)}, bf16[256,1152]{1,0:T(8,128)(2,1)S(1)}, u32[]{:S(2)}, u32[]{:S(2)}) collective-permute-start(bf16[256,1152]{1,0:T(8,128)(2,1)} %get-tuple-element.301), channel_id=1, source_target_pairs={{8,0},{16,8},{24,16},{9,1},{17,9},{25,17},{10,2},{18,10},{26,18},{... | collective-permute-start | bytes 1769480 | tf_op jit(solution)/shard_map/ppermute | solution.py:34
  939.7 34.2 %copy-start.37 = (f32[4,1152]{1,0:T(4,128)S(1)}, f32[4,1152]{1,0:T(4,128)}, u32[]{:S(2)}) copy-start(f32[4,1152]{1,0:T(4,128)} %copy-done.36) | copy-start | bytes 55300
  939.7 34.2 %copy-start.44 = (f32[4,1152]{1,0:T(4,128)S(1)}, f32[4,1152]{1,0:T(4,128)}, u32[]{:S(2)}) copy-start(f32[4,1152]{1,0:T(4,128)} %copy-done.43) | copy-start | bytes 55300
  939.7 34.2 %copy-start.46 = (bf16[4,256,16]{1,2,0:T(8,128)(2,1)S(1)}, bf16[4,256,16]{1,2,0:T(8,128)(2,1)}, u32[]{:S(2)}) copy-start(bf16[4,256,16]{1,2,0:T(8,128)(2,1)} %copy-done.45) | copy-start | bytes 98308
  939.7 34.2 %copy-start.48 = (f32[4,256]{1,0:T(4,128)S(1)}, f32[4,256]{1,0:T(4,128)}, u32[]{:S(2)}) copy-start(f32[4,256]{1,0:T(4,128)} %copy-done.47) | copy-start | bytes 12292
  939.7 34.2 %copy-start.57 = (f32[4,256]{1,0:T(4,128)S(1)}, f32[4,256]{1,0:T(4,128)}, u32[]{:S(2)}) copy-start(f32[4,256]{1,0:T(4,128)} %copy-done.56) | copy-start | bytes 12292
  971.3 20.0 %collective-permute-start.11 = (bf16[256,1152]{1,0:T(8,128)(2,1)}, bf16[256,1152]{1,0:T(8,128)(2,1)S(1)}, u32[]{:S(2)}, u32[]{:S(2)}) collective-permute-start(bf16[256,1152]{1,0:T(8,128)(2,1)} %get-tuple-element.308), channel_id=1, source_target_pairs={{8,0},{16,8},{24,16},{9,1},{17,9},{25,17},{10,2},{18,10},{26,18},{... | collective-permute-start | bytes 1769480 | tf_op jit(solution)/shard_map/ppermute | solution.py:34
  992.1 33.8 %copy-start.39 = (bf16[4,256,16]{1,2,0:T(8,128)(2,1)S(1)}, bf16[4,256,16]{1,2,0:T(8,128)(2,1)}, u32[]{:S(2)}) copy-start(bf16[4,256,16]{1,2,0:T(8,128)(2,1)} %copy-done.38) | copy-start | bytes 98308
  1058.3 61.7 %collective-permute-start.12 = (bf16[4,144,1152]{2,1,0:T(8,128)(2,1)}, bf16[4,144,1152]{2,1,0:T(8,128)(2,1)S(1)}, u32[]{:S(2)}, u32[]{:S(2)}) collective-permute-start(bf16[4,144,1152]{2,1,0:T(8,128)(2,1)} %get-tuple-element.321), channel_id=1, source_target_pairs={{0,2},{1,3},{2,4},{3,5},{4,6},{5,7},{6,0},{7,1},{8,10},{9,11},{10,... | collective-permute-start | bytes 3981320 | tf_op jit(solution)/shard_map/ppermute | solution.py:477
  1059.1 202.5 %collective-permute-start.13 = (bf16[4,144,1152]{2,1,0:T(8,128)(2,1)}, bf16[4,144,1152]{2,1,0:T(8,128)(2,1)S(1)}, u32[]{:S(2)}, u32[]{:S(2)}) collective-permute-start(bf16[4,144,1152]{2,1,0:T(8,128)(2,1)} %get-tuple-element.322), channel_id=1, source_target_pairs={{0,4},{1,5},{2,6},{3,7},{4,0},{5,1},{6,2},{7,3},{8,12},{9,13},{10,... | collective-permute-start | bytes 3981320 | tf_op jit(solution)/shard_map/ppermute | solution.py:477
  1061.5 200.2 %collective-permute-start.14 = (bf16[4,144,1152]{2,1,0:T(8,128)(2,1)}, bf16[4,144,1152]{2,1,0:T(8,128)(2,1)}, u32[]{:S(2)}, u32[]{:S(2)}) collective-permute-start(bf16[4,144,1152]{2,1,0:T(8,128)(2,1)} %get-tuple-element.323), channel_id=1, source_target_pairs={{0,6},{1,7},{2,0},{3,1},{4,2},{5,3},{6,4},{7,5},{8,14},{9,15},{10,... | collective-permute-start | bytes 3981320 | tf_op jit(solution)/shard_map/ppermute | solution.py:477
  1110.2 315.5 %collective-permute-start.15 = (bf16[8,144,1152]{2,1,0:T(8,128)(2,1)}, bf16[8,144,1152]{2,1,0:T(8,128)(2,1)}, u32[]{:S(2)}, u32[]{:S(2)}) collective-permute-start(bf16[8,144,1152]{2,1,0:T(8,128)(2,1)} %get-tuple-element.335), channel_id=1, source_target_pairs={{0,2},{1,3},{2,4},{3,5},{4,6},{5,7},{6,0},{7,1},{8,10},{9,11},{10,... | collective-permute-start | bytes 7962632 | tf_op jit(solution)/shard_map/ppermute | solution.py:477
  1110.8 314.9 %collective-permute-start.16 = (bf16[8,144,1152]{2,1,0:T(8,128)(2,1)}, bf16[8,144,1152]{2,1,0:T(8,128)(2,1)}, u32[]{:S(2)}, u32[]{:S(2)}) collective-permute-start(bf16[8,144,1152]{2,1,0:T(8,128)(2,1)} %get-tuple-element.336), channel_id=1, source_target_pairs={{0,4},{1,5},{2,6},{3,7},{4,0},{5,1},{6,2},{7,3},{8,12},{9,13},{10,... | collective-permute-start | bytes 7962632 | tf_op jit(solution)/shard_map/ppermute | solution.py:477
  1112.6 153.6 %copy-start.42 = (bf16[1,4,6,1152]{3,1,2,0:T(4,128)(2,1)S(1)}, bf16[1,4,6,1152]{3,1,2,0:T(4,128)(2,1)}, u32[]{:S(2)}) copy-start(bf16[1,4,6,1152]{3,1,2,0:T(4,128)(2,1)} %copy.164) | copy-start | bytes 165892
  1120.0 141.7 %copy-start.15 = (bf16[4,144,1152]{2,1,0:T(8,128)(2,1)}, bf16[4,144,1152]{2,1,0:T(8,128)(2,1)S(1)}, u32[]{:S(2)}) copy-start(bf16[4,144,1152]{2,1,0:T(8,128)(2,1)S(1)} %collective-permute-done.12) | copy-start | bytes 3981316
  1120.0 305.7 %collective-permute-start.17 = (bf16[8,144,1152]{2,1,0:T(8,128)(2,1)}, bf16[8,144,1152]{2,1,0:T(8,128)(2,1)}, u32[]{:S(2)}, u32[]{:S(2)}) collective-permute-start(bf16[8,144,1152]{2,1,0:T(8,128)(2,1)} %get-tuple-element.337), channel_id=1, source_target_pairs={{0,6},{1,7},{2,0},{3,1},{4,2},{5,3},{6,4},{7,5},{8,14},{9,15},{10,... | collective-permute-start | bytes 7962632 | tf_op jit(solution)/shard_map/ppermute | solution.py:477
  1262.7 27.2 %copy-start.10 = (bf16[144,1186]{1,0:T(8,128)(2,1)S(1)}, bf16[144,1186]{1,0:T(8,128)(2,1)}, u32[]{:S(2)}) copy-start(bf16[144,1186]{1,0:T(8,128)(2,1)} %copy-done.9) | copy-start | bytes 1024708
  1262.7 27.2 %copy-start.17 = (bf16[32,2304]{1,0:T(8,128)(2,1)S(1)}, bf16[32,2304]{1,0:T(8,128)(2,1)}, u32[]{:S(2)}) copy-start(bf16[32,2304]{1,0:T(8,128)(2,1)} %slice_bitcast_fusion.12) | copy-start | bytes 442372
  1266.2 143.7 %copy-start.6 = (bf16[144,1186]{1,0:T(8,128)(2,1)S(1)}, bf16[144,1186]{1,0:T(8,128)(2,1)}, u32[]{:S(2)}) copy-start(bf16[144,1186]{1,0:T(8,128)(2,1)} %copy-done.5) | copy-start | bytes 1024708
  1266.2 145.4 %copy-start.72 = (f32[16]{0:T(128)S(1)}, f32[16]{0:T(128)}, u32[]{:S(2)}) copy-start(f32[16]{0:T(128)} %get-tuple-element.375) | copy-start | bytes 196
  1431.8 7.3 copy-start.1
  1432.8 7.1 copy-start.50
  1432.8 7.1 copy-start.52
  1432.8 7.1 copy-start.55
  1432.8 8.0 copy-start.53
  1432.8 8.0 copy-start.71
  1433.8 8.1 copy-start.14
  1436.4 8.1 copy-start.64
  1450.4 38.0 %copy-start.8 = (f32[144,1186]{1,0:T(8,128)S(1)}, f32[144,1186]{1,0:T(8,128)}, u32[]{:S(2)}) copy-start(f32[144,1186]{1,0:T(8,128)} %param.28) | copy-start | bytes 2049412
  1457.1 34.7 %copy-start.59 = (f32[1444]{0:T(1024)S(1)}, f32[1444]{0:T(1024)}, u32[]{:S(2)}) copy-start(f32[1444]{0:T(1024)} %param.29) | copy-start | bytes 17332
  1491.9 10.5 slice-start
  1493.4 8.2 copy-start.61
  1493.4 8.2 copy-start.68
  1493.4 8.2 copy-start.69
  1493.5 8.9 slice-start.1
  1493.5 8.9 slice-start.2
  (36 other events, 99.1 us)
Sparse Core Ops, SparseCore 0:
  14.3 39.9 all-gather.7
  56.5 106.9 all-gather.5
  165.7 98.9 all-gather.11
  266.8 98.8 all-gather.9

commit v5 on v4

--- a/solution.py
+++ b/solution.py
@@ -552,32 +552,31 @@
 
 
 ROW_BLOCK = 64
+HOPS = 3
+RESIDUAL, MIXED_ONE, QKV, ATT, BRANCH, MIDDLE = range(6)
+MIXED_TWO, PRE, ACT, SECOND, OUTPUT = range(6, 11)
+D_SECOND, D_PRE, D_BRANCH, D_QKV, D_RESIDUAL = range(5)
+WIDE, LOW = (jnp.float32, jnp.bfloat16)
 KEPT = (
-    ("residual", D, jnp.float32),
-    ("mixed_one", D, jnp.bfloat16),
-    ("qkv", 3 * D, jnp.bfloat16),
-    ("att", D, jnp.bfloat16),
-    ("branch", D, jnp.float32),
-    ("middle", D, jnp.float32),
-    ("mixed_two", D, jnp.bfloat16),
-    ("pre", FF, jnp.float32),
-    ("act", FF, jnp.bfloat16),
-    ("second", D, jnp.float32),
-    ("output", D, jnp.float32),
+    (D, WIDE),
+    (D, LOW),
+    (3 * D, LOW),
+    (D, LOW),
+    (D, WIDE),
+    (D, WIDE),
+    (D, LOW),
+    (FF, WIDE),
+    (FF, LOW),
+    (D, WIDE),
+    (D, WIDE),
 )
-READ = ("residual", "qkv", "branch", "middle", "pre", "second")
-MADE = (
-    ("d_second", D, jnp.bfloat16),
-    ("d_pre", FF, jnp.bfloat16),
-    ("d_branch", D, jnp.bfloat16),
-    ("d_qkv", 3 * D, jnp.bfloat16),
-    ("d_residual", D, jnp.bfloat16),
-)
+READ = (RESIDUAL, QKV, BRANCH, MIDDLE, PRE, SECOND)
+MADE = ((D, LOW), (FF, LOW), (D, LOW), (3 * D, LOW), (D, LOW))
 WEIGHTS = ((D, 3 * D), (D, D), (D, FF), (FF, D))
 
 
-def kept_shape(name, width, kind, patches):
-    return (width, patches) if name == "qkv" else (patches, width)
+def kept_shape(name, width, patches):
+    return (width, patches) if name == QKV else (patches, width)
 
 
 def by_rows(patches, step):
@@ -592,127 +591,170 @@
     return copy
 
 
-def forward_kernel(
-    patches, given, meta, arrived, bias, qkv_bias, ada, tokens, wq, wp, wh, ws, *refs
-):
-    count = len(KEPT)
-    send, outs = (refs[given], refs[given + 1 : given + 1 + count])
-    scratch = refs[given + 1 + count :]
-    kept = {name: scratch[i] for i, (name, unused, kind) in enumerate(KEPT)}
-    att_down, wq_v, wp_v, wh_v, ws_v, w_sem, x_sem, out_sem = scratch[count:]
-    loads = [started(wq.at[:, pl.ds(i * D, D)], wq_v.at[:, pl.ds(i * D, D)], w_sem.at[i]) for i in range(3)]
+def parts_of(whole, parts):
+    width = whole // parts
+    return [slice(part * width, part * width + width) for part in range(parts)]
+
+
+def wait_first(image, loads):
+    @pl.when(image == 0)
+    def wait():
+        for load in loads:
+            load.wait()
+
+
+def hop_of(send, received, send_sem, recv_sem, target):
+    def hop(image, part):
+        cols = pl.ds(part * (D // HOPS), D // HOPS)
+        return pltpu.make_async_remote_copy(
+            src_ref=send.at[image, :, cols],
+            dst_ref=received.at[image, :, cols],
+            send_sem=send_sem.at[image, part],
+            recv_sem=recv_sem.at[image, part],
+            device_id={"section": target},
+            device_id_type=MESH,
+        )
+
+    return hop
+
+
+def forward_kernel(sections, images, bias, qkv_bias, ada, tokens, wq, wp, wh, ws, *refs):
+    count, patches = (len(KEPT), tokens.shape[1])
+    outs, scratch = (refs[:count], refs[count:])
+    kept = scratch[:count]
+    (
+        att_down,
+        send,
+        received,
+        wq_v,
+        wp_v,
+        wh_v,
+        ws_v,
+        w_sem,
+        x_sem,
+        out_sem,
+        send_sem,
+        recv_sem,
+    ) = scratch[count:]
+    section = lax.axis_index("section")
+    loads = [
+        started(wq.at[:, cols], wq_v.at[:, cols], w_sem.at[i])
+        for i, cols in enumerate(parts_of(3 * D, 3))
+    ]
     loads.append(started(wp, wp_v, w_sem.at[3]))
-    loads += [
-        started(wh.at[:, pl.ds(i * D, D)], wh_v.at[:, pl.ds(i * D, D)], w_sem.at[4 + i])
-        for i in range(FF // D)
-    ]
-    third = D // 3
-    loads += [
-        started(ws.at[:, pl.ds(i * third, third)], ws_v.at[:, pl.ds(i * third, third)], w_sem.at[8 + i])
-        for i in range(3)
-    ]
-    saves = []
-
-    def start_if_valid(copy):
-        @pl.when(meta[3] == 1)
-        def start():
-            copy.start()
-
-    def save(name):
-        index = [item[0] for item in KEPT].index(name)
-        saves.append(pltpu.make_async_copy(kept[name], outs[index].at[meta[0]], out_sem.at[index]))
-        start_if_valid(saves[-1])
-
-    residual = kept["residual"]
-
-    @pl.when(meta[2] == 1)
-    def take_tokens():
-        started(tokens.at[meta[1]], residual, x_sem).wait()
-
-    @pl.when(meta[2] == 0)
-    def take_arrived():
-        residual[...] = arrived[...].astype(jnp.float32)
-
-    save("residual")
-    modulation = ada[meta[0]]
-
-    def mix_one(at):
-        normed, unused = normalize(residual[at])
-        kept["mixed_one"][at] = (normed * (1.0 + modulation[1:2]) + modulation[0:1]).astype(
-            jnp.bfloat16
-        )
-
-    by_rows(patches, mix_one)
-    save("mixed_one")
-    for part in range(3):
-        loads[part].wait()
-        cols = slice(part * D, part * D + D)
-        kept["qkv"][cols] = (
-            contract(wq_v[:, cols], kept["mixed_one"][...], 0, 1) + qkv_bias[cols]
-        ).astype(jnp.bfloat16)
-    save("qkv")
-    attend_kernel(kept["qkv"], att_down)
-    loads[3].wait()
-    kept["branch"][...] = contract(att_down[...], wp_v[...], 0, 0) + bias[:, :D]
-    kept["att"][...] = att_down[...].T
-    save("branch")
-    save("att")
-    for load in loads[4:]:
-        load.wait()
-
-    def mix_two(at):
-        middle = residual[at] + modulation[2:3] * kept["branch"][at]
-        kept["middle"][at] = middle
-        normed, unused = normalize(middle)
-        kept["mixed_two"][at] = (normed * (1.0 + modulation[4:5]) + modulation[3:4]).astype(
-            jnp.bfloat16
-        )
-
-    by_rows(patches, mix_two)
-    save("middle")
-    save("mixed_two")
-    for part in range(FF // D):
-        cols = slice(part * D, part * D + D)
-        pre = (
-            matmul(kept["mixed_two"][...], wh_v[:, cols])
-            + bias[:, D + part * D : 2 * D + part * D]
-        )
-        kept["pre"][:, cols] = pre
-        kept["act"][:, cols] = gelu_tanh(pre).astype(jnp.bfloat16)
-    save("pre")
-    save("act")
-    for part in range(3):
-        cols = slice(part * third, part * third + third)
-        second = (
-            matmul(kept["act"][...], ws_v[:, cols])
-            + bias[:, D + FF + part * third : D + FF + part * third + third]
-        )
-        kept["second"][:, cols] = second
-        output = kept["middle"][:, cols] + modulation[5:6, cols] * second
-        kept["output"][:, cols] = output
-        send[:, cols] = output.astype(jnp.bfloat16)
-    save("second")
-    save("output")
-
-    @pl.when(meta[3] == 1)
-    def finish():
+    loads.append(started(wh, wh_v, w_sem.at[4]))
+    loads.append(started(ws, ws_v, w_sem.at[5]))
+    meet("section", sections, section)
+    hop = hop_of(send, received, send_sem, recv_sem, lax.rem(section + 1, sections))
+    residual = kept[RESIDUAL]
+
+    @pl.loop(0, images)
+    def run(image):
+        saves = []
+
+        def save(name):
+            saves.append(started(kept[name], outs[name].at[image], out_sem.at[name]))
+
+        @pl.when(section == 0)
+        def take_tokens():
+            started(tokens.at[image], residual, x_sem).wait()
+
+        @pl.when(section > 0)
+        def take_received():
+            for part in range(HOPS):
+                hop(image, part).wait_recv()
+            residual[...] = received[image].astype(jnp.float32)
+
+        save(RESIDUAL)
+        modulation = ada[image]
+
+        def mix_one(at):
+            normed, unused = normalize(residual[at])
+            kept[MIXED_ONE][at] = (normed * (1.0 + modulation[1:2]) + modulation[0:1]).astype(
+                jnp.bfloat16
+            )
+
+        by_rows(patches, mix_one)
+        save(MIXED_ONE)
+        wait_first(image, loads[:3])
+        for cols in parts_of(3 * D, 3):
+            kept[QKV][cols] = (
+                contract(wq_v[:, cols], kept[MIXED_ONE][...], 0, 1) + qkv_bias[cols]
+            ).astype(jnp.bfloat16)
+        save(QKV)
+        attend_kernel(kept[QKV], att_down)
+        wait_first(image, loads[3:4])
+        kept[BRANCH][...] = contract(att_down[...], wp_v[...], 0, 0) + bias[:, :D]
+        kept[ATT][...] = att_down[...].T
+        save(BRANCH)
+        save(ATT)
+
+        def mix_two(at):
+            middle = residual[at] + modulation[2:3] * kept[BRANCH][at]
+            kept[MIDDLE][at] = middle
+            normed, unused = normalize(middle)
+            kept[MIXED_TWO][at] = (normed * (1.0 + modulation[4:5]) + modulation[3:4]).astype(
+                jnp.bfloat16
+            )
+
+        by_rows(patches, mix_two)
+        save(MIDDLE)
+        save(MIXED_TWO)
+        wait_first(image, loads[4:5])
+        for part, cols in enumerate(parts_of(FF, FF // D)):
+            pre = (
+                matmul(kept[MIXED_TWO][...], wh_v[:, cols])
+                + bias[:, D + part * D : 2 * D + part * D]
+            )
+            kept[PRE][:, cols] = pre
+            kept[ACT][:, cols] = gelu_tanh(pre).astype(jnp.bfloat16)
+        save(PRE)
+        save(ACT)
+        wait_first(image, loads[5:])
+        for part, cols in enumerate(parts_of(D, HOPS)):
+            second = (
+                matmul(kept[ACT][...], ws_v[:, cols])
+                + bias[:, D + FF + cols.start : D + FF + cols.stop]
+            )
+            kept[SECOND][:, cols] = second
+            output = kept[MIDDLE][:, cols] + modulation[5:6, cols] * second
+            kept[OUTPUT][:, cols] = output
+            send[image, :, cols] = output.astype(jnp.bfloat16)
+
+            @pl.when(section < sections - 1)
+            def pass_on(part=part):
+                hop(image, part).start()
+
+        save(SECOND)
+        save(OUTPUT)
         for copy in saves:
             copy.wait()
 
-
-def backward_kernel(patches, given, meta, arrived, ada, head_grad, wq, wp, wh, ws, *refs):
-    reads, made = (len(READ), len(MADE))
-    sources, refs = (refs[:reads], refs[reads + given :])
-    send, outs, ada_out = (refs[0], refs[1 : made + 1], refs[made + 1])
-    scratch = refs[made + 2 :]
-    kept = {name: scratch[i] for i, name in enumerate(READ)}
-    grads = {name: scratch[reads + i] for i, (name, unused, kind) in enumerate(MADE)}
+    @pl.when(section < sections - 1)
+    def finish():
+        for image in range(images):
+            for part in range(HOPS):
+                hop(image, part).wait_send()
+
+
+def backward_kernel(sections, images, direct, ada, head_grad, wq, wp, wh, ws, *refs):
+    reads, made, patches = (len(READ), len(MADE), head_grad.shape[1])
+    sources, refs = (refs[:reads], refs[reads:])
+    if direct:
+        film, refs = (refs[0], refs[1:])
+    outs, ada_out, refs = (refs[:made], refs[made], refs[made + 1 :])
+    if direct:
+        film_rows, film_out, refs = (refs[0], refs[1], refs[2:])
+    kept = {name: refs[i] for i, name in enumerate(READ)}
+    grads = refs[reads : reads + made - 1]
     (
         flow,
         mixed,
         att_grad,
         qkv_grad,
         sums,
+        send,
+        received,
         wq_v,
         wp_v,
         wh_v,
@@ -721,183 +763,259 @@
         in_sem,
         x_sem,
         out_sem,
-    ) = scratch[reads + made :]
-
-    def fetch(name):
+        send_sem,
+        recv_sem,
+        film_send,
+        film_recv,
+    ) = refs[reads + made - 1 :]
+    section = lax.axis_index("section")
+    here = lax.axis_index("dp")
+
+    def fetching(name, image):
         index = READ.index(name)
-        return started(sources[index].at[meta[0]], kept[name], in_sem.at[index])
-
-    fetched = {"second": fetch("second")}
-    loads = [started(ws.at[pl.ds(i * D, D)], ws_v.at[pl.ds(i * D, D)], w_sem.at[i]) for i in range(FF // D)]
-    for name in ("pre", "middle", "branch", "qkv", "residual"):
-        fetched[name] = fetch(name)
-    third = D // 3
-    loads += [
-        started(wh.at[pl.ds(i * third, third)], wh_v.at[pl.ds(i * third, third)], w_sem.at[4 + i])
-        for i in range(3)
-    ]
-    loads.append(started(wp, wp_v, w_sem.at[7]))
-    loads += [
-        started(wq.at[pl.ds(i * third, third)], wq_v.at[pl.ds(i * third, third)], w_sem.at[8 + i])
-        for i in range(3)
-    ]
-    saves = []
-
-    def start_if_valid(copy):
-        @pl.when(meta[3] == 1)
-        def start():
+        return pltpu.make_async_copy(sources[index].at[image], kept[name], in_sem.at[index])
+
+    fetching(SECOND, 0).start()
+    loads = [started(ws, ws_v, w_sem.at[0])]
+    for name in READ:
+        if name != SECOND:
+            fetching(name, 0).start()
+    loads.append(started(wh, wh_v, w_sem.at[1]))
+    loads.append(started(wp, wp_v, w_sem.at[2]))
+    loads.append(started(wq, wq_v, w_sem.at[3]))
+    spreading, passing = ([], [])
+    if direct:
+        barrier = pltpu.get_barrier_semaphore()
+        for axis, me, size in (("section", section, sections), ("dp", here, DIRECT)):
+            for step in range(1, size):
+                pl.semaphore_signal(
+                    barrier, inc=1, device_id={axis: lax.rem(me + step, size)}, device_id_type=MESH
+                )
+        pl.semaphore_wait(barrier, sections + DIRECT - 2)
+        for step in range(1, DIRECT):
+            copy = pltpu.make_async_remote_copy(
+                src_ref=film,
+                dst_ref=film_rows.at[here],
+                send_sem=film_send.at[step - 1],
+                recv_sem=film_recv.at[step - 1],
+                device_id={"dp": lax.rem(here + step, DIRECT)},
+                device_id_type=MESH,
+            )
             copy.start()
-
-    def save(name):
-        index = [item[0] for item in MADE].index(name)
-        saves.append(pltpu.make_async_copy(grads[name], outs[index].at[meta[0]], out_sem.at[index]))
-        start_if_valid(saves[-1])
-
-    @pl.when(meta[2] == 1)
-    def take_head():
-        started(head_grad.at[meta[1]], flow, x_sem).wait()
-
-    @pl.when(meta[2] == 0)
-    def take_arrived():
-        flow[...] = arrived[...].astype(jnp.float32)
-
-    modulation = ada[meta[0]]
-    sums[...] = jnp.zeros_like(sums)
-
-    def add_sum(row, values):
-        sums[row : row + 1] += jnp.sum(values, axis=0, keepdims=True)
-
-    fetched["second"].wait()
-
-    def open_second(at):
-        grad = flow[at]
-        grads["d_second"][at] = (grad * modulation[5:6]).astype(jnp.bfloat16)
-        add_sum(5, grad * kept["second"][at])
-
-    by_rows(patches, open_second)
-    save("d_second")
-    fetched["pre"].wait()
-    for load in loads[:4]:
-        load.wait()
-    for part in range(FF // D):
-        cols = slice(part * D, part * D + D)
-        grads["d_pre"][:, cols] = (
-            matmul_nt(grads["d_second"][...], ws_v[cols]) * gelu_grad(kept["pre"][:, cols])
-        ).astype(jnp.bfloat16)
-    save("d_pre")
-    for load in loads[4:7]:
-        load.wait()
-    for part in range(3):
-        cols = slice(part * third, part * third + third)
-        mixed[:, cols] = matmul_nt(grads["d_pre"][...], wh_v[cols])
-    fetched["middle"].wait()
-    fetched["branch"].wait()
-
-    def through_two(at):
-        normed, invstd = normalize(kept["middle"][at])
-        grad = mixed[at]
-        add_sum(3, grad)
-        add_sum(4, grad * normed)
-        total = flow[at] + norm_back(grad * (1.0 + modulation[4:5]), normed, invstd)
-        flow[at] = total
-        add_sum(2, total * kept["branch"][at])
-        grads["d_branch"][at] = (total * modulation[2:3]).astype(jnp.bfloat16)
-
-    by_rows(patches, through_two)
-    save("d_branch")
-    loads[7].wait()
-    att_grad[...] = contract(wp_v[...], grads["d_branch"][...], 1, 1).astype(jnp.bfloat16)
-    fetched["qkv"].wait()
-    attend_back_kernel(kept["qkv"], att_grad, qkv_grad)
-    for load in loads[8:]:
-        load.wait()
-    for part in range(3):
-        cols = slice(part * third, part * third + third)
-        mixed[:, cols] = contract(qkv_grad[...], wq_v[cols], 0, 1)
-    grads["d_qkv"][...] = qkv_grad[...].T
-    save("d_qkv")
-    fetched["residual"].wait()
-
-    def through_one(at):
-        normed, invstd = normalize(kept["residual"][at])
-        grad = mixed[at]
-        add_sum(0, grad)
-        add_sum(1, grad * normed)
-        total = flow[at] + norm_back(grad * (1.0 + modulation[1:2]), normed, invstd)
-        low = total.astype(jnp.bfloat16)
-        grads["d_residual"][at] = low
-        send[at] = low
-
-    by_rows(patches, through_one)
-    save("d_residual")
-    saves.append(pltpu.make_async_copy(sums, ada_out.at[meta[0]], x_sem))
-    start_if_valid(saves[-1])
-
-    @pl.when(meta[3] == 1)
-    def finish():
+            spreading.append(copy)
+        film_rows[here] = film[...]
+        for step in range(1, sections):
+            passing.append(
+                pltpu.make_async_remote_copy(
+                    src_ref=film_rows,
+                    dst_ref=film_out,
+                    send_sem=film_send.at[DIRECT - 2 + step],
+                    recv_sem=film_recv.at[DIRECT - 2 + step],
+                    device_id={"section": lax.rem(section + step, sections)},
+                    device_id_type=MESH,
+                )
+            )
+    else:
+        meet("section", sections, section)
+    hop = hop_of(send, received, send_sem, recv_sem, lax.rem(section + sections - 1, sections))
+
+    @pl.loop(0, images)
+    def run(image):
+        saves = []
+
+        def save(name, value=None):
+            source = grads[name] if value is None else value
+            saves.append(started(source, outs[name].at[image], out_sem.at[name]))
+
+        def fetch_next(*names):
+            @pl.when(image + 1 < images)
+            def start():
+                for name in names:
+                    fetching(name, image + 1).start()
+
+        @pl.when(section == sections - 1)
+        def take_head():
+            started(head_grad.at[image], flow, x_sem).wait()
+
+        @pl.when(section < sections - 1)
+        def take_received():
+            for part in range(HOPS):
+                hop(image, part).wait_recv()
+            flow[...] = received[image].astype(jnp.float32)
+
+        modulation = ada[image]
+        sums[...] = jnp.zeros_like(sums)
+
+        def add_sum(row, values):
+            sums[row : row + 1] += jnp.sum(values, axis=0, keepdims=True)
+
+        fetching(SECOND, image).wait()
+
+        def open_second(at):
+            grad = flow[at]
+            grads[D_SECOND][at] = (grad * modulation[5:6]).astype(jnp.bfloat16)
+            add_sum(5, grad * kept[SECOND][at])
+
+        by_rows(patches, open_second)
+        fetch_next(SECOND)
+        save(D_SECOND)
+        fetching(PRE, image).wait()
+        wait_first(image, loads[:1])
+        for cols in parts_of(FF, FF // D):
+            grads[D_PRE][:, cols] = (
+                matmul_nt(grads[D_SECOND][...], ws_v[cols]) * gelu_grad(kept[PRE][:, cols])
+            ).astype(jnp.bfloat16)
+        fetch_next(PRE)
+        save(D_PRE)
+        wait_first(image, loads[1:2])
+        for cols in parts_of(D, 3):
+            mixed[:, cols] = matmul_nt(grads[D_PRE][...], wh_v[cols])
+        fetching(MIDDLE, image).wait()
+        fetching(BRANCH, image).wait()
+
+        def through_two(at):
+            normed, invstd = normalize(kept[MIDDLE][at])
+            grad = mixed[at]
+            add_sum(3, grad)
+            add_sum(4, grad * normed)
+            total = flow[at] + norm_back(grad * (1.0 + modulation[4:5]), normed, invstd)
+            flow[at] = total
+            add_sum(2, total * kept[BRANCH][at])
+            grads[D_BRANCH][at] = (total * modulation[2:3]).astype(jnp.bfloat16)
+
+        by_rows(patches, through_two)
+        fetch_next(MIDDLE, BRANCH)
+        save(D_BRANCH)
+        wait_first(image, loads[2:3])
+        att_grad[...] = contract(wp_v[...], grads[D_BRANCH][...], 1, 1).astype(jnp.bfloat16)
+        fetching(QKV, image).wait()
+        attend_back_kernel(kept[QKV], att_grad, qkv_grad)
+        fetch_next(QKV)
+        wait_first(image, loads[3:])
+        for cols in parts_of(D, 3):
+            mixed[:, cols] = contract(qkv_grad[...], wq_v[cols], 0, 1)
+        fetching(RESIDUAL, image).wait()
+
+        def through_one(at):
+            normed, invstd = normalize(kept[RESIDUAL][at])
+            grad = mixed[at]
+            add_sum(0, grad)
+            add_sum(1, grad * normed)
+            total = flow[at] + norm_back(grad * (1.0 + modulation[1:2]), normed, invstd)
+            send[image, at] = total.astype(jnp.bfloat16)
+
+        by_rows(patches, through_one)
+
+        @pl.when(section > 0)
+        def pass_on():
+            for part in range(HOPS):
+                hop(image, part).start()
+
+        fetch_next(RESIDUAL)
+        save(D_RESIDUAL, send.at[image])
+        grads[D_QKV][...] = qkv_grad[...].T
+        save(D_QKV)
+        saves.append(started(sums, ada_out.at[image], x_sem))
+        if direct:
+
+            @pl.when(image == 0)
+            def pass_film():
+                for copy in spreading:
+                    copy.wait()
+
+                @pl.when(section == sections - 1)
+                def send_film():
+                    for copy in passing:
+                        copy.start()
+
         for copy in saves:
             copy.wait()
 
+    @pl.when(section > 0)
+    def finish():
+        for image in range(images):
+            for part in range(HOPS):
+                hop(image, part).wait_send()
+
+    if direct:
+
+        @pl.when(section == sections - 1)
+        def own_film():
+            film_out[...] = film_rows[...]
+            for copy in passing:
+                copy.wait_send()
+
+        for step in range(1, sections):
+
+            @pl.when(section == step - 1)
+            def wait_film(step=step):
+                passing[step - 1].wait_recv()
+
 
 def specs(*spaces):
     return [
-        pl.BlockSpec(memory_space={"s": pltpu.SMEM, "v": pltpu.VMEM, "h": pl.ANY}[space])
+        pl.BlockSpec(memory_space={"v": pltpu.VMEM, "h": pl.ANY}[space])
         for space in "".join(spaces)
     ]
 
 
 def weight_scratch():
     return [pltpu.VMEM(shape, jnp.bfloat16) for shape in WEIGHTS] + [
-        pltpu.SemaphoreType.DMA((11,))
+        pltpu.SemaphoreType.DMA((6,))
     ]
 
 
-def block_cost(patches, factor):
+def block_cost(images, patches, factor):
     area = sum(rows * columns for rows, columns in WEIGHTS)
     return pl.CostEstimate(
-        flops=2 * patches * area + factor * patches * patches * D,
-        bytes_accessed=2 * area + 64 * patches * D,
-        transcendentals=patches * (FF + HEADS * patches),
-    )
-
-
-def image_forward(meta, arrived, bias, qkv_bias, ada, tokens, weights, buffers):
-    patches, given, count = (arrived.shape[0], len(buffers), len(KEPT))
-    sizes = [item + (patches,) for item in KEPT]
-    images = ada.shape[0]
+        flops=images * (2 * patches * area + factor * patches * patches * D),
+        bytes_accessed=2 * area + images * 64 * patches * D,
+        transcendentals=images * patches * (FF + HEADS * patches),
+    )
+
+
+def pipeline_forward(bias, qkv_bias, ada, tokens, weights):
+    images, patches, unused = tokens.shape
+    sections = lax.axis_size("section")
+    sizes = [(kept_shape(i, item[0], patches), item[1]) for i, item in enumerate(KEPT)]
+    return pl.pallas_call(
+        functools.partial(forward_kernel, sections, images),
+        out_shape=[
+            jax.ShapeDtypeStruct((images,) + shape, kind) for shape, kind in sizes
+        ],
+        in_specs=specs("vvv", "h" * 5),
+        out_specs=specs("h" * len(KEPT)),
+        scratch_shapes=[pltpu.VMEM(shape, kind) for shape, kind in sizes]
+        + [pltpu.VMEM((D, patches), jnp.bfloat16)]
+        + [pltpu.VMEM((images, patches, D), jnp.bfloat16)] * 2
+        + weight_scratch()
+        + [pltpu.SemaphoreType.DMA, pltpu.SemaphoreType.DMA((len(KEPT),))]
+        + [pltpu.SemaphoreType.DMA((images, HOPS))] * 2,
+        compiler_params=pltpu.CompilerParams(
+            vmem_limit_bytes=62 << 20, collective_id=16, has_side_effects=True
+        ),
+        cost_estimate=block_cost(images, patches, 4),
+        name="pipeline_forward",
+    )(bias, qkv_bias, ada, tokens, *weights)
+
+
+def pipeline_backward(ada, head_grad, weights, sources, film):
+    images, patches, unused = head_grad.shape
+    sections, direct = (lax.axis_size("section"), lax.axis_size("dp") == DIRECT)
+    films = [jax.ShapeDtypeStruct((DIRECT,) + film.shape, film.dtype)] * (2 * direct)
     outs = pl.pallas_call(
-        functools.partial(forward_kernel, patches, given),
-        out_shape=[jax.ShapeDtypeStruct((patches, D), jnp.bfloat16)]
-        + [jax.ShapeDtypeStruct((images,) + kept_shape(*item), item[2]) for item in sizes],
-        in_specs=specs("svvvv", "h" * (5 + given)),
-        out_specs=specs("v", "h" * count),
-        scratch_shapes=[pltpu.VMEM(kept_shape(*item), item[2]) for item in sizes]
-        + [pltpu.VMEM((D, patches), jnp.bfloat16)]
-        + weight_scratch()
-        + [pltpu.SemaphoreType.DMA, pltpu.SemaphoreType.DMA((count,))],
-        input_output_aliases={10 + i: 1 + i for i in range(given)},
-        compiler_params=pltpu.CompilerParams(vmem_limit_bytes=60 << 20),
-        cost_estimate=block_cost(patches, 4),
-        name="image_forward",
-    )(meta, arrived, bias, qkv_bias, ada, tokens, *weights, *buffers)
-    return (outs[0], outs[1:])
-
-
-def image_backward(meta, arrived, ada, head_grad, weights, sources, buffers):
-    patches, given, images = (arrived.shape[0], len(buffers), ada.shape[0])
-    reads, made = (len(READ), len(MADE))
-    kinds = {name: (width, kind) for name, width, kind in KEPT}
-    outs = pl.pallas_call(
-        functools.partial(backward_kernel, patches, given),
-        out_shape=[jax.ShapeDtypeStruct((patches, D), jnp.bfloat16)]
-        + [jax.ShapeDtypeStruct((images, patches, width), kind) for unused, width, kind in MADE]
-        + [jax.ShapeDtypeStruct((images, 8, D), jnp.float32)],
-        in_specs=specs("svv", "h" * (5 + reads + given)),
-        out_specs=specs("v", "h" * (made + 1)),
+        functools.partial(backward_kernel, sections, images, direct),
+        out_shape=[
+            jax.ShapeDtypeStruct((images, patches, width), kind) for width, kind in MADE
+        ]
+        + [jax.ShapeDtypeStruct((images, 8, D), jnp.float32)]
+        + films,
+        in_specs=specs("v", "h" * (5 + len(READ)), "v" * direct),
+        out_specs=specs("h" * (len(MADE) + 1), "v" * len(films)),
         scratch_shapes=[
-            pltpu.VMEM(kept_shape(name, *kinds[name], patches), kinds[name][1]) for name in READ
+            pltpu.VMEM(kept_shape(name, KEPT[name][0], patches), KEPT[name][1]) for name in READ
         ]
-        + [pltpu.VMEM((patches, width), kind) for unused, width, kind in MADE]
+        + [pltpu.VMEM((patches, width), kind) for width, kind in MADE[:-1]]
         + [
             pltpu.VMEM((patches, D), jnp.float32),
             pltpu.VMEM((patches, D), jnp.float32),
@@ -905,18 +1023,27 @@
             pltpu.VMEM((3 * D, patches), jnp.bfloat16),
             pltpu.VMEM((8, D), jnp.float32),
         ]
+        + [pltpu.VMEM((images, patches, D), jnp.bfloat16)] * 2
         + weight_scratch()
         + [
-            pltpu.SemaphoreType.DMA((reads,)),
+            pltpu.SemaphoreType.DMA((len(READ),)),
             pltpu.SemaphoreType.DMA,
-            pltpu.SemaphoreType.DMA((made,)),
-        ],
-        input_output_aliases={8 + reads + i: 1 + i for i in range(given)},
-        compiler_params=pltpu.CompilerParams(vmem_limit_bytes=60 << 20),
-        cost_estimate=block_cost(patches, 10),
-        name="image_backward",
-    )(meta, arrived, ada, head_grad, *weights, *sources, *buffers)
-    return (outs[0], outs[1:])
+            pltpu.SemaphoreType.DMA((len(MADE),)),
+        ]
+        + [pltpu.SemaphoreType.DMA((images, HOPS))] * 2
+        + [pltpu.SemaphoreType.DMA((DIRECT + sections,))] * 2,
+        compiler_params=pltpu.CompilerParams(
+            vmem_limit_bytes=62 << 20, collective_id=17, has_side_effects=True
+        ),
+        cost_estimate=block_cost(images, patches, 10),
+        name="pipeline_backward",
+    )(ada, head_grad, *weights, *sources, *([film] * direct))
+    if direct:
+        film_all = outs[-1].reshape(-1, film.shape[1])
+    else:
+        film_all = lax.all_gather(film, ("section", "dp"), tiled=True)
+        film_all = film_all[-images * lax.axis_size("dp") :]
+    return (outs[: len(MADE) + 1], film_all)
 
 
 def head_step(residual, film, noise_part, mask_part, inv_count, w_out, b_out):
@@ -1074,25 +1201,10 @@
     )
     tokens = tokens + small_used[:D] + positions(patches)[None]
 
-    def meta_of(raw, edge, tick):
-        inside = (raw >= 0) & (raw < images)
-        items = [jnp.clip(raw, 0, images - 1), min(tick, images - 1), edge, inside]
-        return jnp.stack([jnp.asarray(item, jnp.int32) for item in items])
-
-    ticks = images + sections - 1
-    kept_all = []
-    arrived = jnp.zeros((patches, D), low)
-    for tick in range(ticks):
-        meta = meta_of(tick - section_index, is_first, tick)
-        output, kept_all = image_forward(
-            meta, arrived, bias_row, qkv_bias, ada, tokens, weights, kept_all
-        )
-        if tick < ticks - 1:
-            arrived = passed_along(output, "section", 1)
-    kept_of = {item[0]: whole for item, whole in zip(KEPT, kept_all)}
+    kept_all = pipeline_forward(bias_row, qkv_bias, ada, tokens, weights)
 
     squared, head_grad, d_film, g_output, g_out_bias = head_step(
-        kept_of["output"],
+        kept_all[OUTPUT],
         film,
         noise,
         patch_mask,
@@ -1101,23 +1213,9 @@
         small_used[5 * D :],
     )
     loss_part = jnp.where(is_last, squared * inv_count, 0.0)
-    made_all = []
-    arrived = jnp.zeros((patches, D), low)
-    for tick in range(ticks):
-        meta = meta_of(tick - (sections - 1 - section_index), is_last, tick)
-        d_low, made_all = image_backward(
-            meta, arrived, ada, head_grad, weights, [kept_of[name] for name in READ], made_all
-        )
-        if tick < ticks - 1:
-            arrived = passed_along(d_low, "section", -1)
-        if tick == 1:
-            film_all = lax.optimization_barrier((d_film, d_low))[0]
-            film_all = spread(film_all, "dp", 6).reshape(shards * images, 2 * D)
-        elif tick == 2:
-            film_all = lax.optimization_barrier((film_all, d_low))[0]
-            film_all = spread(film_all, "section", 7)[sections - 1]
-        if tick in (1, 2):
-            arrived, film_all = lax.optimization_barrier((arrived, film_all))
+    made_all, film_all = pipeline_backward(
+        ada, head_grad, weights, [kept_all[name] for name in READ], d_film
+    )
 
     def flat(whole):
         return whole.reshape(images * patches, whole.shape[2])
@@ -1132,7 +1230,7 @@
         g_output,
     )
     shard_wide, shard_down, right_sums, late, (token_sums, g_edge), d_ada_all = row_sums(
-        [flat(kept_of[name]) for name in ("mixed_one", "att", "mixed_two", "act")],
+        [flat(kept_all[name]) for name in (MIXED_ONE, ATT, MIXED_TWO, ACT)],
         [d_qkv, d_branch, d_pre, d_second],
         (token_sums, g_edge),
         d_ada,

time: 1540 us -> 1280 us (0.83)
  waiting for transfers between devices: 476 us -> 233 us
  starting transfers between devices: 24.9 us -> 9.36 us
    ppermute x12 -> x0, waiting for transfers between devices: 126 us -> none  [passed_along(): lax.ppermute(value, axis, [(source, source + steps) for source in range(f...]
    ppermute x6, waiting for transfers between devices: 139 us -> 25.7 us  [row_sums(): lax.ppermute(blocks[step - 1], 'dp', [(i, (i + 2 * step) % count) for i i...]
    pallas_call x12 -> x10, Pallas kernels: 298 us -> 371 us  [share(): pl.pallas_call(functools.partial(share_kernel, axis, count, personal), ou...]
    pallas_call x14 -> x2, Pallas kernels: 444 us -> 380 us  [the longest x1 284 us: pipeline_backward(): pl.pallas_call(functools.partial(backward_kernel, sections, images, direc...]
    ppermute x12 -> x0, starting transfers between devices: 15.7 us -> none  [passed_along(): lax.ppermute(value, axis, [(source, source + steps) for source in range(f...]
  transfers between devices with their start and end apart: 22 -> 10, of which waited for: 15 -> 4; matrix products, arithmetic and copies ran while one was open for 5% -> 6% of each run, Pallas kernels for 21% -> 32%
where the time goes in v5:
time: 1280 us; the launch traced here: 1270 us
  Pallas kernels  825 us (64%)
  waiting for transfers between devices  233 us (18%)
  other arithmetic  88.1 us (7%)
  local copies, waits for them, and re-layouts  64.6 us (5%)
  matrix products  32 us (2%)
  between operations  22.1 us (2%)
    pallas_call x10, Pallas kernels, share(): pl.pallas_call(functools.partial(share_kernel, axis, count, personal), ou...  371 us
    pallas_call x1, Pallas kernels, pipeline_backward(): pl.pallas_call(functools.partial(backward_kernel, sections, images, direc...  284 us
    all_gather x4, waiting for transfers between devices, gathered(): return lax.all_gather(value, axis, axis=dim, tiled=True)  208 us
    pallas_call x1, Pallas kernels, pipeline_forward(): pl.pallas_call(functools.partial(forward_kernel, sections, images), out_s...  95.5 us
    pallas_call x2, Pallas kernels, chip_products(): pl.pallas_call(functools.partial(products_kernel, units, rows, len(given)...  74.2 us
    sub x5, other arithmetic, adam_update(): return (weight - RATE * (ratio + DECAY * weight), first_new, second_new)  34.8 us
    ppermute x6, waiting for transfers between devices, row_sums(): lax.ppermute(blocks[step - 1], 'dp', [(i, (i + 2 * step) % count) for i i...  25.7 us
  transfers between devices with their start and end apart: 10, of which 4 were waited for; matrix products, arithmetic and copies ran while one was open for 6% of the time, Pallas kernels for 32%

profile of v5, /device:TPU:0, one launch (start us, length us, event | category | flops | bytes accessed | tf_op | source)
XLA Modules:
  0.0 1274.7 jit_solution(8234211871288917362)
XLA Ops:
  7.2 4.1 convert_bitcast_fusion
  11.4 2.2 copy-done.2
  14.3 2.3 slice.286
  16.7 2.5 slice.288
  21.6 23.8 %share.11 = bf16[4,146,1186]{2,1,0:T(8,128)(2,1)} custom-call(bf16[146,1186]{1,0:T(8,128)(2,1)} %pad_maximum_fusion.4.in_ref), custom_call_target="tpu_custom_call" | custom-call | tf_op jit(solution)/shard_map/share/pallas_call | solution.py:160
  49.3 8.5 share.10
  59.3 1.6 slice_bitcast_fusion.11
  62.4 11.9 share.12
  75.5 1.4 fusion.52.in_ref
  76.9 12.3 share.13
  90.4 2.0 fusion.8
  93.6 46.3 %share.14 = f32[8,288,128]{2,1,0:T(8,128)} custom-call(f32[8,288,128]{2,1,0:T(8,128)} %reshape.317.in_ref), custom_call_target="tpu_custom_call" | custom-call | tf_op jit(solution)/shard_map/share/pallas_call | solution.py:160
  140.0 1.4 reduce_sum.257
  142.6 1.7 broadcast_in_dim.30.qkv_bias
  146.4 3.8 multiply_cosine_fusion
  150.2 1.6 concatenate.80
  152.0 3.0 fusion.2.tokens
  155.0 5.5 all-gather.6.cloned.1.call-done.wq
  160.6 101.2 %all-gather.10.cloned.1.call-done.wh = bf16[1152,4608]{1,0:T(8,128)(2,1)} async-done(((bf16[144,4608]{1,0:T(8,128)(2,1)}), bf16[1152,4608]{1,0:T(8,128)(2,1)}) %all-gather.10.cloned.1.call-update) | async-done | bytes 10616848 | tf_op jit(solution)/shard_map/all_gather | solution.py:1120
  261.8 101.0 %all-gather.12.cloned.1.call-done = bf16[1,4608,1152]{2,1,0:T(8,128)(2,1)} async-done(((bf16[1,576,1152]{2,1,0:T(8,128)(2,1)}), bf16[1,4608,1152]{2,1,0:T(8,128)(2,1)}) %all-gather.12.cloned.1.call-update) | async-done | bytes 10616848 | tf_op jit(solution)/shard_map/all_gather | solution.py:1120
  362.7 95.5 %pipeline_forward.1 = (f32[4,256,1152]{2,1,0:T(8,128)}, bf16[4,256,1152]{2,1,0:T(8,128)(2,1)}, bf16[4,3456,256]{2,1,0:T(8,128)(2,1)}, bf16[4,256,1152]{2,1,0:T(8...) custom-call(f32[1,6912]{1,0:T(1,128)} %broadcast_in_dim.22.bias, ...), custom_call_target="tpu_custom_call" | custom-call | flops 33822867456 | bytes 107347968 | tf_op jit(solution)/shard_map/pipeline_forward/pallas_call | solution.py:981
  458.3 2.6 reduce_sum.258
  460.9 3.1 multiply_reduce_fusion.2
  464.7 1.8 convert_reduce_fusion.4
  466.5 2.9 multiply_reduce_fusion
  470.0 2.9 subtract_multiply_fusion.head_grad
  472.9 284.3 %pipeline_backward.1 = (bf16[4,256,1152]{2,1,0:T(8,128)(2,1)}, bf16[4,256,4608]{2,1,0:T(8,128)(2,1)}, bf16[4,256,1152]{2,1,0:T(8,128)(2,1)}, bf16[4,256,3456]{2,...) custom-call(f32[4,6,1152]{2,1,0:T(8,128)} %reshape.319.ada, ...), custom_call_target="tpu_custom_call" | custom-call | flops 35634806784 | bytes 107347968 | tf_op jit(solution)/shard_map/pipeline_backward/pallas_call | solution.py:1006
  757.2 2.1 convolution_bitcast_fusion.1
  759.3 2.1 convert_reduce_fusion
  761.4 3.2 fusion.5
  765.3 29.0 %chip_products.2 = (f32[4,144,1152]{2,1,0:T(8,128)}, bf16[4,144,1152]{2,1,0:T(8,128)(2,1)}, bf16[4,144,1152]{2,1,0:T(8,128)(2,1)}, bf16[4,144,1152]{2,1,0:T(8,12...) custom-call(bf16[1024,1152]{1,0:T(8,128)(2,1)} %bitcast.152, bf16[1024,1152]{1,0:T(8,128)(2,1)} %bitcast.154, ...), custom_call_target="tpu_custom_call" | custom-call | flops 10871635968 | bytes 18874368 | tf_op jit(solution)/shard_map/chip_products/pallas_call | solution.py:416
  795.6 2.4 collective-permute-start.1
  797.9 1.4 collective-permute-start.2
  799.4 45.3 %chip_products.3 = (f32[8,144,1152]{2,1,0:T(8,128)}, bf16[8,144,1152]{2,1,0:T(8,128)(2,1)}, bf16[8,144,1152]{2,1,0:T(8,128)(2,1)}, bf16[8,144,1152]{2,1,0:T(8,128)(2,1)}, f32[8,8,1152]{2,1,0:T(8,128)}) custom-call(bf16[1024,1152]{1,0:T(8,128)(2,1)} %bitcast.153, bf16[1024,1152]{1,0:T(8,128)(2,1)} %bitcast.155, bf16[1024,1152]{1,0:T(8,128)(2,1)} %bitcast.157, ...), custom_call_target="tpu_custom_call" | custom-call | flops 21743271936 | bytes 37748736 | tf_op jit(solution)/shard_map/chip_products/pallas_call | solution.py:416
  854.0 1.3 constant_dynamic-update-slice_fusion.2
  857.5 2.3 collective-permute-start.5
  859.8 25.7 %collective-permute-done.1 = bf16[4,144,1152]{2,1,0:T(8,128)(2,1)} collective-permute-done((bf16[4,144,1152]{2,1,0:T(8,128)(2,1)}, bf16[4,144,1152]{2,1,0:T(8,128)(2,1)}, u32[]{:S(2)}, u32[]{:S(2)}) %collective-permute-start.1) | collective-permute-done | bytes 1327136 | tf_op jit(solution)/shard_map/ppermute | solution.py:477
  885.5 3.4 convert_add_fusion.1
  888.9 1.9 reshape.333
  890.8 3.0 fusion.19.in_ref
  893.8 6.3 share.15
  900.1 2.1 fusion.22.in_ref
  902.2 240.9 %share.16 = bf16[8,32,144]{2,1,0:T(8,128)(2,1)} custom-call(bf16[32,144]{1,0:T(8,128)(2,1)} %fusion.22.in_ref), custom_call_target="tpu_custom_call" | custom-call | tf_op jit(solution)/shard_map/share/pallas_call | solution.py:160
  1143.1 1.6 copy.47
  1144.8 1.7 reshape.334
  1148.0 1.6 reshape.330
  1149.5 1.8 convert_reduce_fusion.5
  1153.9 7.6 share.17
  1166.1 5.9 convert_add_fusion
  1178.6 1.4 fusion.73
  1181.9 1.6 fusion.56
  1183.4 1.8 fusion.40
  1185.3 3.7 fusion.76
  1190.9 1.3 constant_dynamic-update-slice_fusion.1
  1194.9 1.3 constant_dynamic-update-slice_fusion.3
  1197.4 1.4 multiply_reduce_fusion.6
  1199.5 3.5 concatenate.86
  1203.9 6.8 fusion.1
  1213.9 7.6 share.18
  1222.8 5.8 share.19
  1231.9 1.6 multiply_subtract_fusion.3
  1233.5 3.5 multiply_subtract_fusion.2
  1237.0 8.2 multiply_subtract_fusion.1
  1245.9 20.9 %multiply_subtract_fusion = (f32[1,144,16128]{2,1,0:T(8,128)}, f32[1,144,16128]{2,1,0:T(8,128)}, f32[1,144,16128]{2,1,0:T(8,128)}) fusion(f32[1,144,16128]{2,1,0:T(8,128)S(1)} %bitcast.126, f32[]{:T(128)S(6)} %min.3, f32[1,144,6912]{2,1,0:T(8,128)} %bitcast.127, f32[1,144,9216]{2,1,0:T(8,128)} %bitcast.41, f32[1,144,16128]{2,1,0:T(8,128)} %param.30, ...), kind=kLoop, calls=%fused_computation.5 | loop fusion | flops 39481344 | bytes 65028100 | tf_op jit(solution)/shard_map/sub | solution.py:1079
  (211 shorter events, 58.4 us)
Async XLA Ops:
  7.2 147.9 %all-gather.8.cloned.1.call-start = ((), (), s32[]{:S(2)}) async-start(), calls=%async_computation.1 | async-start | bytes 2985984 | tf_op jit(solution)/shard_map/all_gather | solution.py:1120
  11.3 2.2 copy-start.2
  13.5 5.9 copy-start.3
  14.3 146.3 %all-gather.6.cloned.1.call-start = ((), (), s32[]{:S(2)}) async-start(), calls=%async_computation | async-start | bytes 8957952 | tf_op jit(solution)/shard_map/all_gather | solution.py:1120
  16.7 4.0 copy-start.4
  16.7 4.0 copy-start.20
  16.7 245.1 %all-gather.10.cloned.1.call-start = ((), (), s32[]{:S(2)}) async-start(), calls=%async_computation.2 | async-start | bytes 11943936 | tf_op jit(solution)/shard_map/all_gather | solution.py:1120
  19.3 28.0 %copy-start.25 = (s32[4,256]{1,0:T(4,128)S(1)}, s32[4,256]{1,0:T(4,128)}, u32[]{:S(2)}) copy-start(s32[4,256]{1,0:T(4,128)} %param.24) | copy-start | bytes 12292
  19.3 29.3 %copy-start.32 = (s32[4]{0:T(128)S(1)}, s32[4]{0:T(128)}, u32[]{:S(2)}) copy-start(s32[4]{0:T(128)} %param.22) | copy-start | bytes 52
  19.3 29.3 %copy-start.31 = (s32[4]{0:T(128)S(1)}, s32[4]{0:T(128)}, u32[]{:S(2)}) copy-start(s32[4]{0:T(128)} %param.23) | copy-start | bytes 52
  19.3 29.3 %copy-start.23 = (f32[1,2016]{1,0:T(1,128)S(1)}, f32[1,2016]{1,0:T(1,128)}, u32[]{:S(2)}) copy-start(f32[1,2016]{1,0:T(1,128)} %param.27) | copy-start | bytes 24196
  19.3 343.4 %all-gather.12.cloned.1.call-start = ((), (), s32[]{:S(2)}) async-start(), calls=%async_computation.3 | async-start | bytes 11943936 | tf_op jit(solution)/shard_map/all_gather | solution.py:1120
  59.1 16.2 %copy-start.29 = (s32[32]{0:T(128)}, s32[32]{0:T(128)S(1)}, u32[]{:S(2)}) copy-start(s32[32]{0:T(128)S(1)} %convert_element_type.164) | copy-start | bytes 388
  59.2 33.1 %copy-start.16 = (bf16[32,128]{1,0:T(8,128)(2,1)}, bf16[32,128]{1,0:T(8,128)(2,1)S(1)}, u32[]{:S(2)}) copy-start(bf16[32,128]{1,0:T(8,128)(2,1)S(1)} %get-tuple-element.165) | copy-start | bytes 24580
  60.8 31.6 %copy-start.13 = (bf16[144,1186]{1,0:T(8,128)(2,1)}, bf16[144,1186]{1,0:T(8,128)(2,1)S(1)}, u32[]{:S(2)}) copy-start(bf16[144,1186]{1,0:T(8,128)(2,1)S(1)} %get-tuple-element.140) | copy-start | bytes 1024708
  61.3 29.0 %copy-start.11 = (f32[32,144]{1,0:T(8,128)}, f32[32,144]{1,0:T(8,128)S(1)}, u32[]{:S(2)}) copy-start(f32[32,144]{1,0:T(8,128)S(1)} %convolution_add_fusion.2) | copy-start | bytes 55300
  90.0 50.0 %copy-start.9 = (f32[32,144]{1,0:T(8,128)}, f32[32,144]{1,0:T(8,128)S(1)}, u32[]{:S(2)}) copy-start(f32[32,144]{1,0:T(8,128)S(1)} %reshape.316) | copy-start | bytes 55300
  140.0 11.8 copy-start.33
  140.0 11.8 copy-start.26
  140.0 11.9 copy-start.14
  140.0 11.9 copy-start.18
  458.2 5.8 copy-start.30
  460.9 3.8 copy-start
  757.2 7.4 copy-start.19
  794.3 63.2 %collective-permute-start = (bf16[4,144,1152]{2,1,0:T(8,128)(2,1)}, bf16[4,144,1152]{2,1,0:T(8,128)(2,1)S(1)}, u32[]{:S(2)}, u32[]{:S(2)}) collective-permute-start(bf16[4,144,1152]{2,1,0:T(8,128)(2,1)} %get-tuple-element.83), channel_id=1, source_target_pairs={{0,2},{1,3},{2,4},{3,5},{4,6},{5,7},{6,0},{7,1},{8,10},{9,11},{10,... | collective-permute-start | bytes 3981320 | tf_op jit(solution)/shard_map/ppermute | solution.py:477
  795.6 89.9 %collective-permute-start.1 = (bf16[4,144,1152]{2,1,0:T(8,128)(2,1)}, bf16[4,144,1152]{2,1,0:T(8,128)(2,1)}, u32[]{:S(2)}, u32[]{:S(2)}) collective-permute-start(bf16[4,144,1152]{2,1,0:T(8,128)(2,1)} %get-tuple-element.84), channel_id=1, source_target_pairs={{0,4},{1,5},{2,6},{3,7},{4,0},{5,1},{6,2},{7,3},{8,12},{9,13},{10,... | collective-permute-start | bytes 3981320 | tf_op jit(solution)/shard_map/ppermute | solution.py:477
  797.9 48.5 %copy-start.15 = (bf16[8,4,2304]{2,1,0:T(4,128)(2,1)S(1)}, bf16[8,4,2304]{2,1,0:T(4,128)(2,1)}, u32[]{:S(2)}) copy-start(bf16[8,4,2304]{2,1,0:T(4,128)(2,1)} %get-tuple-element.104) | copy-start | bytes 442372
  797.9 87.5 %collective-permute-start.2 = (bf16[4,144,1152]{2,1,0:T(8,128)(2,1)}, bf16[4,144,1152]{2,1,0:T(8,128)(2,1)}, u32[]{:S(2)}, u32[]{:S(2)}) collective-permute-start(bf16[4,144,1152]{2,1,0:T(8,128)(2,1)} %get-tuple-element.85), channel_id=1, source_target_pairs={{0,6},{1,7},{2,0},{3,1},{4,2},{5,3},{6,4},{7,5},{8,14},{9,15},{10,... | collective-permute-start | bytes 3981320 | tf_op jit(solution)/shard_map/ppermute | solution.py:477
  844.7 321.4 %collective-permute-start.3 = (bf16[8,144,1152]{2,1,0:T(8,128)(2,1)}, bf16[8,144,1152]{2,1,0:T(8,128)(2,1)}, u32[]{:S(2)}, u32[]{:S(2)}) collective-permute-start(bf16[8,144,1152]{2,1,0:T(8,128)(2,1)} %get-tuple-element.97), channel_id=1, source_target_pairs={{0,2},{1,3},{2,4},{3,5},{4,6},{5,7},{6,0},{7,1},{8,10},{9,11},{10,... | collective-permute-start | bytes 7962632 | tf_op jit(solution)/shard_map/ppermute | solution.py:477
  845.3 320.8 %collective-permute-start.4 = (bf16[8,144,1152]{2,1,0:T(8,128)(2,1)}, bf16[8,144,1152]{2,1,0:T(8,128)(2,1)}, u32[]{:S(2)}, u32[]{:S(2)}) collective-permute-start(bf16[8,144,1152]{2,1,0:T(8,128)(2,1)} %get-tuple-element.98), channel_id=1, source_target_pairs={{0,4},{1,5},{2,6},{3,7},{4,0},{5,1},{6,2},{7,3},{8,12},{9,13},{10,... | collective-permute-start | bytes 7962632 | tf_op jit(solution)/shard_map/ppermute | solution.py:477
  857.5 28.0 %copy-start.7 = (bf16[4,144,1152]{2,1,0:T(8,128)(2,1)}, bf16[4,144,1152]{2,1,0:T(8,128)(2,1)S(1)}, u32[]{:S(2)}) copy-start(bf16[4,144,1152]{2,1,0:T(8,128)(2,1)S(1)} %collective-permute-done) | copy-start | bytes 3981316
  857.5 308.6 %collective-permute-start.5 = (bf16[8,144,1152]{2,1,0:T(8,128)(2,1)}, bf16[8,144,1152]{2,1,0:T(8,128)(2,1)}, u32[]{:S(2)}, u32[]{:S(2)}) collective-permute-start(bf16[8,144,1152]{2,1,0:T(8,128)(2,1)} %get-tuple-element.99), channel_id=1, source_target_pairs={{0,6},{1,7},{2,0},{3,1},{4,2},{5,3},{6,4},{7,5},{8,14},{9,15},{10,... | collective-permute-start | bytes 7962632 | tf_op jit(solution)/shard_map/ppermute | solution.py:477
  1172.0 6.6 copy-start.10
  1172.2 16.9 %copy-start.1 = (f32[4,144,1152]{2,1,0:T(8,128)}, f32[4,144,1152]{2,1,0:T(8,128)S(1)}, u32[]{:S(2)}) copy-start(f32[4,144,1152]{2,1,0:T(8,128)S(1)} %slice.304) | copy-start | bytes 7962628
  1172.2 7.8 copy-start.8
  1172.2 8.4 copy-start.12
  1172.2 9.6 copy-start.17
  1180.9 12.6 copy-start.22
  1203.9 28.0 %copy-start.21 = (f32[1444]{0:T(1024)S(1)}, f32[1444]{0:T(1024)}, u32[]{:S(2)}) copy-start(f32[1444]{0:T(1024)} %param.29) | copy-start | bytes 17332
  1203.9 29.6 %copy-start.5 = (f32[144,1186]{1,0:T(8,128)S(1)}, f32[144,1186]{1,0:T(8,128)}, u32[]{:S(2)}) copy-start(f32[144,1186]{1,0:T(8,128)} %param.28) | copy-start | bytes 2049412
  1231.9 5.1 copy-start.6
  1233.5 12.4 slice-start
  1237.0 8.2 copy-start.24
  1237.0 8.2 copy-start.27
  1237.0 8.2 copy-start.28
  1237.0 8.9 slice-start.1
  1237.0 8.9 slice-start.2
Sparse Core Ops, SparseCore 0:
  14.4 36.8 all-gather.7
  53.5 107.0 all-gather.5
  162.8 98.9 all-gather.9
  263.9 98.8 all-gather.11

commit v6 on v5

--- a/solution.py
+++ b/solution.py
@@ -183,52 +183,55 @@
     return share(value, axis, True, ident)
 
 
-def products_kernel(units, rows, extra, *refs):
-    lefts, rights, given = (refs[:4], refs[4:8], refs[8 : 8 + extra])
-    refs = refs[8 + extra :]
-    own_out, block_outs, bias_out, spread_out = (refs[0], refs[1:4], refs[4], refs[5 : 5 + extra])
-    refs = refs[5 + extra :]
+FINAL, LATER, NEAR, FAR, PASS = range(5)
+STEPS = 16
+CHIPS = 4
+
+
+def sums_kernel(units, rows, *refs):
+    lefts, rights, given = (refs[:4], refs[4:8], refs[8])
+    own_out, final_out, later_out, bias_out, spread_out = refs[9:14]
     (
         left_v,
         right_v,
         product,
         got,
         own_v,
-        low_v,
+        stage,
+        near,
+        far,
+        passed,
         left_sem,
         right_sem,
         send_sem,
         recv_sem,
         own_sem,
-        low_sem,
-    ) = refs[:12]
+        stage_sem,
+        block_sem,
+        pass_sem,
+        given_send,
+        given_recv,
+    ) = refs[14:]
     here = lax.axis_index("dp")
     core, chip = (lax.rem(here, 2), here // 2)
-    chips = 4
     partner = {"dp": here + 1 - 2 * core}
+    tall = CHIPS * rows
+    meet("dp", DIRECT, here)
     spreading = []
-    if extra:
-        count = 2 * chips
-        meet("dp", count, here)
-        for step in range(1, count):
-            copy = pltpu.make_async_remote_copy(
-                src_ref=given[0],
-                dst_ref=spread_out[0].at[here],
-                send_sem=refs[12].at[step - 1],
-                recv_sem=refs[13].at[step - 1],
-                device_id={"dp": lax.rem(here + step, count)},
-                device_id_type=MESH,
-            )
-            copy.start()
-            spreading.append(copy)
-        spread_out[0][here] = given[0][...]
-    else:
-        barrier = pltpu.get_barrier_semaphore()
-        pl.semaphore_signal(barrier, inc=1, device_id=partner, device_id_type=MESH)
-        pl.semaphore_wait(barrier, 1)
-    tall = chips * rows
-    plan, last = ([], [None, None])
-    slots = [1, 1]
+    for step in range(1, DIRECT):
+        copy = pltpu.make_async_remote_copy(
+            src_ref=given,
+            dst_ref=spread_out.at[here],
+            send_sem=given_send.at[step - 1],
+            recv_sem=given_recv.at[step - 1],
+            device_id={"dp": lax.rem(here + step, DIRECT)},
+            device_id_type=MESH,
+        )
+        copy.start()
+        spreading.append(copy)
+    spread_out[here] = given[...]
+    places = {FINAL: final_out, LATER: later_out, NEAR: near, FAR: far, PASS: passed}
+    plan, last, slots = ([], [None, None], [1, 1])
     for left, left_at, right, right_at, gathers in units:
         fresh = []
         for side, key in enumerate(((left, left_at), (right, right_at))):
@@ -237,26 +240,33 @@
                 slots[side] = 1 - slots[side]
                 last[side] = key
         plan.append((tuple(slots), tuple(fresh)))
+    slot_of, used = ({}, 0)
+    for index, unit in enumerate(units):
+        slot_of[index] = used
+        used += unit[4] is None
 
     def loads_of(index):
         left, left_at, right, right_at, gathers = units[index]
         (left_slot, right_slot), (left_fresh, right_fresh) = plan[index]
         copies = []
         if left_fresh:
+            source = lefts[left].at[:, pl.ds(left_at, D)]
             copies.append(
-                pltpu.make_async_copy(
-                    lefts[left].at[:, pl.ds(left_at, D)], left_v.at[left_slot], left_sem.at[left_slot]
-                )
+                pltpu.make_async_copy(source, left_v.at[left_slot], left_sem.at[left_slot])
             )
         if right_fresh:
+            source = rights[right].at[:, pl.ds(right_at, D)]
             copies.append(
-                pltpu.make_async_copy(
-                    rights[right].at[:, pl.ds(right_at, D)],
-                    right_v.at[right_slot],
-                    right_sem.at[right_slot],
-                )
+                pltpu.make_async_copy(source, right_v.at[right_slot], right_sem.at[right_slot])
             )
         return copies
+
+    pending, crossing, leaving, keeping = ({}, {}, {}, {})
+
+    def load(index):
+        pending[index] = loads_of(index)
+        for copy in pending[index]:
+            copy.start()
 
     def to_partner(source, target, sems):
         copy = pltpu.make_async_remote_copy(
@@ -270,13 +280,6 @@
         copy.start()
         return copy
 
-    pending, crossing, leaving = ({}, {}, {})
-
-    def load(index):
-        pending[index] = loads_of(index)
-        for copy in pending[index]:
-            copy.start()
-
     def multiply(index):
         gathers = units[index][4]
         left_slot, right_slot = plan[index][0]
@@ -288,12 +291,7 @@
             for copy in crossing[index - 2]:
                 copy.wait_send()
         slot, place = (index % 2, index % 4)
-        product[slot] = lax.dot_general(
-            left_v[left_slot],
-            right_v[right_slot],
-            (((0,), (0,)), ((), ())),
-            preferred_element_type=jnp.float32,
-        )
+        product[slot] = contract(left_v[left_slot], right_v[right_slot], 0, 0)
         if plan[index][1][1]:
             ones = jnp.ones((8, right_v.shape[1]), jnp.bfloat16)
             bias_out[index] = matmul(ones, right_v[right_slot])
@@ -302,190 +300,227 @@
                 to_partner(
                     product.at[slot, pl.ds(pl.multiple_of((2 * i + 1 - core) * rows, 8), rows)],
                     got.at[place, pl.ds(i * rows, rows)],
-                    place * chips + i,
+                    place * CHIPS + i,
                 )
-                for i in range(chips)
+                for i in range(CHIPS)
             ]
         else:
             crossing[index] = [
                 to_partner(
                     product.at[slot, pl.ds(pl.multiple_of((1 - core) * tall, 8), tall)],
                     got.at[place],
-                    place * chips,
+                    place * CHIPS,
                 )
             ]
 
+    def crossed(source, kind, slot, to, sem):
+        return pltpu.make_async_remote_copy(
+            src_ref=source,
+            dst_ref=places[kind].at[slot],
+            send_sem=sem,
+            recv_sem=block_sem.at[kind, slot],
+            device_id={"dp": 2 * to + core},
+            device_id_type=MESH,
+        )
+
+    def landed(kind, slot):
+        crossed(stage.at[0, 0], kind, slot, chip, stage_sem.at[0, 0]).wait_recv()
+
+    def filled(target, index, block, gathers, added=None):
+        slot, place = (index % 2, index % 4)
+        base = (2 * block + core) * rows if gathers is None else core * tall + block * rows
+
+        @pl.loop(0, rows // STEPS)
+        def run(step):
+            at = step * STEPS
+            value = (
+                product[slot, pl.ds(pl.multiple_of(base + at, STEPS), STEPS)]
+                + got[place, pl.ds(pl.multiple_of(block * rows + at, STEPS), STEPS)]
+            )
+            to = pl.ds(pl.multiple_of(at, STEPS), STEPS)
+            if added is not None:
+                value = value + added[to].astype(jnp.float32)
+            target[to] = value.astype(target.dtype)
+
+    def route(index, block, owner, slot, gathers):
+        side = index % 3
+
+        def case(at, kind, to, added=None):
+            copy = crossed(
+                stage.at[side, block], kind, slot, to, stage_sem.at[side, block]
+            )
+
+            @pl.when(chip == at)
+            def act():
+                if added is not None:
+                    landed(added, slot)
+                filled(
+                    stage.at[side, block],
+                    index,
+                    block,
+                    gathers,
+                    None if added is None else places[added].at[slot],
+                )
+                copy.start()
+
+            leaving[index].append((chip == at, copy.wait_send))
+
+        keep = pltpu.make_async_copy(
+            own_v.at[side, block], own_out.at[slot], own_sem.at[side, block]
+        )
+
+        @pl.when(chip == owner)
+        def hold():
+            filled(own_v.at[side, block], index, block, gathers)
+            keep.start()
+
+        leaving[index].append((chip == owner, keep.wait))
+        flip = (lambda at: at) if owner < 2 else (lambda at: CHIPS - 1 - at)
+        if owner in (0, CHIPS - 1):
+            case(flip(3), FAR, flip(2))
+            case(flip(1), FINAL, flip(0))
+            case(flip(2), PASS, flip(1), FAR)
+        else:
+            case(flip(3), NEAR, flip(2))
+            case(flip(0), FINAL, flip(1))
+            case(flip(2), LATER, flip(1), NEAR)
+
+    def blocks_of(index):
+        gathers = units[index][4]
+        if gathers is None:
+            return [(owner, owner, slot_of[index]) for owner in (0, 3, 1, 2)]
+        return [(block, gathers, slot_of[index] + block) for block in range(CHIPS)]
+
     def combine(index):
-        gathers = units[index][4]
-        slot, place, side = (index % 2, index % 4, index % 2)
         for copy in crossing[index]:
             copy.wait_recv()
-        if index >= 2:
-            finish(index - 2)
-        at_slot = slot_of[index]
-        if gathers is None:
-            for step in range(chips):
-                other = lax.rem(chip + step, chips)
-                value = (
-                    product[slot, pl.ds(pl.multiple_of((2 * other + core) * rows, 8), rows)]
-                    + got[place, pl.ds(pl.multiple_of(other * rows, 8), rows)]
-                )
-                if step == 0:
-                    own_v[side, 0:rows] = value
-                else:
-                    low_v[side, (step - 1) * rows : step * rows] = value.astype(jnp.bfloat16)
-            copies = [
-                pltpu.make_async_copy(
-                    own_v.at[side, pl.ds(0, rows)], own_out.at[at_slot], own_sem.at[side]
-                )
-            ]
-            for step in range(1, chips):
-                copies.append(
-                    pltpu.make_async_copy(
-                        low_v.at[side, pl.ds((step - 1) * rows, rows)],
-                        block_outs[step - 1].at[at_slot],
-                        low_sem.at[side, step - 1],
-                    )
-                )
-            for copy in copies:
-                copy.start()
-            leaving[index] = [(None, copies)]
-        else:
-            step_here = lax.rem(gathers + chips - chip, chips)
-            cases = []
-            for step in range(chips):
-                held = own_v if step == 0 else low_v
-                out = own_out if step == 0 else block_outs[step - 1]
-                sem = own_sem.at[side] if step == 0 else low_sem.at[side, step - 1]
-                copies = [
-                    pltpu.make_async_copy(
-                        held.at[side, pl.ds(i * rows, rows)],
-                        out.at[at_slot + i],
-                        sem if i == 0 else more_sem(step, side, i),
-                    )
-                    for i in range(chips)
-                ]
-                cases.append((step_here == step, copies))
-
-                @pl.when(step_here == step)
-                def put(held=held, copies=copies):
-                    value = product[slot, pl.ds(pl.multiple_of(core * tall, 8), tall)] + got[place]
-                    held[side] = value.astype(held.dtype)
-                    for copy in copies:
-                        copy.start()
-
-            leaving[index] = cases
-
-    def more_sem(step, side, i):
-        return own_sem.at[2 + side * 3 + i - 1] if step == 0 else low_sem.at[side, 3 * i + step - 1]
+        if index >= 3:
+            finish(index - 3)
+        leaving[index] = []
+        for block, owner, slot in blocks_of(index):
+            route(index, block, owner, slot, units[index][4])
 
     def finish(index):
-        for condition, copies in leaving[index]:
-            if condition is None:
-                for copy in copies:
-                    copy.wait()
-            else:
-
-                @pl.when(condition)
-                def settle(copies=copies):
-                    for copy in copies:
-                        copy.wait()
-
-    slot_of, used = ({}, 0)
-    for index, unit in enumerate(units):
-        slot_of[index] = used
-        if unit[4] is None:
-            used += 1
+        for condition, wait in leaving[index]:
+
+            @pl.when(condition)
+            def settle(wait=wait):
+                wait()
+
+    def pass_on(index):
+        for block, owner, slot in blocks_of(index):
+            if owner not in (0, CHIPS - 1):
+                continue
+            middle = 1 if owner == 0 else CHIPS - 2
+
+            @pl.when(chip == middle)
+            def forward(slot=slot, owner=owner):
+                landed(PASS, slot)
+                crossed(passed.at[slot], LATER, slot, owner, pass_sem.at[slot]).start()
+
+    total = len(units)
     load(0)
     multiply(0)
-    for index in range(len(units)):
-        if index + 1 < len(units):
+    for index in range(total):
+        if index + 1 < total:
             multiply(index + 1)
         combine(index)
-    for index in range(max(0, len(units) - 2), len(units)):
+        if index >= 1:
+            pass_on(index - 1)
+    pass_on(total - 1)
+    for index in range(max(0, total - 3), total):
         finish(index)
+    for index in range(max(0, total - 2), total):
         for copy in crossing[index]:
             copy.wait_send()
+    for index in range(total):
+        for block, owner, slot in blocks_of(index):
+
+            @pl.when(chip == owner)
+            def received(slot=slot):
+                landed(FINAL, slot)
+                landed(LATER, slot)
+
+            if owner in (0, CHIPS - 1):
+
+                @pl.when(chip == (1 if owner == 0 else CHIPS - 2))
+                def sent(slot=slot, owner=owner):
+                    crossed(passed.at[slot], LATER, slot, owner, pass_sem.at[slot]).wait_send()
+
     for copy in spreading:
         copy.wait()
 
 
-def chip_products(units, lefts, rights, rows, ident, given=()):
+def line_sums(units, lefts, rights, rows, ident, given):
     tokens = lefts[0].shape[0]
-    places = sum(unit[4] is None for unit in units) + 4 * any(unit[4] is not None for unit in units)
+    places = sum(unit[4] is None for unit in units) + 4
+    block = (rows, D)
     outs = pl.pallas_call(
-        functools.partial(products_kernel, units, rows, len(given)),
-        out_shape=[jax.ShapeDtypeStruct((places, rows, D), jnp.float32)]
-        + [jax.ShapeDtypeStruct((places, rows, D), jnp.bfloat16) for unused in range(3)]
-        + [jax.ShapeDtypeStruct((len(units), 8, D), jnp.float32)]
-        + [jax.ShapeDtypeStruct((DIRECT,) + one.shape, one.dtype) for one in given],
-        in_specs=specs("h" * 8, "v" * len(given)),
-        out_specs=specs("h" * 4, "v", "v" * len(given)),
+        functools.partial(sums_kernel, units, rows),
+        out_shape=[
+            jax.ShapeDtypeStruct((places,) + block, jnp.float32),
+            jax.ShapeDtypeStruct((places,) + block, jnp.bfloat16),
+            jax.ShapeDtypeStruct((places,) + block, jnp.bfloat16),
+            jax.ShapeDtypeStruct((len(units), 8, D), jnp.float32),
+            jax.ShapeDtypeStruct((DIRECT,) + given.shape, given.dtype),
+        ],
+        in_specs=specs("h" * 8, "v"),
+        out_specs=specs("hhhvv"),
         scratch_shapes=[
             pltpu.VMEM((2, tokens, D), jnp.bfloat16),
             pltpu.VMEM((2, tokens, D), jnp.bfloat16),
             pltpu.VMEM((2, 8 * rows, D), jnp.float32),
             pltpu.VMEM((4, 4 * rows, D), jnp.float32),
-            pltpu.VMEM((2, 4 * rows, D), jnp.float32),
-            pltpu.VMEM((2, 4 * rows, D), jnp.bfloat16),
+            pltpu.VMEM((3, 4) + block, jnp.float32),
+            pltpu.VMEM((3, 4) + block, jnp.bfloat16),
+            pltpu.VMEM((places,) + block, jnp.bfloat16),
+            pltpu.VMEM((places,) + block, jnp.bfloat16),
+            pltpu.VMEM((places,) + block, jnp.bfloat16),
             pltpu.SemaphoreType.DMA((2,)),
             pltpu.SemaphoreType.DMA((2,)),
             pltpu.SemaphoreType.DMA((16,)),
             pltpu.SemaphoreType.DMA((16,)),
-            pltpu.SemaphoreType.DMA((8,)),
-            pltpu.SemaphoreType.DMA((2, 12)),
-        ]
-        + [pltpu.SemaphoreType.DMA((DIRECT - 1,))] * (2 * len(given)),
+            pltpu.SemaphoreType.DMA((3, 4)),
+            pltpu.SemaphoreType.DMA((3, 4)),
+            pltpu.SemaphoreType.DMA((5, places)),
+            pltpu.SemaphoreType.DMA((places,)),
+            pltpu.SemaphoreType.DMA((DIRECT - 1,)),
+            pltpu.SemaphoreType.DMA((DIRECT - 1,)),
+        ],
         compiler_params=pltpu.CompilerParams(
-            collective_id=ident, has_side_effects=True, vmem_limit_bytes=60 << 20
+            collective_id=ident, has_side_effects=True, vmem_limit_bytes=62 << 20
         ),
         cost_estimate=pl.CostEstimate(
             flops=2 * tokens * D * D * len(units),
             bytes_accessed=len(units) * tokens * D * 4,
             transcendentals=0,
         ),
-        name="chip_products",
-    )(*lefts, *rights, *given)
-    return (outs[0], outs[1:4], outs[4][:, 0], outs[5:])
-
-
-def row_sums(lefts, rights, early, given):
+        name="line_sums",
+    )(*lefts, *rights, given)
+    total = outs[0] + outs[1].astype(jnp.float32) + outs[2].astype(jnp.float32)
+    return (total, outs[3][:, 0], outs[4])
+
+
+def row_sums(lefts, rights, given):
     count = lax.axis_size("dp")
     if count != DIRECT:
         products = [matmul_tn(one, other) for one, other in zip(lefts, rights)]
         sums = [lax.psum_scatter(one, "dp", scatter_dimension=0, tiled=True) for one in products]
         wide = jnp.concatenate([sums[0], sums[1], sums[2]], axis=1)
         given = lax.all_gather(given, "dp")
-        biases = [column_sum(one) for one in rights]
-        return (wide, sums[3], biases, products[3], early, given)
+        return (wide, sums[3], [column_sum(one) for one in rights], given)
     rows = D // count
-    chips = count // 2
     parts = FF // D
-    first = [(0, 0, 0, i * D, None) for i in range(3)] + [(1, 0, 1, 0, None)]
-    rest = [(2, 0, 2, i * D, None) for i in range(parts)] + [
-        (3, i * D, 3, 0, i) for i in range(parts)
-    ]
-    totals, biases, tied, given_all = ([], [], None, None)
-    for ident, units in ((12, first), (13, rest)):
-        if tied is not None:
-            lefts, rights, tied, early = lax.optimization_barrier((lefts, rights, tied, early))
-        total, blocks, bias, shared = chip_products(
-            tuple(units), lefts, rights, rows, ident, (given,) if tied is None else ()
-        )
-        given_all = shared[0] if tied is None else given_all
-        for step in range(1, chips):
-            arrived = lax.ppermute(
-                blocks[step - 1], "dp", [(i, (i + 2 * step) % count) for i in range(count)]
-            )
-            total = total + arrived.astype(jnp.float32)
-        tied = blocks
-        totals.append(total)
-        biases.append(bias)
-    wide = [totals[0][i] for i in range(4)] + [totals[1][i] for i in range(parts)]
-    sums = [biases[0][:3].reshape(-1), biases[0][3], biases[1][:parts].reshape(-1), biases[1][parts]]
-    late = (tied, totals[0])
-    down = totals[1][parts:].reshape(-1, D)
-    return (jnp.concatenate(wide, axis=1), down, sums, late, early, given_all)
+    units = (
+        [(0, 0, 0, i * D, None) for i in range(3)]
+        + [(1, 0, 1, 0, None)]
+        + [(2, 0, 2, i * D, None) for i in range(parts)]
+        + [(3, i * D, 3, 0, i) for i in range(parts)]
+    )
+    total, bias, given_all = line_sums(tuple(units), lefts, rights, rows, 12, given)
+    wide = jnp.concatenate([total[i] for i in range(4 + parts)], axis=1)
+    sums = [bias[:3].reshape(-1), bias[3], bias[4 : 4 + parts].reshape(-1), bias[4 + parts]]
+    return (wide, total[4 + parts :].reshape(-1, D), sums, given_all)
 
 
 GROUP = 4
@@ -1229,13 +1264,11 @@
         matmul_tn(d_tokens, noisy_low.reshape(images * patches, PATCH_IN)),
         g_output,
     )
-    shard_wide, shard_down, right_sums, late, (token_sums, g_edge), d_ada_all = row_sums(
+    shard_wide, shard_down, right_sums, d_ada_all = row_sums(
         [flat(kept_all[name]) for name in (MIXED_ONE, ATT, MIXED_TWO, ACT)],
         [d_qkv, d_branch, d_pre, d_second],
-        (token_sums, g_edge),
         d_ada,
     )
-    d_ada, d_ada_all, unused = lax.optimization_barrier((d_ada, d_ada_all, late))
     d_ada_all = d_ada_all.reshape(shards * images, 6 * D)
 
     cond_piece = matmul_nt(d_ada_all, w_ada) * silu_grad(cond_here)
@@ -1269,18 +1302,6 @@
         axis=1,
     )
     sums = exchange(sums[:, None], "dp", 11)[:, 0]
-    (
-        sums,
-        d_ada_all,
-        d_cond_all,
-        d_cond_rows,
-        d_time,
-        film_all,
-        shard_wide,
-        shard_down,
-    ) = lax.optimization_barrier(
-        (sums, d_ada_all, d_cond_all, d_cond_rows, d_time, film_all, shard_wide, shard_down)
-    )
     shard_ada = matmul_tn(act_here, d_ada_all)
     shard_in = jnp.concatenate([shard_wide, shard_ada], axis=1)
     edge_end = bias_width + rows * PATCH_IN

time: 1280 us -> 1270 us (level)
  waiting for transfers between devices: 233 us -> 213 us
  local copies, waits for them, and re-layouts: 64.6 us -> 83 us
    pallas_call x2 -> x1, Pallas kernels: 74.2 us -> 272 us  [line_sums(): pl.pallas_call(functools.partial(sums_kernel, units, rows), out_shape=[ja...]
    pallas_call x10, Pallas kernels: 371 us -> 177 us  [share(): pl.pallas_call(functools.partial(share_kernel, axis, count, personal), ou...]
    unnamed x94 -> x131, local copies, waits for them, and re-layouts: 23.8 us -> 52.2 us
    ppermute x6 -> x0, waiting for transfers between devices: 25.7 us -> none  [row_sums(): lax.ppermute(blocks[step - 1], 'dp', [(i, (i + 2 * step) % count) for i i...]
  transfers between devices with their start and end apart: 10 -> 4, of which waited for: 4 -> 3; matrix products, arithmetic and copies ran while one was open for 6% -> 3% of each run, Pallas kernels for 32% -> 8%
where the time goes in v6:
time: 1270 us; the launch traced here: 1260 us
  Pallas kernels  829 us (65%)
  waiting for transfers between devices  213 us (17%)
  other arithmetic  83.6 us (7%)
  local copies, waits for them, and re-layouts  83 us (7%)
  matrix products  30.1 us (2%)
  between operations  22.2 us (2%)
    pallas_call x1, Pallas kernels, pipeline_backward(): pl.pallas_call(functools.partial(backward_kernel, sections, images, direc...  284 us
    pallas_call x1, Pallas kernels, line_sums(): pl.pallas_call(functools.partial(sums_kernel, units, rows), out_shape=[ja...  272 us
    all_gather x4, waiting for transfers between devices, gathered(): return lax.all_gather(value, axis, axis=dim, tiled=True)  212 us
    pallas_call x10, Pallas kernels, share(): pl.pallas_call(functools.partial(share_kernel, axis, count, personal), ou...  177 us
    pallas_call x1, Pallas kernels, pipeline_forward(): pl.pallas_call(functools.partial(forward_kernel, sections, images), out_s...  95.5 us
    unnamed x131, local copies, waits for them, and re-layouts  52.2 us
    sub x5, other arithmetic, adam_update(): return (weight - RATE * (ratio + DECAY * weight), first_new, second_new)  32.8 us
  transfers between devices with their start and end apart: 4, of which 3 were waited for; matrix products, arithmetic and copies ran while one was open for 3% of the time, Pallas kernels for 8%

profile of v6, /device:TPU:0, one launch (start us, length us, event | category | flops | bytes accessed | tf_op | source)
XLA Modules:
  0.0 1260.8 jit_solution(7005100173233122636)
XLA Ops:
  7.2 4.1 convert_bitcast_fusion
  11.4 2.2 copy-done.2
  14.3 2.3 slice.285
  16.7 2.5 slice.287
  21.6 23.8 %share.11 = bf16[4,146,1186]{2,1,0:T(8,128)(2,1)} custom-call(bf16[146,1186]{1,0:T(8,128)(2,1)} %pad_maximum_fusion.4.in_ref), custom_call_target="tpu_custom_call" | custom-call | tf_op jit(solution)/shard_map/share/pallas_call | solution.py:160
  50.0 8.5 share.10
  60.5 1.7 broadcast_in_dim.30.qkv_bias
  64.6 12.2 share.12
  78.0 1.4 fusion.44.in_ref
  79.4 11.5 share.13
  92.1 2.0 fusion.7
  95.3 44.7 %share.14 = f32[8,288,128]{2,1,0:T(8,128)} custom-call(f32[8,288,128]{2,1,0:T(8,128)} %reshape.480.in_ref), custom_call_target="tpu_custom_call" | custom-call | tf_op jit(solution)/shard_map/share/pallas_call | solution.py:160
  140.0 1.3 reduce_sum.261
  143.6 2.8 multiply_cosine_fusion
  147.3 3.0 fusion.1.tokens
  150.3 10.3 all-gather.6.cloned.1.call-done.wq
  160.7 101.1 %all-gather.10.cloned.1.call-done.wh = bf16[1152,4608]{1,0:T(8,128)(2,1)} async-done(((bf16[144,4608]{1,0:T(8,128)(2,1)}), bf16[1152,4608]{1,0:T(8,128)(2,1)}) %all-gather.10.cloned.1.call-update) | async-done | bytes 10616848 | tf_op jit(solution)/shard_map/all_gather | solution.py:1155
  261.8 101.0 %all-gather.12.cloned.1.call-done = bf16[1,4608,1152]{2,1,0:T(8,128)(2,1)} async-done(((bf16[1,576,1152]{2,1,0:T(8,128)(2,1)}), bf16[1,4608,1152]{2,1,0:T(8,128)(2,1)}) %all-gather.12.cloned.1.call-update) | async-done | bytes 10616848 | tf_op jit(solution)/shard_map/all_gather | solution.py:1155
  362.8 95.5 %pipeline_forward.1 = (f32[4,256,1152]{2,1,0:T(8,128)}, bf16[4,256,1152]{2,1,0:T(8,128)(2,1)}, bf16[4,3456,256]{2,1,0:T(8,128)(2,1)}, bf16[4,256,1152]{2,1,0:T(8...) custom-call(f32[1,6912]{1,0:T(1,128)} %broadcast_in_dim.22.bias, ...), custom_call_target="tpu_custom_call" | custom-call | flops 33822867456 | bytes 107347968 | tf_op jit(solution)/shard_map/pipeline_forward/pallas_call | solution.py:1016
  458.3 2.6 reduce_sum.262
  461.0 3.1 multiply_reduce_fusion.3
  464.7 1.8 convert_reduce_fusion.4
  466.5 2.9 multiply_reduce_fusion.1
  470.1 2.9 subtract_multiply_fusion.head_grad
  472.9 284.3 %pipeline_backward.1 = (bf16[4,256,1152]{2,1,0:T(8,128)(2,1)}, bf16[4,256,4608]{2,1,0:T(8,128)(2,1)}, bf16[4,256,1152]{2,1,0:T(8,128)(2,1)}, bf16[4,256,3456]{2,...) custom-call(f32[4,6,1152]{2,1,0:T(8,128)} %reshape.482.ada, ...), custom_call_target="tpu_custom_call" | custom-call | flops 35634806784 | bytes 107347968 | tf_op jit(solution)/shard_map/pipeline_backward/pallas_call | solution.py:1041
  758.8 272.1 %line_sums.1 = (f32[12,144,1152]{2,1,0:T(8,128)}, bf16[12,144,1152]{2,1,0:T(8,128)(2,1)}, bf16[12,144,1152]{2,1,0:T(8,128)(2,1)}, f32[12,8,1152]{2,1,0:T(8,128)}, bf16[8,4,6912]{2,1,0:T(4,128)(2,1)}) custom-call(bf16[1024,1152]{1,0:T(8,128)(2,1)} %bitcast.133, bf16[1024,1152]{1,0:T(8,128)(2,1)} %bitcast.134, bf16[1024,1152]{1,0:T(8,128)(2,1)} %bitcast.135, ...), custom_call_target="tpu_custom_call" | custom-call | flops 32614907904 | bytes 56623104 | tf_op jit(solution)/shard_map/line_sums/pallas_call | solution.py:458
  1030.9 6.6 convert_add_fusion
  1038.4 2.8 copy-done.1
  1045.2 2.1 convolution_bitcast_fusion.2
  1055.9 3.3 fusion.4
  1060.0 2.9 fusion.18.in_ref
  1062.9 6.3 share.15
  1069.2 1.9 fusion.21.in_ref
  1071.1 48.4 %share.16 = bf16[8,32,144]{2,1,0:T(8,128)(2,1)} custom-call(bf16[32,144]{1,0:T(8,128)(2,1)} %fusion.21.in_ref), custom_call_target="tpu_custom_call" | custom-call | tf_op jit(solution)/shard_map/share/pallas_call | solution.py:160
  1122.0 9.1 share.17
  1132.2 1.8 fusion.31
  1134.4 1.5 convolution_bitcast_fusion
  1137.9 2.0 slice_dynamic-update-slice_fusion.7
  1140.6 2.0 bitcast_dynamic-update-slice_fusion.8
  1142.5 2.0 bitcast_dynamic-update-slice_fusion.7
  1144.5 2.0 bitcast_dynamic-update-slice_fusion.6
  1146.5 2.0 bitcast_dynamic-update-slice_fusion.5
  1148.4 2.0 bitcast_dynamic-update-slice_fusion.4
  1150.4 2.0 bitcast_dynamic-update-slice_fusion.3
  1152.4 2.0 bitcast_dynamic-update-slice_fusion.2
  1154.4 4.2 bitcast_dynamic-update-slice_fusion.1
  1158.5 6.7 multiply_reduce_fusion
  1169.5 3.5 concatenate.80
  1181.0 1.4 multiply_reduce_fusion.7
  1183.8 7.2 share.18
  1192.2 5.8 share.19
  1200.0 3.6 slice_multiply_fusion
  1203.6 2.1 slice_dynamic-update-slice_fusion.6
  1205.7 2.0 slice_dynamic-update-slice_fusion.5
  1207.7 2.1 slice_dynamic-update-slice_fusion.4
  1209.8 2.0 slice_dynamic-update-slice_fusion.3
  1211.8 2.0 slice_dynamic-update-slice_fusion.2
  1213.7 2.0 slice_dynamic-update-slice_fusion.1
  1215.7 2.1 slice_dynamic-update-slice_fusion
  1217.9 2.2 bitcast_dynamic-update-slice_fusion
  1220.1 2.0 multiply_subtract_fusion.2
  1222.1 1.4 multiply_subtract_fusion.3
  1223.5 20.8 %multiply_subtract_fusion = (f32[1,144,16128]{2,1,0:T(8,128)}, f32[1,144,16128]{2,1,0:T(8,128)}, f32[1,144,16128]{2,1,0:T(8,128)}) fusion(f32[1,144,16128]{2,1,0:T(8,128)S(1)} %bitcast.113, f32[1,144,16128]{2,1,0:T(8,128)} %bitcast_dynamic-update-slice_fusion, f32[]{:T(128)S(6)} %min.3, f32[1,144,16128]{2,1,0:T(8,128)} %param.30, f32[1,144,16128]{2,1,0:T(8,128)} %param.35), kind=kLoop, calls=%fused_computation.2 | loop fusion | flops 37158912 | bytes 65028100 | tf_op jit(solution)/shard_map/sub | solution.py:1114
  1244.4 7.8 multiply_subtract_fusion.1
  (235 shorter events, 53.8 us)
Async XLA Ops:
  7.2 143.1 %all-gather.8.cloned.1.call-start = ((), (), s32[]{:S(2)}) async-start(), calls=%async_computation.1 | async-start | bytes 2985984 | tf_op jit(solution)/shard_map/all_gather | solution.py:1155
  11.3 2.2 copy-start.2
  13.5 5.9 copy-start.3
  14.3 146.4 %all-gather.6.cloned.1.call-start = ((), (), s32[]{:S(2)}) async-start(), calls=%async_computation | async-start | bytes 8957952 | tf_op jit(solution)/shard_map/all_gather | solution.py:1155
  16.7 4.0 copy-start.32
  16.7 4.1 copy-start.10
  16.7 245.1 %all-gather.10.cloned.1.call-start = ((), (), s32[]{:S(2)}) async-start(), calls=%async_computation.2 | async-start | bytes 11943936 | tf_op jit(solution)/shard_map/all_gather | solution.py:1155
  19.3 28.0 %copy-start.47 = (s32[4]{0:T(128)S(1)}, s32[4]{0:T(128)}, u32[]{:S(2)}) copy-start(s32[4]{0:T(128)} %param.22) | copy-start | bytes 52
  19.3 28.0 %copy-start.46 = (s32[4]{0:T(128)S(1)}, s32[4]{0:T(128)}, u32[]{:S(2)}) copy-start(s32[4]{0:T(128)} %param.23) | copy-start | bytes 52
  19.3 28.0 %copy-start.37 = (s32[4,256]{1,0:T(4,128)S(1)}, s32[4,256]{1,0:T(4,128)}, u32[]{:S(2)}) copy-start(s32[4,256]{1,0:T(4,128)} %param.24) | copy-start | bytes 12292
  19.3 29.9 %copy-start.34 = (f32[1,2016]{1,0:T(1,128)S(1)}, f32[1,2016]{1,0:T(1,128)}, u32[]{:S(2)}) copy-start(f32[1,2016]{1,0:T(1,128)} %param.27) | copy-start | bytes 24196
  19.4 343.4 %all-gather.12.cloned.1.call-start = ((), (), s32[]{:S(2)}) async-start(), calls=%async_computation.3 | async-start | bytes 11943936 | tf_op jit(solution)/shard_map/all_gather | solution.py:1155
  45.4 17.3 %copy-start.6 = (bf16[4,146,1186]{2,1,0:T(8,128)(2,1)S(1)}, bf16[4,146,1186]{2,1,0:T(8,128)(2,1)}, u32[]{:S(2)}) copy-start(bf16[4,146,1186]{2,1,0:T(8,128)(2,1)} %share.11) | copy-start | bytes 4155748
  62.4 2.3 copy-start.42
  62.7 1.9 copy-start.25
  62.7 1.9 copy-start.27
  62.9 0.7 copy-start.7
  62.9 31.2 %copy-start.12 = (bf16[144,1186]{1,0:T(8,128)(2,1)}, bf16[144,1186]{1,0:T(8,128)(2,1)S(1)}, u32[]{:S(2)}) copy-start(bf16[144,1186]{1,0:T(8,128)(2,1)S(1)} %get-tuple-element.90) | copy-start | bytes 1024708
  62.9 31.2 %copy-start.19 = (bf16[144,1186]{1,0:T(8,128)(2,1)}, bf16[144,1186]{1,0:T(8,128)(2,1)S(1)}, u32[]{:S(2)}) copy-start(bf16[144,1186]{1,0:T(8,128)(2,1)S(1)} %get-tuple-element.89) | copy-start | bytes 1024708
  91.6 48.4 %copy-start.22 = (f32[32,144]{1,0:T(8,128)}, f32[32,144]{1,0:T(8,128)S(1)}, u32[]{:S(2)}) copy-start(f32[32,144]{1,0:T(8,128)S(1)} %reshape.479) | copy-start | bytes 55300
  95.3 51.8 %copy-start.21 = (f32[4,256,16]{1,2,0:T(8,128)S(1)}, f32[4,256,16]{1,2,0:T(8,128)}, u32[]{:S(2)}) copy-start(f32[4,256,16]{1,2,0:T(8,128)} %param.21) | copy-start | bytes 196612
  95.3 51.8 %copy-start.29 = (f32[4,256,16]{1,2,0:T(8,128)S(1)}, f32[4,256,16]{1,2,0:T(8,128)}, u32[]{:S(2)}) copy-start(f32[4,256,16]{1,2,0:T(8,128)} %param.20) | copy-start | bytes 196612
  458.3 5.8 copy-start.36
  458.3 5.8 copy-start.45
  461.0 3.8 copy-start
  464.1 6.0 copy-start.30
  1037.5 3.7 copy-start.1
  1037.5 9.8 copy-start.5
  1037.5 18.4 %copy-start.31 = (f32[4,256]{1,0:T(4,128)S(1)}, f32[4,256]{1,0:T(4,128)}, u32[]{:S(2)}) copy-start(f32[4,256]{1,0:T(4,128)} %copy-done.30) | copy-start | bytes 12292
  1047.3 12.4 copy-start.17
  1047.3 12.5 copy-start.18
  1047.3 12.6 copy-start.23
  1055.9 13.3 %copy-start.13 = (bf16[144,1186]{1,0:T(8,128)(2,1)S(1)}, bf16[144,1186]{1,0:T(8,128)(2,1)}, u32[]{:S(2)}) copy-start(bf16[144,1186]{1,0:T(8,128)(2,1)} %copy-done.12) | copy-start | bytes 1024708
  1055.9 13.3 %copy-start.20 = (bf16[144,1186]{1,0:T(8,128)(2,1)S(1)}, bf16[144,1186]{1,0:T(8,128)(2,1)}, u32[]{:S(2)}) copy-start(bf16[144,1186]{1,0:T(8,128)(2,1)} %copy-done.19) | copy-start | bytes 1024708
  1059.2 61.5 %copy-start.8 = (bf16[144,1186]{1,0:T(8,128)(2,1)S(1)}, bf16[144,1186]{1,0:T(8,128)(2,1)}, u32[]{:S(2)}) copy-start(bf16[144,1186]{1,0:T(8,128)(2,1)} %copy-done.7) | copy-start | bytes 1024708
  1059.2 61.8 %copy-start.44 = (f32[16]{0:T(128)S(1)}, f32[16]{0:T(128)}, u32[]{:S(2)}) copy-start(f32[16]{0:T(128)} %get-tuple-element.86) | copy-start | bytes 196
  1059.5 72.7 %copy-start.43 = (s32[32]{0:T(128)S(1)}, s32[32]{0:T(128)}, u32[]{:S(2)}) copy-start(s32[32]{0:T(128)} %copy-done.42) | copy-start | bytes 388
  1059.8 74.5 %copy-start.24 = (f32[8,4,144]{2,1,0:T(4,128)S(1)}, f32[8,4,144]{2,1,0:T(4,128)}, u32[]{:S(2)}) copy-start(f32[8,4,144]{2,1,0:T(4,128)} %share.13) | copy-start | bytes 55300
  1119.5 17.1 %copy-start.14 = (bf16[8,32,144]{2,1,0:T(8,128)(2,1)S(1)}, bf16[8,32,144]{2,1,0:T(8,128)(2,1)}, u32[]{:S(2)}) copy-start(bf16[8,32,144]{2,1,0:T(8,128)(2,1)} %share.16) | copy-start | bytes 221188
  1158.5 7.4 copy-start.26
  1158.5 7.4 copy-start.28
  1200.0 23.5 %slice-start = ((s8[9289728]{0:T(1024)(128)(4,1)}), s8[4194304]{0:T(1024)(128)(4,1)S(1)}, s32[]{:S(2)}) async-start(s8[9289728]{0:T(1024)(128)(4,1)} %bitcast.112), calls=%async_computation.4 | async-start | bytes 8388608
  1203.6 14.3 %copy-start.9 = (f32[144,6912,1]{1,0,2:T(8,128)S(1)}, f32[144,6912,1]{1,0,2:T(8,128)}, u32[]{:S(2)}) copy-start(f32[144,6912,1]{1,0,2:T(8,128)} %get-tuple-element.119) | copy-start | bytes 11943940
  1207.7 15.8 %slice-start.1 = ((s8[9289728]{0:T(1024)(128)(4,1)}), s8[4194304]{0:T(1024)(128)(4,1)S(1)}, s32[]{:S(2)}) async-start(s8[9289728]{0:T(1024)(128)(4,1)} %bitcast.112), calls=%async_computation.5 | async-start | bytes 8388608
  1215.7 4.4 copy-start.11
  1215.7 4.4 copy-start.15
  1215.7 4.4 copy-start.16
  1217.8 4.2 copy-start.33
  1217.8 4.2 copy-start.38
  1217.8 4.2 copy-start.39
  1217.8 5.7 slice-start.2
  1223.5 20.9 %copy-start.4 = (f32[1,576,1152]{2,1,0:T(8,128)S(1)}, f32[1,576,1152]{2,1,0:T(8,128)}, u32[]{:S(2)}) copy-start(f32[1,576,1152]{2,1,0:T(8,128)} %param.26) | copy-start | bytes 7962628
  1244.4 7.9 copy-start.35
  1244.4 7.9 copy-start.40
  1244.4 7.9 copy-start.41
Sparse Core Ops, SparseCore 0:
  14.4 36.8 all-gather.7
  53.5 107.1 all-gather.5
  162.9 98.8 all-gather.9
  263.9 98.8 all-gather.11

commit v7 on v6

--- a/solution.py
+++ b/solution.py
@@ -190,7 +190,8 @@
 
 def sums_kernel(units, rows, *refs):
     lefts, rights, given = (refs[:4], refs[4:8], refs[8])
-    own_out, final_out, later_out, bias_out, spread_out = refs[9:14]
+    owns, finals, laters = (refs[9:11], refs[11:13], refs[13:15])
+    bias_out, spread_out, refs = (refs[15], refs[16], refs[17:])
     (
         left_v,
         right_v,
@@ -211,7 +212,7 @@
         pass_sem,
         given_send,
         given_recv,
-    ) = refs[14:]
+    ) = refs
     here = lax.axis_index("dp")
     core, chip = (lax.rem(here, 2), here // 2)
     partner = {"dp": here + 1 - 2 * core}
@@ -230,9 +231,17 @@
         copy.start()
         spreading.append(copy)
     spread_out[here] = given[...]
-    places = {FINAL: final_out, LATER: later_out, NEAR: near, FAR: far, PASS: passed}
+    places = {NEAR: near, FAR: far, PASS: passed}
+
+    def placed(pair, slot):
+        wide, down = pair
+        side_by_side = wide.shape[1] // D
+        if slot < side_by_side:
+            return wide.at[:, pl.ds(slot * D, D)]
+        return down.at[pl.ds((slot - side_by_side) * rows, rows)]
+
     plan, last, slots = ([], [None, None], [1, 1])
-    for left, left_at, right, right_at, gathers in units:
+    for left, left_at, right, right_at, gathers, slot in units:
         fresh = []
         for side, key in enumerate(((left, left_at), (right, right_at))):
             fresh.append(last[side] != key)
@@ -240,13 +249,8 @@
                 slots[side] = 1 - slots[side]
                 last[side] = key
         plan.append((tuple(slots), tuple(fresh)))
-    slot_of, used = ({}, 0)
-    for index, unit in enumerate(units):
-        slot_of[index] = used
-        used += unit[4] is None
-
     def loads_of(index):
-        left, left_at, right, right_at, gathers = units[index]
+        left, left_at, right, right_at, gathers, slot = units[index]
         (left_slot, right_slot), (left_fresh, right_fresh) = plan[index]
         copies = []
         if left_fresh:
@@ -292,9 +296,9 @@
                 copy.wait_send()
         slot, place = (index % 2, index % 4)
         product[slot] = contract(left_v[left_slot], right_v[right_slot], 0, 0)
-        if plan[index][1][1]:
+        if gathers is None or gathers == 0:
             ones = jnp.ones((8, right_v.shape[1]), jnp.bfloat16)
-            bias_out[index] = matmul(ones, right_v[right_slot])
+            bias_out[units[index][5]] = matmul(ones, right_v[right_slot])
         if gathers is None:
             crossing[index] = [
                 to_partner(
@@ -314,9 +318,10 @@
             ]
 
     def crossed(source, kind, slot, to, sem):
+        pair = {FINAL: finals, LATER: laters}.get(kind)
         return pltpu.make_async_remote_copy(
             src_ref=source,
-            dst_ref=places[kind].at[slot],
+            dst_ref=places[kind].at[slot] if pair is None else placed(pair, slot),
             send_sem=sem,
             recv_sem=block_sem.at[kind, slot],
             device_id={"dp": 2 * to + core},
@@ -366,7 +371,7 @@
             leaving[index].append((chip == at, copy.wait_send))
 
         keep = pltpu.make_async_copy(
-            own_v.at[side, block], own_out.at[slot], own_sem.at[side, block]
+            own_v.at[side, block], placed(owns, slot), own_sem.at[side, block]
         )
 
         @pl.when(chip == owner)
@@ -388,8 +393,8 @@
     def blocks_of(index):
         gathers = units[index][4]
         if gathers is None:
-            return [(owner, owner, slot_of[index]) for owner in (0, 3, 1, 2)]
-        return [(block, gathers, slot_of[index] + block) for block in range(CHIPS)]
+            return [(owner, owner, units[index][5]) for owner in (0, 3, 1, 2)]
+        return [(block, gathers, units[index][5] + block) for block in range(CHIPS)]
 
     def combine(index):
         for copy in crossing[index]:
@@ -458,14 +463,16 @@
     outs = pl.pallas_call(
         functools.partial(sums_kernel, units, rows),
         out_shape=[
-            jax.ShapeDtypeStruct((places,) + block, jnp.float32),
-            jax.ShapeDtypeStruct((places,) + block, jnp.bfloat16),
-            jax.ShapeDtypeStruct((places,) + block, jnp.bfloat16),
-            jax.ShapeDtypeStruct((len(units), 8, D), jnp.float32),
+            jax.ShapeDtypeStruct(shape, kind)
+            for kind in (jnp.float32, jnp.bfloat16, jnp.bfloat16)
+            for shape in ((rows, (places - CHIPS) * D), (CHIPS * rows, D))
+        ]
+        + [
+            jax.ShapeDtypeStruct((places - CHIPS + 1, 8, D), jnp.float32),
             jax.ShapeDtypeStruct((DIRECT,) + given.shape, given.dtype),
         ],
         in_specs=specs("h" * 8, "v"),
-        out_specs=specs("hhhvv"),
+        out_specs=specs("h" * 6, "vv"),
         scratch_shapes=[
             pltpu.VMEM((2, tokens, D), jnp.bfloat16),
             pltpu.VMEM((2, tokens, D), jnp.bfloat16),
@@ -497,8 +504,11 @@
         ),
         name="line_sums",
     )(*lefts, *rights, given)
-    total = outs[0] + outs[1].astype(jnp.float32) + outs[2].astype(jnp.float32)
-    return (total, outs[3][:, 0], outs[4])
+    wide, down = [
+        outs[i] + outs[2 + i].astype(jnp.float32) + outs[4 + i].astype(jnp.float32)
+        for i in range(2)
+    ]
+    return (wide, down, outs[6][:, 0], outs[7])
 
 
 def row_sums(lefts, rights, given):
@@ -511,16 +521,13 @@
         return (wide, sums[3], [column_sum(one) for one in rights], given)
     rows = D // count
     parts = FF // D
-    units = (
-        [(0, 0, 0, i * D, None) for i in range(3)]
-        + [(1, 0, 1, 0, None)]
-        + [(2, 0, 2, i * D, None) for i in range(parts)]
-        + [(3, i * D, 3, 0, i) for i in range(parts)]
-    )
-    total, bias, given_all = line_sums(tuple(units), lefts, rights, rows, 12, given)
-    wide = jnp.concatenate([total[i] for i in range(4 + parts)], axis=1)
+    attention = [(0, 0, 0, i * D, None, i) for i in range(3)] + [(1, 0, 1, 0, None, 3)]
+    hidden = [(2, 0, 2, i * D, None, 4 + i) for i in range(parts)]
+    second = [(3, i * D, 3, 0, i, 4 + parts) for i in (0, 3, 1, 2)]
+    units = hidden[:1] + second[:2] + hidden[1:2] + second[2:] + hidden[2:] + attention
+    wide, down, bias, given_all = line_sums(tuple(units), lefts, rights, rows, 12, given)
     sums = [bias[:3].reshape(-1), bias[3], bias[4 : 4 + parts].reshape(-1), bias[4 + parts]]
-    return (wide, total[4 + parts :].reshape(-1, D), sums, given_all)
+    return (wide, down, sums, given_all)
 
 
 GROUP = 4
@@ -653,7 +660,7 @@
     return hop
 
 
-def forward_kernel(sections, images, bias, qkv_bias, ada, tokens, wq, wp, wh, ws, *refs):
+def forward_kernel(sections, images, bias, qkv_bias, ada, tokens, wx, ws, *refs):
     count, patches = (len(KEPT), tokens.shape[1])
     outs, scratch = (refs[:count], refs[count:])
     kept = scratch[:count]
@@ -673,11 +680,11 @@
     ) = scratch[count:]
     section = lax.axis_index("section")
     loads = [
-        started(wq.at[:, cols], wq_v.at[:, cols], w_sem.at[i])
+        started(wx.at[:, cols], wq_v.at[:, cols], w_sem.at[i])
         for i, cols in enumerate(parts_of(3 * D, 3))
     ]
-    loads.append(started(wp, wp_v, w_sem.at[3]))
-    loads.append(started(wh, wh_v, w_sem.at[4]))
+    loads.append(started(wx.at[:, pl.ds(3 * D, D)], wp_v, w_sem.at[3]))
+    loads.append(started(wx.at[:, pl.ds(4 * D, FF)], wh_v, w_sem.at[4]))
     loads.append(started(ws, ws_v, w_sem.at[5]))
     meet("section", sections, section)
     hop = hop_of(send, received, send_sem, recv_sem, lax.rem(section + 1, sections))
@@ -772,7 +779,7 @@
                 hop(image, part).wait_send()
 
 
-def backward_kernel(sections, images, direct, ada, head_grad, wq, wp, wh, ws, *refs):
+def backward_kernel(sections, images, direct, ada, head_grad, wx, ws, *refs):
     reads, made, patches = (len(READ), len(MADE), head_grad.shape[1])
     sources, refs = (refs[:reads], refs[reads:])
     if direct:
@@ -815,9 +822,9 @@
     for name in READ:
         if name != SECOND:
             fetching(name, 0).start()
-    loads.append(started(wh, wh_v, w_sem.at[1]))
-    loads.append(started(wp, wp_v, w_sem.at[2]))
-    loads.append(started(wq, wq_v, w_sem.at[3]))
+    loads.append(started(wx.at[:, pl.ds(4 * D, FF)], wh_v, w_sem.at[1]))
+    loads.append(started(wx.at[:, pl.ds(3 * D, D)], wp_v, w_sem.at[2]))
+    loads.append(started(wx.at[:, pl.ds(0, 3 * D)], wq_v, w_sem.at[3]))
     spreading, passing = ([], [])
     if direct:
         barrier = pltpu.get_barrier_semaphore()
@@ -1018,7 +1025,7 @@
         out_shape=[
             jax.ShapeDtypeStruct((images,) + shape, kind) for shape, kind in sizes
         ],
-        in_specs=specs("vvv", "h" * 5),
+        in_specs=specs("vvv", "h" * 3),
         out_specs=specs("h" * len(KEPT)),
         scratch_shapes=[pltpu.VMEM(shape, kind) for shape, kind in sizes]
         + [pltpu.VMEM((D, patches), jnp.bfloat16)]
@@ -1045,7 +1052,7 @@
         ]
         + [jax.ShapeDtypeStruct((images, 8, D), jnp.float32)]
         + films,
-        in_specs=specs("v", "h" * (5 + len(READ)), "v" * direct),
+        in_specs=specs("v", "h" * (3 + len(READ)), "v" * direct),
         out_specs=specs("h" * (len(MADE) + 1), "v" * len(films)),
         scratch_shapes=[
             pltpu.VMEM(kept_shape(name, KEPT[name][0], patches), KEPT[name][1]) for name in READ
@@ -1156,9 +1163,7 @@
 
     in_low = w_in[0].astype(low)
     w_ada = in_low[:, ada_at:]
-    w_qkv = gathered(in_low[:, : 3 * D])
-    w_proj = gathered(in_low[:, 3 * D : 4 * D])
-    w_hidden = gathered(in_low[:, 4 * D : ada_at])
+    w_tokens = gathered(in_low[:, :ada_at])
     w_second = gathered(w_down[0].astype(low))
 
     small_low = small_mats.astype(low)
@@ -1182,7 +1187,7 @@
     labels_all = blocks[:, ends[3] : ends[4]].reshape(-1).astype(jnp.int32)
     valid_total = jnp.sum(blocks[:, ends[4]])
     inv_count = 1.0 / (valid_total * PATCH_IN)
-    weights = (w_qkv, w_proj, w_hidden, w_second)
+    weights = (w_tokens, w_second)
 
     small_width = small_mats.shape[1]
     sbias_width = small_bias.shape[0]
@@ -1329,6 +1334,9 @@
         sbias_grad, section_index * sbias_width, sbias_width, 0
     )
 
+    shard_in, shard_down, small_shard, sbias_shard, shard_bias = lax.optimization_barrier(
+        (shard_in, shard_down, small_shard, sbias_shard, shard_bias)
+    )
     dp_zero = (dp_index == 0).astype(jnp.float32)
     squares = (
         jnp.sum(shard_in * shard_in)

time: 1270 us -> 1160 us (0.913)
  local copies, waits for them, and re-layouts: 83 us -> 32.2 us
  Pallas kernels: 829 us -> 800 us
  waiting for transfers between devices: 213 us -> 185 us
    pallas_call x10, Pallas kernels: 177 us -> 131 us  [share(): pl.pallas_call(functools.partial(share_kernel, axis, count, personal), ou...]
    unnamed x131 -> x87, local copies, waits for them, and re-layouts: 52.2 us -> 6.92 us
    all_gather x4 -> x2, waiting for transfers between devices: 212 us -> 185 us  [gathered(): return lax.all_gather(value, axis, axis=dim, tiled=True)]
    pallas_call x1, Pallas kernels: 272 us -> 289 us  [line_sums(): pl.pallas_call(functools.partial(sums_kernel, units, rows), out_shape=[ja...]
  transfers between devices with their start and end apart: 4 -> 2, of which waited for: 3 -> 1; matrix products, arithmetic and copies ran while one was open for 3% -> 3% of each run, Pallas kernels for 8% -> 8%
where the time goes in v7:
time: 1160 us; the launch traced here: 1150 us
  Pallas kernels  800 us (69%)
  waiting for transfers between devices  185 us (16%)
  other arithmetic  85.3 us (7%)
  local copies, waits for them, and re-layouts  32.2 us (3%)
  matrix products  27.1 us (2%)
  between operations  22.3 us (2%)
    pallas_call x1, Pallas kernels, line_sums(): pl.pallas_call(functools.partial(sums_kernel, units, rows), out_shape=[ja...  289 us
    pallas_call x1, Pallas kernels, pipeline_backward(): pl.pallas_call(functools.partial(backward_kernel, sections, images, direc...  285 us
    all_gather x2, waiting for transfers between devices, gathered(): return lax.all_gather(value, axis, axis=dim, tiled=True)  185 us
    pallas_call x10, Pallas kernels, share(): pl.pallas_call(functools.partial(share_kernel, axis, count, personal), ou...  131 us
    pallas_call x1, Pallas kernels, pipeline_forward(): pl.pallas_call(functools.partial(forward_kernel, sections, images), out_s...  95.5 us
    sub x5, other arithmetic, adam_update(): return (weight - RATE * (ratio + DECAY * weight), first_new, second_new)  31.3 us
  transfers between devices with their start and end apart: 2, of which 1 were waited for; matrix products, arithmetic and copies ran while one was open for 3% of the time, Pallas kernels for 8%

profile of v7, /device:TPU:0, one launch (start us, length us, event | category | flops | bytes accessed | tf_op | source)
XLA Modules:
  0.0 1152.0 jit_solution(14468659467015753823)
XLA Ops:
  7.2 2.9 convert_element_type.176
  10.3 4.1 convert_bitcast_fusion
  14.4 2.2 copy-done.2
  16.5 1.8 slice.241
  18.5 0.8 pad_maximum_fusion.5.in_ref
  19.3 23.9 %share.11 = bf16[4,146,1186]{2,1,0:T(8,128)(2,1)} custom-call(bf16[146,1186]{1,0:T(8,128)(2,1)} %pad_maximum_fusion.5.in_ref), custom_call_target="tpu_custom_call" | custom-call | tf_op jit(solution)/shard_map/share/pallas_call | solution.py:160
  43.2 1.0 slice.184
  45.7 1.2 fusion.88
  48.3 10.5 share.10
  58.8 0.9 copy.78
  60.8 1.7 broadcast_in_dim.30.qkv_bias
  64.0 0.7 reshape.248.in_ref
  64.7 13.9 %share.12 = f32[8,4,1296]{2,1,0:T(4,128)} custom-call(f32[8,4,1296]{2,1,0:T(4,128)} %reshape.248.in_ref), custom_call_target="tpu_custom_call" | custom-call | tf_op jit(solution)/shard_map/share/pallas_call | solution.py:160
  78.6 1.0 slice_reduce_fusion
  79.8 1.4 fusion.45.in_ref
  81.2 8.4 share.13
  89.6 0.8 reshape.249
  90.8 2.0 fusion.8
  92.9 1.2 reshape.250.in_ref
  94.0 39.7 %share.14 = f32[8,288,128]{2,1,0:T(8,128)} custom-call(f32[8,288,128]{2,1,0:T(8,128)} %reshape.250.in_ref), custom_call_target="tpu_custom_call" | custom-call | tf_op jit(solution)/shard_map/share/pallas_call | solution.py:160
  133.7 1.3 reduce_sum.261
  137.3 3.8 multiply_cosine_fusion
  141.1 1.6 concatenate.60
  144.2 3.0 fusion.2.tokens
  147.3 184.8 %all-gather.4.cloned.1.call-done.wx = bf16[1152,9216]{1,0:T(8,128)(2,1)} async-done(((bf16[144,9216]{1,0:T(8,128)(2,1)}), bf16[1152,9216]{1,0:T(8,128)(2,1)}) %all-gather.4.cloned.1.call-update) | async-done | bytes 21233680 | tf_op jit(solution)/shard_map/all_gather | solution.py:1162
  332.1 95.5 %pipeline_forward.1 = (f32[4,256,1152]{2,1,0:T(8,128)}, bf16[4,256,1152]{2,1,0:T(8,128)(2,1)}, bf16[4,3456,256]{2,1,0:T(8,128)(2,1)}, bf16[4,256,1152]{2,1,0:T(8...) custom-call(f32[1,6912]{1,0:T(1,128)} %broadcast_in_dim.22.bias, ...), custom_call_target="tpu_custom_call" | custom-call | flops 33822867456 | bytes 107347968 | tf_op jit(solution)/shard_map/pipeline_forward/pallas_call | solution.py:1023
  427.6 2.6 reduce_sum.262
  430.2 3.1 multiply_reduce_fusion.3
  434.0 1.8 convert_reduce_fusion.4
  435.8 2.9 multiply_reduce_fusion.1
  439.3 2.9 subtract_multiply_fusion.head_grad
  442.2 284.6 %pipeline_backward.1 = (bf16[4,256,1152]{2,1,0:T(8,128)(2,1)}, bf16[4,256,4608]{2,1,0:T(8,128)(2,1)}, bf16[4,256,1152]{2,1,0:T(8,128)(2,1)}, bf16[4,256,3456]{2,...) custom-call(f32[4,6,1152]{2,1,0:T(8,128)} %reshape.252.ada, ...), custom_call_target="tpu_custom_call" | custom-call | flops 35634806784 | bytes 107347968 | tf_op jit(solution)/shard_map/pipeline_backward/pallas_call | solution.py:1048
  726.8 0.9 fusion.48
  728.4 289.3 %line_sums.1 = (f32[144,9216]{1,0:T(8,128)}, f32[576,1152]{1,0:T(8,128)}, bf16[144,9216]{1,0:T(8,128)(2,1)}, bf16[576,1152]{1,0:T(8,128)(2,1)}, bf16[144,9216]{1...) custom-call(bf16[1024,1152]{1,0:T(8,128)(2,1)} %bitcast.123, ...), custom_call_target="tpu_custom_call" | custom-call | flops 32614907904 | bytes 56623104 | tf_op jit(solution)/shard_map/line_sums/pallas_call | solution.py:463
  1017.7 0.9 slice_reduce_fusion.5
  1018.6 1.0 slice_reduce_fusion.4
  1019.6 2.1 convolution_bitcast_fusion.3
  1021.7 2.1 convert_reduce_fusion
  1023.8 2.8 convolution_bitcast_fusion
  1026.7 2.9 fusion.19.in_ref
  1029.7 6.3 share.15
  1036.0 1.9 fusion.22.in_ref
  1037.9 7.2 share.16
  1045.1 1.0 fusion.32
  1046.1 1.0 copy.62
  1047.9 1.5 convolution_bitcast_fusion.1
  1049.6 3.2 fusion.5
  1053.5 0.8 broadcast_in_dim.28.in_ref
  1054.3 7.8 share.17
  1062.1 0.9 copy.77
  1064.7 5.0 convert_add_fusion
  1069.6 6.4 pad_maximum_fusion
  1076.1 4.1 concatenate.65
  1080.2 1.5 constant_dynamic-slice_fusion
  1081.9 3.3 convert_add_fusion.1
  1085.7 3.0 multiply_reduce_fusion
  1088.7 1.3 multiply_reduce_fusion.5
  1090.5 0.8 multiply_reduce_fusion.6
  1095.9 7.4 share.18
  1103.3 1.3 reduce_sum.287.in_ref
  1104.6 5.8 share.19
  1112.4 23.7 %multiply_subtract_fusion = (f32[1,144,16128]{2,1,0:T(8,128)}, f32[1,144,16128]{2,1,0:T(8,128)}, f32[1,144,16128]{2,1,0:T(8,128)}) fusion(f32[1,144,16128]{2,1,0:T(8,128)} %param.25, f32[144,16128]{1,0:T(8,128)} %pad_maximum_fusion, f32[]{:T(128)S(6)} %min.3, f32[1,144,16128]{2,1,0:T(8,128)} %param.30, f32[1,144,16128]{2,1,0:T(8,128)} %param.35), kind=kLoop, calls=%fused_computation.5 | loop fusion | flops 37158912 | bytes 65028100 | tf_op jit(solution)/shard_map/sub | solution.py:1121
  1136.2 4.5 multiply_subtract_fusion.1
  1140.8 1.7 multiply_subtract_fusion.2
  (184 shorter events, 18.3 us)
Async XLA Ops:
  7.2 140.1 %all-gather.6.cloned.1.call-start = ((), (), s32[]{:S(2)}) async-start(), calls=%async_computation.1 | async-start | bytes 11943936 | tf_op jit(solution)/shard_map/all_gather | solution.py:1162
  10.2 321.9 %all-gather.4.cloned.1.call-start = ((), (), s32[]{:S(2)}) async-start(), calls=%async_computation | async-start | bytes 23887872 | tf_op jit(solution)/shard_map/all_gather | solution.py:1162
  14.4 2.2 copy-start.2
  16.5 1.8 copy-start.21
  16.5 1.9 copy-start.5
  18.3 27.4 %copy-start.36 = (s32[4]{0:T(128)S(1)}, s32[4]{0:T(128)}, u32[]{:S(2)}) copy-start(s32[4]{0:T(128)} %param.22) | copy-start | bytes 52
  18.3 27.4 %copy-start.35 = (s32[4]{0:T(128)S(1)}, s32[4]{0:T(128)}, u32[]{:S(2)}) copy-start(s32[4]{0:T(128)} %param.23) | copy-start | bytes 52
  18.3 27.4 %copy-start.26 = (s32[4,256]{1,0:T(4,128)S(1)}, s32[4,256]{1,0:T(4,128)}, u32[]{:S(2)}) copy-start(s32[4,256]{1,0:T(4,128)} %param.24) | copy-start | bytes 12292
  18.3 29.3 %copy-start.23 = (f32[1,2016]{1,0:T(1,128)S(1)}, f32[1,2016]{1,0:T(1,128)}, u32[]{:S(2)}) copy-start(f32[1,2016]{1,0:T(1,128)} %param.27) | copy-start | bytes 24196
  43.2 19.9 %copy-start.4 = (bf16[4,146,1186]{2,1,0:T(8,128)(2,1)S(1)}, bf16[4,146,1186]{2,1,0:T(8,128)(2,1)}, u32[]{:S(2)}) copy-start(bf16[4,146,1186]{2,1,0:T(8,128)(2,1)} %share.11) | copy-start | bytes 4155748
  62.7 30.0 %copy-start.31 = (s32[32]{0:T(128)}, s32[32]{0:T(128)S(1)}, u32[]{:S(2)}) copy-start(s32[32]{0:T(128)S(1)} %convert_element_type.167) | copy-start | bytes 388
  63.2 29.7 %copy-start.14 = (bf16[144,1186]{1,0:T(8,128)(2,1)}, bf16[144,1186]{1,0:T(8,128)(2,1)S(1)}, u32[]{:S(2)}) copy-start(bf16[144,1186]{1,0:T(8,128)(2,1)S(1)} %get-tuple-element.105) | copy-start | bytes 1024708
  94.0 50.0 %copy-start.16 = (f32[4,256,16]{1,2,0:T(8,128)S(1)}, f32[4,256,16]{1,2,0:T(8,128)}, u32[]{:S(2)}) copy-start(f32[4,256,16]{1,2,0:T(8,128)} %param.21) | copy-start | bytes 196612
  94.0 50.0 %copy-start.19 = (f32[4,256,16]{1,2,0:T(8,128)S(1)}, f32[4,256,16]{1,2,0:T(8,128)}, u32[]{:S(2)}) copy-start(f32[4,256,16]{1,2,0:T(8,128)} %param.20) | copy-start | bytes 196612
  141.1 6.1 copy-start.20
  427.6 5.8 copy-start.25
  427.6 5.8 copy-start.34
  430.2 3.8 copy-start
  728.4 291.2 %copy-start.17 = (f32[4,8,1152]{2,1,0:T(8,128)S(1)}, f32[4,8,1152]{2,1,0:T(8,128)}, u32[]{:S(2)}) copy-start(f32[4,8,1152]{2,1,0:T(8,128)} %get-tuple-element.63) | copy-start | bytes 442372
  1017.7 6.1 copy-start.13
  1017.7 6.1 copy-start.18
  1023.8 2.9 copy-start.12
  1023.8 12.2 %copy-start.15 = (bf16[144,1186]{1,0:T(8,128)(2,1)S(1)}, bf16[144,1186]{1,0:T(8,128)(2,1)}, u32[]{:S(2)}) copy-start(bf16[144,1186]{1,0:T(8,128)(2,1)} %copy-done.14) | copy-start | bytes 1024708
  1026.6 18.5 %copy-start.32 = (s32[32]{0:T(128)S(1)}, s32[32]{0:T(128)}, u32[]{:S(2)}) copy-start(s32[32]{0:T(128)} %copy-done.31) | copy-start | bytes 388
  1049.4 13.9 %copy-start.9 = (bf16[8,32,144]{2,1,0:T(8,128)(2,1)S(1)}, bf16[8,32,144]{2,1,0:T(8,128)(2,1)}, u32[]{:S(2)}) copy-start(bf16[8,32,144]{2,1,0:T(8,128)(2,1)} %share.16) | copy-start | bytes 221188
  1076.1 5.7 copy-start.33
  1080.2 5.5 copy-start.1
  1112.4 23.8 %copy-start.3 = (f32[1,576,1152]{2,1,0:T(8,128)S(1)}, f32[1,576,1152]{2,1,0:T(8,128)}, u32[]{:S(2)}) copy-start(f32[1,576,1152]{2,1,0:T(8,128)} %param.26) | copy-start | bytes 7962628
  1112.4 23.8 %copy-start.7 = (f32[1,576,1152]{2,1,0:T(8,128)S(1)}, f32[1,576,1152]{2,1,0:T(8,128)}, u32[]{:S(2)}) copy-start(f32[1,576,1152]{2,1,0:T(8,128)} %param.31) | copy-start | bytes 7962628
  1112.4 23.8 %copy-start.8 = (f32[1,576,1152]{2,1,0:T(8,128)S(1)}, f32[1,576,1152]{2,1,0:T(8,128)}, u32[]{:S(2)}) copy-start(f32[1,576,1152]{2,1,0:T(8,128)} %param.36) | copy-start | bytes 7962628
  1136.2 4.6 copy-start.6
  1136.2 4.6 copy-start.10
  1136.2 4.6 copy-start.11
  1140.8 1.8 copy-start.22
  1140.8 1.8 copy-start.27
  1140.8 1.8 copy-start.28
  1140.8 2.4 copy-start.24
  1140.8 2.4 copy-start.29
  1140.8 2.4 copy-start.30
Sparse Core Ops, SparseCore 0:
  10.3 133.9 all-gather.5
  146.6 185.4 all-gather.3

commit v8 on v7

--- a/solution.py
+++ b/solution.py
@@ -124,41 +124,54 @@
     return lax.reduce_precision(values, 8, 7)
 
 
-def meet(axis, count, here):
+def meet(axis, count, here, stride=1):
     barrier = pltpu.get_barrier_semaphore()
     for step in range(1, count):
         pl.semaphore_signal(
-            barrier, inc=1, device_id={axis: lax.rem(here + step, count)}, device_id_type=MESH
+            barrier,
+            inc=1,
+            device_id={axis: lax.rem(here + step * stride, count * stride)},
+            device_id_type=MESH,
         )
     pl.semaphore_wait(barrier, count - 1)
 
 
-def share_kernel(axis, count, personal, in_ref, out_ref, send_sem, recv_sem):
+def meet_both(sections, section, here):
+    barrier = pltpu.get_barrier_semaphore()
+    for axis, me, size in (("section", section, sections), ("dp", here, DIRECT)):
+        for step in range(1, size):
+            pl.semaphore_signal(
+                barrier, inc=1, device_id={axis: lax.rem(me + step, size)}, device_id_type=MESH
+            )
+    pl.semaphore_wait(barrier, sections + DIRECT - 2)
+
+
+def share_kernel(axis, count, stride, personal, in_ref, out_ref, send_sem, recv_sem):
     here = lax.axis_index(axis)
-    meet(axis, count, here)
+    meet(axis, count, here, stride)
+    place = here // stride
     copies = []
     for step in range(1, count):
-        target = lax.rem(here + step, count)
         copy = pltpu.make_async_remote_copy(
-            src_ref=in_ref.at[target] if personal else in_ref,
-            dst_ref=out_ref.at[here],
+            src_ref=in_ref.at[lax.rem(place + step, count)] if personal else in_ref,
+            dst_ref=out_ref.at[place],
             send_sem=send_sem.at[step - 1],
             recv_sem=recv_sem.at[step - 1],
-            device_id={axis: target},
+            device_id={axis: lax.rem(here + step * stride, count * stride)},
             device_id_type=MESH,
         )
         copy.start()
         copies.append(copy)
-    out_ref[here] = in_ref[here] if personal else in_ref[...]
+    out_ref[place] = in_ref[place] if personal else in_ref[...]
     for copy in copies:
         copy.wait()
 
 
-def share(value, axis, personal, ident):
-    count = lax.axis_size(axis)
+def share(value, axis, personal, ident, stride=1):
+    count = lax.axis_size(axis) // stride
     shape = value.shape if personal else (count,) + value.shape
     return pl.pallas_call(
-        functools.partial(share_kernel, axis, count, personal),
+        functools.partial(share_kernel, axis, count, stride, personal),
         out_shape=jax.ShapeDtypeStruct(shape, value.dtype),
         in_specs=[pl.BlockSpec(memory_space=pltpu.VMEM)],
         out_specs=pl.BlockSpec(memory_space=pltpu.VMEM),
@@ -177,6 +190,18 @@
     return share(value, axis, False, ident)
 
 
+def exchanged_sum(value, ident):
+    count = lax.axis_size("dp")
+    if count != DIRECT:
+        return jnp.sum(exchange(value, "dp", ident), axis=0)
+    core = lax.axis_index("dp") % 2
+    parted = value.reshape((count // 2, 2) + value.shape[1:])
+    other = lax.dynamic_index_in_dim(parted, 1 - core, 1, keepdims=False)
+    same = lax.dynamic_index_in_dim(parted, core, 1, keepdims=False)
+    both = same + lax.ppermute(other, "dp", [(i, i ^ 1) for i in range(count)])
+    return jnp.sum(share(both, "dp", True, ident, 2), axis=0)
+
+
 def exchange(value, axis, ident):
     if lax.axis_size(axis) > DIRECT:
         return lax.all_to_all(value, axis, 0, 0)
@@ -188,10 +213,11 @@
 CHIPS = 4
 
 
-def sums_kernel(units, rows, *refs):
-    lefts, rights, given = (refs[:4], refs[4:8], refs[8])
-    owns, finals, laters = (refs[9:11], refs[11:13], refs[13:15])
-    bias_out, spread_out, refs = (refs[15], refs[16], refs[17:])
+def sums_kernel(units, rows, sections, *refs):
+    lefts, rights = (refs[:4], refs[4:8])
+    given, w_ada, slope, head_part, refs = (refs[8], refs[9], refs[10], refs[11], refs[12:])
+    owns, finals, laters = (refs[0:2], refs[2:4], refs[4:6])
+    bias_out, spread_out, cond_out, refs = (refs[6], refs[7], refs[8], refs[9:])
     (
         left_v,
         right_v,
@@ -212,12 +238,17 @@
         pass_sem,
         given_send,
         given_recv,
+        cond_pieces,
+        cond_low,
+        cond_send,
+        cond_recv,
     ) = refs
     here = lax.axis_index("dp")
     core, chip = (lax.rem(here, 2), here // 2)
     partner = {"dp": here + 1 - 2 * core}
     tall = CHIPS * rows
-    meet("dp", DIRECT, here)
+    section = lax.axis_index("section")
+    meet_both(sections, section, here)
     spreading = []
     for step in range(1, DIRECT):
         copy = pltpu.make_async_remote_copy(
@@ -232,6 +263,48 @@
         spreading.append(copy)
     spread_out[here] = given[...]
     places = {NEAR: near, FAR: far, PASS: passed}
+    shared = []
+
+    def share_pieces():
+        for copy in spreading:
+            copy.wait()
+        each = given.shape[0]
+        for i in range(DIRECT):
+            at = slice(i * each, (i + 1) * each)
+            cond_pieces[section, at] = contract(spread_out[i], w_ada[...], 1, 1) * slope[at]
+        for step in range(1, sections):
+            copy = pltpu.make_async_remote_copy(
+                src_ref=cond_pieces.at[section],
+                dst_ref=cond_pieces.at[section],
+                send_sem=cond_send.at[step - 1],
+                recv_sem=cond_recv.at[step - 1],
+                device_id={"section": lax.rem(section + step, sections)},
+                device_id_type=MESH,
+            )
+            copy.start()
+            shared.append(copy)
+
+    def share_rows():
+        for copy in shared:
+            copy.wait()
+        value = head_part[...]
+        for layer in reversed(range(sections)):
+            value = (value + cond_pieces[layer]).astype(jnp.bfloat16).astype(jnp.float32)
+        cond_low[...] = value.astype(jnp.bfloat16)
+        cond_out[here] = value.astype(jnp.bfloat16)
+        shared.clear()
+        for step in range(1, DIRECT):
+            copy = pltpu.make_async_remote_copy(
+                src_ref=cond_low,
+                dst_ref=cond_out.at[here],
+                send_sem=cond_send.at[sections + step],
+                recv_sem=cond_recv.at[sections + step],
+                device_id={"dp": lax.rem(here + step, DIRECT)},
+                device_id_type=MESH,
+            )
+            copy.start()
+            shared.append(copy)
+
 
     def placed(pair, slot):
         wide, down = pair
@@ -295,7 +368,12 @@
             for copy in crossing[index - 2]:
                 copy.wait_send()
         slot, place = (index % 2, index % 4)
-        product[slot] = contract(left_v[left_slot], right_v[right_slot], 0, 0)
+
+        @pl.loop(0, 3)
+        def tile(step):
+            at = pl.ds(pl.multiple_of(step * (D // 3), 128), D // 3)
+            product[slot, at] = contract(left_v[left_slot, :, at], right_v[right_slot], 0, 0)
+
         if gathers is None or gathers == 0:
             ones = jnp.ones((8, right_v.shape[1]), jnp.bfloat16)
             bias_out[units[index][5]] = matmul(ones, right_v[right_slot])
@@ -432,6 +510,10 @@
         combine(index)
         if index >= 1:
             pass_on(index - 1)
+        if index == 2:
+            share_pieces()
+        elif index == 5:
+            share_rows()
     pass_on(total - 1)
     for index in range(max(0, total - 3), total):
         finish(index)
@@ -452,16 +534,17 @@
                 def sent(slot=slot, owner=owner):
                     crossed(passed.at[slot], LATER, slot, owner, pass_sem.at[slot]).wait_send()
 
-    for copy in spreading:
+    for copy in shared:
         copy.wait()
 
 
-def line_sums(units, lefts, rights, rows, ident, given):
+def line_sums(units, lefts, rights, rows, ident, given, w_ada, slope, head_part):
+    sections = lax.axis_size("section")
     tokens = lefts[0].shape[0]
     places = sum(unit[4] is None for unit in units) + 4
     block = (rows, D)
     outs = pl.pallas_call(
-        functools.partial(sums_kernel, units, rows),
+        functools.partial(sums_kernel, units, rows, sections),
         out_shape=[
             jax.ShapeDtypeStruct(shape, kind)
             for kind in (jnp.float32, jnp.bfloat16, jnp.bfloat16)
@@ -470,9 +553,10 @@
         + [
             jax.ShapeDtypeStruct((places - CHIPS + 1, 8, D), jnp.float32),
             jax.ShapeDtypeStruct((DIRECT,) + given.shape, given.dtype),
+            jax.ShapeDtypeStruct((DIRECT,) + slope.shape, jnp.bfloat16),
         ],
-        in_specs=specs("h" * 8, "v"),
-        out_specs=specs("h" * 6, "vv"),
+        in_specs=specs("h" * 8, "vvvv"),
+        out_specs=specs("h" * 6, "vvv"),
         scratch_shapes=[
             pltpu.VMEM((2, tokens, D), jnp.bfloat16),
             pltpu.VMEM((2, tokens, D), jnp.bfloat16),
@@ -493,6 +577,10 @@
             pltpu.SemaphoreType.DMA((places,)),
             pltpu.SemaphoreType.DMA((DIRECT - 1,)),
             pltpu.SemaphoreType.DMA((DIRECT - 1,)),
+            pltpu.VMEM((sections,) + slope.shape, jnp.float32),
+            pltpu.VMEM(slope.shape, jnp.bfloat16),
+            pltpu.SemaphoreType.DMA((sections + DIRECT,)),
+            pltpu.SemaphoreType.DMA((sections + DIRECT,)),
         ],
         compiler_params=pltpu.CompilerParams(
             collective_id=ident, has_side_effects=True, vmem_limit_bytes=62 << 20
@@ -503,31 +591,38 @@
             transcendentals=0,
         ),
         name="line_sums",
-    )(*lefts, *rights, given)
+    )(*lefts, *rights, given, w_ada, slope, head_part)
     wide, down = [
         outs[i] + outs[2 + i].astype(jnp.float32) + outs[4 + i].astype(jnp.float32)
         for i in range(2)
     ]
-    return (wide, down, outs[6][:, 0], outs[7])
-
-
-def row_sums(lefts, rights, given):
+    return (wide, down, outs[6][:, 0], outs[7], outs[8])
+
+
+def row_sums(lefts, rights, given, w_ada, slope, head_part):
     count = lax.axis_size("dp")
     if count != DIRECT:
         products = [matmul_tn(one, other) for one, other in zip(lefts, rights)]
         sums = [lax.psum_scatter(one, "dp", scatter_dimension=0, tiled=True) for one in products]
         wide = jnp.concatenate([sums[0], sums[1], sums[2]], axis=1)
         given = lax.all_gather(given, "dp")
-        return (wide, sums[3], [column_sum(one) for one in rights], given)
+        pieces = matmul_nt(given.reshape(-1, given.shape[2]), w_ada) * slope
+        pieces = lax.all_gather(pieces, "section")
+        for layer in reversed(range(lax.axis_size("section"))):
+            head_part = rounded(head_part + pieces[layer])
+        conds = lax.all_gather(head_part.astype(jnp.bfloat16), "dp")
+        return (wide, sums[3], [column_sum(one) for one in rights], given, conds)
     rows = D // count
     parts = FF // D
     attention = [(0, 0, 0, i * D, None, i) for i in range(3)] + [(1, 0, 1, 0, None, 3)]
     hidden = [(2, 0, 2, i * D, None, 4 + i) for i in range(parts)]
     second = [(3, i * D, 3, 0, i, 4 + parts) for i in (0, 3, 1, 2)]
     units = hidden[:1] + second[:2] + hidden[1:2] + second[2:] + hidden[2:] + attention
-    wide, down, bias, given_all = line_sums(tuple(units), lefts, rights, rows, 12, given)
+    wide, down, bias, given_all, conds = line_sums(
+        tuple(units), lefts, rights, rows, 12, given, w_ada, slope, head_part
+    )
     sums = [bias[:3].reshape(-1), bias[3], bias[4 : 4 + parts].reshape(-1), bias[4 + parts]]
-    return (wide, down, sums, given_all)
+    return (wide, down, sums, given_all, conds)
 
 
 GROUP = 4
@@ -827,13 +922,7 @@
     loads.append(started(wx.at[:, pl.ds(0, 3 * D)], wq_v, w_sem.at[3]))
     spreading, passing = ([], [])
     if direct:
-        barrier = pltpu.get_barrier_semaphore()
-        for axis, me, size in (("section", section, sections), ("dp", here, DIRECT)):
-            for step in range(1, size):
-                pl.semaphore_signal(
-                    barrier, inc=1, device_id={axis: lax.rem(me + step, size)}, device_id_type=MESH
-                )
-        pl.semaphore_wait(barrier, sections + DIRECT - 2)
+        meet_both(sections, section, here)
         for step in range(1, DIRECT):
             copy = pltpu.make_async_remote_copy(
                 src_ref=film,
@@ -1225,8 +1314,8 @@
     ada_part = jnp.concatenate(
         [matmul(act_here, w_ada), matmul(act_later, small_rows[:, o_film:o_out])], axis=1
     )
-    ada_got = exchange(ada_part.reshape(shards, images * 8 * D // 128, 128), "dp", 5)
-    ada_own = jnp.sum(ada_got, axis=0).reshape(images, 8 * D)
+    ada_own = exchanged_sum(ada_part.reshape(shards, images * 8 * D // 128, 128), 5)
+    ada_own = ada_own.reshape(images, 8 * D)
     film = ada_own[:, 6 * D :] + small_used[3 * D : 5 * D]
     ada = (ada_own[:, : 6 * D] + bias_full[ada_at:]).reshape(images, 6, D)
     qkv_bias = jnp.concatenate(
@@ -1269,20 +1358,19 @@
         matmul_tn(d_tokens, noisy_low.reshape(images * patches, PATCH_IN)),
         g_output,
     )
-    shard_wide, shard_down, right_sums, d_ada_all = row_sums(
+    d_cond = matmul_nt(film_all, small_rows[:, o_film:o_out]) * silu_grad(cond_later)
+    shard_wide, shard_down, right_sums, d_ada_all, conds = row_sums(
         [flat(kept_all[name]) for name in (MIXED_ONE, ATT, MIXED_TWO, ACT)],
         [d_qkv, d_branch, d_pre, d_second],
         d_ada,
+        w_ada,
+        silu_grad(cond_here),
+        d_cond,
     )
     d_ada_all = d_ada_all.reshape(shards * images, 6 * D)
 
-    cond_piece = matmul_nt(d_ada_all, w_ada) * silu_grad(cond_here)
-    cond_pieces = spread(cond_piece, "section", 9)
-    d_cond = matmul_nt(film_all, small_rows[:, o_film:o_out]) * silu_grad(cond_later)
-    for layer in reversed(range(sections)):
-        d_cond = rounded(d_cond + cond_pieces[layer])
-    d_cond_rows = d_cond.astype(low)
-    d_cond_all = jnp.swapaxes(spread(d_cond_rows, "dp", 10), 0, 1).reshape(shards * images, D)
+    d_cond_rows = lax.dynamic_index_in_dim(conds, dp_index, 0, keepdims=False)
+    d_cond_all = jnp.swapaxes(conds, 0, 1).reshape(shards * images, D)
     d_time = (
         matmul_nt(d_cond_all, small_rows[:, o_second:o_film]) * silu_grad(time_hidden)
     ).astype(low)

time: 1160 us -> 1120 us (0.966)
  Pallas kernels: 800 us -> 775 us
  waiting for transfers between devices: 185 us -> 172 us
    pallas_call x11 -> x9, Pallas kernels: 420 us -> 390 us  [the longest x1 293 us: line_sums(): pl.pallas_call(functools.partial(sums_kernel, units, rows, sections), out...]
    all_gather x2, waiting for transfers between devices: 185 us -> 172 us  [gathered(): return lax.all_gather(value, axis, axis=dim, tiled=True)]
  transfers between devices with their start and end apart: 2 -> 3, of which waited for: 1 -> 1; matrix products, arithmetic and copies ran while one was open for 3% -> 4% of each run, Pallas kernels for 8% -> 7%
where the time goes in v8:
time: 1120 us
  Pallas kernels  775 us (69%)
  waiting for transfers between devices  172 us (15%)
  other arithmetic  91.7 us (8%)
  local copies, waits for them, and re-layouts  33.2 us (3%)
  between operations  22.5 us (2%)
  matrix products  22.3 us (2%)
    pallas_call x1, Pallas kernels, line_sums(): pl.pallas_call(functools.partial(sums_kernel, units, rows, sections), out...  293 us
    pallas_call x1, Pallas kernels, pipeline_backward(): pl.pallas_call(functools.partial(backward_kernel, sections, images, direc...  290 us
    all_gather x2, waiting for transfers between devices, gathered(): return lax.all_gather(value, axis, axis=dim, tiled=True)  172 us
    pallas_call x8, Pallas kernels, share(): pl.pallas_call(functools.partial(share_kernel, axis, count, stride, perso...  97.5 us
    pallas_call x1, Pallas kernels, pipeline_forward(): pl.pallas_call(functools.partial(forward_kernel, sections, images), out_s...  95.5 us
    sub x5, other arithmetic, adam_update(): return (weight - RATE * (ratio + DECAY * weight), first_new, second_new)  32.8 us
  transfers between devices with their start and end apart: 3, of which 1 were waited for; matrix products, arithmetic and copies ran while one was open for 4% of the time, Pallas kernels for 7%

profile of v8, /device:TPU:0, one launch (start us, length us, event | category | flops | bytes accessed | tf_op | source)
XLA Modules:
  0.0 1118.2 jit_solution(700184288403528626)
XLA Ops:
  7.2 2.9 convert_element_type.173
  10.3 4.1 convert_bitcast_fusion
  14.4 2.2 copy-done.2
  16.6 1.8 slice.225
  18.6 1.2 fusion.77
  21.4 11.9 %share.8 = f32[8,1,4329]{2,1,0:T(1,128)} custom-call(f32[1,4329]{1,0:T(1,128)} %broadcast_in_dim.21.in_ref), custom_call_target="tpu_custom_call" | custom-call | tf_op jit(solution)/shard_map/share/pallas_call | solution.py:173
  33.3 0.9 copy.86
  34.5 0.8 pad_maximum_fusion.5.in_ref
  35.3 22.9 %share.9 = bf16[4,146,1186]{2,1,0:T(8,128)(2,1)} custom-call(bf16[146,1186]{1,0:T(8,128)(2,1)} %pad_maximum_fusion.5.in_ref), custom_call_target="tpu_custom_call" | custom-call | tf_op jit(solution)/shard_map/share/pallas_call | solution.py:173
  58.1 0.9 slice.172
  60.2 1.4 slice_bitcast_fusion.3
  62.5 0.7 reshape.243.in_ref
  63.2 12.6 %share.10 = f32[8,4,1296]{2,1,0:T(4,128)} custom-call(f32[8,4,1296]{2,1,0:T(4,128)} %reshape.243.in_ref), custom_call_target="tpu_custom_call" | custom-call | tf_op jit(solution)/shard_map/share/pallas_call | solution.py:173
  75.8 0.9 slice_reduce_fusion
  76.8 1.4 fusion.29.in_ref
  78.2 10.3 share.11
  88.5 0.8 reshape.244
  89.7 2.0 fusion.35
  91.9 0.9 dynamic-slice_bitcast_fusion
  92.8 1.0 collective-permute-start
  94.4 3.0 slice.220.refs_9_
  99.0 1.7 broadcast_in_dim.30.qkv_bias
  100.8 1.4 slice_reduce_fusion.10
  102.8 3.8 multiply_cosine_fusion
  106.7 1.8 concatenate.60
  109.9 0.9 add_convert_fusion.1
  110.8 1.3 broadcast_multiply_fusion
  112.1 3.7 fusion.2.tokens
  115.8 2.0 bitcast_add_fusion.2.in_ref
  117.8 18.8 %share.12 = f32[4,288,128]{2,1,0:T(8,128)} custom-call(f32[4,288,128]{2,1,0:T(8,128)} %bitcast_add_fusion.2.in_ref), custom_call_target="tpu_custom_call" | custom-call | tf_op jit(solution)/shard_map/share/pallas_call | solution.py:173
  136.5 1.1 reduce_sum.261
  138.6 172.0 %all-gather.4.cloned.1.call-done.wx = bf16[1152,9216]{1,0:T(8,128)(2,1)} async-done(((bf16[144,9216]{1,0:T(8,128)(2,1)}), bf16[1152,9216]{1,0:T(8,128)(2,1)}) %all-gather.4.cloned.1.call-update) | async-done | bytes 21233680 | tf_op jit(solution)/shard_map/all_gather | solution.py:1251
  310.5 95.5 %pipeline_forward.1 = (f32[4,256,1152]{2,1,0:T(8,128)}, bf16[4,256,1152]{2,1,0:T(8,128)(2,1)}, bf16[4,3456,256]{2,1,0:T(8,128)(2,1)}, bf16[4,256,1152]{2,1,0:T(8...) custom-call(f32[1,6912]{1,0:T(1,128)} %broadcast_in_dim.22.bias, ...), custom_call_target="tpu_custom_call" | custom-call | flops 33822867456 | bytes 107347968 | tf_op jit(solution)/shard_map/pipeline_forward/pallas_call | solution.py:1112
  406.1 2.7 reduce_sum.262
  408.7 3.1 multiply_reduce_fusion.3
  412.5 1.8 convert_reduce_fusion.4
  414.3 2.9 multiply_reduce_fusion.1
  417.8 2.9 subtract_multiply_fusion.head_grad
  420.7 289.5 %pipeline_backward.1 = (bf16[4,256,1152]{2,1,0:T(8,128)(2,1)}, bf16[4,256,4608]{2,1,0:T(8,128)(2,1)}, bf16[4,256,1152]{2,1,0:T(8,128)(2,1)}, bf16[4,256,3456]{2,...) custom-call(f32[4,6,1152]{2,1,0:T(8,128)} %reshape.246.ada, ...), custom_call_target="tpu_custom_call" | custom-call | flops 35634806784 | bytes 107347968 | tf_op jit(solution)/shard_map/pipeline_backward/pallas_call | solution.py:1137
  710.3 2.1 convert_reduce_fusion
  712.4 2.1 convolution_bitcast_fusion.3
  715.9 1.1 convolution_multiply_fusion.refs_11_
  717.0 292.9 %line_sums.1 = (f32[144,9216]{1,0:T(8,128)}, f32[576,1152]{1,0:T(8,128)}, bf16[144,9216]{1,0:T(8,128)(2,1)}, bf16[576,1152]{1,0:T(8,128)(2,1)}, bf16[144,9216]{1...) custom-call(bf16[1024,1152]{1,0:T(8,128)(2,1)} %bitcast.126, ...), custom_call_target="tpu_custom_call" | custom-call | flops 32614907904 | bytes 56623104 | tf_op jit(solution)/shard_map/line_sums/pallas_call | solution.py:546
  1009.9 1.0 slice_reduce_fusion.4
  1010.9 0.9 slice_reduce_fusion.5
  1011.8 3.2 fusion.5
  1016.6 0.8 broadcast_in_dim.28.in_ref
  1017.4 7.7 share.13
  1025.1 0.9 copy.85
  1028.6 2.8 convolution_bitcast_fusion
  1031.5 2.8 concatenate.65
  1034.4 1.4 constant_dynamic-slice_fusion
  1035.8 5.0 convert_add_fusion
  1040.7 6.4 pad_maximum_fusion
  1047.2 3.0 convert_add_fusion.1
  1050.8 0.8 multiply_reduce_fusion.6
  1052.2 1.3 multiply_reduce_fusion.5
  1053.5 3.0 multiply_reduce_fusion
  1060.4 7.6 share.14
  1068.0 1.3 reduce_sum.287.in_ref
  1069.3 5.8 share.15
  1077.7 3.4 multiply_subtract_fusion.2
  1081.2 7.4 multiply_subtract_fusion.1
  1088.6 20.7 %multiply_subtract_fusion = (f32[1,144,16128]{2,1,0:T(8,128)}, f32[1,144,16128]{2,1,0:T(8,128)}, f32[1,144,16128]{2,1,0:T(8,128)}) fusion(f32[1,144,16128]{2,1,0:T(8,128)} %param.25, f32[144,16128]{1,0:T(8,128)S(1)} %bitcast.106, f32[]{:T(128)S(6)} %min.3, f32[1,144,16128]{2,1,0:T(8,128)} %param.30, f32[1,144,16128]{2,1,0:T(8,128)} %param.35), kind=kLoop, calls=%fused_computation.5 | loop fusion | flops 37158912 | bytes 65028100 | tf_op jit(solution)/shard_map/sub | solution.py:1210
  (193 shorter events, 19.0 us)
Async XLA Ops:
  7.2 131.4 %all-gather.6.cloned.1.call-start = ((), (), s32[]{:S(2)}) async-start(), calls=%async_computation.1 | async-start | bytes 11943936 | tf_op jit(solution)/shard_map/all_gather | solution.py:1251
  10.2 300.3 %all-gather.4.cloned.1.call-start = ((), (), s32[]{:S(2)}) async-start(), calls=%async_computation | async-start | bytes 23887872 | tf_op jit(solution)/shard_map/all_gather | solution.py:1251
  14.4 2.2 copy-start.2
  16.5 1.9 copy-start.34
  16.5 1.9 copy-start.35
  16.5 1.9 copy-start.18
  16.5 2.0 copy-start.24
  16.5 3.9 copy-start.4
  16.6 4.1 copy-start.20
  34.2 63.1 %copy-start.9 = (f32[8,1,4329]{2,0,1:T(8,128)}, f32[8,1,4329]{2,0,1:T(8,128)S(1)}, u32[]{:S(2)}) copy-start(f32[8,1,4329]{2,0,1:T(8,128)S(1)} %copy.86) | copy-start | bytes 415588
  34.5 27.4 %copy-start.29 = (s32[32]{0:T(128)}, s32[32]{0:T(128)S(1)}, u32[]{:S(2)}) copy-start(s32[32]{0:T(128)S(1)} %convert_element_type.164) | copy-start | bytes 388
  61.6 30.1 %copy-start.10 = (bf16[144,1186]{1,0:T(8,128)(2,1)}, bf16[144,1186]{1,0:T(8,128)(2,1)S(1)}, u32[]{:S(2)}) copy-start(bf16[144,1186]{1,0:T(8,128)(2,1)S(1)} %get-tuple-element.107) | copy-start | bytes 1024708
  92.8 23.0 %collective-permute-start = (f32[4,288,128]{2,1,0:T(8,128)}, f32[4,288,128]{2,1,0:T(8,128)}, u32[]{:S(2)}, u32[]{:S(2)}) collective-permute-start(f32[4,288,128]{2,1,0:T(8,128)} %dynamic-slice_bitcast_fusion), channel_id=1, source_target_pairs={{0,1},{1,0},{2,3},{3,2},{4,5},{5,4},{6,7},{7,6},{8,9},{9,8},{10,11... | collective-permute-start | bytes 1769480 | tf_op jit(solution)/shard_map/ppermute | solution.py:201
  99.0 16.8 %copy-start.5 = (bf16[1152,16]{1,0:T(8,128)(2,1)}, bf16[1152,16]{1,0:T(8,128)(2,1)S(1)}, u32[]{:S(2)}) copy-start(bf16[1152,16]{1,0:T(8,128)(2,1)S(1)} %convert_element_type.170) | copy-start | bytes 110596
  112.1 25.6 %copy-start.15 = (f32[6912]{0:T(1024)S(1)}, f32[6912]{0:T(1024)}, u32[]{:S(2)}) copy-start(f32[6912]{0:T(1024)} %get-tuple-element.113) | copy-start | bytes 82948
  406.0 5.8 copy-start.6
  406.0 5.8 copy-start.12
  406.0 5.8 copy-start.22
  406.0 5.8 copy-start.23
  406.1 5.8 copy-start.33
  408.7 3.8 copy-start
  710.3 4.2 copy-start.13
  710.3 4.3 copy-start.8
  710.3 5.6 copy-start.11
  1009.9 5.2 copy-start.7
  1009.9 5.3 copy-start.16
  1009.9 6.6 copy-start.32
  1011.8 14.9 %copy-start.14 = (f32[8,4,144]{2,1,0:T(4,128)S(1)}, f32[8,4,144]{2,1,0:T(4,128)}, u32[]{:S(2)}) copy-start(f32[8,4,144]{2,1,0:T(4,128)} %share.11) | copy-start | bytes 55300
  1015.6 12.7 %copy-start.30 = (s32[32]{0:T(128)S(1)}, s32[32]{0:T(128)}, u32[]{:S(2)}) copy-start(s32[32]{0:T(128)} %copy-done.29) | copy-start | bytes 388
  1016.0 12.6 %copy-start.36 = (bf16[8,4,6912]{2,1,0:T(4,128)(2,1)S(1)}, bf16[8,4,6912]{2,1,0:T(4,128)(2,1)}, u32[]{:S(2)}) copy-start(bf16[8,4,6912]{2,1,0:T(4,128)(2,1)} %get-tuple-element.69) | copy-start | bytes 1327108
  1028.6 2.8 copy-start.31
  1028.6 2.8 copy-start.17
  1047.2 6.3 copy-start.1
  1053.5 23.6 %copy-start.19 = (f32[1444]{0:T(1024)S(1)}, f32[1444]{0:T(1024)}, u32[]{:S(2)}) copy-start(f32[1444]{0:T(1024)} %param.29) | copy-start | bytes 17332
  1053.5 23.6 %copy-start.25 = (f32[1444]{0:T(1024)S(1)}, f32[1444]{0:T(1024)}, u32[]{:S(2)}) copy-start(f32[1444]{0:T(1024)} %param.34) | copy-start | bytes 17332
  1053.5 23.6 %copy-start.26 = (f32[1444]{0:T(1024)S(1)}, f32[1444]{0:T(1024)}, u32[]{:S(2)}) copy-start(f32[1444]{0:T(1024)} %param.39) | copy-start | bytes 17332
  1077.1 4.1 copy-start.3
  1077.7 10.8 slice-start
  1081.2 7.4 slice-start.1
  1081.2 7.4 slice-start.2
  1088.6 20.7 %copy-start.21 = (f32[1,2016]{1,0:T(1,128)S(1)}, f32[1,2016]{1,0:T(1,128)}, u32[]{:S(2)}) copy-start(f32[1,2016]{1,0:T(1,128)} %param.27) | copy-start | bytes 24196
  1088.6 20.7 %copy-start.27 = (f32[1,2016]{1,0:T(1,128)S(1)}, f32[1,2016]{1,0:T(1,128)}, u32[]{:S(2)}) copy-start(f32[1,2016]{1,0:T(1,128)} %param.32) | copy-start | bytes 24196
  1088.6 20.7 %copy-start.28 = (f32[1,2016]{1,0:T(1,128)S(1)}, f32[1,2016]{1,0:T(1,128)}, u32[]{:S(2)}) copy-start(f32[1,2016]{1,0:T(1,128)} %param.37) | copy-start | bytes 24196
Sparse Core Ops, SparseCore 0:
  10.3 110.6 all-gather.5
  123.2 187.2 all-gather.3

commit v9 on v8

--- a/solution.py
+++ b/solution.py
@@ -784,13 +784,26 @@
     meet("section", sections, section)
     hop = hop_of(send, received, send_sem, recv_sem, lax.rem(section + 1, sections))
     residual = kept[RESIDUAL]
+    late = (PRE, ACT, SECOND, OUTPUT)
+
+    def saving(name, image):
+        return pltpu.make_async_copy(kept[name], outs[name].at[image], out_sem.at[name])
 
     @pl.loop(0, images)
     def run(image):
         saves = []
 
         def save(name):
-            saves.append(started(kept[name], outs[name].at[image], out_sem.at[name]))
+            copy = saving(name, image)
+            copy.start()
+            if name not in late:
+                saves.append(copy)
+
+        def settle(*names):
+            @pl.when(image > 0)
+            def wait():
+                for name in names:
+                    saving(name, image - 1).wait()
 
         @pl.when(section == 0)
         def take_tokens():
@@ -838,6 +851,7 @@
         save(MIDDLE)
         save(MIXED_TWO)
         wait_first(image, loads[4:5])
+        settle(PRE, ACT)
         for part, cols in enumerate(parts_of(FF, FF // D)):
             pre = (
                 matmul(kept[MIXED_TWO][...], wh_v[:, cols])
@@ -848,6 +862,7 @@
         save(PRE)
         save(ACT)
         wait_first(image, loads[5:])
+        settle(SECOND, OUTPUT)
         for part, cols in enumerate(parts_of(D, HOPS)):
             second = (
                 matmul(kept[ACT][...], ws_v[:, cols])
@@ -866,6 +881,9 @@
         save(OUTPUT)
         for copy in saves:
             copy.wait()
+
+    for name in late:
+        saving(name, images - 1).wait()
 
     @pl.when(section < sections - 1)
     def finish():
@@ -950,13 +968,27 @@
         meet("section", sections, section)
     hop = hop_of(send, received, send_sem, recv_sem, lax.rem(section + sections - 1, sections))
 
+    late = (D_QKV, D_RESIDUAL)
+    sums[...] = jnp.zeros_like(sums)
+
+    def saving(name, image):
+        source = send.at[image] if name == D_RESIDUAL else grads[name]
+        return pltpu.make_async_copy(source, outs[name].at[image], out_sem.at[name])
+
     @pl.loop(0, images)
     def run(image):
         saves = []
 
-        def save(name, value=None):
-            source = grads[name] if value is None else value
-            saves.append(started(source, outs[name].at[image], out_sem.at[name]))
+        def save(name):
+            copy = saving(name, image)
+            copy.start()
+            if name not in late:
+                saves.append(copy)
+
+        def settle(name):
+            @pl.when(image > 0)
+            def wait():
+                saving(name, image - 1).wait()
 
         def fetch_next(*names):
             @pl.when(image + 1 < images)
@@ -975,10 +1007,9 @@
             flow[...] = received[image].astype(jnp.float32)
 
         modulation = ada[image]
-        sums[...] = jnp.zeros_like(sums)
 
         def add_sum(row, values):
-            sums[row : row + 1] += jnp.sum(values, axis=0, keepdims=True)
+            sums[image, row : row + 1] += jnp.sum(values, axis=0, keepdims=True)
 
         fetching(SECOND, image).wait()
 
@@ -1043,10 +1074,11 @@
                 hop(image, part).start()
 
         fetch_next(RESIDUAL)
-        save(D_RESIDUAL, send.at[image])
+        settle(D_RESIDUAL)
+        save(D_RESIDUAL)
+        settle(D_QKV)
         grads[D_QKV][...] = qkv_grad[...].T
         save(D_QKV)
-        saves.append(started(sums, ada_out.at[image], x_sem))
         if direct:
 
             @pl.when(image == 0)
@@ -1061,6 +1093,10 @@
 
         for copy in saves:
             copy.wait()
+
+    started(sums, ada_out, x_sem).wait()
+    for name in late:
+        saving(name, images - 1).wait()
 
     @pl.when(section > 0)
     def finish():
@@ -1152,7 +1188,7 @@
             pltpu.VMEM((patches, D), jnp.float32),
             pltpu.VMEM((D, patches), jnp.bfloat16),
             pltpu.VMEM((3 * D, patches), jnp.bfloat16),
-            pltpu.VMEM((8, D), jnp.float32),
+            pltpu.VMEM((images, 8, D), jnp.float32),
         ]
         + [pltpu.VMEM((images, patches, D), jnp.bfloat16)] * 2
         + weight_scratch()

time: 1120 us -> 1120 us (level)
  no operation moved by 1% of the time
where the time goes in v9:
time: 1120 us; the launch traced here: 1110 us
  Pallas kernels  772 us (69%)
  waiting for transfers between devices  172 us (15%)
  other arithmetic  91.7 us (8%)
  local copies, waits for them, and re-layouts  33 us (3%)
  between operations  22.5 us (2%)
  matrix products  22.3 us (2%)
    pallas_call x1, Pallas kernels, line_sums(): pl.pallas_call(functools.partial(sums_kernel, units, rows, sections), out...  293 us
    pallas_call x1, Pallas kernels, pipeline_backward(): pl.pallas_call(functools.partial(backward_kernel, sections, images, direc...  288 us
    all_gather x2, waiting for transfers between devices, gathered(): return lax.all_gather(value, axis, axis=dim, tiled=True)  172 us
    pallas_call x8, Pallas kernels, share(): pl.pallas_call(functools.partial(share_kernel, axis, count, stride, perso...  97.5 us
    pallas_call x1, Pallas kernels, pipeline_forward(): pl.pallas_call(functools.partial(forward_kernel, sections, images), out_s...  93.8 us
    sub x5, other arithmetic, adam_update(): return (weight - RATE * (ratio + DECAY * weight), first_new, second_new)  32.8 us
  transfers between devices with their start and end apart: 3, of which 1 were waited for; matrix products, arithmetic and copies ran while one was open for 4% of the time, Pallas kernels for 7%

profile of v9, /device:TPU:0, one launch (start us, length us, event | category | flops | bytes accessed | tf_op | source)
XLA Modules:
  0.0 1114.8 jit_solution(14769922079356024868)
XLA Ops:
  7.2 2.9 convert_element_type.173
  10.3 4.1 convert_bitcast_fusion
  14.4 2.2 copy-done.2
  16.6 1.8 slice.225
  18.6 1.2 fusion.77
  21.4 11.9 %share.8 = f32[8,1,4329]{2,1,0:T(1,128)} custom-call(f32[1,4329]{1,0:T(1,128)} %broadcast_in_dim.21.in_ref), custom_call_target="tpu_custom_call" | custom-call | tf_op jit(solution)/shard_map/share/pallas_call | solution.py:173
  33.3 0.9 copy.86
  34.5 0.8 pad_maximum_fusion.5.in_ref
  35.3 22.9 %share.9 = bf16[4,146,1186]{2,1,0:T(8,128)(2,1)} custom-call(bf16[146,1186]{1,0:T(8,128)(2,1)} %pad_maximum_fusion.5.in_ref), custom_call_target="tpu_custom_call" | custom-call | tf_op jit(solution)/shard_map/share/pallas_call | solution.py:173
  58.1 0.9 slice.172
  60.2 1.4 slice_bitcast_fusion.3
  62.5 0.7 reshape.243.in_ref
  63.2 12.6 %share.10 = f32[8,4,1296]{2,1,0:T(4,128)} custom-call(f32[8,4,1296]{2,1,0:T(4,128)} %reshape.243.in_ref), custom_call_target="tpu_custom_call" | custom-call | tf_op jit(solution)/shard_map/share/pallas_call | solution.py:173
  75.8 0.9 slice_reduce_fusion
  76.8 1.4 fusion.29.in_ref
  78.2 10.3 share.11
  88.5 0.8 reshape.244
  89.7 2.0 fusion.35
  91.9 0.9 dynamic-slice_bitcast_fusion
  92.8 1.0 collective-permute-start
  94.4 3.0 slice.220.refs_9_
  99.0 1.7 broadcast_in_dim.30.qkv_bias
  100.8 1.4 slice_reduce_fusion.10
  102.8 3.8 multiply_cosine_fusion
  106.7 1.8 concatenate.60
  109.9 0.9 add_convert_fusion.1
  110.8 1.3 broadcast_multiply_fusion
  112.1 3.7 fusion.2.tokens
  115.8 2.0 bitcast_add_fusion.2.in_ref
  117.8 18.8 %share.12 = f32[4,288,128]{2,1,0:T(8,128)} custom-call(f32[4,288,128]{2,1,0:T(8,128)} %bitcast_add_fusion.2.in_ref), custom_call_target="tpu_custom_call" | custom-call | tf_op jit(solution)/shard_map/share/pallas_call | solution.py:173
  136.5 1.1 reduce_sum.261
  138.6 172.0 %all-gather.4.cloned.1.call-done.wx = bf16[1152,9216]{1,0:T(8,128)(2,1)} async-done(((bf16[144,9216]{1,0:T(8,128)(2,1)}), bf16[1152,9216]{1,0:T(8,128)(2,1)}) %all-gather.4.cloned.1.call-update) | async-done | bytes 21233680 | tf_op jit(solution)/shard_map/all_gather | solution.py:1287
  310.5 93.8 %pipeline_forward.1 = (f32[4,256,1152]{2,1,0:T(8,128)}, bf16[4,256,1152]{2,1,0:T(8,128)(2,1)}, bf16[4,3456,256]{2,1,0:T(8,128)(2,1)}, bf16[4,256,1152]{2,1,0:T(8...) custom-call(f32[1,6912]{1,0:T(1,128)} %broadcast_in_dim.22.bias, ...), custom_call_target="tpu_custom_call" | custom-call | flops 33822867456 | bytes 107347968 | tf_op jit(solution)/shard_map/pipeline_forward/pallas_call | solution.py:1148
  404.4 2.7 reduce_sum.262
  407.1 3.1 multiply_reduce_fusion.3
  410.8 1.8 convert_reduce_fusion.4
  412.7 2.9 multiply_reduce_fusion.1
  416.2 2.9 subtract_multiply_fusion.head_grad
  419.0 288.2 %pipeline_backward.1 = (bf16[4,256,1152]{2,1,0:T(8,128)(2,1)}, bf16[4,256,4608]{2,1,0:T(8,128)(2,1)}, bf16[4,256,1152]{2,1,0:T(8,128)(2,1)}, bf16[4,256,3456]{2,...) custom-call(f32[4,6,1152]{2,1,0:T(8,128)} %reshape.246.ada, ...), custom_call_target="tpu_custom_call" | custom-call | flops 35634806784 | bytes 107347968 | tf_op jit(solution)/shard_map/pipeline_backward/pallas_call | solution.py:1173
  707.3 2.1 convert_reduce_fusion
  709.4 2.1 convolution_bitcast_fusion.3
  712.9 1.1 convolution_multiply_fusion.refs_11_
  714.0 292.8 %line_sums.1 = (f32[144,9216]{1,0:T(8,128)}, f32[576,1152]{1,0:T(8,128)}, bf16[144,9216]{1,0:T(8,128)(2,1)}, bf16[576,1152]{1,0:T(8,128)(2,1)}, bf16[144,9216]{1...) custom-call(bf16[1024,1152]{1,0:T(8,128)(2,1)} %bitcast.126, ...), custom_call_target="tpu_custom_call" | custom-call | flops 32614907904 | bytes 56623104 | tf_op jit(solution)/shard_map/line_sums/pallas_call | solution.py:546
  1006.8 1.0 slice_reduce_fusion.4
  1007.8 0.9 slice_reduce_fusion.5
  1008.7 3.2 fusion.5
  1013.5 0.8 broadcast_in_dim.28.in_ref
  1014.3 7.7 share.13
  1022.0 0.9 copy.85
  1025.5 2.8 convolution_bitcast_fusion
  1028.5 2.6 concatenate.65
  1031.1 1.4 constant_dynamic-slice_fusion
  1032.5 5.0 convert_add_fusion
  1037.4 6.4 pad_maximum_fusion
  1043.9 3.0 convert_add_fusion.1
  1047.5 0.8 multiply_reduce_fusion.6
  1048.9 1.3 multiply_reduce_fusion.5
  1050.2 3.0 multiply_reduce_fusion
  1057.1 7.6 share.14
  1064.7 1.3 reduce_sum.287.in_ref
  1066.0 5.8 share.15
  1074.5 3.4 multiply_subtract_fusion.2
  1077.9 7.4 multiply_subtract_fusion.1
  1085.3 20.7 %multiply_subtract_fusion = (f32[1,144,16128]{2,1,0:T(8,128)}, f32[1,144,16128]{2,1,0:T(8,128)}, f32[1,144,16128]{2,1,0:T(8,128)}) fusion(f32[1,144,16128]{2,1,0:T(8,128)} %param.25, f32[144,16128]{1,0:T(8,128)S(1)} %bitcast.106, f32[]{:T(128)S(6)} %min.3, f32[1,144,16128]{2,1,0:T(8,128)} %param.30, f32[1,144,16128]{2,1,0:T(8,128)} %param.35), kind=kLoop, calls=%fused_computation.5 | loop fusion | flops 37158912 | bytes 65028100 | tf_op jit(solution)/shard_map/sub | solution.py:1246
  (193 shorter events, 19.0 us)
Async XLA Ops:
  7.2 131.4 %all-gather.6.cloned.1.call-start = ((), (), s32[]{:S(2)}) async-start(), calls=%async_computation.1 | async-start | bytes 11943936 | tf_op jit(solution)/shard_map/all_gather | solution.py:1287
  10.2 300.3 %all-gather.4.cloned.1.call-start = ((), (), s32[]{:S(2)}) async-start(), calls=%async_computation | async-start | bytes 23887872 | tf_op jit(solution)/shard_map/all_gather | solution.py:1287
  14.4 2.2 copy-start.2
  16.5 1.9 copy-start.34
  16.5 1.9 copy-start.35
  16.5 1.9 copy-start.18
  16.5 2.0 copy-start.24
  16.5 3.9 copy-start.4
  16.6 4.1 copy-start.20
  34.2 63.1 %copy-start.9 = (f32[8,1,4329]{2,0,1:T(8,128)}, f32[8,1,4329]{2,0,1:T(8,128)S(1)}, u32[]{:S(2)}) copy-start(f32[8,1,4329]{2,0,1:T(8,128)S(1)} %copy.86) | copy-start | bytes 415588
  34.5 27.4 %copy-start.29 = (s32[32]{0:T(128)}, s32[32]{0:T(128)S(1)}, u32[]{:S(2)}) copy-start(s32[32]{0:T(128)S(1)} %convert_element_type.164) | copy-start | bytes 388
  61.6 30.1 %copy-start.10 = (bf16[144,1186]{1,0:T(8,128)(2,1)}, bf16[144,1186]{1,0:T(8,128)(2,1)S(1)}, u32[]{:S(2)}) copy-start(bf16[144,1186]{1,0:T(8,128)(2,1)S(1)} %get-tuple-element.107) | copy-start | bytes 1024708
  92.8 23.0 %collective-permute-start = (f32[4,288,128]{2,1,0:T(8,128)}, f32[4,288,128]{2,1,0:T(8,128)}, u32[]{:S(2)}, u32[]{:S(2)}) collective-permute-start(f32[4,288,128]{2,1,0:T(8,128)} %dynamic-slice_bitcast_fusion), channel_id=1, source_target_pairs={{0,1},{1,0},{2,3},{3,2},{4,5},{5,4},{6,7},{7,6},{8,9},{9,8},{10,11... | collective-permute-start | bytes 1769480 | tf_op jit(solution)/shard_map/ppermute | solution.py:201
  99.0 16.8 %copy-start.5 = (bf16[1152,16]{1,0:T(8,128)(2,1)}, bf16[1152,16]{1,0:T(8,128)(2,1)S(1)}, u32[]{:S(2)}) copy-start(bf16[1152,16]{1,0:T(8,128)(2,1)S(1)} %convert_element_type.170) | copy-start | bytes 110596
  112.1 25.6 %copy-start.15 = (f32[6912]{0:T(1024)S(1)}, f32[6912]{0:T(1024)}, u32[]{:S(2)}) copy-start(f32[6912]{0:T(1024)} %get-tuple-element.113) | copy-start | bytes 82948
  404.3 5.8 copy-start.6
  404.4 5.8 copy-start.12
  404.4 5.8 copy-start.22
  404.4 5.8 copy-start.23
  404.4 5.8 copy-start.33
  407.1 3.8 copy-start
  707.2 4.2 copy-start.13
  707.2 4.3 copy-start.8
  707.3 5.6 copy-start.11
  1006.8 5.2 copy-start.7
  1006.8 5.3 copy-start.16
  1006.8 6.6 copy-start.32
  1008.7 14.9 %copy-start.14 = (f32[8,4,144]{2,1,0:T(4,128)S(1)}, f32[8,4,144]{2,1,0:T(4,128)}, u32[]{:S(2)}) copy-start(f32[8,4,144]{2,1,0:T(4,128)} %share.11) | copy-start | bytes 55300
  1012.5 12.7 %copy-start.30 = (s32[32]{0:T(128)S(1)}, s32[32]{0:T(128)}, u32[]{:S(2)}) copy-start(s32[32]{0:T(128)} %copy-done.29) | copy-start | bytes 388
  1012.9 12.6 %copy-start.36 = (bf16[8,4,6912]{2,1,0:T(4,128)(2,1)S(1)}, bf16[8,4,6912]{2,1,0:T(4,128)(2,1)}, u32[]{:S(2)}) copy-start(bf16[8,4,6912]{2,1,0:T(4,128)(2,1)} %get-tuple-element.69) | copy-start | bytes 1327108
  1025.5 2.8 copy-start.31
  1025.5 2.8 copy-start.17
  1043.9 6.3 copy-start.1
  1050.2 23.6 %copy-start.19 = (f32[1444]{0:T(1024)S(1)}, f32[1444]{0:T(1024)}, u32[]{:S(2)}) copy-start(f32[1444]{0:T(1024)} %param.29) | copy-start | bytes 17332
  1050.2 23.6 %copy-start.25 = (f32[1444]{0:T(1024)S(1)}, f32[1444]{0:T(1024)}, u32[]{:S(2)}) copy-start(f32[1444]{0:T(1024)} %param.34) | copy-start | bytes 17332
  1050.2 23.6 %copy-start.26 = (f32[1444]{0:T(1024)S(1)}, f32[1444]{0:T(1024)}, u32[]{:S(2)}) copy-start(f32[1444]{0:T(1024)} %param.39) | copy-start | bytes 17332
  1073.8 4.1 copy-start.3
  1074.5 10.8 slice-start
  1077.9 7.4 slice-start.1
  1077.9 7.4 slice-start.2
  1085.3 20.7 %copy-start.21 = (f32[1,2016]{1,0:T(1,128)S(1)}, f32[1,2016]{1,0:T(1,128)}, u32[]{:S(2)}) copy-start(f32[1,2016]{1,0:T(1,128)} %param.27) | copy-start | bytes 24196
  1085.3 20.7 %copy-start.27 = (f32[1,2016]{1,0:T(1,128)S(1)}, f32[1,2016]{1,0:T(1,128)}, u32[]{:S(2)}) copy-start(f32[1,2016]{1,0:T(1,128)} %param.32) | copy-start | bytes 24196
  1085.3 20.7 %copy-start.28 = (f32[1,2016]{1,0:T(1,128)S(1)}, f32[1,2016]{1,0:T(1,128)}, u32[]{:S(2)}) copy-start(f32[1,2016]{1,0:T(1,128)} %param.37) | copy-start | bytes 24196
Sparse Core Ops, SparseCore 0:
  10.3 110.6 all-gather.5
  123.2 187.2 all-gather.3

commit v10 on v9

--- a/solution.py
+++ b/solution.py
@@ -188,6 +188,49 @@
     if lax.axis_size(axis) > DIRECT:
         return lax.all_gather(value, axis)
     return share(value, axis, False, ident)
+
+
+def share_all_kernel(sections, count, in_ref, out_ref, send_sem, recv_sem):
+    section, here = (lax.axis_index("section"), lax.axis_index("dp"))
+    targets = [
+        {"section": lax.rem(section + i // count, sections), "dp": lax.rem(here + i % count, count)}
+        for i in range(1, sections * count)
+    ]
+    barrier = pltpu.get_barrier_semaphore()
+    for target in targets:
+        pl.semaphore_signal(barrier, inc=1, device_id=target, device_id_type=MESH)
+    pl.semaphore_wait(barrier, len(targets))
+    copies = []
+    for i, target in enumerate(targets):
+        copy = pltpu.make_async_remote_copy(
+            src_ref=in_ref,
+            dst_ref=out_ref.at[section, here],
+            send_sem=send_sem.at[i],
+            recv_sem=recv_sem.at[i],
+            device_id=target,
+            device_id_type=MESH,
+        )
+        copy.start()
+        copies.append(copy)
+    out_ref[section, here] = in_ref[...]
+    for copy in copies:
+        copy.wait()
+
+
+def sum_all(value, ident):
+    sections, count = (lax.axis_size("section"), lax.axis_size("dp"))
+    if count != DIRECT:
+        return lax.psum(value, ("section", "dp"))
+    shared = pl.pallas_call(
+        functools.partial(share_all_kernel, sections, count),
+        out_shape=jax.ShapeDtypeStruct((sections, count) + value.shape, value.dtype),
+        in_specs=[pl.BlockSpec(memory_space=pltpu.VMEM)],
+        out_specs=pl.BlockSpec(memory_space=pltpu.VMEM),
+        scratch_shapes=[pltpu.SemaphoreType.DMA((sections * count - 1,))] * 2,
+        compiler_params=pltpu.CompilerParams(collective_id=ident, has_side_effects=True),
+        name="share_all",
+    )(value)
+    return jnp.sum(shared, axis=(0, 1))
 
 
 def exchanged_sum(value, ident):
@@ -784,26 +827,13 @@
     meet("section", sections, section)
     hop = hop_of(send, received, send_sem, recv_sem, lax.rem(section + 1, sections))
     residual = kept[RESIDUAL]
-    late = (PRE, ACT, SECOND, OUTPUT)
-
-    def saving(name, image):
-        return pltpu.make_async_copy(kept[name], outs[name].at[image], out_sem.at[name])
 
     @pl.loop(0, images)
     def run(image):
         saves = []
 
         def save(name):
-            copy = saving(name, image)
-            copy.start()
-            if name not in late:
-                saves.append(copy)
-
-        def settle(*names):
-            @pl.when(image > 0)
-            def wait():
-                for name in names:
-                    saving(name, image - 1).wait()
+            saves.append(started(kept[name], outs[name].at[image], out_sem.at[name]))
 
         @pl.when(section == 0)
         def take_tokens():
@@ -851,7 +881,6 @@
         save(MIDDLE)
         save(MIXED_TWO)
         wait_first(image, loads[4:5])
-        settle(PRE, ACT)
         for part, cols in enumerate(parts_of(FF, FF // D)):
             pre = (
                 matmul(kept[MIXED_TWO][...], wh_v[:, cols])
@@ -862,7 +891,6 @@
         save(PRE)
         save(ACT)
         wait_first(image, loads[5:])
-        settle(SECOND, OUTPUT)
         for part, cols in enumerate(parts_of(D, HOPS)):
             second = (
                 matmul(kept[ACT][...], ws_v[:, cols])
@@ -881,9 +909,6 @@
         save(OUTPUT)
         for copy in saves:
             copy.wait()
-
-    for name in late:
-        saving(name, images - 1).wait()
 
     @pl.when(section < sections - 1)
     def finish():
@@ -1470,8 +1495,7 @@
         + dp_zero * jnp.sum(sbias_shard * sbias_shard)
     )
     pair = jnp.broadcast_to(jnp.stack([squares, loss_part])[:, None], (2, 128))
-    pair = jnp.sum(spread(pair, "dp", 14), axis=0)
-    pair = jnp.sum(spread(pair, "section", 15), axis=0)
+    pair = sum_all(pair, 14)
     norm_square, loss = (pair[0, 0], pair[1, 0])
     grad_norm = jnp.sqrt(norm_square)
     scaling = jnp.minimum(1.0, CLIP / grad_norm)

time: 1120 us -> 1120 us (level)
    pallas_call x8 -> x6, Pallas kernels: 97.5 us -> 84.1 us  [share(): pl.pallas_call(functools.partial(share_kernel, axis, count, stride, perso...]
where the time goes in v10:
time: 1120 us; the launch traced here: 1110 us
  Pallas kernels  771 us (69%)
  waiting for transfers between devices  172 us (15%)
  other arithmetic  90.6 us (8%)
  local copies, waits for them, and re-layouts  33 us (3%)
  between operations  22.5 us (2%)
  matrix products  22.3 us (2%)
    pallas_call x1, Pallas kernels, line_sums(): pl.pallas_call(functools.partial(sums_kernel, units, rows, sections), out...  293 us
    pallas_call x1, Pallas kernels, pipeline_backward(): pl.pallas_call(functools.partial(backward_kernel, sections, images, direc...  288 us
    all_gather x2, waiting for transfers between devices, gathered(): return lax.all_gather(value, axis, axis=dim, tiled=True)  172 us
    pallas_call x1, Pallas kernels, pipeline_forward(): pl.pallas_call(functools.partial(forward_kernel, sections, images), out_s...  95.5 us
    pallas_call x6, Pallas kernels, share(): pl.pallas_call(functools.partial(share_kernel, axis, count, stride, perso...  84.1 us
    sub x5, other arithmetic, adam_update(): return (weight - RATE * (ratio + DECAY * weight), first_new, second_new)  32.8 us
  transfers between devices with their start and end apart: 3, of which 1 were waited for; matrix products, arithmetic and copies ran while one was open for 4% of the time, Pallas kernels for 7%

profile of v10, /device:TPU:0, one launch (start us, length us, event | category | flops | bytes accessed | tf_op | source)
XLA Modules:
  0.0 1112.0 jit_solution(4765183043585966606)
XLA Ops:
  7.2 2.9 convert_element_type.173
  10.3 4.1 convert_bitcast_fusion
  14.4 2.2 copy-done.2
  16.6 1.8 slice.225
  18.6 1.2 fusion.77
  21.4 11.9 %share.6 = f32[8,1,4329]{2,1,0:T(1,128)} custom-call(f32[1,4329]{1,0:T(1,128)} %broadcast_in_dim.21.in_ref), custom_call_target="tpu_custom_call" | custom-call | tf_op jit(solution)/shard_map/share/pallas_call | solution.py:173
  33.3 0.9 copy.86
  34.5 0.8 pad_maximum_fusion.5.in_ref
  35.3 22.9 %share.7 = bf16[4,146,1186]{2,1,0:T(8,128)(2,1)} custom-call(bf16[146,1186]{1,0:T(8,128)(2,1)} %pad_maximum_fusion.5.in_ref), custom_call_target="tpu_custom_call" | custom-call | tf_op jit(solution)/shard_map/share/pallas_call | solution.py:173
  58.1 0.9 slice.172
  60.2 1.4 slice_bitcast_fusion.3
  62.5 0.7 reshape.243.in_ref
  63.2 12.6 %share.8 = f32[8,4,1296]{2,1,0:T(4,128)} custom-call(f32[8,4,1296]{2,1,0:T(4,128)} %reshape.243.in_ref), custom_call_target="tpu_custom_call" | custom-call | tf_op jit(solution)/shard_map/share/pallas_call | solution.py:173
  75.8 0.9 slice_reduce_fusion
  76.8 1.4 fusion.29.in_ref
  78.2 10.3 share.9
  88.5 0.8 reshape.244
  89.7 2.0 fusion.35
  91.9 0.9 dynamic-slice_bitcast_fusion
  92.8 1.0 collective-permute-start
  94.4 3.0 slice.220.refs_9_
  99.0 1.7 broadcast_in_dim.30.qkv_bias
  100.8 1.4 slice_reduce_fusion.10
  102.8 3.8 multiply_cosine_fusion
  106.7 1.8 concatenate.60
  109.9 0.9 add_convert_fusion.1
  110.8 1.3 broadcast_multiply_fusion
  112.1 3.7 fusion.2.tokens
  115.8 2.0 bitcast_add_fusion.2.in_ref
  117.8 18.8 %share.10 = f32[4,288,128]{2,1,0:T(8,128)} custom-call(f32[4,288,128]{2,1,0:T(8,128)} %bitcast_add_fusion.2.in_ref), custom_call_target="tpu_custom_call" | custom-call | tf_op jit(solution)/shard_map/share/pallas_call | solution.py:173
  136.6 1.1 reduce_sum.252
  137.8 0.7 reshape.246.ada
  138.6 172.0 %all-gather.4.cloned.1.call-done.wx = bf16[1152,9216]{1,0:T(8,128)(2,1)} async-done(((bf16[144,9216]{1,0:T(8,128)(2,1)}), bf16[1152,9216]{1,0:T(8,128)(2,1)}) %all-gather.4.cloned.1.call-update) | async-done | bytes 21233680 | tf_op jit(solution)/shard_map/all_gather | solution.py:1312
  310.5 95.5 %pipeline_forward.1 = (f32[4,256,1152]{2,1,0:T(8,128)}, bf16[4,256,1152]{2,1,0:T(8,128)(2,1)}, bf16[4,3456,256]{2,1,0:T(8,128)(2,1)}, bf16[4,256,1152]{2,1,0:T(8...) custom-call(f32[1,6912]{1,0:T(1,128)} %broadcast_in_dim.22.bias, ...), custom_call_target="tpu_custom_call" | custom-call | flops 33822867456 | bytes 107347968 | tf_op jit(solution)/shard_map/pipeline_forward/pallas_call | solution.py:1173
  406.1 2.7 reduce_sum.253
  408.8 3.1 multiply_reduce_fusion.3
  412.5 1.8 convert_reduce_fusion.4
  414.3 2.9 multiply_reduce_fusion.1
  417.8 2.9 subtract_multiply_fusion.head_grad
  420.7 288.3 %pipeline_backward.1 = (bf16[4,256,1152]{2,1,0:T(8,128)(2,1)}, bf16[4,256,4608]{2,1,0:T(8,128)(2,1)}, bf16[4,256,1152]{2,1,0:T(8,128)(2,1)}, bf16[4,256,3456]{2,...) custom-call(f32[4,6,1152]{2,1,0:T(8,128)} %reshape.246.ada, ...), custom_call_target="tpu_custom_call" | custom-call | flops 35634806784 | bytes 107347968 | tf_op jit(solution)/shard_map/pipeline_backward/pallas_call | solution.py:1198
  709.1 2.1 convert_reduce_fusion
  711.2 2.1 convolution_bitcast_fusion.3
  714.7 1.1 convolution_multiply_fusion.refs_11_
  715.8 292.8 %line_sums.1 = (f32[144,9216]{1,0:T(8,128)}, f32[576,1152]{1,0:T(8,128)}, bf16[144,9216]{1,0:T(8,128)(2,1)}, bf16[576,1152]{1,0:T(8,128)(2,1)}, bf16[144,9216]{1...) custom-call(bf16[1024,1152]{1,0:T(8,128)(2,1)} %bitcast.126, ...), custom_call_target="tpu_custom_call" | custom-call | flops 32614907904 | bytes 56623104 | tf_op jit(solution)/shard_map/line_sums/pallas_call | solution.py:589
  1008.6 1.0 slice_reduce_fusion.4
  1009.6 0.9 slice_reduce_fusion.5
  1010.5 3.2 fusion.5
  1015.3 0.8 broadcast_in_dim.28.in_ref
  1016.1 7.7 share.11
  1023.8 0.9 copy.85
  1027.3 2.8 convolution_bitcast_fusion
  1030.2 2.6 concatenate.65
  1032.8 1.4 constant_dynamic-slice_fusion
  1034.2 5.0 convert_add_fusion
  1039.2 6.4 pad_maximum_fusion
  1045.6 3.0 convert_add_fusion.1
  1049.3 0.8 multiply_reduce_fusion.6
  1050.6 1.3 multiply_reduce_fusion.5
  1051.9 3.0 multiply_reduce_fusion
  1058.9 10.0 share_all.1
  1068.9 0.8 reduce_sum.278
  1071.7 3.4 multiply_subtract_fusion.2
  1075.1 7.4 multiply_subtract_fusion.1
  1082.5 20.7 %multiply_subtract_fusion = (f32[1,144,16128]{2,1,0:T(8,128)}, f32[1,144,16128]{2,1,0:T(8,128)}, f32[1,144,16128]{2,1,0:T(8,128)}) fusion(f32[1,144,16128]{2,1,0:T(8,128)} %param.25, f32[144,16128]{1,0:T(8,128)S(1)} %bitcast.106, f32[]{:T(128)S(6)} %min.3, f32[1,144,16128]{2,1,0:T(8,128)} %param.30, f32[1,144,16128]{2,1,0:T(8,128)} %param.35), kind=kLoop, calls=%fused_computation.5 | loop fusion | flops 37158912 | bytes 65028100 | tf_op jit(solution)/shard_map/sub | solution.py:1271
  (191 shorter events, 17.6 us)
Async XLA Ops:
  7.2 131.4 %all-gather.6.cloned.1.call-start = ((), (), s32[]{:S(2)}) async-start(), calls=%async_computation.1 | async-start | bytes 11943936 | tf_op jit(solution)/shard_map/all_gather | solution.py:1312
  10.2 300.3 %all-gather.4.cloned.1.call-start = ((), (), s32[]{:S(2)}) async-start(), calls=%async_computation | async-start | bytes 23887872 | tf_op jit(solution)/shard_map/all_gather | solution.py:1312
  14.4 2.2 copy-start.2
  16.5 1.9 copy-start.34
  16.5 1.9 copy-start.35
  16.5 1.9 copy-start.18
  16.5 2.0 copy-start.24
  16.5 3.9 copy-start.4
  16.6 4.1 copy-start.20
  34.2 63.1 %copy-start.9 = (f32[8,1,4329]{2,0,1:T(8,128)}, f32[8,1,4329]{2,0,1:T(8,128)S(1)}, u32[]{:S(2)}) copy-start(f32[8,1,4329]{2,0,1:T(8,128)S(1)} %copy.86) | copy-start | bytes 415588
  34.5 27.4 %copy-start.29 = (s32[32]{0:T(128)}, s32[32]{0:T(128)S(1)}, u32[]{:S(2)}) copy-start(s32[32]{0:T(128)S(1)} %convert_element_type.164) | copy-start | bytes 388
  61.6 30.1 %copy-start.10 = (bf16[144,1186]{1,0:T(8,128)(2,1)}, bf16[144,1186]{1,0:T(8,128)(2,1)S(1)}, u32[]{:S(2)}) copy-start(bf16[144,1186]{1,0:T(8,128)(2,1)S(1)} %get-tuple-element.107) | copy-start | bytes 1024708
  92.8 23.0 %collective-permute-start = (f32[4,288,128]{2,1,0:T(8,128)}, f32[4,288,128]{2,1,0:T(8,128)}, u32[]{:S(2)}, u32[]{:S(2)}) collective-permute-start(f32[4,288,128]{2,1,0:T(8,128)} %dynamic-slice_bitcast_fusion), channel_id=1, source_target_pairs={{0,1},{1,0},{2,3},{3,2},{4,5},{5,4},{6,7},{7,6},{8,9},{9,8},{10,11... | collective-permute-start | bytes 1769480 | tf_op jit(solution)/shard_map/ppermute | solution.py:244
  99.0 16.8 %copy-start.5 = (bf16[1152,16]{1,0:T(8,128)(2,1)}, bf16[1152,16]{1,0:T(8,128)(2,1)S(1)}, u32[]{:S(2)}) copy-start(bf16[1152,16]{1,0:T(8,128)(2,1)S(1)} %convert_element_type.170) | copy-start | bytes 110596
  112.1 25.7 %copy-start.15 = (f32[6912]{0:T(1024)S(1)}, f32[6912]{0:T(1024)}, u32[]{:S(2)}) copy-start(f32[6912]{0:T(1024)} %get-tuple-element.113) | copy-start | bytes 82948
  406.0 5.8 copy-start.6
  406.0 5.8 copy-start.12
  406.0 5.8 copy-start.22
  406.1 5.8 copy-start.23
  406.1 5.8 copy-start.33
  408.7 3.8 copy-start
  709.0 4.2 copy-start.13
  709.0 4.3 copy-start.8
  709.1 5.6 copy-start.11
  1008.5 5.2 copy-start.7
  1008.5 5.3 copy-start.16
  1008.6 6.6 copy-start.32
  1010.5 14.9 %copy-start.14 = (f32[8,4,144]{2,1,0:T(4,128)S(1)}, f32[8,4,144]{2,1,0:T(4,128)}, u32[]{:S(2)}) copy-start(f32[8,4,144]{2,1,0:T(4,128)} %share.9) | copy-start | bytes 55300
  1014.3 12.7 %copy-start.30 = (s32[32]{0:T(128)S(1)}, s32[32]{0:T(128)}, u32[]{:S(2)}) copy-start(s32[32]{0:T(128)} %copy-done.29) | copy-start | bytes 388
  1014.6 12.6 %copy-start.36 = (bf16[8,4,6912]{2,1,0:T(4,128)(2,1)S(1)}, bf16[8,4,6912]{2,1,0:T(4,128)(2,1)}, u32[]{:S(2)}) copy-start(bf16[8,4,6912]{2,1,0:T(4,128)(2,1)} %get-tuple-element.69) | copy-start | bytes 1327108
  1027.2 2.8 copy-start.31
  1027.2 2.8 copy-start.17
  1045.6 6.3 copy-start.1
  1051.9 19.1 %copy-start.19 = (f32[1444]{0:T(1024)S(1)}, f32[1444]{0:T(1024)}, u32[]{:S(2)}) copy-start(f32[1444]{0:T(1024)} %param.29) | copy-start | bytes 17332
  1051.9 19.1 %copy-start.25 = (f32[1444]{0:T(1024)S(1)}, f32[1444]{0:T(1024)}, u32[]{:S(2)}) copy-start(f32[1444]{0:T(1024)} %param.34) | copy-start | bytes 17332
  1051.9 19.1 %copy-start.26 = (f32[1444]{0:T(1024)S(1)}, f32[1444]{0:T(1024)}, u32[]{:S(2)}) copy-start(f32[1444]{0:T(1024)} %param.39) | copy-start | bytes 17332
  1071.0 4.1 copy-start.3
  1071.7 10.8 slice-start
  1075.1 7.4 slice-start.1
  1075.1 7.4 slice-start.2
  1082.5 20.7 %copy-start.21 = (f32[1,2016]{1,0:T(1,128)S(1)}, f32[1,2016]{1,0:T(1,128)}, u32[]{:S(2)}) copy-start(f32[1,2016]{1,0:T(1,128)} %param.27) | copy-start | bytes 24196
  1082.5 20.7 %copy-start.27 = (f32[1,2016]{1,0:T(1,128)S(1)}, f32[1,2016]{1,0:T(1,128)}, u32[]{:S(2)}) copy-start(f32[1,2016]{1,0:T(1,128)} %param.32) | copy-start | bytes 24196
  1082.5 20.7 %copy-start.28 = (f32[1,2016]{1,0:T(1,128)S(1)}, f32[1,2016]{1,0:T(1,128)}, u32[]{:S(2)}) copy-start(f32[1,2016]{1,0:T(1,128)} %param.37) | copy-start | bytes 24196
Sparse Core Ops, SparseCore 0:
  10.3 110.6 all-gather.5
  123.2 187.2 all-gather.3
